TPU v7x, 32 devices: a whole 2x2x4 slice. The times are simulated.
32 devices in a mesh: dp: 16 (over z, y, core), mp: 2 (over x).
Axes of the slice: x: 2, y: 2, z: 4, core: 2. Of those that a mesh axis runs over, the one named last changes fastest.
Arguments:
- inputs: bfloat16 [16384, 768], P('dp'), may hold values from -8 to 8
- encoded: bfloat16 [16384, 768], P('dp'), may hold values from -6 to 6
- cotangent: bfloat16 [16384, 768], P('dp'), may hold values from -6 to 6
- buckets: int32 [512], replicated, may hold values from 0 to 31, as said below
- rel_table: bfloat16 [12, 32], P('mp'), may hold values from -6 to 6
- query_self: bfloat16 [768, 768], P('dp', 'mp'), may hold values from -0.02734375 to 0.02734375
- keys_self: bfloat16 [768, 768], P('dp', 'mp'), may hold values from -0.21875 to 0.21875
- values_self: bfloat16 [768, 768], P('dp', 'mp'), may hold values from -0.21875 to 0.21875
- output_self: bfloat16 [768, 768], P('mp', 'dp'), may hold values from -0.875 to 0.875
- query_cross: bfloat16 [768, 768], P('dp', 'mp'), may hold values from -0.02734375 to 0.02734375
- keys_cross: bfloat16 [768, 768], P('dp', 'mp'), may hold values from -0.21875 to 0.21875
- values_cross: bfloat16 [768, 768], P('dp', 'mp'), may hold values from -0.21875 to 0.21875
- output_cross: bfloat16 [768, 768], P('mp', 'dp'), may hold values from -1.75 to 1.75
- gate_weight: bfloat16 [768, 2048], P('dp', 'mp'), may hold values from -0.21875 to 0.21875
- up_weight: bfloat16 [768, 2048], P('dp', 'mp'), may hold values from -0.21875 to 0.21875
- down_weight: bfloat16 [2048, 768], P('mp', 'dp'), may hold values from -0.125 to 0.125
- gain_first: bfloat16 [768], P('dp'), may hold values from 0.099609375 to 1.8984375
- gain_second: bfloat16 [768], P('dp'), may hold values from 0.099609375 to 1.8984375
- gain_third: bfloat16 [768], P('dp'), may hold values from 0.099609375 to 1.8984375
Outputs:
- layer_output: float32 [16384, 768], P('dp')
- input_gradient: float32 [16384, 768], P('dp')
- encoded_gradient: float32 [16384, 768], P('dp')
- table_gradient: float32 [12, 32], P('mp')
- query_self_gradient: float32 [768, 768], P('dp', 'mp')
- keys_self_gradient: float32 [768, 768], P('dp', 'mp')
- values_self_gradient: float32 [768, 768], P('dp', 'mp')
- output_self_gradient: float32 [768, 768], P('mp', 'dp')
- query_cross_gradient: float32 [768, 768], P('dp', 'mp')
- keys_cross_gradient: float32 [768, 768], P('dp', 'mp')
- values_cross_gradient: float32 [768, 768], P('dp', 'mp')
- output_cross_gradient: float32 [768, 768], P('mp', 'dp')
- gate_weight_gradient: float32 [768, 2048], P('dp', 'mp')
- up_weight_gradient: float32 [768, 2048], P('dp', 'mp')
- down_weight_gradient: float32 [2048, 768], P('mp', 'dp')
- gain_first_gradient: float32 [768], P('dp')
- gain_second_gradient: float32 [768], P('dp')
- gain_third_gradient: float32 [768], P('dp')
Inputs may be any that keep to these rules, and one draw needn't show every extreme that they name: `buckets`: the bucket of offset o is o for o < 16; beyond it never falls, rises by at most one from one offset to the next, and is 31 at offset 512 - 1.
All inputs are finite; a program needn't handle non-finite values.
Results may differ from a plain program's by a relative error of at most 0.02.
Values may be sent and summed in bfloat16 or wider, within the bound.
No kernel may reach another device: no remote copies, remote signals or barrier semaphores. Data moves between devices by JAX's collectives and lax.ppermute only.
A program may use at most 256 MiB of HBM per device.

v0:
```python
import jax
import jax.numpy as jnp
from jax import lax
from jax.experimental import pallas as pl
from jax.experimental.pallas import tpu as pltpu
from jax.sharding import PartitionSpec as P


DH = 64
NB = 32
L = 512
LANE = 128
QB = 128
EPS = 1e-06
NEG = -1e30
GELU_C = 0.7978845608028654
GELU_A = 0.044715
AXES = ("dp", "mp")
F32 = jnp.float32
BF16 = jnp.bfloat16
VMEM_LIMIT = 58 * 1024 * 1024


def nn(left, right):
    return lax.dot_general(left, right, (((1,), (0,)), ((), ())), preferred_element_type=F32)


def nt(left, right):
    return lax.dot_general(left, right, (((1,), (1,)), ((), ())), preferred_element_type=F32)


class Grid:
    def __init__(self, n_dp, n_mp):
        assert n_mp == 2 and n_dp % 8 == 0
        self.n_dp, self.n_mp = n_dp, n_mp
        self.n_z = n_dp // 4

    def perm(self, move):
        pairs = []
        for z in range(self.n_z):
            for y in range(2):
                for c in range(2):
                    for m in range(2):
                        tz, ty, tc, tm = move(z, y, c, m)
                        pairs.append(
                            (
                                (((z * 2 + y) * 2) + c) * 2 + m,
                                (((tz * 2 + ty) * 2) + tc) * 2 + tm,
                            )
                        )
        return pairs

    def send(self, v, move):
        return lax.ppermute(v, AXES, self.perm(move))

    def swap_m(self, v):
        return self.send(v, lambda z, y, c, m: (z, y, c, 1 - m))

    def swap_y(self, v):
        return self.send(v, lambda z, y, c, m: (z, 1 - y, c, m))

    def swap_c(self, v):
        return self.send(v, lambda z, y, c, m: (z, y, 1 - c, m))

    def shift_z(self, v, d):
        n = self.n_z
        return self.send(v, lambda z, y, c, m: ((z + d) % n, y, c, m))


def place():
    dp = lax.axis_index("dp")
    return dp // 4, (dp // 2) % 2, dp % 2, lax.axis_index("mp")


def gather(grid, block):
    rows, cols = block.shape
    n = grid.n_z
    z, y, c, _ = place()
    got = [block] + [grid.shift_z(block, d) for d in range(1, n)]
    own = jnp.zeros((n, rows, cols), block.dtype)
    for d in range(n):
        own = lax.dynamic_update_slice(own, got[d][None], (lax.rem(z - d + n, n), 0, 0))
    half = n // 2
    by_m = grid.swap_m(own)
    by_y = grid.swap_y(own)
    part_a = by_m[:half]
    part_b = by_y[half:]
    diag_a = grid.swap_y(part_a)
    diag_b = grid.swap_m(part_b)
    pieces = [(own, 0, 0, 0), (by_y, 0, 1, 0), (by_m, 1, 0, 0), (diag_a, 1, 1, 0), (diag_b, 1, 1, half)]
    out = [(a, m, b, 0, j) for a, m, b, j in pieces]
    out += [(grid.swap_c(p[0]),) + p[1:3] + (1, p[3]) for p in pieces]
    if rows % 16 == 0:
        return out
    stacks = []
    for m in range(2):
        for b in range(2):
            for e in range(2):
                mine = sorted((p for p in out if p[1:4] == (m, b, e)), key=lambda p: p[4])
                stacks.append(jnp.concatenate([p[0] for p in mine], axis=0))
    whole = jnp.stack(stacks).reshape(2, 2, 2, n, rows, cols)
    whole = jnp.take(whole, jnp.arange(2) ^ y, axis=1)
    whole = jnp.take(whole, jnp.arange(2) ^ c, axis=2)
    whole = whole.transpose(0, 3, 1, 2, 4, 5).reshape(2, n * 4 * rows, cols)
    return [(whole[m], m, None, None, 0) for m in range(2)]


class Weights:
    def __init__(self, pieces, n_z, half=None):
        chosen = [p for p in pieces if half is None or p[1] == half]
        self.arrays = [p[0] for p in chosen]
        self.metas = [p[1:] for p in chosen]
        self.packed = self.metas[0][1] is None
        self.n_z = n_z
        self.rows = pieces[0][0].shape[1] if not self.packed else pieces[0][0].shape[0] // (4 * n_z)
        self.half = half

    def specs(self):
        return [(a, True) for a in self.arrays]

    def scratch(self, n):
        if self.packed:
            return pltpu.VMEM((4 * self.n_z * self.rows, n), BF16)
        return pltpu.VMEM((self.n_z, 2, 2, self.rows, n), BF16)

    def sems(self):
        return pltpu.SemaphoreType.DMA((len(self.arrays),))

    def start(self, refs, dest, sems, src, n, at=0):
        _, y, c, _ = place()
        copies = []
        for i, ((m, b, e, j), ref) in enumerate(zip(self.metas, refs)):
            to = pl.ds(at + (0 if self.half is not None else m * n), n)
            if self.packed:
                cp = pltpu.make_async_copy(ref.at[:, pl.ds(src, n)], dest.at[:, to], sems.at[i])
            else:
                k = ref.shape[0]
                cp = pltpu.make_async_copy(
                    ref.at[:, :, pl.ds(src, n)], dest.at[pl.ds(j, k), y ^ b, c ^ e, :, to], sems.at[i]
                )
            cp.start()
            copies.append(cp)
        return copies

    def value(self, dest, first, last):
        if self.packed:
            return dest[:, first:last]
        return dest[:, :, :, :, first:last].reshape(4 * self.n_z * self.rows, last - first)

    def columns(self, dest, first, size):
        if self.packed:
            return dest[:, pl.ds(first, size)]
        return dest[:, :, :, :, pl.ds(first, size)].reshape(4 * self.n_z * self.rows, size)


def wait(copies):
    for cp in copies:
        cp.wait()


def rms(values, gain):
    return values * lax.rsqrt(jnp.mean(values * values, axis=-1, keepdims=True) + EPS) * gain


def rms_back(values, gain, back):
    scale = lax.rsqrt(jnp.mean(values * values, axis=-1, keepdims=True) + EPS)
    unit = values * scale
    incoming = back * gain
    grad = scale * (incoming - unit * jnp.mean(incoming * unit, axis=-1, keepdims=True))
    return grad, jnp.sum(back * unit, axis=0, keepdims=True)


def lane_masks():
    lane = lax.broadcasted_iota(jnp.int32, (1, LANE), 1)
    low = (lane < DH).astype(F32)
    return [low.astype(BF16), (1.0 - low).astype(BF16)]


def bias_strip(base):
    first = pltpu.roll(jnp.broadcast_to(base, (8, L)), 0, 1, stride=1, stride_axis=0)
    return jnp.concatenate([first] + [pltpu.roll(first, 8 * g, 1) for g in range(1, QB // 8)], axis=0)


def fold_band(band):
    total = band[0:8]
    for g in range(1, QB // 8):
        total = total + pltpu.roll(band[8 * g : 8 * g + 8], L - 8 * g, 1)
    row = lax.broadcasted_iota(jnp.int32, (8, L), 0)
    for bit in range(3):
        total = jnp.where(((row >> bit) & 1) == 1, pltpu.roll(total, L - (1 << bit), 1), total)
    return jnp.sum(total, axis=0, keepdims=True)


def attend_loop(q_ref, k_ref, v_ref, o_ref, base_ref):
    masks = lane_masks()

    def step(t, carry):
        at = pl.ds(pl.multiple_of(t * LANE, LANE), LANE)
        q, k, v = q_ref[:, at], k_ref[:, at], v_ref[:, at]
        outs = [None] * (L // QB)
        for hh in range(2):
            km, vm = k * masks[hh], v * masks[hh]
            if base_ref is not None:
                strip = bias_strip(base_ref[pl.ds(t * 2 + hh, 1), :])
                row = lax.broadcasted_iota(jnp.int32, (QB, L), 0)
                col = lax.broadcasted_iota(jnp.int32, (QB, L), 1)
                strip = jnp.where(row + (L - QB) >= col, strip, NEG)
            for b in range(L // QB):
                n = (b + 1) * QB if base_ref is not None else k.shape[0]
                s = nt(q[b * QB : (b + 1) * QB], km[:n])
                if base_ref is not None:
                    s = s + strip[:, L - n :]
                e = jnp.exp(s - jnp.max(s, axis=-1, keepdims=True))
                mixed = nn(e.astype(BF16), vm[:n]) * (1.0 / jnp.sum(e, axis=-1, keepdims=True))
                outs[b] = mixed if hh == 0 else outs[b] + mixed
        o_ref[:, at] = jnp.concatenate(outs, axis=0).astype(BF16)
        return carry

    lax.fori_loop(0, q_ref.shape[1] // LANE, step, 0)


def attend_back_loop(q_ref, k_ref, v_ref, do_ref, dq_ref, dk_ref, dv_ref, base_ref, off_ref):
    masks = lane_masks()
    causal = base_ref is not None
    wide = 256

    def step(t, carry):
        at = pl.ds(pl.multiple_of(t * LANE, LANE), LANE)
        q, k, v, do = q_ref[:, at], k_ref[:, at], v_ref[:, at], do_ref[:, at]
        kt = k.T
        dq = [None] * (L // wide)
        dk = dv = None
        for hh in range(2):
            km, vm, qm, dom = k * masks[hh], v * masks[hh], q * masks[hh], do * masks[hh]
            none = jnp.zeros_like(kt[:DH])
            ktm = jnp.concatenate([kt[:DH], none] if hh == 0 else [none, kt[DH:]], axis=0)
            band = None
            if causal:
                strip = bias_strip(base_ref[pl.ds(t * 2 + hh, 1), :])
                row = lax.broadcasted_iota(jnp.int32, (QB, L), 0)
                col = lax.broadcasted_iota(jnp.int32, (QB, L), 1)
                strip = jnp.where(col >= row, strip, NEG)
            for b in range(L // wide):
                n = (b + 1) * wide if causal else k.shape[0]
                cols = slice(b * wide, (b + 1) * wide)
                s = nt(km[:n], q[cols])
                if causal:
                    parts = []
                    for kb in range(n // QB):
                        lo = b * wide - kb * QB
                        if lo >= 0:
                            parts.append(strip[:, lo : lo + wide])
                        else:
                            parts.append(
                                jnp.concatenate([jnp.full((QB, -lo), NEG, F32), strip[:, : wide + lo]], axis=1)
                            )
                    s = s + jnp.concatenate(parts, axis=0)
                e = jnp.exp(s - jnp.max(s, axis=0, keepdims=True))
                prob = e * (1.0 / jnp.sum(e, axis=0, keepdims=True))
                dvb = nn(prob.astype(BF16), dom[cols])
                dp = nt(vm[:n], do[cols])
                ds = prob * (dp - jnp.sum(prob * dp, axis=0, keepdims=True))
                low = ds.astype(BF16)
                dkb = nn(low, qm[cols])
                dqb = nn(ktm[:, :n], low)
                dq[b] = dqb if hh == 0 else dq[b] + dqb
                if n < k.shape[0]:
                    pad = jnp.zeros((k.shape[0] - n, LANE), F32)
                    dvb, dkb = jnp.concatenate([dvb, pad], axis=0), jnp.concatenate([dkb, pad], axis=0)
                dk = dkb if dk is None else dk + dkb
                dv = dvb if dv is None else dv + dvb
                if causal:
                    for kb in range(n // QB):
                        lo = b * wide - kb * QB
                        part = ds[kb * QB : (kb + 1) * QB]
                        if lo < 0:
                            part, lo = part[:, -lo:], 0
                        sides = []
                        if lo:
                            sides.append(jnp.zeros((QB, lo), F32))
                        sides.append(part)
                        if lo + part.shape[1] < L:
                            sides.append(jnp.zeros((QB, L - lo - part.shape[1]), F32))
                        part = jnp.concatenate(sides, axis=1) if len(sides) > 1 else part
                        band = part if band is None else band + part
            if causal:
                off_ref[pl.ds(t * 2 + hh, 1), :] = fold_band(band)
        dq_ref[:, at] = jnp.concatenate(dq, axis=1).T.astype(BF16)
        dk_ref[:, at] = dk.astype(BF16)
        dv_ref[:, at] = dv.astype(BF16)
        return carry

    lax.fori_loop(0, q_ref.shape[1] // LANE, step, 0)


def call(body, outs, args, scratch, flops):
    return pl.pallas_call(
        body,
        out_shape=tuple(jax.ShapeDtypeStruct(s, d) for s, d in outs),
        in_specs=[pl.BlockSpec(memory_space=pl.ANY if far else pltpu.VMEM) for _, far in args],
        out_specs=tuple(pl.BlockSpec(memory_space=pltpu.VMEM) for _ in outs),
        scratch_shapes=scratch,
        compiler_params=pltpu.CompilerParams(vmem_limit_bytes=VMEM_LIMIT),
        cost_estimate=pl.CostEstimate(flops=flops, transcendentals=0, bytes_accessed=10_000_000),
    )(*[a for a, _ in args])


def sequence_copy(ref, dest, sem):
    m = lax.axis_index("mp")
    cp = pltpu.make_async_copy(ref.at[pl.ds(pl.multiple_of(m * L, L), L), :], dest, sem)
    cp.start()
    return cp


def near(*arrays):
    return [(a, False) for a in arrays]


class Parts:
    def __init__(self, grid, d, cols, halves):
        self.n = grid.n_z
        self.rows = d // (4 * self.n)
        self.sorted = self.rows % 16 == 0
        self.d, self.cols, self.halves = d, cols, halves

    def outs(self):
        lead = (2,) if self.halves else ()
        if self.sorted:
            return [(lead + (2, self.n, self.rows, self.cols), BF16)] * 2
        return [(lead + (self.d, self.cols), BF16)]

    def count(self):
        return 2 if self.sorted else 1

    def put(self, refs, half, at, value):
        low = value.astype(BF16)
        size = low.shape[1]
        cols = pl.ds(at, size)
        if not self.sorted:
            if half is None:
                refs[0][:, cols] = low
            else:
                refs[0][half, :, cols] = low
            return
        z, y, c, _ = place()
        low = low.reshape(self.n, 2, 2, self.rows, size)
        for i in range(self.n):
            for b in range(2):
                first, second = low[i, b, 0], low[i, b, 1]
                where = (b ^ y, lax.rem(i - z + self.n, self.n), slice(None), cols)
                if half is not None:
                    where = (half,) + where
                refs[0][where] = lax.select(c == 0, first, second)
                refs[1][where] = lax.select(c == 0, second, first)

    def put_halves(self, refs, at, n, value):
        self.put(refs, 0, at, value[:, :n])
        self.put(refs, 1, at, value[:, n:])

    def split(self, arrays):
        if self.sorted:
            return arrays
        z, y, c, _ = place()
        v = arrays[0]
        v = v.reshape(v.shape[:-2] + (self.n, 2, 2, self.rows, self.cols))
        lead = v.ndim - 5
        v = jnp.moveaxis(v, (lead + 2, lead + 1, lead), (0, lead + 1, lead + 2))
        v = jnp.take(v, (z + jnp.arange(self.n)) % self.n, axis=lead + 2)
        v = jnp.take(v, jnp.arange(2) ^ y, axis=lead + 1)
        v = jnp.take(v, jnp.arange(2) ^ c, axis=0)
        return v[0], v[1]


DMA = pltpu.SemaphoreType.DMA


def self_forward(grid, inputs, base_hot, pieces, d, hd, heads):
    ws = Weights(pieces, grid.n_z)
    k = len(ws.arrays)
    w2 = 2 * hd

    def body(*refs):
        x_ref, hot_ref = refs[:2]
        w_refs = refs[2 : 2 + k]
        n1_ref, q_ref, k_ref, v_ref, o_ref, gain_ref, base_ref = refs[2 + k : 9 + k]
        x_v, we, wq, wk, wv, fwd_base, sem_x, s_e, s_q, s_k, s_v = refs[9 + k :]
        cx = sequence_copy(x_ref, x_v, sem_x)
        ce = ws.start(w_refs, we, s_e, 3 * hd, LANE)
        cq = ws.start(w_refs, wq, s_q, 0, hd)
        ck = ws.start(w_refs, wk, s_k, hd, hd)
        cv = ws.start(w_refs, wv, s_v, 2 * hd, hd)
        cx.wait()
        x = x_v[...].astype(F32)
        scaled = x * lax.rsqrt(jnp.mean(x * x, axis=-1, keepdims=True) + EPS)
        wait(ce)
        extra = ws.value(we, 0, 2 * LANE)
        rows = ws.rows
        lane = lax.broadcasted_iota(jnp.int32, (LANE, d), 0)
        column = lax.broadcasted_iota(jnp.int32, (LANE, d), 1)
        spread = (lane == lax.rem(column, rows)).astype(F32).astype(BF16)
        wide = nn(extra[:, :LANE], spread)
        row = lax.broadcasted_iota(jnp.int32, (d, d), 0)
        column = lax.broadcasted_iota(jnp.int32, (d, d), 1)
        gains = [
            jnp.sum(jnp.where(row == (column // rows) * rows + heads + i, wide, 0.0), axis=0, keepdims=True)
            for i in range(3)
        ]
        gains = jnp.concatenate(gains + [jnp.zeros((5, d), F32)], axis=0)
        gain_ref[...] = gains
        fwd_base[...] = jnp.zeros_like(fwd_base)
        base_ref[...] = jnp.zeros_like(base_ref)
        for a in range(2):
            both = nn(extra[0:16, a * LANE : (a + 1) * LANE], hot_ref[...])[:heads]
            fwd_base[a * heads : (a + 1) * heads, :] = both[:, :L]
            base_ref[a * heads : (a + 1) * heads, :] = both[:, L:]
        n1 = (scaled * gains[0:1]).astype(BF16)
        n1_ref[...] = n1
        wait(cq)
        q_ref[...] = nn(n1, ws.value(wq, 0, w2)).astype(BF16)
        wait(ck)
        k_ref[...] = nn(n1, ws.value(wk, 0, w2)).astype(BF16)
        wait(cv)
        v_ref[...] = nn(n1, ws.value(wv, 0, w2)).astype(BF16)
        attend_loop(q_ref, k_ref, v_ref, o_ref, fwd_base)

    row = ((L, w2), BF16)
    return call(
        body,
        [((L, d), BF16), row, row, row, row, ((8, d), F32), ((16, L), F32)],
        [(inputs, True), (base_hot, False)] + ws.specs(),
        [
            pltpu.VMEM((L, d), BF16),
            ws.scratch(2 * LANE),
            ws.scratch(w2),
            ws.scratch(w2),
            ws.scratch(w2),
            pltpu.VMEM((16, L), F32),
            DMA,
            ws.sems(),
            ws.sems(),
            ws.sems(),
            ws.sems(),
        ],
        3_000_000_000,
    )


def cross_forward(grid, inputs, encoded, attn_one, gains, pieces, d, hd):
    ws = Weights(pieces, grid.n_z)
    k = len(ws.arrays)
    w2 = 2 * hd

    def body(*refs):
        x_ref, enc_ref, a1_ref, gain_ref = refs[:4]
        w_refs = refs[4 : 4 + k]
        r1_ref, r2_ref, n2_ref, q_ref, k_ref, v_ref, o_ref, n3_ref = refs[4 + k : 12 + k]
        x_v, enc_v, w1, wq, wk, wv, w2v, sem_x, sem_e, s_1, s_q, s_k, s_v, s_2 = refs[12 + k :]
        ce = sequence_copy(enc_ref, enc_v, sem_e)
        ck = ws.start(w_refs, wk, s_k, 2 * hd, hd)
        cv = ws.start(w_refs, wv, s_v, 3 * hd, hd)
        cx = sequence_copy(x_ref, x_v, sem_x)
        c1 = ws.start(w_refs, w1, s_1, 0, hd)
        cq = ws.start(w_refs, wq, s_q, hd, hd)
        c2 = ws.start(w_refs, w2v, s_2, 4 * hd, hd)
        ce.wait()
        wait(ck)
        k_ref[...] = nn(enc_v[...], ws.value(wk, 0, w2)).astype(BF16)
        wait(cv)
        v_ref[...] = nn(enc_v[...], ws.value(wv, 0, w2)).astype(BF16)
        cx.wait()
        wait(c1)
        r1 = x_v[...].astype(F32) + nt(a1_ref[...], ws.value(w1, 0, w2))
        r1_ref[...] = r1
        n2 = rms(r1, gain_ref[1:2, :]).astype(BF16)
        n2_ref[...] = n2
        wait(cq)
        q_ref[...] = nn(n2, ws.value(wq, 0, w2)).astype(BF16)
        attend_loop(q_ref, k_ref, v_ref, o_ref, None)
        wait(c2)
        r2 = r1_ref[...] + nt(o_ref[...], ws.value(w2v, 0, w2))
        r2_ref[...] = r2
        n3_ref[...] = rms(r2, gain_ref[2:3, :]).astype(BF16)

    row = ((L, w2), BF16)
    wide = ((L, d), BF16)
    return call(
        body,
        [((L, d), F32), ((L, d), F32), wide, row, row, row, row, wide],
        [(inputs, True), (encoded, True)] + near(attn_one, gains) + ws.specs(),
        [pltpu.VMEM((L, d), BF16), pltpu.VMEM((L, d), BF16)]
        + [ws.scratch(w2) for _ in range(5)]
        + [DMA, DMA]
        + [ws.sems() for _ in range(5)],
        5_000_000_000,
    )


def feed_forward(grid, cotangent, n3, r2, gains, carried, pieces, half, d, ff):
    ws = Weights(pieces, grid.n_z, half)
    k = len(ws.arrays)
    tile = min(512, ff)
    last = carried is not None
    extra_in = 4 if last else 0
    parts = Parts(grid, d, 3 * ff, False)
    ng = parts.count()

    def body(*refs):
        cot_ref, n3_ref = refs[:2]
        w_refs = refs[2 + extra_in : 2 + extra_in + k]
        rest = refs[2 + extra_in + k :]
        if last:
            r2_ref, gain_ref, yin_ref, bin_ref = refs[2:6]
            y_ref, b2_ref, dg_ref, y_acc, b3_acc = rest[ng : ng + 5]
        else:
            y_acc, b3_acc = rest[ng : ng + 2]
        g_refs, rest = rest[:ng], rest[ng + (5 if last else 2) :]
        cot_v, wg, wu, wd, cot_t, n3_t, sem_c, s_g, s_u, s_d = rest
        cc = sequence_copy(cot_ref, cot_v, sem_c)
        cg = ws.start(w_refs, wg, s_g, 0, ff)
        cu = ws.start(w_refs, wu, s_u, ff, ff)
        cd = ws.start(w_refs, wd, s_d, 2 * ff, ff)
        if last:
            y_acc[...] = r2_ref[...] + yin_ref[...]
            b3_acc[...] = bin_ref[...]
        else:
            y_acc[...] = jnp.zeros_like(y_acc)
            b3_acc[...] = jnp.zeros_like(b3_acc)
        n3_t[...] = n3_ref[...].T
        cc.wait()
        cot_t[...] = cot_v[...].T
        wait(cg)
        wait(cu)
        wait(cd)

        def step(t, carry):
            at = pl.multiple_of(t * tile, LANE)
            gate, upw, down = ws.columns(wg, at, tile), ws.columns(wu, at, tile), ws.columns(wd, at, tile)
            u = nn(n3_ref[...], gate)
            up = nn(n3_ref[...], upw)
            bh = nn(cot_v[...], down)
            sq = u * u
            th = jnp.tanh(GELU_C * (u + GELU_A * (sq * u)))
            both = 0.5 * (1.0 + th)
            gelu = u * both
            slope = both + 0.5 * u * (1.0 - th * th) * (GELU_C * (1.0 + (3.0 * GELU_A) * sq))
            hidden = (gelu * up).astype(BF16)
            gate_low = (bh * up * slope).astype(BF16)
            up_low = (bh * gelu).astype(BF16)
            y_acc[...] += nt(hidden, down)
            b3_acc[...] += nt(gate_low, gate) + nt(up_low, upw)
            parts.put(g_refs, None, at, nn(n3_t[...], gate_low))
            parts.put(g_refs, None, pl.multiple_of(ff + at, LANE), nn(n3_t[...], up_low))
            parts.put(g_refs, None, pl.multiple_of(2 * ff + at, LANE), nn(cot_t[...], hidden))
            return carry

        lax.fori_loop(0, ff // tile, step, 0)
        if last:
            y_ref[...] = y_acc[...].astype(BF16)
            grad, dg = rms_back(r2_ref[...], gain_ref[2:3, :], b3_acc[...])
            b2_ref[...] = cot_v[...].astype(F32) + grad
            dg_ref[...] = dg

    full = ((L, d), F32)
    outs = parts.outs()
    outs += [((L, d), BF16), full, ((1, d), F32)] if last else [full, full]
    scratch = [pltpu.VMEM((L, d), F32), pltpu.VMEM((L, d), F32)] if last else []
    result = call(
        body,
        outs,
        [(cotangent, True)] + near(n3) + (near(r2, gains, *carried) if last else []) + ws.specs(),
        scratch
        + [
            pltpu.VMEM((L, d), BF16),
            ws.scratch(ff),
            ws.scratch(ff),
            ws.scratch(ff),
            pltpu.VMEM((d, L), BF16),
            pltpu.VMEM((d, L), BF16),
            DMA,
            ws.sems(),
            ws.sems(),
            ws.sems(),
        ],
        7_500_000_000,
    )
    return parts.split(result[:ng]), result[ng:]


def attention_backward(grid, back, q, k, v, base, pieces, first_col, hd):
    ws = Weights(pieces, grid.n_z)
    n = len(ws.arrays)
    w2 = 2 * hd
    causal = base is not None

    def body(*refs):
        b_ref, q_ref, k_ref, v_ref = refs[:4]
        base_ref = refs[4] if causal else None
        refs = refs[5 if causal else 4 :]
        w_refs = refs[:n]
        dq_ref, dk_ref, dv_ref = refs[n : n + 3]
        off_ref = refs[n + 3] if causal else None
        wo, do, s_o = refs[n + (4 if causal else 3) :]
        co = ws.start(w_refs, wo, s_o, first_col, hd)
        if causal:
            off_ref[...] = jnp.zeros_like(off_ref)
        low = b_ref[...].astype(BF16)
        wait(co)
        do[...] = nn(low, ws.value(wo, 0, w2)).astype(BF16)
        attend_back_loop(q_ref, k_ref, v_ref, do, dq_ref, dk_ref, dv_ref, base_ref, off_ref)

    row = ((L, w2), BF16)
    return call(
        body,
        [row, row, row] + ([((16, L), F32)] if causal else []),
        near(back, q, k, v) + (near(base) if causal else []) + ws.specs(),
        [ws.scratch(w2), pltpu.VMEM((L, w2), BF16), ws.sems()],
        3_000_000_000,
    )


def cross_finish(grid, encoded, b2, r1, n2, dq, dk, dv, attn_one, attn_two, gains, pieces, d, hd):
    ws = Weights(pieces, grid.n_z)
    k = len(ws.arrays)
    w2 = 2 * hd
    parts = Parts(grid, d, 5 * hd, True)
    ng = parts.count()

    def body(*refs):
        enc_ref, b2_ref, r1_ref, n2_ref, dq_ref, dk_ref, dv_ref, a1_ref, a2_ref, gain_ref = refs[:10]
        w_refs = refs[10 : 10 + k]
        b1_ref, eg_ref, dg_ref = refs[10 + k : 13 + k]
        g_refs = refs[13 + k : 13 + k + ng]
        enc_v, wq, wk, wv, sem_e, s_q, s_k, s_v = refs[13 + k + ng :]
        cq = ws.start(w_refs, wq, s_q, hd, hd)
        ce = sequence_copy(enc_ref, enc_v, sem_e)
        ck = ws.start(w_refs, wk, s_k, 2 * hd, hd)
        cv = ws.start(w_refs, wv, s_v, 3 * hd, hd)
        parts.put_halves(g_refs, hd, hd, nn(n2_ref[...].T, dq_ref[...]))
        wait(cq)
        grad, dg = rms_back(r1_ref[...], gain_ref[1:2, :], nt(dq_ref[...], ws.value(wq, 0, w2)))
        dg_ref[...] = dg
        b1 = b2_ref[...] + grad
        b1_ref[...] = b1
        parts.put_halves(g_refs, 0, hd, nn(b1.astype(BF16).T, a1_ref[...]))
        ce.wait()
        enc_t = enc_v[...].T
        parts.put_halves(g_refs, 2 * hd, hd, nn(enc_t, dk_ref[...]))
        parts.put_halves(g_refs, 3 * hd, hd, nn(enc_t, dv_ref[...]))
        parts.put_halves(g_refs, 4 * hd, hd, nn(b2_ref[...].astype(BF16).T, a2_ref[...]))
        wait(ck)
        wait(cv)
        eg = nt(dk_ref[...], ws.value(wk, 0, w2)) + nt(dv_ref[...], ws.value(wv, 0, w2))
        eg_ref[...] = eg.astype(BF16)

    result = call(
        body,
        [((L, d), F32), ((L, d), BF16), ((1, d), F32)] + parts.outs(),
        [(encoded, True)] + near(b2, r1, n2, dq, dk, dv, attn_one, attn_two, gains) + ws.specs(),
        [pltpu.VMEM((L, d), BF16)]
        + [ws.scratch(w2) for _ in range(3)]
        + [DMA]
        + [ws.sems() for _ in range(3)],
        5_000_000_000,
    )
    return result[:3], parts.split(result[3:])


def self_finish(grid, inputs, b1, n1, dq, dk, dv, off, dg2, dg3, base_hot, gains, pieces, d, hd, heads):
    ws = Weights(pieces, grid.n_z)
    k = len(ws.arrays)
    w2 = 2 * hd
    parts = Parts(grid, d, 3 * hd + LANE, True)
    ng = parts.count()

    def body(*refs):
        x_ref, b1_ref, n1_ref, dq_ref, dk_ref, dv_ref, off_ref, dg2_ref, dg3_ref, hot_ref, gain_ref = refs[:11]
        w_refs = refs[11 : 11 + k]
        dx_ref = refs[11 + k]
        g_refs = refs[12 + k : 12 + k + ng]
        x_v, wq, wk, wv, sem_x, s_q, s_k, s_v = refs[12 + k + ng :]
        cq = ws.start(w_refs, wq, s_q, 0, hd)
        ck = ws.start(w_refs, wk, s_k, hd, hd)
        cv = ws.start(w_refs, wv, s_v, 2 * hd, hd)
        cx = sequence_copy(x_ref, x_v, sem_x)
        n1_t = n1_ref[...].T
        parts.put_halves(g_refs, 0, hd, nn(n1_t, dq_ref[...]))
        parts.put_halves(g_refs, hd, hd, nn(n1_t, dk_ref[...]))
        parts.put_halves(g_refs, 2 * hd, hd, nn(n1_t, dv_ref[...]))
        wait(cq)
        back = nt(dq_ref[...], ws.value(wq, 0, w2))
        wait(ck)
        back = back + nt(dk_ref[...], ws.value(wk, 0, w2))
        wait(cv)
        back = back + nt(dv_ref[...], ws.value(wv, 0, w2))
        cx.wait()
        grad, dg = rms_back(x_v[...].astype(F32), gain_ref[0:1, :], back)
        dx_ref[...] = (b1_ref[...] + grad).astype(BF16)
        dgs = jnp.concatenate([dg, dg2_ref[...], dg3_ref[...], jnp.zeros((5, d), F32)], axis=0)
        turned = jnp.concatenate([jnp.zeros((NB, d), F32), dgs, jnp.zeros((LANE - NB - 8, d), F32)], axis=0).T
        hot = hot_ref[:, L:]
        sums = off_ref[...]
        table = jnp.zeros((16, LANE), F32)
        for _ in range(3):
            low = sums.astype(BF16)
            table = table + nt(low, hot)
            sums = sums - low.astype(F32)
        table = table.astype(BF16)
        shard_row = lax.rem(lax.broadcasted_iota(jnp.int32, (d, 16), 0), parts.rows)
        column = lax.broadcasted_iota(jnp.int32, (d, 16), 1)
        for a in range(2):
            spread = ((shard_row + a * heads == column) & (shard_row < heads)).astype(F32).astype(BF16)
            parts.put(g_refs, a, 3 * hd, nn(spread, table) + turned)

    result = call(
        body,
        [((L, d), BF16)] + parts.outs(),
        [(inputs, True)] + near(b1, n1, dq, dk, dv, off, dg2, dg3, base_hot, gains) + ws.specs(),
        [pltpu.VMEM((L, d), BF16)]
        + [ws.scratch(w2) for _ in range(3)]
        + [DMA]
        + [ws.sems() for _ in range(3)],
        4_000_000_000,
    )
    return result[0], parts.split(result[1:])


def added(left, right):
    return (left.astype(F32) + right.astype(F32)).astype(BF16)


def scatter(grid, own, own_got, other, other_got, first):
    n = grid.n_z
    got = grid.swap_m(added(other[..., :first], other_got[..., :first]))
    got_own = grid.swap_y(added(own[1, ..., first:], own_got[1, ..., first:]))
    got_other = grid.swap_y(added(other[1, ..., first:], other_got[1, ..., first:]))

    def a_sum(i):
        return added3(own[i, ..., :first], own_got[i, ..., :first], got[i])

    def b_sum(v, v_got, v_far):
        return added3(v[0, ..., first:], v_got[0, ..., first:], v_far)

    far_a = grid.swap_y(a_sum(1))
    far_b = grid.swap_m(b_sum(other, other_got, got_other))
    wa, wb = a_sum(0), b_sum(own, own_got, got_own)
    w = [
        jnp.concatenate([added(wa[d], far_a[d]), added(wb[d], far_b[d])], axis=-1) for d in range(n)
    ]
    return w


def settle(grid, w, gate=None):
    sent = w[1:]
    if gate is not None:
        sent, gate = lax.optimization_barrier((sent, gate))
    return [w[0]] + [grid.shift_z(v, d + 1) for d, v in enumerate(sent)], gate


def summed(arrays):
    out = arrays[0].astype(F32)
    for v in arrays[1:]:
        out = out + v.astype(F32)
    return out


def added3(a, b, c):
    return (a.astype(F32) + b.astype(F32) + c.astype(F32)).astype(BF16)


def both_sequences(mine, other):
    first = lax.axis_index("mp") == 0
    low = jnp.where(first, mine, other)
    high = jnp.where(first, other, mine)
    return jnp.concatenate([low, high], axis=0).astype(F32)


def make(grid):
    def step(
        inputs,
        encoded,
        cotangent,
        buckets,
        rel_table,
        query_self,
        keys_self,
        values_self,
        output_self,
        query_cross,
        keys_cross,
        values_cross,
        output_cross,
        gate_weight,
        up_weight,
        down_weight,
        gain_first,
        gain_second,
        gain_third,
    ):
        d = inputs.shape[1]
        hd = query_self.shape[1]
        ff = gate_weight.shape[1]
        rows = query_self.shape[0]
        heads = rel_table.shape[0]
        assert inputs.shape[0] == 2 * L and heads + 3 <= rows <= LANE and heads <= 8
        extra = jnp.concatenate(
            [
                jnp.pad(rel_table, ((0, 0), (0, LANE - NB))),
                jnp.pad(jnp.stack([gain_first, gain_second, gain_third]), ((0, rows - heads - 3), (0, LANE - rows))),
            ],
            axis=0,
        )
        group_one = jnp.concatenate([query_self, keys_self, values_self, extra], axis=1)
        group_two = jnp.concatenate([output_self.T, query_cross, keys_cross, values_cross, output_cross.T], axis=1)
        group_three = jnp.concatenate([gate_weight, up_weight, down_weight.T], axis=1)
        pieces_one = gather(grid, group_one)
        pieces_two = gather(grid, group_two)
        pieces_three = gather(grid, group_three)

        turned = jnp.roll(buckets[::-1], L - QB + 1)
        both = jnp.concatenate([turned, buckets])
        base_hot = (both[None, :] == lax.broadcasted_iota(jnp.int32, (LANE, 2 * L), 0)).astype(BF16)

        n1, q1, k1, v1, at1, gains, base = self_forward(grid, inputs, base_hot, pieces_one, d, hd, heads)
        r1, r2, n2, q2, k2, v2, at2, n3 = cross_forward(grid, inputs, encoded, at1, gains, pieces_two, d, hd)
        (own3, gone), (ya, ba) = feed_forward(grid, cotangent, n3, r2, gains, None, pieces_three, 0, d, ff)
        own3_got = grid.swap_c(gone)
        (other3, gone), (y, b2, dg3) = feed_forward(
            grid, cotangent, n3, r2, gains, (ya, ba), pieces_three, 1, d, ff
        )
        other3_got = grid.swap_c(gone)
        y_far = grid.swap_m(y)
        w3 = scatter(grid, own3, own3_got, other3, other3_got, ff * 3 // 4 // LANE * LANE)
        dq, dk, dv = attention_backward(grid, b2, q2, k2, v2, None, pieces_two, 4 * hd, hd)
        (b1, eg, dg2), (kept, gone) = cross_finish(
            grid, encoded, b2, r1, n2, dq, dk, dv, at1, at2, gains, pieces_two, d, hd
        )
        eg_far = grid.swap_m(eg)
        got = grid.swap_c(gone)
        z3, _ = settle(grid, w3)
        w2 = scatter(grid, kept[0], got[0], kept[1], got[1], 4 * LANE)
        dq, dk, dv, off = attention_backward(grid, b1, q1, k1, v1, base, pieces_two, 0, hd)
        dx, (kept, gone) = self_finish(
            grid, inputs, b1, n1, dq, dk, dv, off, dg2, dg3, base_hot, gains, pieces_one, d, hd, heads
        )
        got = grid.swap_c(gone)
        z2, _ = settle(grid, w2)
        w1 = scatter(grid, kept[0], got[0], kept[1], got[1], 4 * LANE)
        dx_far = grid.swap_m(dx)
        z1, (y, eg, z20, z30) = settle(grid, w1, (y, eg, z2[0], z3[0]))
        layer_output = both_sequences(y, y_far)
        encoded_gradient = both_sequences(eg, eg_far)
        input_gradient = both_sequences(dx, dx_far)
        s3 = summed([z30] + z3[1:])
        s2 = summed([z20] + z2[1:])
        s1 = summed(z1)
        small = s1[:, 3 * hd :]
        table_gradient = small[:heads, :NB]
        dgs = [small[:, NB + i] for i in range(3)]
        return (
            layer_output,
            input_gradient,
            encoded_gradient,
            table_gradient,
            s1[:, :hd],
            s1[:, hd : 2 * hd],
            s1[:, 2 * hd : 3 * hd],
            s2[:, :hd].T,
            s2[:, hd : 2 * hd],
            s2[:, 2 * hd : 3 * hd],
            s2[:, 3 * hd : 4 * hd],
            s2[:, 4 * hd :].T,
            s3[:, :ff],
            s3[:, ff : 2 * ff],
            s3[:, 2 * ff :].T,
            dgs[0],
            dgs[1],
            dgs[2],
        )

    return step


def solution(mesh):
    weight, turned, row, gain = P("dp", "mp"), P("mp", "dp"), P("dp", None), P("dp")
    weights = (weight, weight, weight, turned, weight, weight, weight, turned, weight, weight, turned)
    gains = (gain, gain, gain)
    return jax.shard_map(
        make(Grid(mesh.shape["dp"], mesh.shape["mp"])),
        mesh=mesh,
        in_specs=(row, row, row, P(), P("mp", None)) + weights + gains,
        out_specs=(row, row, row, P("mp", None)) + weights + gains,
        check_vma=False,
    )
```

profile of v0, /device:TPU:0, one launch (start us, length us, event | category | flops | bytes accessed | tf_op | source)
XLA Modules:
  0.0 492.8 jit_solution(2465294192403080399)
XLA Ops:
  4.6 5.1 %collective-permute-start.14 = (bf16[48,1920]{1,0:T(8,128)(2,1)S(1)}, bf16[48,1920]{1,0:T(8,128)(2,1)S(1)}, u32[]{:S(2)}, u32[]{:S(2)}) collective-permute-start(bf16[48,1920]{1,0:T(8,128)(2,1)S(1)} %bitcast_dynamic-update-slice_fusion.12), channel_id=1, source_target_pairs={{0,24},{1,25},{2,26},{3,27},{4,28},{5,29},{6,30},{7,31},{8,0},{9,1... | collective-permute-start | bytes 552968 | tf_op jit(solution)/shard_map/ppermute | solution.py:54
  12.9 1.9 collective-permute-start.1
  16.7 11.2 %collective-permute-done = bf16[48,1280]{1,0:T(8,128)(2,1)} collective-permute-done((bf16[48,1280]{1,0:T(8,128)(2,1)}, bf16[48,1280]{1,0:T(8,128)(2,1)}, u32[]{:S(2)}, u32[]{:S(2)}) %collective-permute-start) | collective-permute-done | bytes 122912 | tf_op jit(solution)/shard_map/ppermute | solution.py:54
  28.8 4.6 collective-permute-done.1
  33.3 6.5 %collective-permute-start.25 = (bf16[48,3072]{1,0:T(8,128)(2,1)S(1)}, bf16[48,3072]{1,0:T(8,128)(2,1)S(1)}, u32[]{:S(2)}, u32[]{:S(2)}) collective-permute-start(bf16[48,3072]{1,0:T(8,128)(2,1)S(1)} %pad_maximum_fusion), channel_id=1, source_target_pairs={{0,16},{1,17},{2,18},{3,19},{4,20},{5,21},{6,22},{7,23},{8,24},{9,... | collective-permute-start | bytes 884744 | tf_op jit(solution)/shard_map/ppermute | solution.py:54
  40.7 14.2 %collective-permute-start.24 = (bf16[48,3072]{1,0:T(8,128)(2,1)S(1)}, bf16[48,3072]{1,0:T(8,128)(2,1)S(1)}, u32[]{:S(2)}, u32[]{:S(2)}) collective-permute-start(bf16[48,3072]{1,0:T(8,128)(2,1)S(1)} %pad_maximum_fusion), channel_id=1, source_target_pairs={{0,8},{1,9},{2,10},{3,11},{4,12},{5,13},{6,14},{7,15},{8,16},{9,17... | collective-permute-start | bytes 884744 | tf_op jit(solution)/shard_map/ppermute | solution.py:54
  62.2 7.7 %collective-permute-done.4.refs_4_.refs_13_ = bf16[4,48,1280]{2,1,0:T(8,128)(2,1)S(1)} collective-permute-done((bf16[4,48,1280]{2,1,0:T(8,128)(2,1)S(1)}, bf16[4,48,1280]{2,1,0:T(8,128)(2,1)S(1)}, u32[]{:S(2)}, u32[]{:S(2)}) %collective-permute-start.4) | collective-permute-done | bytes 491552 | tf_op jit(solution)/shard_map/ppermute | solution.py:54
  71.5 1.6 collective-permute-start.15
  74.3 20.3 %collective-permute-done.5.refs_5_.refs_14_ = bf16[2,48,1280]{2,1,0:T(8,128)(2,1)S(1)} collective-permute-done((bf16[2,48,1280]{2,1,0:T(8,128)(2,1)S(1)}, bf16[2,48,1280]{2,1,0:T(8,128)(2,1)S(1)}, u32[]{:S(2)}, u32[]{:S(2)}) %collective-permute-start.5) | collective-permute-done | bytes 245792 | tf_op jit(solution)/shard_map/ppermute | solution.py:54
  103.2 25.8 %collective-permute-done.17.refs_7_.refs_13_.refs_8_ = bf16[2,48,1920]{2,1,0:T(8,128)(2,1)S(1)} collective-permute-done((bf16[2,48,1920]{2,1,0:T(8,128)(2,1)S(1)}, bf16[2,48,1920]{2,1,0:T(8,128)(2,1)S(1)}, u32[]{:S(2)}, u32[]{:S(2)}) %collective-permute-start.17) | collective-permute-done | bytes 368672 | tf_op jit(solution)/shard_map/ppermute | solution.py:54
  133.9 1.6 collective-permute-start.31
  137.4 21.1 %shard_map.322 = (bf16[512,768]{1,0:T(8,128)(2,1)}, bf16[512,768]{1,0:T(8,128)(2,1)}, bf16[512,768]{1,0:T(8,128)(2,1)}, bf16[512,768]{1,0:T(8,128)(2,1)}, bf16[5...) custom-call(bf16[1024,768]{1,0:T(8,128)(2,1)} %refs_0_.11, bf16[128,1024]{1,0:T(8,128)(2,1)} %fusion.10.refs_1_.refs_9_, ...), custom_call_target="tpu_custom_call" | custom-call | flops 3000000000 | bytes 10000000 | tf_op jit(solution)/shard_map/pallas_call | solution.py:297
  158.5 23.8 %shard_map.323 = (f32[512,768]{1,0:T(8,128)}, f32[512,768]{1,0:T(8,128)}, bf16[512,768]{1,0:T(8,128)(2,1)}, bf16[512,768]{1,0:T(8,128)(2,1)}, bf16[512,768]{1,0:...) custom-call(bf16[1024,768]{1,0:T(8,128)(2,1)} %refs_0_.11, ...), custom_call_target="tpu_custom_call" | custom-call | flops 5000000000 | bytes 10000000 | tf_op jit(solution)/shard_map/pallas_call | solution.py:297
  183.0 14.9 %shard_map.324 = (bf16[2,4,48,3072]{3,2,1,0:T(8,128)(2,1)}, bf16[2,4,48,3072]{3,2,1,0:T(8,128)(2,1)}, f32[512,768]{1,0:T(8,128)}, f32[512,768]{1,0:T(8,128)}) custom-call(bf16[1024,768]{1,0:T(8,128)(2,1)} %refs_0_.9, bf16[512,768]{1,0:T(8,128)(2,1)} %get-tuple-element.66.refs_1_, bf16[4,48,3072]{2,1,0:T(8,128)(2,1)} %copy-done.3, ...), custom_call_target="tpu_custom_call" | custom-call | flops 7500000256 | bytes 10000000 | tf_op jit(solution)/shard_map/pallas_call | solution.py:297
  199.3 16.3 %shard_map.325 = (bf16[2,4,48,3072]{3,2,1,0:T(8,128)(2,1)}, bf16[2,4,48,3072]{3,2,1,0:T(8,128)(2,1)}, bf16[512,768]{1,0:T(8,128)(2,1)}, f32[512,768]{1,0:T(8,128)}, f32[1,768]{1,0:T(1,128)}) custom-call(bf16[1024,768]{1,0:T(8,128)(2,1)} %refs_0_.9, bf16[512,768]{1,0:T(8,128)(2,1)} %get-tuple-element.66.refs_1_, f32[512,768]{1,0:T(8,128)} %get-tuple-element.67.refs_2_, ...), custom_call_target="tpu_custom_call" | custom-call | flops 7500000256 | bytes 10000000 | tf_op jit(solution)/shard_map/pallas_call | solution.py:297
  215.6 19.2 %shard_map.326 = (bf16[512,768]{1,0:T(8,128)(2,1)}, bf16[512,768]{1,0:T(8,128)(2,1)}, bf16[512,768]{1,0:T(8,128)(2,1)}) custom-call(f32[512,768]{1,0:T(8,128)} %get-tuple-element.70.refs_0_.refs_1_, bf16[512,768]{1,0:T(8,128)(2,1)} %get-tuple-element.73.refs_1_, bf16[512,768]{1,0:T(8,128)(2,1)} %get-tuple-element.74.refs_2_, ...), custom_call_target="tpu_custom_call" | custom-call | flops 3000000000 | bytes 10000000 | tf_op jit(solution)/shard_map/pallas_call | solution.py:297
  234.8 12.7 %shard_map.327 = (f32[512,768]{1,0:T(8,128)}, bf16[512,768]{1,0:T(8,128)(2,1)}, f32[1,768]{1,0:T(1,128)}, bf16[2,2,4,48,1920]{4,3,2,1,0:T(8,128)(2,1)}, bf16[2,2,4,48,1920]{4,3,2,1,0:T(8,128)(2,1)}) custom-call(bf16[1024,768]{1,0:T(8,128)(2,1)} %refs_0_.10, f32[512,768]{1,0:T(8,128)} %get-tuple-element.70.refs_0_.refs_1_, ...), custom_call_target="tpu_custom_call" | custom-call | flops 5000000000 | bytes 10000000 | tf_op jit(solution)/shard_map/pallas_call | solution.py:297
  247.5 20.6 %shard_map.328 = (bf16[512,768]{1,0:T(8,128)(2,1)}, bf16[512,768]{1,0:T(8,128)(2,1)}, bf16[512,768]{1,0:T(8,128)(2,1)}, f32[16,512]{1,0:T(8,128)}) custom-call(f32[512,768]{1,0:T(8,128)} %get-tuple-element.80.refs_0_.refs_1_, bf16[512,768]{1,0:T(8,128)(2,1)} %get-tuple-element.82.refs_1_, bf16[512,768]{1,0:T(8,128)(2,1)} %get-tuple-element.83.refs_2_, ...), custom_call_target="tpu_custom_call" | custom-call | flops 3000000000 | bytes 10000000 | tf_op jit(solution)/shard_map/pallas_call | solution.py:297
  268.2 11.5 %shard_map.329 = (bf16[512,768]{1,0:T(8,128)(2,1)}, bf16[2,2,4,48,1280]{4,3,2,1,0:T(8,128)(2,1)}, bf16[2,2,4,48,1280]{4,3,2,1,0:T(8,128)(2,1)}) custom-call(bf16[1024,768]{1,0:T(8,128)(2,1)} %refs_0_.11, f32[512,768]{1,0:T(8,128)} %get-tuple-element.80.refs_0_.refs_1_, bf16[512,768]{1,0:T(8,128)(2,1)} %get-tuple-element.81.refs_2_, ...), custom_call_target="tpu_custom_call" | custom-call | flops 4000000000 | bytes 10000000 | tf_op jit(solution)/shard_map/pallas_call | solution.py:297
  280.7 1.8 slice_bitcast_fusion.7
  282.5 1.6 collective-permute-start.57
  284.3 16.5 %collective-permute-done.56 = bf16[512,768]{1,0:T(8,128)(2,1)S(1)} collective-permute-done((bf16[512,768]{1,0:T(8,128)(2,1)}, bf16[512,768]{1,0:T(8,128)(2,1)S(1)}, u32[]{:S(2)}, u32[]{:S(2)}) %collective-permute-start.56) | collective-permute-done | bytes 786464 | tf_op jit(solution)/shard_map/ppermute | solution.py:54
  301.0 1.9 maximum_convert_fusion.1
  303.1 1.6 collective-permute-start.40
  305.4 7.6 %collective-permute-done.40 = bf16[4,48,768]{2,1,0:T(8,128)(2,1)S(1)} collective-permute-done((bf16[4,48,768]{2,1,0:T(8,128)(2,1)S(1)}, bf16[4,48,768]{2,1,0:T(8,128)(2,1)S(1)}, u32[]{:S(2)}, u32[]{:S(2)}) %collective-permute-start.40) | collective-permute-done | bytes 294944 | tf_op jit(solution)/shard_map/ppermute | solution.py:54
  313.7 3.7 collective-permute-done.39
  318.0 8.1 %collective-permute-done.37 = bf16[2,4,48,512]{3,2,1,0:T(8,128)(2,1)S(1)} collective-permute-done((bf16[2,4,48,512]{3,2,1,0:T(8,128)(2,1)S(1)}, bf16[2,4,48,512]{3,2,1,0:T(8,128)(2,1)S(1)}, u32[]{:S(2)}, u32[]{:S(2)}) %collective-permute-start.37) | collective-permute-done | bytes 393248 | tf_op jit(solution)/shard_map/ppermute | solution.py:54
  327.2 1.6 collective-permute-start.38
  329.3 19.5 %collective-permute-done.41 = bf16[4,48,768]{2,1,0:T(8,128)(2,1)S(1)} collective-permute-done((bf16[4,48,768]{2,1,0:T(8,128)(2,1)S(1)}, bf16[4,48,768]{2,1,0:T(8,128)(2,1)S(1)}, u32[]{:S(2)}, u32[]{:S(2)}) %collective-permute-start.41) | collective-permute-done | bytes 294944 | tf_op jit(solution)/shard_map/ppermute | solution.py:54
  349.4 1.6 collective-permute-start.53
  351.1 12.5 %collective-permute-done.50 = bf16[2,4,48,768]{3,2,1,0:T(8,128)(2,1)S(1)} collective-permute-done((bf16[2,4,48,768]{3,2,1,0:T(8,128)(2,1)S(1)}, bf16[2,4,48,768]{3,2,1,0:T(8,128)(2,1)S(1)}, u32[]{:S(2)}, u32[]{:S(2)}) %collective-permute-start.50) | collective-permute-done | bytes 589856 | tf_op jit(solution)/shard_map/ppermute | solution.py:54
  366.5 5.4 %collective-permute-done.53 = bf16[4,48,2304]{2,1,0:T(8,128)(2,1)S(1)} collective-permute-done((bf16[4,48,2304]{2,1,0:T(8,128)(2,1)S(1)}, bf16[4,48,2304]{2,1,0:T(8,128)(2,1)S(1)}, u32[]{:S(2)}, u32[]{:S(2)}) %collective-permute-start.53) | collective-permute-done | bytes 884768 | tf_op jit(solution)/shard_map/ppermute | solution.py:54
  373.8 17.1 %collective-permute-done.52 = bf16[4,48,2304]{2,1,0:T(8,128)(2,1)S(1)} collective-permute-done((bf16[4,48,2304]{2,1,0:T(8,128)(2,1)S(1)}, bf16[4,48,2304]{2,1,0:T(8,128)(2,1)S(1)}, u32[]{:S(2)}, u32[]{:S(2)}) %collective-permute-start.52) | collective-permute-done | bytes 884768 | tf_op jit(solution)/shard_map/ppermute | solution.py:54
  392.8 4.4 collective-permute-done.51
  400.6 8.3 %collective-permute-done.46 = bf16[4,48,1408]{2,1,0:T(8,128)(2,1)S(1)} collective-permute-done((bf16[4,48,1408]{2,1,0:T(8,128)(2,1)S(1)}, bf16[4,48,1408]{2,1,0:T(8,128)(2,1)S(1)}, u32[]{:S(2)}, u32[]{:S(2)}) %collective-permute-start.46) | collective-permute-done | bytes 540704 | tf_op jit(solution)/shard_map/ppermute | solution.py:54
  410.5 9.9 %collective-permute-done.45 = bf16[4,48,1408]{2,1,0:T(8,128)(2,1)S(1)} collective-permute-done((bf16[4,48,1408]{2,1,0:T(8,128)(2,1)S(1)}, bf16[4,48,1408]{2,1,0:T(8,128)(2,1)S(1)}, u32[]{:S(2)}, u32[]{:S(2)}) %collective-permute-start.45) | collective-permute-done | bytes 540704 | tf_op jit(solution)/shard_map/ppermute | solution.py:54
  423.0 8.3 %collective-permute-done.47 = bf16[4,48,1408]{2,1,0:T(8,128)(2,1)S(1)} collective-permute-done((bf16[4,48,1408]{2,1,0:T(8,128)(2,1)S(1)}, bf16[4,48,1408]{2,1,0:T(8,128)(2,1)S(1)}, u32[]{:S(2)}, u32[]{:S(2)}) %collective-permute-start.47) | collective-permute-done | bytes 540704 | tf_op jit(solution)/shard_map/ppermute | solution.py:54
  431.8 10.4 %collective-permute-start.62 = (bf16[48,1920]{1,0:T(8,128)(2,1)S(1)}, bf16[48,1920]{1,0:T(8,128)(2,1)S(1)}, u32[]{:S(2)}, u32[]{:S(2)}) collective-permute-start(bf16[48,1920]{1,0:T(8,128)(2,1)S(1)} %pad_maximum_fusion.7), channel_id=1, source_target_pairs={{0,16},{1,17},{2,18},{3,19},{4,20},{5,21},{6,22},{7,23},{8,24},{9,... | collective-permute-start | bytes 552968 | tf_op jit(solution)/shard_map/ppermute | solution.py:54
  442.7 1.6 collective-permute-start.61
  444.9 1.9 maximum_convert_fusion
  446.8 2.4 collective-permute-start.66
  449.3 1.9 maximum_convert_fusion.2
  451.2 5.2 %collective-permute-done.62 = bf16[48,1920]{1,0:T(8,128)(2,1)S(1)} collective-permute-done((bf16[48,1920]{1,0:T(8,128)(2,1)S(1)}, bf16[48,1920]{1,0:T(8,128)(2,1)S(1)}, u32[]{:S(2)}, u32[]{:S(2)}) %collective-permute-start.62) | collective-permute-done | bytes 184352 | tf_op jit(solution)/shard_map/ppermute | solution.py:54
  456.4 9.1 %collective-permute-start.59 = (bf16[48,1280]{1,0:T(8,128)(2,1)S(1)}, bf16[48,1280]{1,0:T(8,128)(2,1)S(1)}, u32[]{:S(2)}, u32[]{:S(2)}) collective-permute-start(bf16[48,1280]{1,0:T(8,128)(2,1)S(1)} %get-tuple-element.106), channel_id=1, source_target_pairs={{0,16},{1,17},{2,18},{3,19},{4,20},{5,21},{6,22},{7,23},{8,24},{9,... | collective-permute-start | bytes 368648 | tf_op jit(solution)/shard_map/ppermute | solution.py:54
  465.5 3.4 collective-permute-start.60
  469.7 1.7 collective-permute-done.58
  471.4 11.0 %collective-permute-start.64 = (bf16[48,3072]{1,0:T(8,128)(2,1)S(1)}, bf16[48,3072]{1,0:T(8,128)(2,1)S(1)}, u32[]{:S(2)}, u32[]{:S(2)}) collective-permute-start(bf16[48,3072]{1,0:T(8,128)(2,1)S(1)} %pad_maximum_fusion.2), channel_id=1, source_target_pairs={{0,8},{1,9},{2,10},{3,11},{4,12},{5,13},{6,14},{7,15},{8,16},{9,17... | collective-permute-start | bytes 884744 | tf_op jit(solution)/shard_map/ppermute | solution.py:54
  482.4 6.9 %collective-permute-done.59 = bf16[48,1280]{1,0:T(8,128)(2,1)S(1)} collective-permute-done((bf16[48,1280]{1,0:T(8,128)(2,1)S(1)}, bf16[48,1280]{1,0:T(8,128)(2,1)S(1)}, u32[]{:S(2)}, u32[]{:S(2)}) %collective-permute-start.59) | collective-permute-done | bytes 122912 | tf_op jit(solution)/shard_map/ppermute | solution.py:54
  (242 shorter events, 63.5 us)
Async XLA Ops:
  4.6 51.6 %collective-permute-start.14 = (bf16[48,1920]{1,0:T(8,128)(2,1)S(1)}, bf16[48,1920]{1,0:T(8,128)(2,1)S(1)}, u32[]{:S(2)}, u32[]{:S(2)}) collective-permute-start(bf16[48,1920]{1,0:T(8,128)(2,1)S(1)} %bitcast_dynamic-update-slice_fusion.12), channel_id=1, source_target_pairs={{0,24},{1,25},{2,26},{3,27},{4,28},{5,29},{6,30},{7,31},{8,0},{9,1... | collective-permute-start | bytes 552968 | tf_op jit(solution)/shard_map/ppermute | solution.py:54
  9.7 46.4 %collective-permute-start.13 = (bf16[48,1920]{1,0:T(8,128)(2,1)S(1)}, bf16[48,1920]{1,0:T(8,128)(2,1)S(1)}, u32[]{:S(2)}, u32[]{:S(2)}) collective-permute-start(bf16[48,1920]{1,0:T(8,128)(2,1)S(1)} %bitcast_dynamic-update-slice_fusion.12), channel_id=1, source_target_pairs={{0,16},{1,17},{2,18},{3,19},{4,20},{5,21},{6,22},{7,23},{8,24},{9,... | collective-permute-start | bytes 552968 | tf_op jit(solution)/shard_map/ppermute | solution.py:54
  9.7 45.3 %collective-permute-start.12 = (bf16[48,1920]{1,0:T(8,128)(2,1)S(1)}, bf16[48,1920]{1,0:T(8,128)(2,1)}, u32[]{:S(2)}, u32[]{:S(2)}) collective-permute-start(bf16[48,1920]{1,0:T(8,128)(2,1)S(1)} %bitcast_dynamic-update-slice_fusion.12), channel_id=1, source_target_pairs={{0,8},{1,9},{2,10},{3,11},{4,12},{5,13},{6,14},{7,15},{8,16},{9,17... | collective-permute-start | bytes 552968 | tf_op jit(solution)/shard_map/ppermute | solution.py:54
  12.9 20.4 %collective-permute-start.1 = (bf16[48,1280]{1,0:T(8,128)(2,1)}, bf16[48,1280]{1,0:T(8,128)(2,1)}, u32[]{:S(2)}, u32[]{:S(2)}) collective-permute-start(bf16[48,1280]{1,0:T(8,128)(2,1)} %get-tuple-element.114), channel_id=1, source_target_pairs={{0,16},{1,17},{2,18},{3,19},{4,20},{5,21},{6,22},{7,23},{8,24},{9,... | collective-permute-start | bytes 368648 | tf_op jit(solution)/shard_map/ppermute | solution.py:54
  33.3 28.8 %collective-permute-start.25 = (bf16[48,3072]{1,0:T(8,128)(2,1)S(1)}, bf16[48,3072]{1,0:T(8,128)(2,1)S(1)}, u32[]{:S(2)}, u32[]{:S(2)}) collective-permute-start(bf16[48,3072]{1,0:T(8,128)(2,1)S(1)} %pad_maximum_fusion), channel_id=1, source_target_pairs={{0,16},{1,17},{2,18},{3,19},{4,20},{5,21},{6,22},{7,23},{8,24},{9,... | collective-permute-start | bytes 884744 | tf_op jit(solution)/shard_map/ppermute | solution.py:54
  40.7 18.4 %collective-permute-start.24 = (bf16[48,3072]{1,0:T(8,128)(2,1)S(1)}, bf16[48,3072]{1,0:T(8,128)(2,1)S(1)}, u32[]{:S(2)}, u32[]{:S(2)}) collective-permute-start(bf16[48,3072]{1,0:T(8,128)(2,1)S(1)} %pad_maximum_fusion), channel_id=1, source_target_pairs={{0,8},{1,9},{2,10},{3,11},{4,12},{5,13},{6,14},{7,15},{8,16},{9,17... | collective-permute-start | bytes 884744 | tf_op jit(solution)/shard_map/ppermute | solution.py:54
  55.0 18.1 %collective-permute-start.26 = (bf16[48,3072]{1,0:T(8,128)(2,1)S(1)}, bf16[48,3072]{1,0:T(8,128)(2,1)S(1)}, u32[]{:S(2)}, u32[]{:S(2)}) collective-permute-start(bf16[48,3072]{1,0:T(8,128)(2,1)S(1)} %pad_maximum_fusion), channel_id=1, source_target_pairs={{0,24},{1,25},{2,26},{3,27},{4,28},{5,29},{6,30},{7,31},{8,0},{9,1... | collective-permute-start | bytes 884744 | tf_op jit(solution)/shard_map/ppermute | solution.py:54
  56.1 17.6 %collective-permute-start.7 = (bf16[4,48,1280]{2,1,0:T(8,128)(2,1)S(1)}, bf16[4,48,1280]{2,1,0:T(8,128)(2,1)S(1)}, u32[]{:S(2)}, u32[]{:S(2)}) collective-permute-start(bf16[4,48,1280]{2,1,0:T(8,128)(2,1)S(1)} %bitcast_dynamic-update-slice_fusion.8.refs_2_.refs_11_), channel_id=1, source_target_pairs={{0,2},{1,3},{2,0},{3,1},{4,6},{5,7},{6,4},{7,5},{8,10},{9,11},{10,... | collective-permute-start | bytes 1474568 | tf_op jit(solution)/shard_map/ppermute | solution.py:54
  62.2 34.5 %collective-permute-start.19 = (bf16[4,48,1920]{2,1,0:T(8,128)(2,1)S(1)}, bf16[4,48,1920]{2,1,0:T(8,128)(2,1)S(1)}, u32[]{:S(2)}, u32[]{:S(2)}) collective-permute-start(bf16[4,48,1920]{2,1,0:T(8,128)(2,1)S(1)} %bitcast_dynamic-update-slice_fusion.4.refs_4_.refs_10_.refs_5_), channel_id=1, source_target_pairs={{0,2},{1,3},{2,0},{3,1},{4,6},{5,7},{6,4},{7,5},{8,10},{9,11},{10,... | collective-permute-start | bytes 2211848 | tf_op jit(solution)/shard_map/ppermute | solution.py:54
  69.9 26.7 %collective-permute-start.16 = (bf16[4,48,1920]{2,1,0:T(8,128)(2,1)S(1)}, bf16[4,48,1920]{2,1,0:T(8,128)(2,1)}, u32[]{:S(2)}, u32[]{:S(2)}) collective-permute-start(bf16[4,48,1920]{2,1,0:T(8,128)(2,1)S(1)} %bitcast_dynamic-update-slice_fusion.4.refs_4_.refs_10_.refs_5_), channel_id=1, source_target_pairs={{0,1},{1,0},{2,3},{3,2},{4,5},{5,4},{6,7},{7,6},{8,9},{9,8},{10,11... | collective-permute-start | bytes 2211848 | tf_op jit(solution)/shard_map/ppermute | solution.py:54
  71.5 25.7 %collective-permute-start.15 = (bf16[4,48,1920]{2,1,0:T(8,128)(2,1)S(1)}, bf16[4,48,1920]{2,1,0:T(8,128)(2,1)}, u32[]{:S(2)}, u32[]{:S(2)}) collective-permute-start(bf16[4,48,1920]{2,1,0:T(8,128)(2,1)S(1)} %bitcast_dynamic-update-slice_fusion.4.refs_4_.refs_10_.refs_5_), channel_id=1, source_target_pairs={{0,4},{1,5},{2,6},{3,7},{4,0},{5,1},{6,2},{7,3},{8,12},{9,13},{10,... | collective-permute-start | bytes 2211848 | tf_op jit(solution)/shard_map/ppermute | solution.py:54
  73.1 21.4 %collective-permute-start.5 = (bf16[2,48,1280]{2,1,0:T(8,128)(2,1)S(1)}, bf16[2,48,1280]{2,1,0:T(8,128)(2,1)S(1)}, u32[]{:S(2)}, u32[]{:S(2)}) collective-permute-start(bf16[2,48,1280]{2,1,0:T(8,128)(2,1)S(1)} %slice.571), channel_id=1, source_target_pairs={{0,4},{1,5},{2,6},{3,7},{4,0},{5,1},{6,2},{7,3},{8,12},{9,13},{10,... | collective-permute-start | bytes 737288 | tf_op jit(solution)/shard_map/ppermute | solution.py:54
  73.7 21.4 %collective-permute-start.6 = (bf16[2,48,1280]{2,1,0:T(8,128)(2,1)S(1)}, bf16[2,48,1280]{2,1,0:T(8,128)(2,1)S(1)}, u32[]{:S(2)}, u32[]{:S(2)}) collective-permute-start(bf16[2,48,1280]{2,1,0:T(8,128)(2,1)S(1)} %slice.572), channel_id=1, source_target_pairs={{0,1},{1,0},{2,3},{3,2},{4,5},{5,4},{6,7},{7,6},{8,9},{9,8},{10,11... | collective-permute-start | bytes 737288 | tf_op jit(solution)/shard_map/ppermute | solution.py:54
  94.6 35.0 %collective-permute-start.30 = (bf16[4,48,3072]{2,1,0:T(8,128)(2,1)S(1)}, bf16[4,48,3072]{2,1,0:T(8,128)(2,1)S(1)}, u32[]{:S(2)}, u32[]{:S(2)}) collective-permute-start(bf16[4,48,3072]{2,1,0:T(8,128)(2,1)S(1)} %bitcast_dynamic-update-slice_fusion.refs_2_), channel_id=1, source_target_pairs={{0,1},{1,0},{2,3},{3,2},{4,5},{5,4},{6,7},{7,6},{8,9},{9,8},{10,11... | collective-permute-start | bytes 3538952 | tf_op jit(solution)/shard_map/ppermute | solution.py:54
  95.1 34.6 %collective-permute-start.27 = (bf16[4,48,3072]{2,1,0:T(8,128)(2,1)S(1)}, bf16[4,48,3072]{2,1,0:T(8,128)(2,1)}, u32[]{:S(2)}, u32[]{:S(2)}) collective-permute-start(bf16[4,48,3072]{2,1,0:T(8,128)(2,1)S(1)} %bitcast_dynamic-update-slice_fusion.refs_2_), channel_id=1, source_target_pairs={{0,4},{1,5},{2,6},{3,7},{4,0},{5,1},{6,2},{7,3},{8,12},{9,13},{10,... | collective-permute-start | bytes 3538952 | tf_op jit(solution)/shard_map/ppermute | solution.py:54
  98.5 30.6 %collective-permute-start.17 = (bf16[2,48,1920]{2,1,0:T(8,128)(2,1)S(1)}, bf16[2,48,1920]{2,1,0:T(8,128)(2,1)S(1)}, u32[]{:S(2)}, u32[]{:S(2)}) collective-permute-start(bf16[2,48,1920]{2,1,0:T(8,128)(2,1)S(1)} %slice.573), channel_id=1, source_target_pairs={{0,4},{1,5},{2,6},{3,7},{4,0},{5,1},{6,2},{7,3},{8,12},{9,13},{10,... | collective-permute-start | bytes 1105928 | tf_op jit(solution)/shard_map/ppermute | solution.py:54
  100.0 29.1 %collective-permute-start.18 = (bf16[2,48,1920]{2,1,0:T(8,128)(2,1)S(1)}, bf16[2,48,1920]{2,1,0:T(8,128)(2,1)}, u32[]{:S(2)}, u32[]{:S(2)}) collective-permute-start(bf16[2,48,1920]{2,1,0:T(8,128)(2,1)S(1)} %slice.574), channel_id=1, source_target_pairs={{0,1},{1,0},{2,3},{3,2},{4,5},{5,4},{6,7},{7,6},{8,9},{9,8},{10,11... | collective-permute-start | bytes 1105928 | tf_op jit(solution)/shard_map/ppermute | solution.py:54
  103.1 30.7 %collective-permute-start.21 = (bf16[4,48,1920]{2,1,0:T(8,128)(2,1)}, bf16[4,48,1920]{2,1,0:T(8,128)(2,1)}, u32[]{:S(2)}, u32[]{:S(2)}) collective-permute-start(bf16[4,48,1920]{2,1,0:T(8,128)(2,1)} %collective-permute-done.16.refs_6_.refs_12_.refs_7_), channel_id=1, source_target_pairs={{0,2},{1,3},{2,0},{3,1},{4,6},{5,7},{6,4},{7,5},{8,10},{9,11},{10,... | collective-permute-start | bytes 2211848 | tf_op jit(solution)/shard_map/ppermute | solution.py:54
  129.6 53.4 %collective-permute-start.28 = (bf16[4,48,3072]{2,1,0:T(8,128)(2,1)S(1)}, bf16[4,48,3072]{2,1,0:T(8,128)(2,1)}, u32[]{:S(2)}, u32[]{:S(2)}) collective-permute-start(bf16[4,48,3072]{2,1,0:T(8,128)(2,1)S(1)} %bitcast_dynamic-update-slice_fusion.refs_2_), channel_id=1, source_target_pairs={{0,2},{1,3},{2,0},{3,1},{4,6},{5,7},{6,4},{7,5},{8,10},{9,11},{10,... | collective-permute-start | bytes 3538952 | tf_op jit(solution)/shard_map/ppermute | solution.py:54
  129.7 53.3 %collective-permute-start.29 = (bf16[4,48,3072]{2,1,0:T(8,128)(2,1)}, bf16[4,48,3072]{2,1,0:T(8,128)(2,1)}, u32[]{:S(2)}, u32[]{:S(2)}) collective-permute-start(bf16[4,48,3072]{2,1,0:T(8,128)(2,1)} %collective-permute-done.27.refs_3_), channel_id=1, source_target_pairs={{0,2},{1,3},{2,0},{3,1},{4,6},{5,7},{6,4},{7,5},{8,10},{9,11},{10,... | collective-permute-start | bytes 3538952 | tf_op jit(solution)/shard_map/ppermute | solution.py:54
  133.9 48.5 %collective-permute-start.31 = (bf16[2,48,3072]{2,1,0:T(8,128)(2,1)S(1)}, bf16[2,48,3072]{2,1,0:T(8,128)(2,1)S(1)}, u32[]{:S(2)}, u32[]{:S(2)}) collective-permute-start(bf16[2,48,3072]{2,1,0:T(8,128)(2,1)S(1)} %slice.575), channel_id=1, source_target_pairs={{0,4},{1,5},{2,6},{3,7},{4,0},{5,1},{6,2},{7,3},{8,12},{9,13},{10,... | collective-permute-start | bytes 1769480 | tf_op jit(solution)/shard_map/ppermute | solution.py:54
  135.9 47.1 %collective-permute-start.32 = (bf16[2,48,3072]{2,1,0:T(8,128)(2,1)S(1)}, bf16[2,48,3072]{2,1,0:T(8,128)(2,1)}, u32[]{:S(2)}, u32[]{:S(2)}) collective-permute-start(bf16[2,48,3072]{2,1,0:T(8,128)(2,1)S(1)} %slice.576), channel_id=1, source_target_pairs={{0,1},{1,0},{2,3},{3,2},{4,5},{5,4},{6,7},{7,6},{8,9},{9,8},{10,11... | collective-permute-start | bytes 1769480 | tf_op jit(solution)/shard_map/ppermute | solution.py:54
  137.3 60.6 %collective-permute-start.33 = (bf16[4,48,3072]{2,1,0:T(8,128)(2,1)S(1)}, bf16[4,48,3072]{2,1,0:T(8,128)(2,1)S(1)}, u32[]{:S(2)}, u32[]{:S(2)}) collective-permute-start(bf16[4,48,3072]{2,1,0:T(8,128)(2,1)S(1)} %collective-permute-done.30.refs_6_), channel_id=1, source_target_pairs={{0,2},{1,3},{2,0},{3,1},{4,6},{5,7},{6,4},{7,5},{8,10},{9,11},{10,... | collective-permute-start | bytes 3538952 | tf_op jit(solution)/shard_map/ppermute | solution.py:54
  182.4 15.6 %collective-permute-start.34 = (bf16[2,48,3072]{2,1,0:T(8,128)(2,1)S(1)}, bf16[2,48,3072]{2,1,0:T(8,128)(2,1)S(1)}, u32[]{:S(2)}, u32[]{:S(2)}) collective-permute-start(bf16[2,48,3072]{2,1,0:T(8,128)(2,1)S(1)} %collective-permute-done.31.refs_7_), channel_id=1, source_target_pairs={{0,2},{1,3},{2,0},{3,1},{4,6},{5,7},{6,4},{7,5},{8,10},{9,11},{10,... | collective-permute-start | bytes 1769480 | tf_op jit(solution)/shard_map/ppermute | solution.py:54
  182.9 15.0 %collective-permute-start.35 = (bf16[2,48,3072]{2,1,0:T(8,128)(2,1)}, bf16[2,48,3072]{2,1,0:T(8,128)(2,1)S(1)}, u32[]{:S(2)}, u32[]{:S(2)}) collective-permute-start(bf16[2,48,3072]{2,1,0:T(8,128)(2,1)} %collective-permute-done.32.refs_8_), channel_id=1, source_target_pairs={{0,2},{1,3},{2,0},{3,1},{4,6},{5,7},{6,4},{7,5},{8,10},{9,11},{10,... | collective-permute-start | bytes 1769480 | tf_op jit(solution)/shard_map/ppermute | solution.py:54
  279.6 23.2 %collective-permute-start.36 = (bf16[2,2,4,48,1280]{4,3,2,1,0:T(8,128)(2,1)}, bf16[2,2,4,48,1280]{4,3,2,1,0:T(8,128)(2,1)S(1)}, u32[]{:S(2)}, u32[]{:S(2)}) collective-permute-start(bf16[2,2,4,48,1280]{4,3,2,1,0:T(8,128)(2,1)} %get-tuple-element.93), channel_id=1, source_target_pairs={{0,2},{1,3},{2,0},{3,1},{4,6},{5,7},{6,4},{7,5},{8,10},{9,11},{10,... | collective-permute-start | bytes 5898248 | tf_op jit(solution)/shard_map/ppermute | solution.py:54
  280.1 47.0 %collective-permute-start.48 = (bf16[2,4,48,3072]{3,2,1,0:T(8,128)(2,1)}, bf16[2,4,48,3072]{3,2,1,0:T(8,128)(2,1)S(1)}, u32[]{:S(2)}, u32[]{:S(2)}) collective-permute-start(bf16[2,4,48,3072]{3,2,1,0:T(8,128)(2,1)} %get-tuple-element.99), channel_id=1, source_target_pairs={{0,2},{1,3},{2,0},{3,1},{4,6},{5,7},{6,4},{7,5},{8,10},{9,11},{10,... | collective-permute-start | bytes 7077896 | tf_op jit(solution)/shard_map/ppermute | solution.py:54
  280.2 20.6 %collective-permute-start.56 = (bf16[512,768]{1,0:T(8,128)(2,1)}, bf16[512,768]{1,0:T(8,128)(2,1)S(1)}, u32[]{:S(2)}, u32[]{:S(2)}) collective-permute-start(bf16[512,768]{1,0:T(8,128)(2,1)} %get-tuple-element.103), channel_id=1, source_target_pairs={{0,1},{1,0},{2,3},{3,2},{4,5},{5,4},{6,7},{7,6},{8,9},{9,8},{10,11... | collective-permute-start | bytes 2359304 | tf_op jit(solution)/shard_map/ppermute | solution.py:54
  282.5 164.3 %collective-permute-start.57 = (bf16[512,768]{1,0:T(8,128)(2,1)S(1)}, bf16[512,768]{1,0:T(8,128)(2,1)S(1)}, u32[]{:S(2)}, u32[]{:S(2)}) collective-permute-start(bf16[512,768]{1,0:T(8,128)(2,1)S(1)} %copy-done.5), channel_id=1, source_target_pairs={{0,1},{1,0},{2,3},{3,2},{4,5},{5,4},{6,7},{7,6},{8,9},{9,8},{10,11... | collective-permute-start | bytes 2359304 | tf_op jit(solution)/shard_map/ppermute | solution.py:54
  284.1 42.2 %collective-permute-start.49 = (bf16[2,4,48,3072]{3,2,1,0:T(8,128)(2,1)}, bf16[2,4,48,3072]{3,2,1,0:T(8,128)(2,1)S(1)}, u32[]{:S(2)}, u32[]{:S(2)}) collective-permute-start(bf16[2,4,48,3072]{3,2,1,0:T(8,128)(2,1)} %get-tuple-element.101), channel_id=1, source_target_pairs={{0,2},{1,3},{2,0},{3,1},{4,6},{5,7},{6,4},{7,5},{8,10},{9,11},{10,... | collective-permute-start | bytes 7077896 | tf_op jit(solution)/shard_map/ppermute | solution.py:54
  317.4 127.2 %collective-permute-start.55 = (bf16[512,768]{1,0:T(8,128)(2,1)S(1)}, bf16[512,768]{1,0:T(8,128)(2,1)S(1)}, u32[]{:S(2)}, u32[]{:S(2)}) collective-permute-start(bf16[512,768]{1,0:T(8,128)(2,1)S(1)} %copy-done.4), channel_id=1, source_target_pairs={{0,1},{1,0},{2,3},{3,2},{4,5},{5,4},{6,7},{7,6},{8,9},{9,8},{10,11... | collective-permute-start | bytes 2359304 | tf_op jit(solution)/shard_map/ppermute | solution.py:54
  326.1 39.2 %collective-permute-start.42 = (bf16[2,2,4,48,1920]{4,3,2,1,0:T(8,128)(2,1)S(1)}, bf16[2,2,4,48,1920]{4,3,2,1,0:T(8,128)(2,1)S(1)}, u32[]{:S(2)}, u32[]{:S(2)}) collective-permute-start(bf16[2,2,4,48,1920]{4,3,2,1,0:T(8,128)(2,1)S(1)} %copy-done.16), channel_id=1, source_target_pairs={{0,2},{1,3},{2,0},{3,1},{4,6},{5,7},{6,4},{7,5},{8,10},{9,11},{10,... | collective-permute-start | bytes 8847368 | tf_op jit(solution)/shard_map/ppermute | solution.py:54
  326.3 22.5 %collective-permute-start.41 = (bf16[4,48,768]{2,1,0:T(8,128)(2,1)S(1)}, bf16[4,48,768]{2,1,0:T(8,128)(2,1)S(1)}, u32[]{:S(2)}, u32[]{:S(2)}) collective-permute-start(bf16[4,48,768]{2,1,0:T(8,128)(2,1)S(1)} %fusion.6), channel_id=1, source_target_pairs={{0,1},{1,0},{2,3},{3,2},{4,5},{5,4},{6,7},{7,6},{8,9},{9,8},{10,11... | collective-permute-start | bytes 884744 | tf_op jit(solution)/shard_map/ppermute | solution.py:54
  327.2 22.2 %collective-permute-start.38 = (bf16[4,48,512]{2,1,0:T(8,128)(2,1)S(1)}, bf16[4,48,512]{2,1,0:T(8,128)(2,1)S(1)}, u32[]{:S(2)}, u32[]{:S(2)}) collective-permute-start(bf16[4,48,512]{2,1,0:T(8,128)(2,1)S(1)} %get-tuple-element.124), channel_id=1, source_target_pairs={{0,4},{1,5},{2,6},{3,7},{4,0},{5,1},{6,2},{7,3},{8,12},{9,13},{10,... | collective-permute-start | bytes 589832 | tf_op jit(solution)/shard_map/ppermute | solution.py:54
  349.4 22.6 %collective-permute-start.53 = (bf16[4,48,2304]{2,1,0:T(8,128)(2,1)S(1)}, bf16[4,48,2304]{2,1,0:T(8,128)(2,1)S(1)}, u32[]{:S(2)}, u32[]{:S(2)}) collective-permute-start(bf16[4,48,2304]{2,1,0:T(8,128)(2,1)S(1)} %fusion.5), channel_id=1, source_target_pairs={{0,4},{1,5},{2,6},{3,7},{4,0},{5,1},{6,2},{7,3},{8,12},{9,13},{10,... | collective-permute-start | bytes 2654216 | tf_op jit(solution)/shard_map/ppermute | solution.py:54
  363.6 27.4 %collective-permute-start.52 = (bf16[4,48,2304]{2,1,0:T(8,128)(2,1)S(1)}, bf16[4,48,2304]{2,1,0:T(8,128)(2,1)S(1)}, u32[]{:S(2)}, u32[]{:S(2)}) collective-permute-start(bf16[4,48,2304]{2,1,0:T(8,128)(2,1)S(1)} %fusion.4), channel_id=1, source_target_pairs={{0,4},{1,5},{2,6},{3,7},{4,0},{5,1},{6,2},{7,3},{8,12},{9,13},{10,... | collective-permute-start | bytes 2654216 | tf_op jit(solution)/shard_map/ppermute | solution.py:54
  365.4 31.9 %collective-permute-start.51 = (bf16[4,48,768]{2,1,0:T(8,128)(2,1)S(1)}, bf16[4,48,768]{2,1,0:T(8,128)(2,1)S(1)}, u32[]{:S(2)}, u32[]{:S(2)}) collective-permute-start(bf16[4,48,768]{2,1,0:T(8,128)(2,1)S(1)} %get-tuple-element.116), channel_id=1, source_target_pairs={{0,4},{1,5},{2,6},{3,7},{4,0},{5,1},{6,2},{7,3},{8,12},{9,13},{10,... | collective-permute-start | bytes 884744 | tf_op jit(solution)/shard_map/ppermute | solution.py:54
  372.0 26.9 %collective-permute-start.43 = (bf16[2,4,48,512]{3,2,1,0:T(8,128)(2,1)S(1)}, bf16[2,4,48,512]{3,2,1,0:T(8,128)(2,1)S(1)}, u32[]{:S(2)}, u32[]{:S(2)}) collective-permute-start(bf16[2,4,48,512]{3,2,1,0:T(8,128)(2,1)S(1)} %add_convert_fusion.5), channel_id=1, source_target_pairs={{0,1},{1,0},{2,3},{3,2},{4,5},{5,4},{6,7},{7,6},{8,9},{9,8},{10,11... | collective-permute-start | bytes 1179656 | tf_op jit(solution)/shard_map/ppermute | solution.py:54
  390.9 17.9 %collective-permute-start.46 = (bf16[4,48,1408]{2,1,0:T(8,128)(2,1)S(1)}, bf16[4,48,1408]{2,1,0:T(8,128)(2,1)S(1)}, u32[]{:S(2)}, u32[]{:S(2)}) collective-permute-start(bf16[4,48,1408]{2,1,0:T(8,128)(2,1)S(1)} %fusion.9), channel_id=1, source_target_pairs={{0,4},{1,5},{2,6},{3,7},{4,0},{5,1},{6,2},{7,3},{8,12},{9,13},{10,... | collective-permute-start | bytes 1622024 | tf_op jit(solution)/shard_map/ppermute | solution.py:54
  397.2 23.2 %collective-permute-start.45 = (bf16[4,48,1408]{2,1,0:T(8,128)(2,1)S(1)}, bf16[4,48,1408]{2,1,0:T(8,128)(2,1)S(1)}, u32[]{:S(2)}, u32[]{:S(2)}) collective-permute-start(bf16[4,48,1408]{2,1,0:T(8,128)(2,1)S(1)} %fusion.8), channel_id=1, source_target_pairs={{0,4},{1,5},{2,6},{3,7},{4,0},{5,1},{6,2},{7,3},{8,12},{9,13},{10,... | collective-permute-start | bytes 1622024 | tf_op jit(solution)/shard_map/ppermute | solution.py:54
  398.8 43.9 %collective-permute-start.54 = (bf16[4,48,2304]{2,1,0:T(8,128)(2,1)S(1)}, bf16[4,48,2304]{2,1,0:T(8,128)(2,1)S(1)}, u32[]{:S(2)}, u32[]{:S(2)}) collective-permute-start(bf16[4,48,2304]{2,1,0:T(8,128)(2,1)S(1)} %fusion), channel_id=1, source_target_pairs={{0,1},{1,0},{2,3},{3,2},{4,5},{5,4},{6,7},{7,6},{8,9},{9,8},{10,11... | collective-permute-start | bytes 2654216 | tf_op jit(solution)/shard_map/ppermute | solution.py:54
  431.8 24.6 %collective-permute-start.62 = (bf16[48,1920]{1,0:T(8,128)(2,1)S(1)}, bf16[48,1920]{1,0:T(8,128)(2,1)S(1)}, u32[]{:S(2)}, u32[]{:S(2)}) collective-permute-start(bf16[48,1920]{1,0:T(8,128)(2,1)S(1)} %pad_maximum_fusion.7), channel_id=1, source_target_pairs={{0,16},{1,17},{2,18},{3,19},{4,20},{5,21},{6,22},{7,23},{8,24},{9,... | collective-permute-start | bytes 552968 | tf_op jit(solution)/shard_map/ppermute | solution.py:54
  442.7 22.8 %collective-permute-start.61 = (bf16[48,1920]{1,0:T(8,128)(2,1)S(1)}, bf16[48,1920]{1,0:T(8,128)(2,1)S(1)}, u32[]{:S(2)}, u32[]{:S(2)}) collective-permute-start(bf16[48,1920]{1,0:T(8,128)(2,1)S(1)} %pad_maximum_fusion.6), channel_id=1, source_target_pairs={{0,8},{1,9},{2,10},{3,11},{4,12},{5,13},{6,14},{7,15},{8,16},{9,17... | collective-permute-start | bytes 552968 | tf_op jit(solution)/shard_map/ppermute | solution.py:54
  444.7 46.7 %collective-permute-start.65 = (bf16[48,3072]{1,0:T(8,128)(2,1)S(1)}, bf16[48,3072]{1,0:T(8,128)(2,1)S(1)}, u32[]{:S(2)}, u32[]{:S(2)}) collective-permute-start(bf16[48,3072]{1,0:T(8,128)(2,1)S(1)} %pad_maximum_fusion.3), channel_id=1, source_target_pairs={{0,16},{1,17},{2,18},{3,19},{4,20},{5,21},{6,22},{7,23},{8,24},{9,... | collective-permute-start | bytes 884744 | tf_op jit(solution)/shard_map/ppermute | solution.py:54
  446.8 44.6 %collective-permute-start.66 = (bf16[48,3072]{1,0:T(8,128)(2,1)S(1)}, bf16[48,3072]{1,0:T(8,128)(2,1)S(1)}, u32[]{:S(2)}, u32[]{:S(2)}) collective-permute-start(bf16[48,3072]{1,0:T(8,128)(2,1)S(1)} %pad_maximum_fusion.4), channel_id=1, source_target_pairs={{0,24},{1,25},{2,26},{3,27},{4,28},{5,29},{6,30},{7,31},{8,0},{9,1... | collective-permute-start | bytes 884744 | tf_op jit(solution)/shard_map/ppermute | solution.py:54
  456.4 32.9 %collective-permute-start.59 = (bf16[48,1280]{1,0:T(8,128)(2,1)S(1)}, bf16[48,1280]{1,0:T(8,128)(2,1)S(1)}, u32[]{:S(2)}, u32[]{:S(2)}) collective-permute-start(bf16[48,1280]{1,0:T(8,128)(2,1)S(1)} %get-tuple-element.106), channel_id=1, source_target_pairs={{0,16},{1,17},{2,18},{3,19},{4,20},{5,21},{6,22},{7,23},{8,24},{9,... | collective-permute-start | bytes 368648 | tf_op jit(solution)/shard_map/ppermute | solution.py:54
  465.5 23.8 %collective-permute-start.60 = (bf16[48,1280]{1,0:T(8,128)(2,1)S(1)}, bf16[48,1280]{1,0:T(8,128)(2,1)S(1)}, u32[]{:S(2)}, u32[]{:S(2)}) collective-permute-start(bf16[48,1280]{1,0:T(8,128)(2,1)S(1)} %pad_maximum_fusion.11), channel_id=1, source_target_pairs={{0,24},{1,25},{2,26},{3,27},{4,28},{5,29},{6,30},{7,31},{8,0},{9,1... | collective-permute-start | bytes 368648 | tf_op jit(solution)/shard_map/ppermute | solution.py:54
  471.4 20.0 %collective-permute-start.64 = (bf16[48,3072]{1,0:T(8,128)(2,1)S(1)}, bf16[48,3072]{1,0:T(8,128)(2,1)S(1)}, u32[]{:S(2)}, u32[]{:S(2)}) collective-permute-start(bf16[48,3072]{1,0:T(8,128)(2,1)S(1)} %pad_maximum_fusion.2), channel_id=1, source_target_pairs={{0,8},{1,9},{2,10},{3,11},{4,12},{5,13},{6,14},{7,15},{8,16},{9,17... | collective-permute-start | bytes 884744 | tf_op jit(solution)/shard_map/ppermute | solution.py:54
  (50 other events, 931.0 us)
where the time goes:
time: 500 us; the launch traced here: 493 us
  waiting for transfers between devices  211 us (42%)
  Pallas kernels  140 us (28%)
  starting transfers between devices  107 us (21%)
  local copies, waits for them, and re-layouts  18.6 us (4%)
  other arithmetic  13.7 us (3%)
    ppermute x67, waiting for transfers between devices, send(): return lax.ppermute(v, AXES, self.perm(move))  211 us
    pallas_call x8, Pallas kernels, call(): pl.pallas_call(body, out_shape=tuple((jax.ShapeDtypeStruct(s, d) for s, d...  140 us
    ppermute x67, starting transfers between devices, send(): return lax.ppermute(v, AXES, self.perm(move))  107 us
  transfers between devices with their start and end apart: 67, of which 27 were waited for; matrix products, arithmetic and copies ran while one was open for 5% of the time, Pallas kernels for 12%

commit v1 on v0

--- a/solution.py
+++ b/solution.py
@@ -18,7 +18,8 @@
 AXES = ("dp", "mp")
 F32 = jnp.float32
 BF16 = jnp.bfloat16
-VMEM_LIMIT = 58 * 1024 * 1024
+MIB = 1024 * 1024
+VMEM_LIMIT = {"ka": 13, "kb": 16, "kca": 20, "kcb": 22, "kd1": 12, "kd2": 18, "ke1": 12, "ke2": 16}
 
 
 def nn(left, right):
@@ -191,118 +192,137 @@
     return jnp.sum(total, axis=0, keepdims=True)
 
 
-def attend_loop(q_ref, k_ref, v_ref, o_ref, base_ref):
+WIDE = 256
+
+
+def masked_strip(base_ref, row):
+    strip = bias_strip(base_ref[pl.ds(row, 1), :])
+    at_row = lax.broadcasted_iota(jnp.int32, (QB, L), 0)
+    at_col = lax.broadcasted_iota(jnp.int32, (QB, L), 1)
+    return jnp.where(at_col >= at_row, strip, NEG)
+
+
+def bias_tile(strip, first_key, keys, first_query):
+    parts = []
+    for k in range(first_key, first_key + keys, QB):
+        lo = first_query - k
+        if lo >= 0:
+            parts.append(strip[:, lo : lo + WIDE])
+        else:
+            parts.append(jnp.concatenate([jnp.full((QB, -lo), NEG, F32), strip[:, : WIDE + lo]], axis=1))
+    return jnp.concatenate(parts, axis=0)
+
+
+def half_rows(turned):
+    none = jnp.zeros_like(turned[:DH])
+    return [jnp.concatenate([turned[:DH], none], axis=0), jnp.concatenate([none, turned[DH:]], axis=0)]
+
+
+def attend_loop(q_ref, k_ref, v_ref, o_ref, lse_ref, base_ref):
     masks = lane_masks()
+    causal = base_ref is not None
 
     def step(t, carry):
         at = pl.ds(pl.multiple_of(t * LANE, LANE), LANE)
         q, k, v = q_ref[:, at], k_ref[:, at], v_ref[:, at]
-        outs = [None] * (L // QB)
-        for hh in range(2):
-            km, vm = k * masks[hh], v * masks[hh]
-            if base_ref is not None:
-                strip = bias_strip(base_ref[pl.ds(t * 2 + hh, 1), :])
-                row = lax.broadcasted_iota(jnp.int32, (QB, L), 0)
-                col = lax.broadcasted_iota(jnp.int32, (QB, L), 1)
-                strip = jnp.where(row + (L - QB) >= col, strip, NEG)
-            for b in range(L // QB):
-                n = (b + 1) * QB if base_ref is not None else k.shape[0]
-                s = nt(q[b * QB : (b + 1) * QB], km[:n])
-                if base_ref is not None:
-                    s = s + strip[:, L - n :]
-                e = jnp.exp(s - jnp.max(s, axis=-1, keepdims=True))
-                mixed = nn(e.astype(BF16), vm[:n]) * (1.0 / jnp.sum(e, axis=-1, keepdims=True))
-                outs[b] = mixed if hh == 0 else outs[b] + mixed
-        o_ref[:, at] = jnp.concatenate(outs, axis=0).astype(BF16)
+        vt = half_rows(v.T)
+        outs = [None] * (L // WIDE)
+        keys = [k * masks[hh] for hh in range(2)]
+        strips = [masked_strip(base_ref, t * 2 + hh) if causal else None for hh in range(2)]
+        order = [(hh, b) for b in range(L // WIDE) for hh in range(2)]
+
+        def scores(hh, b):
+            n = (b + 1) * WIDE if causal else k.shape[0]
+            s = nt(keys[hh][:n], q[b * WIDE : (b + 1) * WIDE])
+            return s + bias_tile(strips[hh], 0, n, b * WIDE) if causal else s
+
+        ahead = scores(*order[0])
+        for i, (hh, b) in enumerate(order):
+            s = ahead
+            if i + 1 < len(order):
+                ahead = scores(*order[i + 1])
+            top = jnp.max(s, axis=0, keepdims=True)
+            e = jnp.exp(s - top)
+            total = jnp.sum(e, axis=0, keepdims=True)
+            mixed = nn(vt[hh][:, : s.shape[0]], e.astype(BF16)) * (1.0 / total)
+            outs[b] = mixed if outs[b] is None else outs[b] + mixed
+            lse_ref[pl.ds(t * 2 + hh, 1), b * WIDE : (b + 1) * WIDE] = top + jnp.log(total)
+        o_ref[:, at] = jnp.concatenate(outs, axis=1).T.astype(BF16)
         return carry
 
     lax.fori_loop(0, q_ref.shape[1] // LANE, step, 0)
 
 
-def attend_back_loop(q_ref, k_ref, v_ref, do_ref, dq_ref, dk_ref, dv_ref, base_ref, off_ref):
+def attend_back_loop(q_ref, k_ref, v_ref, o_ref, do_ref, lse_ref, dq_ref, dk_ref, dv_ref, p_ref, ds_ref, base_ref, off_ref, band_ref):
     masks = lane_masks()
     causal = base_ref is not None
-    wide = 256
+    blocks = L // WIDE
 
     def step(t, carry):
         at = pl.ds(pl.multiple_of(t * LANE, LANE), LANE)
         q, k, v, do = q_ref[:, at], k_ref[:, at], v_ref[:, at], do_ref[:, at]
-        kt = k.T
-        dq = [None] * (L // wide)
-        dk = dv = None
+        prod = (do.astype(F32) * o_ref[:, at].astype(F32)).T
+        kt = half_rows(k.T)
         for hh in range(2):
-            km, vm, qm, dom = k * masks[hh], v * masks[hh], q * masks[hh], do * masks[hh]
-            none = jnp.zeros_like(kt[:DH])
-            ktm = jnp.concatenate([kt[:DH], none] if hh == 0 else [none, kt[DH:]], axis=0)
-            band = None
+            km, vm = k * masks[hh], v * masks[hh]
+            lse = lse_ref[pl.ds(t * 2 + hh, 1), :]
+            delta = jnp.sum(prod[hh * DH : (hh + 1) * DH], axis=0, keepdims=True)
             if causal:
-                strip = bias_strip(base_ref[pl.ds(t * 2 + hh, 1), :])
-                row = lax.broadcasted_iota(jnp.int32, (QB, L), 0)
-                col = lax.broadcasted_iota(jnp.int32, (QB, L), 1)
-                strip = jnp.where(col >= row, strip, NEG)
-            for b in range(L // wide):
-                n = (b + 1) * wide if causal else k.shape[0]
-                cols = slice(b * wide, (b + 1) * wide)
-                s = nt(km[:n], q[cols])
-                if causal:
-                    parts = []
-                    for kb in range(n // QB):
-                        lo = b * wide - kb * QB
-                        if lo >= 0:
-                            parts.append(strip[:, lo : lo + wide])
-                        else:
-                            parts.append(
-                                jnp.concatenate([jnp.full((QB, -lo), NEG, F32), strip[:, : wide + lo]], axis=1)
-                            )
-                    s = s + jnp.concatenate(parts, axis=0)
-                e = jnp.exp(s - jnp.max(s, axis=0, keepdims=True))
-                prob = e * (1.0 / jnp.sum(e, axis=0, keepdims=True))
-                dvb = nn(prob.astype(BF16), dom[cols])
-                dp = nt(vm[:n], do[cols])
-                ds = prob * (dp - jnp.sum(prob * dp, axis=0, keepdims=True))
-                low = ds.astype(BF16)
-                dkb = nn(low, qm[cols])
-                dqb = nn(ktm[:, :n], low)
-                dq[b] = dqb if hh == 0 else dq[b] + dqb
-                if n < k.shape[0]:
-                    pad = jnp.zeros((k.shape[0] - n, LANE), F32)
-                    dvb, dkb = jnp.concatenate([dvb, pad], axis=0), jnp.concatenate([dkb, pad], axis=0)
-                dk = dkb if dk is None else dk + dkb
-                dv = dvb if dv is None else dv + dvb
-                if causal:
-                    for kb in range(n // QB):
-                        lo = b * wide - kb * QB
-                        part = ds[kb * QB : (kb + 1) * QB]
-                        if lo < 0:
-                            part, lo = part[:, -lo:], 0
-                        sides = []
-                        if lo:
-                            sides.append(jnp.zeros((QB, lo), F32))
-                        sides.append(part)
-                        if lo + part.shape[1] < L:
-                            sides.append(jnp.zeros((QB, L - lo - part.shape[1]), F32))
-                        part = jnp.concatenate(sides, axis=1) if len(sides) > 1 else part
-                        band = part if band is None else band + part
+                strip = masked_strip(base_ref, t * 2 + hh)
+                band_ref[...] = jnp.zeros_like(band_ref)
+            for b in range(blocks):
+                cols = slice(b * WIDE, (b + 1) * WIDE)
+                to = slice((b * 2 + hh) * WIDE, (b * 2 + hh + 1) * WIDE)
+                for kb in range(b + 1 if causal else k.shape[0] // WIDE):
+                    rows = slice(kb * WIDE, (kb + 1) * WIDE)
+                    s = nt(km[rows], q[cols])
+                    if causal:
+                        s = s + bias_tile(strip, kb * WIDE, WIDE, b * WIDE)
+                    prob = jnp.exp(s - lse[:, cols])
+                    p_ref[rows, to] = prob.astype(BF16)
+                    ds = prob * (nt(vm[rows], do[cols]) - delta[:, cols])
+                    ds_ref[rows, to] = ds.astype(BF16)
+                    if causal:
+                        for i in range(WIDE // QB):
+                            lo = b * WIDE - kb * WIDE - i * QB
+                            part = ds[i * QB : (i + 1) * QB]
+                            if lo < 0:
+                                part, lo = part[:, -lo:], 0
+                            band_ref[:, lo : lo + part.shape[1]] += part
             if causal:
-                off_ref[pl.ds(t * 2 + hh, 1), :] = fold_band(band)
+                off_ref[pl.ds(t * 2 + hh, 1), :] = fold_band(band_ref[...])
+        do2 = jnp.concatenate([do[b * WIDE : (b + 1) * WIDE] * masks[hh] for b in range(blocks) for hh in range(2)], axis=0)
+        q2 = jnp.concatenate([q[b * WIDE : (b + 1) * WIDE] * masks[hh] for b in range(blocks) for hh in range(2)], axis=0)
+        if causal:
+            for kb in range(blocks):
+                rows = slice(kb * WIDE, (kb + 1) * WIDE)
+                dv_ref[rows, at] = nn(p_ref[rows, kb * 2 * WIDE :], do2[kb * 2 * WIDE :]).astype(BF16)
+                dk_ref[rows, at] = nn(ds_ref[rows, kb * 2 * WIDE :], q2[kb * 2 * WIDE :]).astype(BF16)
+        else:
+            dv_ref[:, at] = nn(p_ref[...], do2).astype(BF16)
+            dk_ref[:, at] = nn(ds_ref[...], q2).astype(BF16)
+        dq = []
+        for b in range(blocks):
+            n = (b + 1) * WIDE if causal else k.shape[0]
+            dq.append(
+                sum(nn(kt[hh][:, :n], ds_ref[:n, (b * 2 + hh) * WIDE : (b * 2 + hh + 1) * WIDE]) for hh in range(2))
+            )
         dq_ref[:, at] = jnp.concatenate(dq, axis=1).T.astype(BF16)
-        dk_ref[:, at] = dk.astype(BF16)
-        dv_ref[:, at] = dv.astype(BF16)
         return carry
 
     lax.fori_loop(0, q_ref.shape[1] // LANE, step, 0)
 
 
-def call(body, outs, args, scratch, flops):
+def call(body, outs, args, scratch, name, flops):
     return pl.pallas_call(
         body,
         out_shape=tuple(jax.ShapeDtypeStruct(s, d) for s, d in outs),
-        in_specs=[pl.BlockSpec(memory_space=pl.ANY if far else pltpu.VMEM) for _, far in args],
+        in_specs=[pl.BlockSpec(memory_space=pltpu.HBM if far else pltpu.VMEM) for _, far in args],
         out_specs=tuple(pl.BlockSpec(memory_space=pltpu.VMEM) for _ in outs),
         scratch_shapes=scratch,
-        compiler_params=pltpu.CompilerParams(vmem_limit_bytes=VMEM_LIMIT),
+        compiler_params=pltpu.CompilerParams(vmem_limit_bytes=VMEM_LIMIT[name] * MIB),
         cost_estimate=pl.CostEstimate(flops=flops, transcendentals=0, bytes_accessed=10_000_000),
-    )(*[a for a, _ in args])
+    )(*[pltpu.with_memory_space_constraint(a, pltpu.HBM) if far else a for a, far in args])
 
 
 def sequence_copy(ref, dest, sem):
@@ -382,8 +402,8 @@
     def body(*refs):
         x_ref, hot_ref = refs[:2]
         w_refs = refs[2 : 2 + k]
-        n1_ref, q_ref, k_ref, v_ref, o_ref, gain_ref, base_ref = refs[2 + k : 9 + k]
-        x_v, we, wq, wk, wv, fwd_base, sem_x, s_e, s_q, s_k, s_v = refs[9 + k :]
+        n1_ref, q_ref, k_ref, v_ref, o_ref, gain_ref, base_ref, lse_ref = refs[2 + k : 10 + k]
+        x_v, we, wq, wk, wv, sem_x, s_e, s_q, s_k, s_v = refs[10 + k :]
         cx = sequence_copy(x_ref, x_v, sem_x)
         ce = ws.start(w_refs, we, s_e, 3 * hd, LANE)
         cq = ws.start(w_refs, wq, s_q, 0, hd)
@@ -395,38 +415,39 @@
         wait(ce)
         extra = ws.value(we, 0, 2 * LANE)
         rows = ws.rows
+        shards = d // rows
+        column = lax.broadcasted_iota(jnp.int32, (3 * shards, d), 1)
+        row = lax.broadcasted_iota(jnp.int32, (3 * shards, d), 0)
+        wanted = lax.rem(row, shards) * rows + heads + row // shards
+        packed = nn((column == wanted).astype(F32).astype(BF16), extra[:, :LANE]).astype(BF16)
         lane = lax.broadcasted_iota(jnp.int32, (LANE, d), 0)
         column = lax.broadcasted_iota(jnp.int32, (LANE, d), 1)
-        spread = (lane == lax.rem(column, rows)).astype(F32).astype(BF16)
-        wide = nn(extra[:, :LANE], spread)
-        row = lax.broadcasted_iota(jnp.int32, (d, d), 0)
-        column = lax.broadcasted_iota(jnp.int32, (d, d), 1)
+        wide = nn(packed, (lane == lax.rem(column, rows)).astype(F32).astype(BF16))
+        column = lax.broadcasted_iota(jnp.int32, (shards, d), 1)
+        mine = column // rows == lax.broadcasted_iota(jnp.int32, (shards, d), 0)
         gains = [
-            jnp.sum(jnp.where(row == (column // rows) * rows + heads + i, wide, 0.0), axis=0, keepdims=True)
-            for i in range(3)
+            jnp.sum(jnp.where(mine, wide[i * shards : (i + 1) * shards], 0.0), axis=0, keepdims=True) for i in range(3)
         ]
         gains = jnp.concatenate(gains + [jnp.zeros((5, d), F32)], axis=0)
         gain_ref[...] = gains
-        fwd_base[...] = jnp.zeros_like(fwd_base)
+        lse_ref[...] = jnp.zeros_like(lse_ref)
         base_ref[...] = jnp.zeros_like(base_ref)
         for a in range(2):
-            both = nn(extra[0:16, a * LANE : (a + 1) * LANE], hot_ref[...])[:heads]
-            fwd_base[a * heads : (a + 1) * heads, :] = both[:, :L]
-            base_ref[a * heads : (a + 1) * heads, :] = both[:, L:]
+            base_ref[a * heads : (a + 1) * heads, :] = nn(extra[0:16, a * LANE : (a + 1) * LANE], hot_ref[...])[:heads]
         n1 = (scaled * gains[0:1]).astype(BF16)
         n1_ref[...] = n1
         wait(cq)
-        q_ref[...] = nn(n1, ws.value(wq, 0, w2)).astype(BF16)
+        q_ref[...] = nn(n1_ref[...], ws.value(wq, 0, w2)).astype(BF16)
         wait(ck)
-        k_ref[...] = nn(n1, ws.value(wk, 0, w2)).astype(BF16)
+        k_ref[...] = nn(n1_ref[...], ws.value(wk, 0, w2)).astype(BF16)
         wait(cv)
-        v_ref[...] = nn(n1, ws.value(wv, 0, w2)).astype(BF16)
-        attend_loop(q_ref, k_ref, v_ref, o_ref, fwd_base)
+        v_ref[...] = nn(n1_ref[...], ws.value(wv, 0, w2)).astype(BF16)
+        attend_loop(q_ref, k_ref, v_ref, o_ref, lse_ref, base_ref)
 
     row = ((L, w2), BF16)
     return call(
         body,
-        [((L, d), BF16), row, row, row, row, ((8, d), F32), ((16, L), F32)],
+        [((L, d), BF16), row, row, row, row, ((8, d), F32), ((16, L), F32), ((16, L), F32)],
         [(inputs, True), (base_hot, False)] + ws.specs(),
         [
             pltpu.VMEM((L, d), BF16),
@@ -434,13 +455,13 @@
             ws.scratch(w2),
             ws.scratch(w2),
             ws.scratch(w2),
-            pltpu.VMEM((16, L), F32),
             DMA,
             ws.sems(),
             ws.sems(),
             ws.sems(),
             ws.sems(),
         ],
+        "ka",
         3_000_000_000,
     )
 
@@ -453,8 +474,8 @@
     def body(*refs):
         x_ref, enc_ref, a1_ref, gain_ref = refs[:4]
         w_refs = refs[4 : 4 + k]
-        r1_ref, r2_ref, n2_ref, q_ref, k_ref, v_ref, o_ref, n3_ref = refs[4 + k : 12 + k]
-        x_v, enc_v, w1, wq, wk, wv, w2v, sem_x, sem_e, s_1, s_q, s_k, s_v, s_2 = refs[12 + k :]
+        r1_ref, r2_ref, n2_ref, q_ref, k_ref, v_ref, o_ref, n3_ref, lse_ref = refs[4 + k : 13 + k]
+        x_v, enc_v, w1, wq, wk, wv, w2v, sem_x, sem_e, s_1, s_q, s_k, s_v, s_2 = refs[13 + k :]
         ce = sequence_copy(enc_ref, enc_v, sem_e)
         ck = ws.start(w_refs, wk, s_k, 2 * hd, hd)
         cv = ws.start(w_refs, wv, s_v, 3 * hd, hd)
@@ -475,7 +496,8 @@
         n2_ref[...] = n2
         wait(cq)
         q_ref[...] = nn(n2, ws.value(wq, 0, w2)).astype(BF16)
-        attend_loop(q_ref, k_ref, v_ref, o_ref, None)
+        lse_ref[...] = jnp.zeros_like(lse_ref)
+        attend_loop(q_ref, k_ref, v_ref, o_ref, lse_ref, None)
         wait(c2)
         r2 = r1_ref[...] + nt(o_ref[...], ws.value(w2v, 0, w2))
         r2_ref[...] = r2
@@ -485,12 +507,13 @@
     wide = ((L, d), BF16)
     return call(
         body,
-        [((L, d), F32), ((L, d), F32), wide, row, row, row, row, wide],
+        [((L, d), F32), ((L, d), F32), wide, row, row, row, row, wide, ((16, L), F32)],
         [(inputs, True), (encoded, True)] + near(attn_one, gains) + ws.specs(),
         [pltpu.VMEM((L, d), BF16), pltpu.VMEM((L, d), BF16)]
         + [ws.scratch(w2) for _ in range(5)]
         + [DMA, DMA]
         + [ws.sems() for _ in range(5)],
+        "kb",
         5_000_000_000,
     )
 
@@ -498,7 +521,7 @@
 def feed_forward(grid, cotangent, n3, r2, gains, carried, pieces, half, d, ff):
     ws = Weights(pieces, grid.n_z, half)
     k = len(ws.arrays)
-    tile = min(512, ff)
+    tile = min(256, ff)
     last = carried is not None
     extra_in = 4 if last else 0
     parts = Parts(grid, d, 3 * ff, False)
@@ -581,39 +604,51 @@
             ws.sems(),
             ws.sems(),
         ],
+        "kcb" if last else "kca",
         7_500_000_000,
     )
     return parts.split(result[:ng]), result[ng:]
 
 
-def attention_backward(grid, back, q, k, v, base, pieces, first_col, hd):
+def attention_backward(grid, back, q, k, v, attn, lse, base, pieces, first_col, hd, name):
     ws = Weights(pieces, grid.n_z)
     n = len(ws.arrays)
     w2 = 2 * hd
     causal = base is not None
 
     def body(*refs):
-        b_ref, q_ref, k_ref, v_ref = refs[:4]
-        base_ref = refs[4] if causal else None
-        refs = refs[5 if causal else 4 :]
+        b_ref, q_ref, k_ref, v_ref, o_ref, lse_ref = refs[:6]
+        base_ref = refs[6] if causal else None
+        refs = refs[7 if causal else 6 :]
         w_refs = refs[:n]
         dq_ref, dk_ref, dv_ref = refs[n : n + 3]
         off_ref = refs[n + 3] if causal else None
-        wo, do, s_o = refs[n + (4 if causal else 3) :]
+        wo, do, p_ref, ds_ref = refs[n + (4 if causal else 3) : n + (8 if causal else 7)]
+        band_ref, s_o = refs[-2:]
         co = ws.start(w_refs, wo, s_o, first_col, hd)
         if causal:
             off_ref[...] = jnp.zeros_like(off_ref)
         low = b_ref[...].astype(BF16)
         wait(co)
         do[...] = nn(low, ws.value(wo, 0, w2)).astype(BF16)
-        attend_back_loop(q_ref, k_ref, v_ref, do, dq_ref, dk_ref, dv_ref, base_ref, off_ref)
+        attend_back_loop(
+            q_ref, k_ref, v_ref, o_ref, do, lse_ref, dq_ref, dk_ref, dv_ref, p_ref, ds_ref, base_ref, off_ref, band_ref
+        )
 
     row = ((L, w2), BF16)
     return call(
         body,
         [row, row, row] + ([((16, L), F32)] if causal else []),
-        near(back, q, k, v) + (near(base) if causal else []) + ws.specs(),
-        [ws.scratch(w2), pltpu.VMEM((L, w2), BF16), ws.sems()],
+        near(back, q, k, v, attn, lse) + (near(base) if causal else []) + ws.specs(),
+        [
+            ws.scratch(w2),
+            pltpu.VMEM((L, w2), BF16),
+            pltpu.VMEM((L, 2 * L), BF16),
+            pltpu.VMEM((L, 2 * L), BF16),
+            pltpu.VMEM((QB, L), F32),
+            ws.sems(),
+        ],
+        name,
         3_000_000_000,
     )
 
@@ -660,6 +695,7 @@
         + [ws.scratch(w2) for _ in range(3)]
         + [DMA]
         + [ws.sems() for _ in range(3)],
+        "kd2",
         5_000_000_000,
     )
     return result[:3], parts.split(result[3:])
@@ -697,7 +733,7 @@
         dx_ref[...] = (b1_ref[...] + grad).astype(BF16)
         dgs = jnp.concatenate([dg, dg2_ref[...], dg3_ref[...], jnp.zeros((5, d), F32)], axis=0)
         turned = jnp.concatenate([jnp.zeros((NB, d), F32), dgs, jnp.zeros((LANE - NB - 8, d), F32)], axis=0).T
-        hot = hot_ref[:, L:]
+        hot = hot_ref[...]
         sums = off_ref[...]
         table = jnp.zeros((16, LANE), F32)
         for _ in range(3):
@@ -719,6 +755,7 @@
         + [ws.scratch(w2) for _ in range(3)]
         + [DMA]
         + [ws.sems() for _ in range(3)],
+        "ke2",
         4_000_000_000,
     )
     return result[0], parts.split(result[1:])
@@ -728,25 +765,47 @@
     return (left.astype(F32) + right.astype(F32)).astype(BF16)
 
 
-def scatter(grid, own, own_got, other, other_got, first):
+def scatter(grid, own, own_got, other, other_got, first, held=None):
+    sent_a = added(other[..., :first], other_got[..., :first])
+    sent_b = jnp.stack([added(v[1, ..., first:], g[1, ..., first:]) for v, g in ((own, own_got), (other, other_got))])
+    if held is not None:
+        sent_a, sent_b, held = lax.optimization_barrier((sent_a, sent_b, held))
+    got = grid.swap_m(sent_a)
+    got_b = grid.swap_y(sent_b)
+
+    def a_sum(i):
+        return added3(own[i, ..., :first], own_got[i, ..., :first], got[i])
+
+    far_a = grid.swap_y(a_sum(1))
+    far_b = grid.swap_m(added3(other[0, ..., first:], other_got[0, ..., first:], got_b[1]))
+    wa, wb = a_sum(0), added3(own[0, ..., first:], own_got[0, ..., first:], got_b[0])
+    return (wa, wb), (far_a, far_b), held
+
+
+def joined(kept, far):
+    return [
+        jnp.concatenate([added(v[d], f[d]) for v, f in zip(kept, far)], axis=-1) for d in range(kept[0].shape[0])
+    ]
+
+
+def scatter_wide(grid, own, own_got, other, other_got, first):
     n = grid.n_z
-    got = grid.swap_m(added(other[..., :first], other_got[..., :first]))
     got_own = grid.swap_y(added(own[1, ..., first:], own_got[1, ..., first:]))
     got_other = grid.swap_y(added(other[1, ..., first:], other_got[1, ..., first:]))
+    got = grid.swap_m(added(other[..., :first], other_got[..., :first]))
 
     def a_sum(i):
         return added3(own[i, ..., :first], own_got[i, ..., :first], got[i])
 
-    def b_sum(v, v_got, v_far):
-        return added3(v[0, ..., first:], v_got[0, ..., first:], v_far)
-
     far_a = grid.swap_y(a_sum(1))
-    far_b = grid.swap_m(b_sum(other, other_got, got_other))
-    wa, wb = a_sum(0), b_sum(own, own_got, got_own)
-    w = [
-        jnp.concatenate([added(wa[d], far_a[d]), added(wb[d], far_b[d])], axis=-1) for d in range(n)
-    ]
-    return w
+    wa = a_sum(0)
+    parts = []
+    for v, g, far in ((own, own_got, got_own), (other, other_got, got_other)):
+        w = [added3(v[0, d, :, first:], g[0, d, :, first:], far[d]) for d in range(n)]
+        parts.append([w[0]] + [grid.shift_z(w[d], d) for d in range(1, n)])
+    a = [added(wa[d], far_a[d]) for d in range(n)]
+    a = [a[0]] + [grid.shift_z(a[d], d) for d in range(1, n)]
+    return a, parts[0], parts[1]
 
 
 def settle(grid, w, gate=None):
@@ -816,12 +875,10 @@
         pieces_two = gather(grid, group_two)
         pieces_three = gather(grid, group_three)
 
-        turned = jnp.roll(buckets[::-1], L - QB + 1)
-        both = jnp.concatenate([turned, buckets])
-        base_hot = (both[None, :] == lax.broadcasted_iota(jnp.int32, (LANE, 2 * L), 0)).astype(BF16)
-
-        n1, q1, k1, v1, at1, gains, base = self_forward(grid, inputs, base_hot, pieces_one, d, hd, heads)
-        r1, r2, n2, q2, k2, v2, at2, n3 = cross_forward(grid, inputs, encoded, at1, gains, pieces_two, d, hd)
+        base_hot = (buckets[None, :] == lax.broadcasted_iota(jnp.int32, (LANE, L), 0)).astype(BF16)
+
+        n1, q1, k1, v1, at1, gains, base, lse1 = self_forward(grid, inputs, base_hot, pieces_one, d, hd, heads)
+        r1, r2, n2, q2, k2, v2, at2, n3, lse2 = cross_forward(grid, inputs, encoded, at1, gains, pieces_two, d, hd)
         (own3, gone), (ya, ba) = feed_forward(grid, cotangent, n3, r2, gains, None, pieces_three, 0, d, ff)
         own3_got = grid.swap_c(gone)
         (other3, gone), (y, b2, dg3) = feed_forward(
@@ -829,28 +886,31 @@
         )
         other3_got = grid.swap_c(gone)
         y_far = grid.swap_m(y)
-        w3 = scatter(grid, own3, own3_got, other3, other3_got, ff * 3 // 4 // LANE * LANE)
-        dq, dk, dv = attention_backward(grid, b2, q2, k2, v2, None, pieces_two, 4 * hd, hd)
+        a3, bo3, bt3 = scatter_wide(grid, own3, own3_got, other3, other3_got, ff * 3 // 4 // LANE * LANE)
+        dq, dk, dv = attention_backward(grid, b2, q2, k2, v2, at2, lse2, None, pieces_two, 4 * hd, hd, "kd1")
         (b1, eg, dg2), (kept, gone) = cross_finish(
             grid, encoded, b2, r1, n2, dq, dk, dv, at1, at2, gains, pieces_two, d, hd
         )
         eg_far = grid.swap_m(eg)
         got = grid.swap_c(gone)
-        z3, _ = settle(grid, w3)
-        w2 = scatter(grid, kept[0], got[0], kept[1], got[1], 4 * LANE)
-        dq, dk, dv, off = attention_backward(grid, b1, q1, k1, v1, base, pieces_two, 0, hd)
+        kept2, far2, _ = scatter(grid, kept[0], got[0], kept[1], got[1], 7 * LANE)
+        dq, dk, dv, off = attention_backward(grid, b1, q1, k1, v1, at1, lse1, base, pieces_two, 0, hd, "ke1")
         dx, (kept, gone) = self_finish(
             grid, inputs, b1, n1, dq, dk, dv, off, dg2, dg3, base_hot, gains, pieces_one, d, hd, heads
         )
         got = grid.swap_c(gone)
-        z2, _ = settle(grid, w2)
-        w1 = scatter(grid, kept[0], got[0], kept[1], got[1], 4 * LANE)
+        kept1, far1, (kept2, bt30, y, eg) = scatter(
+            grid, kept[0], got[0], kept[1], got[1], 5 * LANE, (kept2, bt3[0], y, eg)
+        )
+        b3 = bo3 + [grid.swap_m(summed([bt30] + bt3[1:]).astype(BF16))]
+        z2, _ = settle(grid, joined(kept2, far2))
+        w1 = joined(kept1, far1)
         dx_far = grid.swap_m(dx)
-        z1, (y, eg, z20, z30) = settle(grid, w1, (y, eg, z2[0], z3[0]))
+        z1, (z20, a30, b30) = settle(grid, w1, (z2[0], a3[0], b3[0]))
         layer_output = both_sequences(y, y_far)
         encoded_gradient = both_sequences(eg, eg_far)
         input_gradient = both_sequences(dx, dx_far)
-        s3 = summed([z30] + z3[1:])
+        s3 = jnp.concatenate([summed([a30] + a3[1:]), summed([b30] + b3[1:])], axis=-1)
         s2 = summed([z20] + z2[1:])
         s1 = summed(z1)
         small = s1[:, 3 * hd :]

time: 500 us -> 454 us (0.908)
  Pallas kernels: 140 us -> 92.1 us
  local copies, waits for them, and re-layouts: 18.6 us -> 30.8 us
  starting transfers between devices: 107 us -> 101 us
    pallas_call x8, Pallas kernels: 140 us -> 92.1 us  [call(): pl.pallas_call(body, out_shape=tuple((jax.ShapeDtypeStruct(s, d) for s, d...]
    unnamed x68 -> x102, local copies, waits for them, and re-layouts: 5.31 us -> 17.7 us
    ppermute x67 -> x71, starting transfers between devices: 107 us -> 101 us  [send(): return lax.ppermute(v, AXES, self.perm(move))]
    ppermute x67 -> x71, waiting for transfers between devices: 211 us -> 209 us  [send(): return lax.ppermute(v, AXES, self.perm(move))]
  transfers between devices with their start and end apart: 67 -> 71, of which waited for: 27 -> 29; matrix products, arithmetic and copies ran while one was open for 5% -> 5% of each run, Pallas kernels for 12% -> 9%
where the time goes in v1:
time: 454 us; the launch traced here: 448 us
  waiting for transfers between devices  209 us (46%)
  starting transfers between devices  101 us (22%)
  Pallas kernels  92.1 us (20%)
  local copies, waits for them, and re-layouts  30.8 us (7%)
  other arithmetic  12.9 us (3%)
    ppermute x71, waiting for transfers between devices, send(): return lax.ppermute(v, AXES, self.perm(move))  209 us
    ppermute x71, starting transfers between devices, send(): return lax.ppermute(v, AXES, self.perm(move))  101 us
    pallas_call x8, Pallas kernels, call(): pl.pallas_call(body, out_shape=tuple((jax.ShapeDtypeStruct(s, d) for s, d...  92.1 us
    unnamed x102, local copies, waits for them, and re-layouts  17.7 us
  transfers between devices with their start and end apart: 71, of which 29 were waited for; matrix products, arithmetic and copies ran while one was open for 5% of the time, Pallas kernels for 9%

profile of v1, /device:TPU:0, one launch (start us, length us, event | category | flops | bytes accessed | tf_op | source)
XLA Modules:
  0.0 447.9 jit_solution(16933774477325979925)
XLA Ops:
  7.7 5.1 %collective-permute-start.14 = (bf16[48,1920]{1,0:T(8,128)(2,1)}, bf16[48,1920]{1,0:T(8,128)(2,1)}, u32[]{:S(2)}, u32[]{:S(2)}) collective-permute-start(bf16[48,1920]{1,0:T(8,128)(2,1)} %bitcast_dynamic-update-slice_fusion.12), channel_id=1, source_target_pairs={{0,24},{1,25},{2,26},{3,27},{4,28},{5,29},{6,30},{7,31},{8,0},{9,1... | collective-permute-start | bytes 552968 | tf_op jit(solution)/shard_map/ppermute | solution.py:55
  15.4 2.0 collective-permute-start.1
  20.1 11.0 %collective-permute-done = bf16[48,1280]{1,0:T(8,128)(2,1)S(1)} collective-permute-done((bf16[48,1280]{1,0:T(8,128)(2,1)S(1)}, bf16[48,1280]{1,0:T(8,128)(2,1)S(1)}, u32[]{:S(2)}, u32[]{:S(2)}) %collective-permute-start) | collective-permute-done | bytes 122912 | tf_op jit(solution)/shard_map/ppermute | solution.py:55
  31.0 5.6 %collective-permute-done.1 = bf16[48,1280]{1,0:T(8,128)(2,1)} collective-permute-done((bf16[48,1280]{1,0:T(8,128)(2,1)S(1)}, bf16[48,1280]{1,0:T(8,128)(2,1)}, u32[]{:S(2)}, u32[]{:S(2)}) %collective-permute-start.1) | collective-permute-done | bytes 122912 | tf_op jit(solution)/shard_map/ppermute | solution.py:55
  36.6 5.5 %collective-permute-start.25 = (bf16[48,3072]{1,0:T(8,128)(2,1)S(1)}, bf16[48,3072]{1,0:T(8,128)(2,1)S(1)}, u32[]{:S(2)}, u32[]{:S(2)}) collective-permute-start(bf16[48,3072]{1,0:T(8,128)(2,1)S(1)} %pad_maximum_fusion.2), channel_id=1, source_target_pairs={{0,16},{1,17},{2,18},{3,19},{4,20},{5,21},{6,22},{7,23},{8,24},{9,... | collective-permute-start | bytes 884744 | tf_op jit(solution)/shard_map/ppermute | solution.py:55
  43.0 14.9 %collective-permute-start.24 = (bf16[48,3072]{1,0:T(8,128)(2,1)S(1)}, bf16[48,3072]{1,0:T(8,128)(2,1)S(1)}, u32[]{:S(2)}, u32[]{:S(2)}) collective-permute-start(bf16[48,3072]{1,0:T(8,128)(2,1)S(1)} %pad_maximum_fusion.2), channel_id=1, source_target_pairs={{0,8},{1,9},{2,10},{3,11},{4,12},{5,13},{6,14},{7,15},{8,16},{9,17... | collective-permute-start | bytes 884744 | tf_op jit(solution)/shard_map/ppermute | solution.py:55
  65.1 8.7 %collective-permute-done.4.refs_4_.refs_13_ = bf16[4,48,1280]{2,1,0:T(8,128)(2,1)S(1)} collective-permute-done((bf16[4,48,1280]{2,1,0:T(8,128)(2,1)S(1)}, bf16[4,48,1280]{2,1,0:T(8,128)(2,1)S(1)}, u32[]{:S(2)}, u32[]{:S(2)}) %collective-permute-start.4) | collective-permute-done | bytes 491552 | tf_op jit(solution)/shard_map/ppermute | solution.py:55
  78.7 20.3 %collective-permute-done.5.refs_5_.refs_14_ = bf16[2,48,1280]{2,1,0:T(8,128)(2,1)S(1)} collective-permute-done((bf16[2,48,1280]{2,1,0:T(8,128)(2,1)S(1)}, bf16[2,48,1280]{2,1,0:T(8,128)(2,1)S(1)}, u32[]{:S(2)}, u32[]{:S(2)}) %collective-permute-start.5) | collective-permute-done | bytes 245792 | tf_op jit(solution)/shard_map/ppermute | solution.py:55
  103.2 1.9 collective-permute-start.18
  106.8 26.6 %collective-permute-done.17.refs_7_.refs_9_.refs_13_.refs_10_ = bf16[2,48,1920]{2,1,0:T(8,128)(2,1)S(1)} collective-permute-done((bf16[2,48,1920]{2,1,0:T(8,128)(2,1)S(1)}, bf16[2,48,1920]{2,1,0:T(8,128)(2,1)S(1)}, u32[]{:S(2)}, u32[]{:S(2)}) %collective-permute-start.17) | collective-permute-done | bytes 368672 | tf_op jit(solution)/shard_map/ppermute | solution.py:55
  137.0 3.0 collective-permute-done.23.refs_13_.refs_15_.refs_19_.refs_16_
  140.0 1.7 collective-permute-start.32
  141.8 12.2 %shard_map.322 = (bf16[512,768]{1,0:T(8,128)(2,1)S(1)}, bf16[512,768]{1,0:T(8,128)(2,1)S(1)}, bf16[512,768]{1,0:T(8,128)(2,1)S(1)}, bf16[512,768]{1,0:T(8,128)(2...) custom-call(bf16[1024,768]{1,0:T(8,128)(2,1)} %refs_0_.11, ...), custom_call_target="tpu_custom_call" | custom-call | flops 3000000000 | bytes 10000000 | tf_op jit(solution)/shard_map/pallas_call | solution.py:317
  154.0 14.7 %shard_map.323 = (f32[512,768]{1,0:T(8,128)S(1)}, f32[512,768]{1,0:T(8,128)S(1)}, bf16[512,768]{1,0:T(8,128)(2,1)S(1)}, bf16[512,768]{1,0:T(8,128)(2,1)S(1)}, bf...) custom-call(bf16[1024,768]{1,0:T(8,128)(2,1)} %refs_0_.11, ...), custom_call_target="tpu_custom_call" | custom-call | flops 5000000000 | bytes 10000000 | tf_op jit(solution)/shard_map/pallas_call | solution.py:317
  170.7 11.9 %shard_map.324 = (bf16[2,4,48,3072]{3,2,1,0:T(8,128)(2,1)S(1)}, bf16[2,4,48,3072]{3,2,1,0:T(8,128)(2,1)S(1)}, f32[512,768]{1,0:T(8,128)S(1)}, f32[512,768]{1,0:T(8,128)S(1)}) custom-call(bf16[1024,768]{1,0:T(8,128)(2,1)} %refs_0_.9, bf16[512,768]{1,0:T(8,128)(2,1)S(1)} %get-tuple-element.74.refs_1_, bf16[4,48,3072]{2,1,0:T(8,128)(2,1)} %copy-done.15, ...), custom_call_target="tpu_custom_call" | custom-call | flops 7500000256 | bytes 10000000 | tf_op jit(solution)/shard_map/pallas_call | solution.py:317
  187.0 13.0 %shard_map.325 = (bf16[2,4,48,3072]{3,2,1,0:T(8,128)(2,1)S(1)}, bf16[2,4,48,3072]{3,2,1,0:T(8,128)(2,1)S(1)}, bf16[512,768]{1,0:T(8,128)(2,1)S(1)}, f32[512,768]{1,0:T(8,128)S(1)}, f32[1,768]{1,0:T(1,128)S(1)}) custom-call(bf16[1024,768]{1,0:T(8,128)(2,1)} %refs_0_.9, bf16[512,768]{1,0:T(8,128)(2,1)S(1)} %get-tuple-element.74.refs_1_, ...), custom_call_target="tpu_custom_call" | custom-call | flops 7500000256 | bytes 10000000 | tf_op jit(solution)/shard_map/pallas_call | solution.py:317
  200.0 12.4 %shard_map.326 = (bf16[512,768]{1,0:T(8,128)(2,1)S(1)}, bf16[512,768]{1,0:T(8,128)(2,1)S(1)}, bf16[512,768]{1,0:T(8,128)(2,1)S(1)}) custom-call(f32[512,768]{1,0:T(8,128)S(1)} %get-tuple-element.78.refs_0_.refs_1_, bf16[512,768]{1,0:T(8,128)(2,1)S(1)} %get-tuple-element.81.refs_1_, bf16[512,768]{1,0:T(8,128)(2,1)S(1)} %get-tuple-element.82.refs_2_, ...), custom_call_target="tpu_custom_call" | custom-call | flops 3000000000 | bytes 10000000 | tf_op jit(solution)/shard_map/pallas_call | solution.py:317
  212.4 8.2 %shard_map.327 = (f32[512,768]{1,0:T(8,128)S(1)}, bf16[512,768]{1,0:T(8,128)(2,1)S(1)}, f32[1,768]{1,0:T(1,128)S(1)}, bf16[2,2,4,48,1920]{4,3,2,1,0:T(8,128)(2,1)S(1)}, bf16[2,2,4,48,1920]{4,3,2,1,0:T(8,128)(2,1)S(1)}) custom-call(bf16[1024,768]{1,0:T(8,128)(2,1)} %refs_0_.10, f32[512,768]{1,0:T(8,128)S(1)} %get-tuple-element.78.refs_0_.refs_1_, ...), custom_call_target="tpu_custom_call" | custom-call | flops 5000000000 | bytes 10000000 | tf_op jit(solution)/shard_map/pallas_call | solution.py:317
  222.2 11.5 %shard_map.328 = (bf16[512,768]{1,0:T(8,128)(2,1)S(1)}, bf16[512,768]{1,0:T(8,128)(2,1)S(1)}, bf16[512,768]{1,0:T(8,128)(2,1)S(1)}, f32[16,512]{1,0:T(8,128)S(1)}) custom-call(f32[512,768]{1,0:T(8,128)S(1)} %get-tuple-element.89.refs_0_.refs_1_, bf16[512,768]{1,0:T(8,128)(2,1)S(1)} %get-tuple-element.91.refs_1_, ...), custom_call_target="tpu_custom_call" | custom-call | flops 3000000000 | bytes 10000000 | tf_op jit(solution)/shard_map/pallas_call | solution.py:317
  233.7 8.3 %shard_map.329 = (bf16[512,768]{1,0:T(8,128)(2,1)S(1)}, bf16[2,2,4,48,1280]{4,3,2,1,0:T(8,128)(2,1)S(1)}, bf16[2,2,4,48,1280]{4,3,2,1,0:T(8,128)(2,1)}) custom-call(bf16[1024,768]{1,0:T(8,128)(2,1)} %refs_0_.11, f32[512,768]{1,0:T(8,128)S(1)} %get-tuple-element.89.refs_0_.refs_1_, bf16[512,768]{1,0:T(8,128)(2,1)S(1)} %get-tuple-element.90.refs_2_, ...), custom_call_target="tpu_custom_call" | custom-call | flops 4000000000 | bytes 10000000 | tf_op jit(solution)/shard_map/pallas_call | solution.py:317
  245.0 1.7 collective-permute-start.43
  246.8 1.6 slice_bitcast_fusion.6
  248.6 32.9 %collective-permute-done.43 = bf16[512,768]{1,0:T(8,128)(2,1)S(1)} collective-permute-done((bf16[512,768]{1,0:T(8,128)(2,1)}, bf16[512,768]{1,0:T(8,128)(2,1)S(1)}, u32[]{:S(2)}, u32[]{:S(2)}) %collective-permute-start.43) | collective-permute-done | bytes 786464 | tf_op jit(solution)/shard_map/ppermute | solution.py:55
  281.9 1.9 maximum_convert_fusion.1
  284.9 1.6 slice_bitcast_fusion.4
  288.6 1.8 collective-permute-start.52
  292.5 20.5 %collective-permute-done.52 = bf16[2,4,48,768]{3,2,1,0:T(8,128)(2,1)S(1)} collective-permute-done((bf16[2,4,48,768]{3,2,1,0:T(8,128)(2,1)S(1)}, bf16[2,4,48,768]{3,2,1,0:T(8,128)(2,1)S(1)}, u32[]{:S(2)}, u32[]{:S(2)}) %collective-permute-start.52) | collective-permute-done | bytes 589856 | tf_op jit(solution)/shard_map/ppermute | solution.py:55
  316.8 18.7 %collective-permute-done.54 = bf16[4,48,2304]{2,1,0:T(8,128)(2,1)S(1)} collective-permute-done((bf16[4,48,2304]{2,1,0:T(8,128)(2,1)S(1)}, bf16[4,48,2304]{2,1,0:T(8,128)(2,1)S(1)}, u32[]{:S(2)}, u32[]{:S(2)}) %collective-permute-start.54) | collective-permute-done | bytes 884768 | tf_op jit(solution)/shard_map/ppermute | solution.py:55
  337.4 4.4 collective-permute-done.53
  341.9 4.7 %collective-permute-start.67 = (bf16[48,2304]{1,0:T(8,128)(2,1)S(1)}, bf16[48,2304]{1,0:T(8,128)(2,1)S(1)}, u32[]{:S(2)}, u32[]{:S(2)}) collective-permute-start(bf16[48,2304]{1,0:T(8,128)(2,1)S(1)} %get-tuple-element.135), channel_id=1, source_target_pairs={{0,8},{1,9},{2,10},{3,11},{4,12},{5,13},{6,14},{7,15},{8,16},{9,17... | collective-permute-start | bytes 663560 | tf_op jit(solution)/shard_map/ppermute | solution.py:55
  347.0 9.3 %collective-permute-done.39 = bf16[2,4,48,1024]{3,2,1,0:T(8,128)(2,1)S(1)} collective-permute-done((bf16[2,4,48,1024]{3,2,1,0:T(8,128)(2,1)S(1)}, bf16[2,4,48,1024]{3,2,1,0:T(8,128)(2,1)S(1)}, u32[]{:S(2)}, u32[]{:S(2)}) %collective-permute-start.39) | collective-permute-done | bytes 786464 | tf_op jit(solution)/shard_map/ppermute | solution.py:55
  356.3 6.6 %collective-permute-start.68 = (bf16[48,2304]{1,0:T(8,128)(2,1)S(1)}, bf16[48,2304]{1,0:T(8,128)(2,1)S(1)}, u32[]{:S(2)}, u32[]{:S(2)}) collective-permute-start(bf16[48,2304]{1,0:T(8,128)(2,1)S(1)} %get-tuple-element.137), channel_id=1, source_target_pairs={{0,16},{1,17},{2,18},{3,19},{4,20},{5,21},{6,22},{7,23},{8,24},{9,... | collective-permute-start | bytes 663560 | tf_op jit(solution)/shard_map/ppermute | solution.py:55
  363.4 4.1 collective-permute-start.63
  369.3 5.4 %collective-permute-done.68 = bf16[48,2304]{1,0:T(8,128)(2,1)S(1)} collective-permute-done((bf16[48,2304]{1,0:T(8,128)(2,1)S(1)}, bf16[48,2304]{1,0:T(8,128)(2,1)S(1)}, u32[]{:S(2)}, u32[]{:S(2)}) %collective-permute-start.68) | collective-permute-done | bytes 221216 | tf_op jit(solution)/shard_map/ppermute | solution.py:55
  376.3 1.9 maximum_convert_fusion
  378.2 1.9 maximum_convert_fusion.2
  380.8 5.9 %collective-permute-done.50 = bf16[4,48,1024]{2,1,0:T(8,128)(2,1)S(1)} collective-permute-done((bf16[4,48,1024]{2,1,0:T(8,128)(2,1)S(1)}, bf16[4,48,1024]{2,1,0:T(8,128)(2,1)S(1)}, u32[]{:S(2)}, u32[]{:S(2)}) %collective-permute-start.50) | collective-permute-done | bytes 393248 | tf_op jit(solution)/shard_map/ppermute | solution.py:55
  388.4 6.8 %collective-permute-done.45 = bf16[2,4,48,640]{3,2,1,0:T(8,128)(2,1)S(1)} collective-permute-done((bf16[2,4,48,640]{3,2,1,0:T(8,128)(2,1)S(1)}, bf16[2,4,48,640]{3,2,1,0:T(8,128)(2,1)S(1)}, u32[]{:S(2)}, u32[]{:S(2)}) %collective-permute-start.45) | collective-permute-done | bytes 491552 | tf_op jit(solution)/shard_map/ppermute | solution.py:55
  399.3 3.2 collective-permute-done.46
  404.1 2.4 collective-permute-start.66
  408.2 2.8 collective-permute-start.59
  411.0 1.7 collective-permute-done.64
  412.7 2.9 collective-permute-done.66
  415.6 8.3 %collective-permute-start.58 = (bf16[48,1920]{1,0:T(8,128)(2,1)S(1)}, bf16[48,1920]{1,0:T(8,128)(2,1)S(1)}, u32[]{:S(2)}, u32[]{:S(2)}) collective-permute-start(bf16[48,1920]{1,0:T(8,128)(2,1)S(1)} %pad_maximum_fusion.5), channel_id=1, source_target_pairs={{0,8},{1,9},{2,10},{3,11},{4,12},{5,13},{6,14},{7,15},{8,16},{9,17... | collective-permute-start | bytes 552968 | tf_op jit(solution)/shard_map/ppermute | solution.py:55
  424.0 6.9 %collective-permute-done.65 = bf16[48,2304]{1,0:T(8,128)(2,1)S(1)} collective-permute-done((bf16[48,2304]{1,0:T(8,128)(2,1)S(1)}, bf16[48,2304]{1,0:T(8,128)(2,1)S(1)}, u32[]{:S(2)}, u32[]{:S(2)}) %collective-permute-start.65) | collective-permute-done | bytes 221216 | tf_op jit(solution)/shard_map/ppermute | solution.py:55
  431.9 3.4 collective-permute-start.56
  436.3 3.1 collective-permute-done.59
  440.4 4.8 %collective-permute-done.56 = bf16[48,1280]{1,0:T(8,128)(2,1)S(1)} collective-permute-done((bf16[48,1280]{1,0:T(8,128)(2,1)S(1)}, bf16[48,1280]{1,0:T(8,128)(2,1)S(1)}, u32[]{:S(2)}, u32[]{:S(2)}) %collective-permute-start.56) | collective-permute-done | bytes 122912 | tf_op jit(solution)/shard_map/ppermute | solution.py:55
  (276 shorter events, 76.3 us)
Async XLA Ops:
  7.7 52.4 %collective-permute-start.14 = (bf16[48,1920]{1,0:T(8,128)(2,1)}, bf16[48,1920]{1,0:T(8,128)(2,1)}, u32[]{:S(2)}, u32[]{:S(2)}) collective-permute-start(bf16[48,1920]{1,0:T(8,128)(2,1)} %bitcast_dynamic-update-slice_fusion.12), channel_id=1, source_target_pairs={{0,24},{1,25},{2,26},{3,27},{4,28},{5,29},{6,30},{7,31},{8,0},{9,1... | collective-permute-start | bytes 552968 | tf_op jit(solution)/shard_map/ppermute | solution.py:55
  12.7 46.3 %collective-permute-start.13 = (bf16[48,1920]{1,0:T(8,128)(2,1)}, bf16[48,1920]{1,0:T(8,128)(2,1)}, u32[]{:S(2)}, u32[]{:S(2)}) collective-permute-start(bf16[48,1920]{1,0:T(8,128)(2,1)} %bitcast_dynamic-update-slice_fusion.12), channel_id=1, source_target_pairs={{0,16},{1,17},{2,18},{3,19},{4,20},{5,21},{6,22},{7,23},{8,24},{9,... | collective-permute-start | bytes 552968 | tf_op jit(solution)/shard_map/ppermute | solution.py:55
  12.7 45.2 %collective-permute-start.12 = (bf16[48,1920]{1,0:T(8,128)(2,1)}, bf16[48,1920]{1,0:T(8,128)(2,1)}, u32[]{:S(2)}, u32[]{:S(2)}) collective-permute-start(bf16[48,1920]{1,0:T(8,128)(2,1)} %bitcast_dynamic-update-slice_fusion.12), channel_id=1, source_target_pairs={{0,8},{1,9},{2,10},{3,11},{4,12},{5,13},{6,14},{7,15},{8,16},{9,17... | collective-permute-start | bytes 552968 | tf_op jit(solution)/shard_map/ppermute | solution.py:55
  15.4 21.2 %collective-permute-start.1 = (bf16[48,1280]{1,0:T(8,128)(2,1)S(1)}, bf16[48,1280]{1,0:T(8,128)(2,1)}, u32[]{:S(2)}, u32[]{:S(2)}) collective-permute-start(bf16[48,1280]{1,0:T(8,128)(2,1)S(1)} %get-tuple-element.130), channel_id=1, source_target_pairs={{0,16},{1,17},{2,18},{3,19},{4,20},{5,21},{6,22},{7,23},{8,24},{9,... | collective-permute-start | bytes 368648 | tf_op jit(solution)/shard_map/ppermute | solution.py:55
  36.6 28.5 %collective-permute-start.25 = (bf16[48,3072]{1,0:T(8,128)(2,1)S(1)}, bf16[48,3072]{1,0:T(8,128)(2,1)S(1)}, u32[]{:S(2)}, u32[]{:S(2)}) collective-permute-start(bf16[48,3072]{1,0:T(8,128)(2,1)S(1)} %pad_maximum_fusion.2), channel_id=1, source_target_pairs={{0,16},{1,17},{2,18},{3,19},{4,20},{5,21},{6,22},{7,23},{8,24},{9,... | collective-permute-start | bytes 884744 | tf_op jit(solution)/shard_map/ppermute | solution.py:55
  43.0 19.6 %collective-permute-start.24 = (bf16[48,3072]{1,0:T(8,128)(2,1)S(1)}, bf16[48,3072]{1,0:T(8,128)(2,1)S(1)}, u32[]{:S(2)}, u32[]{:S(2)}) collective-permute-start(bf16[48,3072]{1,0:T(8,128)(2,1)S(1)} %pad_maximum_fusion.2), channel_id=1, source_target_pairs={{0,8},{1,9},{2,10},{3,11},{4,12},{5,13},{6,14},{7,15},{8,16},{9,17... | collective-permute-start | bytes 884744 | tf_op jit(solution)/shard_map/ppermute | solution.py:55
  57.9 19.6 %collective-permute-start.26 = (bf16[48,3072]{1,0:T(8,128)(2,1)S(1)}, bf16[48,3072]{1,0:T(8,128)(2,1)S(1)}, u32[]{:S(2)}, u32[]{:S(2)}) collective-permute-start(bf16[48,3072]{1,0:T(8,128)(2,1)S(1)} %pad_maximum_fusion.2), channel_id=1, source_target_pairs={{0,24},{1,25},{2,26},{3,27},{4,28},{5,29},{6,30},{7,31},{8,0},{9,1... | collective-permute-start | bytes 884744 | tf_op jit(solution)/shard_map/ppermute | solution.py:55
  59.0 19.1 %collective-permute-start.7 = (bf16[4,48,1280]{2,1,0:T(8,128)(2,1)S(1)}, bf16[4,48,1280]{2,1,0:T(8,128)(2,1)S(1)}, u32[]{:S(2)}, u32[]{:S(2)}) collective-permute-start(bf16[4,48,1280]{2,1,0:T(8,128)(2,1)S(1)} %bitcast_dynamic-update-slice_fusion.8.refs_2_.refs_11_), channel_id=1, source_target_pairs={{0,2},{1,3},{2,0},{3,1},{4,6},{5,7},{6,4},{7,5},{8,10},{9,11},{10,... | collective-permute-start | bytes 1474568 | tf_op jit(solution)/shard_map/ppermute | solution.py:55
  65.1 35.6 %collective-permute-start.19 = (bf16[4,48,1920]{2,1,0:T(8,128)(2,1)S(1)}, bf16[4,48,1920]{2,1,0:T(8,128)(2,1)S(1)}, u32[]{:S(2)}, u32[]{:S(2)}) collective-permute-start(bf16[4,48,1920]{2,1,0:T(8,128)(2,1)S(1)} %bitcast_dynamic-update-slice_fusion.4.refs_4_.refs_6_.refs_10_.refs_7_), channel_id=1, source_target_pairs={{0,2},{1,3},{2,0},{3,1},{4,6},{5,7},{6,4},{7,5},{8,10},{9,11},{10,... | collective-permute-start | bytes 2211848 | tf_op jit(solution)/shard_map/ppermute | solution.py:55
  73.8 26.9 %collective-permute-start.16 = (bf16[4,48,1920]{2,1,0:T(8,128)(2,1)S(1)}, bf16[4,48,1920]{2,1,0:T(8,128)(2,1)S(1)}, u32[]{:S(2)}, u32[]{:S(2)}) collective-permute-start(bf16[4,48,1920]{2,1,0:T(8,128)(2,1)S(1)} %bitcast_dynamic-update-slice_fusion.4.refs_4_.refs_6_.refs_10_.refs_7_), channel_id=1, source_target_pairs={{0,1},{1,0},{2,3},{3,2},{4,5},{5,4},{6,7},{7,6},{8,9},{9,8},{10,11... | collective-permute-start | bytes 2211848 | tf_op jit(solution)/shard_map/ppermute | solution.py:55
  76.0 25.2 %collective-permute-start.15 = (bf16[4,48,1920]{2,1,0:T(8,128)(2,1)S(1)}, bf16[4,48,1920]{2,1,0:T(8,128)(2,1)S(1)}, u32[]{:S(2)}, u32[]{:S(2)}) collective-permute-start(bf16[4,48,1920]{2,1,0:T(8,128)(2,1)S(1)} %bitcast_dynamic-update-slice_fusion.4.refs_4_.refs_6_.refs_10_.refs_7_), channel_id=1, source_target_pairs={{0,4},{1,5},{2,6},{3,7},{4,0},{5,1},{6,2},{7,3},{8,12},{9,13},{10,... | collective-permute-start | bytes 2211848 | tf_op jit(solution)/shard_map/ppermute | solution.py:55
  77.6 21.5 %collective-permute-start.5 = (bf16[2,48,1280]{2,1,0:T(8,128)(2,1)S(1)}, bf16[2,48,1280]{2,1,0:T(8,128)(2,1)S(1)}, u32[]{:S(2)}, u32[]{:S(2)}) collective-permute-start(bf16[2,48,1280]{2,1,0:T(8,128)(2,1)S(1)} %slice.617), channel_id=1, source_target_pairs={{0,4},{1,5},{2,6},{3,7},{4,0},{5,1},{6,2},{7,3},{8,12},{9,13},{10,... | collective-permute-start | bytes 737288 | tf_op jit(solution)/shard_map/ppermute | solution.py:55
  78.1 21.0 %collective-permute-start.6 = (bf16[2,48,1280]{2,1,0:T(8,128)(2,1)S(1)}, bf16[2,48,1280]{2,1,0:T(8,128)(2,1)S(1)}, u32[]{:S(2)}, u32[]{:S(2)}) collective-permute-start(bf16[2,48,1280]{2,1,0:T(8,128)(2,1)S(1)} %slice.618), channel_id=1, source_target_pairs={{0,1},{1,0},{2,3},{3,2},{4,5},{5,4},{6,7},{7,6},{8,9},{9,8},{10,11... | collective-permute-start | bytes 737288 | tf_op jit(solution)/shard_map/ppermute | solution.py:55
  99.0 34.9 %collective-permute-start.30 = (bf16[4,48,3072]{2,1,0:T(8,128)(2,1)S(1)}, bf16[4,48,3072]{2,1,0:T(8,128)(2,1)S(1)}, u32[]{:S(2)}, u32[]{:S(2)}) collective-permute-start(bf16[4,48,3072]{2,1,0:T(8,128)(2,1)S(1)} %bitcast_dynamic-update-slice_fusion.refs_2_), channel_id=1, source_target_pairs={{0,1},{1,0},{2,3},{3,2},{4,5},{5,4},{6,7},{7,6},{8,9},{9,8},{10,11... | collective-permute-start | bytes 3538952 | tf_op jit(solution)/shard_map/ppermute | solution.py:55
  99.2 34.8 %collective-permute-start.27 = (bf16[4,48,3072]{2,1,0:T(8,128)(2,1)S(1)}, bf16[4,48,3072]{2,1,0:T(8,128)(2,1)S(1)}, u32[]{:S(2)}, u32[]{:S(2)}) collective-permute-start(bf16[4,48,3072]{2,1,0:T(8,128)(2,1)S(1)} %bitcast_dynamic-update-slice_fusion.refs_2_), channel_id=1, source_target_pairs={{0,4},{1,5},{2,6},{3,7},{4,0},{5,1},{6,2},{7,3},{8,12},{9,13},{10,... | collective-permute-start | bytes 3538952 | tf_op jit(solution)/shard_map/ppermute | solution.py:55
  102.5 30.8 %collective-permute-start.17 = (bf16[2,48,1920]{2,1,0:T(8,128)(2,1)S(1)}, bf16[2,48,1920]{2,1,0:T(8,128)(2,1)S(1)}, u32[]{:S(2)}, u32[]{:S(2)}) collective-permute-start(bf16[2,48,1920]{2,1,0:T(8,128)(2,1)S(1)} %slice.619), channel_id=1, source_target_pairs={{0,4},{1,5},{2,6},{3,7},{4,0},{5,1},{6,2},{7,3},{8,12},{9,13},{10,... | collective-permute-start | bytes 1105928 | tf_op jit(solution)/shard_map/ppermute | solution.py:55
  103.2 30.1 %collective-permute-start.18 = (bf16[2,48,1920]{2,1,0:T(8,128)(2,1)S(1)}, bf16[2,48,1920]{2,1,0:T(8,128)(2,1)S(1)}, u32[]{:S(2)}, u32[]{:S(2)}) collective-permute-start(bf16[2,48,1920]{2,1,0:T(8,128)(2,1)S(1)} %slice.620), channel_id=1, source_target_pairs={{0,1},{1,0},{2,3},{3,2},{4,5},{5,4},{6,7},{7,6},{8,9},{9,8},{10,11... | collective-permute-start | bytes 1105928 | tf_op jit(solution)/shard_map/ppermute | solution.py:55
  106.7 28.7 %collective-permute-start.21 = (bf16[4,48,1920]{2,1,0:T(8,128)(2,1)S(1)}, bf16[4,48,1920]{2,1,0:T(8,128)(2,1)S(1)}, u32[]{:S(2)}, u32[]{:S(2)}) collective-permute-start(bf16[4,48,1920]{2,1,0:T(8,128)(2,1)S(1)} %collective-permute-done.16.refs_6_.refs_8_.refs_12_.refs_9_), channel_id=1, source_target_pairs={{0,2},{1,3},{2,0},{3,1},{4,6},{5,7},{6,4},{7,5},{8,10},{9,11},{10,... | collective-permute-start | bytes 2211848 | tf_op jit(solution)/shard_map/ppermute | solution.py:55
  133.9 35.4 %collective-permute-start.28 = (bf16[4,48,3072]{2,1,0:T(8,128)(2,1)S(1)}, bf16[4,48,3072]{2,1,0:T(8,128)(2,1)S(1)}, u32[]{:S(2)}, u32[]{:S(2)}) collective-permute-start(bf16[4,48,3072]{2,1,0:T(8,128)(2,1)S(1)} %bitcast_dynamic-update-slice_fusion.refs_2_), channel_id=1, source_target_pairs={{0,2},{1,3},{2,0},{3,1},{4,6},{5,7},{6,4},{7,5},{8,10},{9,11},{10,... | collective-permute-start | bytes 3538952 | tf_op jit(solution)/shard_map/ppermute | solution.py:55
  134.0 35.3 %collective-permute-start.29 = (bf16[4,48,3072]{2,1,0:T(8,128)(2,1)S(1)}, bf16[4,48,3072]{2,1,0:T(8,128)(2,1)S(1)}, u32[]{:S(2)}, u32[]{:S(2)}) collective-permute-start(bf16[4,48,3072]{2,1,0:T(8,128)(2,1)S(1)} %collective-permute-done.27.refs_3_), channel_id=1, source_target_pairs={{0,2},{1,3},{2,0},{3,1},{4,6},{5,7},{6,4},{7,5},{8,10},{9,11},{10,... | collective-permute-start | bytes 3538952 | tf_op jit(solution)/shard_map/ppermute | solution.py:55
  135.4 33.3 %collective-permute-start.31 = (bf16[2,48,3072]{2,1,0:T(8,128)(2,1)S(1)}, bf16[2,48,3072]{2,1,0:T(8,128)(2,1)S(1)}, u32[]{:S(2)}, u32[]{:S(2)}) collective-permute-start(bf16[2,48,3072]{2,1,0:T(8,128)(2,1)S(1)} %slice.621), channel_id=1, source_target_pairs={{0,4},{1,5},{2,6},{3,7},{4,0},{5,1},{6,2},{7,3},{8,12},{9,13},{10,... | collective-permute-start | bytes 1769480 | tf_op jit(solution)/shard_map/ppermute | solution.py:55
  140.0 29.0 %collective-permute-start.32 = (bf16[2,48,3072]{2,1,0:T(8,128)(2,1)S(1)}, bf16[2,48,3072]{2,1,0:T(8,128)(2,1)S(1)}, u32[]{:S(2)}, u32[]{:S(2)}) collective-permute-start(bf16[2,48,3072]{2,1,0:T(8,128)(2,1)S(1)} %slice.622), channel_id=1, source_target_pairs={{0,1},{1,0},{2,3},{3,2},{4,5},{5,4},{6,7},{7,6},{8,9},{9,8},{10,11... | collective-permute-start | bytes 1769480 | tf_op jit(solution)/shard_map/ppermute | solution.py:55
  141.7 43.9 %collective-permute-start.33 = (bf16[4,48,3072]{2,1,0:T(8,128)(2,1)S(1)}, bf16[4,48,3072]{2,1,0:T(8,128)(2,1)S(1)}, u32[]{:S(2)}, u32[]{:S(2)}) collective-permute-start(bf16[4,48,3072]{2,1,0:T(8,128)(2,1)S(1)} %collective-permute-done.30.refs_6_), channel_id=1, source_target_pairs={{0,2},{1,3},{2,0},{3,1},{4,6},{5,7},{6,4},{7,5},{8,10},{9,11},{10,... | collective-permute-start | bytes 3538952 | tf_op jit(solution)/shard_map/ppermute | solution.py:55
  168.7 16.9 %collective-permute-start.34 = (bf16[2,48,3072]{2,1,0:T(8,128)(2,1)S(1)}, bf16[2,48,3072]{2,1,0:T(8,128)(2,1)S(1)}, u32[]{:S(2)}, u32[]{:S(2)}) collective-permute-start(bf16[2,48,3072]{2,1,0:T(8,128)(2,1)S(1)} %collective-permute-done.31.refs_7_), channel_id=1, source_target_pairs={{0,2},{1,3},{2,0},{3,1},{4,6},{5,7},{6,4},{7,5},{8,10},{9,11},{10,... | collective-permute-start | bytes 1769480 | tf_op jit(solution)/shard_map/ppermute | solution.py:55
  244.2 39.6 %collective-permute-start.36 = (bf16[2,2,4,48,1280]{4,3,2,1,0:T(8,128)(2,1)}, bf16[2,2,4,48,1280]{4,3,2,1,0:T(8,128)(2,1)}, u32[]{:S(2)}, u32[]{:S(2)}) collective-permute-start(bf16[2,2,4,48,1280]{4,3,2,1,0:T(8,128)(2,1)} %get-tuple-element.103), channel_id=1, source_target_pairs={{0,2},{1,3},{2,0},{3,1},{4,6},{5,7},{6,4},{7,5},{8,10},{9,11},{10,... | collective-permute-start | bytes 5898248 | tf_op jit(solution)/shard_map/ppermute | solution.py:55
  244.5 46.1 %collective-permute-start.51 = (bf16[2,4,48,3072]{3,2,1,0:T(8,128)(2,1)}, bf16[2,4,48,3072]{3,2,1,0:T(8,128)(2,1)S(1)}, u32[]{:S(2)}, u32[]{:S(2)}) collective-permute-start(bf16[2,4,48,3072]{3,2,1,0:T(8,128)(2,1)} %copy-done.13), channel_id=1, source_target_pairs={{0,2},{1,3},{2,0},{3,1},{4,6},{5,7},{6,4},{7,5},{8,10},{9,11},{10,... | collective-permute-start | bytes 7077896 | tf_op jit(solution)/shard_map/ppermute | solution.py:55
  244.7 118.5 %collective-permute-start.42 = (bf16[512,768]{1,0:T(8,128)(2,1)}, bf16[512,768]{1,0:T(8,128)(2,1)S(1)}, u32[]{:S(2)}, u32[]{:S(2)}) collective-permute-start(bf16[512,768]{1,0:T(8,128)(2,1)} %copy-done.5), channel_id=1, source_target_pairs={{0,1},{1,0},{2,3},{3,2},{4,5},{5,4},{6,7},{7,6},{8,9},{9,8},{10,11... | collective-permute-start | bytes 2359304 | tf_op jit(solution)/shard_map/ppermute | solution.py:55
  245.0 41.8 %collective-permute-start.40 = (bf16[2,4,48,3072]{3,2,1,0:T(8,128)(2,1)}, bf16[2,4,48,3072]{3,2,1,0:T(8,128)(2,1)S(1)}, u32[]{:S(2)}, u32[]{:S(2)}) collective-permute-start(bf16[2,4,48,3072]{3,2,1,0:T(8,128)(2,1)} %copy-done.14), channel_id=1, source_target_pairs={{0,2},{1,3},{2,0},{3,1},{4,6},{5,7},{6,4},{7,5},{8,10},{9,11},{10,... | collective-permute-start | bytes 7077896 | tf_op jit(solution)/shard_map/ppermute | solution.py:55
  245.0 36.5 %collective-permute-start.43 = (bf16[512,768]{1,0:T(8,128)(2,1)}, bf16[512,768]{1,0:T(8,128)(2,1)S(1)}, u32[]{:S(2)}, u32[]{:S(2)}) collective-permute-start(bf16[512,768]{1,0:T(8,128)(2,1)} %copy-done.9), channel_id=1, source_target_pairs={{0,1},{1,0},{2,3},{3,2},{4,5},{5,4},{6,7},{7,6},{8,9},{9,8},{10,11... | collective-permute-start | bytes 2359304 | tf_op jit(solution)/shard_map/ppermute | solution.py:55
  281.5 81.9 %collective-permute-start.44 = (bf16[512,768]{1,0:T(8,128)(2,1)S(1)}, bf16[512,768]{1,0:T(8,128)(2,1)S(1)}, u32[]{:S(2)}, u32[]{:S(2)}) collective-permute-start(bf16[512,768]{1,0:T(8,128)(2,1)S(1)} %copy-done.8), channel_id=1, source_target_pairs={{0,1},{1,0},{2,3},{3,2},{4,5},{5,4},{6,7},{7,6},{8,9},{9,8},{10,11... | collective-permute-start | bytes 2359304 | tf_op jit(solution)/shard_map/ppermute | solution.py:55
  284.9 29.9 %collective-permute-start.37 = (bf16[2,2,4,48,1920]{4,3,2,1,0:T(8,128)(2,1)S(1)}, bf16[2,2,4,48,1920]{4,3,2,1,0:T(8,128)(2,1)S(1)}, u32[]{:S(2)}, u32[]{:S(2)}) collective-permute-start(bf16[2,2,4,48,1920]{4,3,2,1,0:T(8,128)(2,1)S(1)} %copy-done.12), channel_id=1, source_target_pairs={{0,2},{1,3},{2,0},{3,1},{4,6},{5,7},{6,4},{7,5},{8,10},{9,11},{10,... | collective-permute-start | bytes 8847368 | tf_op jit(solution)/shard_map/ppermute | solution.py:55
  288.6 24.5 %collective-permute-start.52 = (bf16[2,4,48,768]{3,2,1,0:T(8,128)(2,1)S(1)}, bf16[2,4,48,768]{3,2,1,0:T(8,128)(2,1)S(1)}, u32[]{:S(2)}, u32[]{:S(2)}) collective-permute-start(bf16[2,4,48,768]{3,2,1,0:T(8,128)(2,1)S(1)} %add_convert_fusion.3), channel_id=1, source_target_pairs={{0,1},{1,0},{2,3},{3,2},{4,5},{5,4},{6,7},{7,6},{8,9},{9,8},{10,11... | collective-permute-start | bytes 1769480 | tf_op jit(solution)/shard_map/ppermute | solution.py:55
  290.7 25.5 %collective-permute-start.41 = (bf16[4,48,2304]{2,1,0:T(8,128)(2,1)S(1)}, bf16[4,48,2304]{2,1,0:T(8,128)(2,1)S(1)}, u32[]{:S(2)}, u32[]{:S(2)}) collective-permute-start(bf16[4,48,2304]{2,1,0:T(8,128)(2,1)S(1)} %fusion), channel_id=1, source_target_pairs={{0,4},{1,5},{2,6},{3,7},{4,0},{5,1},{6,2},{7,3},{8,12},{9,13},{10,... | collective-permute-start | bytes 2654216 | tf_op jit(solution)/shard_map/ppermute | solution.py:55
  313.0 22.5 %collective-permute-start.54 = (bf16[4,48,2304]{2,1,0:T(8,128)(2,1)S(1)}, bf16[4,48,2304]{2,1,0:T(8,128)(2,1)S(1)}, u32[]{:S(2)}, u32[]{:S(2)}) collective-permute-start(bf16[4,48,2304]{2,1,0:T(8,128)(2,1)S(1)} %fusion.1), channel_id=1, source_target_pairs={{0,4},{1,5},{2,6},{3,7},{4,0},{5,1},{6,2},{7,3},{8,12},{9,13},{10,... | collective-permute-start | bytes 2654216 | tf_op jit(solution)/shard_map/ppermute | solution.py:55
  314.9 27.0 %collective-permute-start.53 = (bf16[4,48,768]{2,1,0:T(8,128)(2,1)S(1)}, bf16[4,48,768]{2,1,0:T(8,128)(2,1)S(1)}, u32[]{:S(2)}, u32[]{:S(2)}) collective-permute-start(bf16[4,48,768]{2,1,0:T(8,128)(2,1)S(1)} %get-tuple-element.140), channel_id=1, source_target_pairs={{0,4},{1,5},{2,6},{3,7},{4,0},{5,1},{6,2},{7,3},{8,12},{9,13},{10,... | collective-permute-start | bytes 884744 | tf_op jit(solution)/shard_map/ppermute | solution.py:55
  316.1 30.6 %collective-permute-start.38 = (bf16[2,4,48,896]{3,2,1,0:T(8,128)(2,1)S(1)}, bf16[2,4,48,896]{3,2,1,0:T(8,128)(2,1)S(1)}, u32[]{:S(2)}, u32[]{:S(2)}) collective-permute-start(bf16[2,4,48,896]{3,2,1,0:T(8,128)(2,1)S(1)} %add_convert_fusion.2), channel_id=1, source_target_pairs={{0,1},{1,0},{2,3},{3,2},{4,5},{5,4},{6,7},{7,6},{8,9},{9,8},{10,11... | collective-permute-start | bytes 2064392 | tf_op jit(solution)/shard_map/ppermute | solution.py:55
  335.5 20.8 %collective-permute-start.39 = (bf16[2,4,48,1024]{3,2,1,0:T(8,128)(2,1)S(1)}, bf16[2,4,48,1024]{3,2,1,0:T(8,128)(2,1)S(1)}, u32[]{:S(2)}, u32[]{:S(2)}) collective-permute-start(bf16[2,4,48,1024]{3,2,1,0:T(8,128)(2,1)S(1)} %pad_maximum_fusion), channel_id=1, source_target_pairs={{0,4},{1,5},{2,6},{3,7},{4,0},{5,1},{6,2},{7,3},{8,12},{9,13},{10,... | collective-permute-start | bytes 2359304 | tf_op jit(solution)/shard_map/ppermute | solution.py:55
  341.9 25.8 %collective-permute-start.67 = (bf16[48,2304]{1,0:T(8,128)(2,1)S(1)}, bf16[48,2304]{1,0:T(8,128)(2,1)S(1)}, u32[]{:S(2)}, u32[]{:S(2)}) collective-permute-start(bf16[48,2304]{1,0:T(8,128)(2,1)S(1)} %get-tuple-element.135), channel_id=1, source_target_pairs={{0,8},{1,9},{2,10},{3,11},{4,12},{5,13},{6,14},{7,15},{8,16},{9,17... | collective-permute-start | bytes 663560 | tf_op jit(solution)/shard_map/ppermute | solution.py:55
  346.7 21.1 %collective-permute-start.69 = (bf16[48,2304]{1,0:T(8,128)(2,1)S(1)}, bf16[48,2304]{1,0:T(8,128)(2,1)S(1)}, u32[]{:S(2)}, u32[]{:S(2)}) collective-permute-start(bf16[48,2304]{1,0:T(8,128)(2,1)S(1)} %get-tuple-element.136), channel_id=1, source_target_pairs={{0,24},{1,25},{2,26},{3,27},{4,28},{5,29},{6,30},{7,31},{8,0},{9,1... | collective-permute-start | bytes 663560 | tf_op jit(solution)/shard_map/ppermute | solution.py:55
  356.3 18.4 %collective-permute-start.68 = (bf16[48,2304]{1,0:T(8,128)(2,1)S(1)}, bf16[48,2304]{1,0:T(8,128)(2,1)S(1)}, u32[]{:S(2)}, u32[]{:S(2)}) collective-permute-start(bf16[48,2304]{1,0:T(8,128)(2,1)S(1)} %get-tuple-element.137), channel_id=1, source_target_pairs={{0,16},{1,17},{2,18},{3,19},{4,20},{5,21},{6,22},{7,23},{8,24},{9,... | collective-permute-start | bytes 663560 | tf_op jit(solution)/shard_map/ppermute | solution.py:55
  363.2 43.4 %collective-permute-start.61 = (bf16[48,768]{1,0:T(8,128)(2,1)S(1)}, bf16[48,768]{1,0:T(8,128)(2,1)S(1)}, u32[]{:S(2)}, u32[]{:S(2)}) collective-permute-start(bf16[48,768]{1,0:T(8,128)(2,1)S(1)} %get-tuple-element.170), channel_id=1, source_target_pairs={{0,8},{1,9},{2,10},{3,11},{4,12},{5,13},{6,14},{7,15},{8,16},{9,17... | collective-permute-start | bytes 221192 | tf_op jit(solution)/shard_map/ppermute | solution.py:55
  363.4 43.2 %collective-permute-start.63 = (bf16[48,768]{1,0:T(8,128)(2,1)S(1)}, bf16[48,768]{1,0:T(8,128)(2,1)S(1)}, u32[]{:S(2)}, u32[]{:S(2)}) collective-permute-start(bf16[48,768]{1,0:T(8,128)(2,1)S(1)} %get-tuple-element.171), channel_id=1, source_target_pairs={{0,24},{1,25},{2,26},{3,27},{4,28},{5,29},{6,30},{7,31},{8,0},{9,1... | collective-permute-start | bytes 221192 | tf_op jit(solution)/shard_map/ppermute | solution.py:55
  367.7 40.5 %collective-permute-start.62 = (bf16[48,768]{1,0:T(8,128)(2,1)S(1)}, bf16[48,768]{1,0:T(8,128)(2,1)S(1)}, u32[]{:S(2)}, u32[]{:S(2)}) collective-permute-start(bf16[48,768]{1,0:T(8,128)(2,1)S(1)} %get-tuple-element.172), channel_id=1, source_target_pairs={{0,16},{1,17},{2,18},{3,19},{4,20},{5,21},{6,22},{7,23},{8,24},{9,... | collective-permute-start | bytes 221192 | tf_op jit(solution)/shard_map/ppermute | solution.py:55
  406.6 24.2 %collective-permute-start.65 = (bf16[48,2304]{1,0:T(8,128)(2,1)S(1)}, bf16[48,2304]{1,0:T(8,128)(2,1)S(1)}, u32[]{:S(2)}, u32[]{:S(2)}) collective-permute-start(bf16[48,2304]{1,0:T(8,128)(2,1)S(1)} %get-tuple-element.133), channel_id=1, source_target_pairs={{0,16},{1,17},{2,18},{3,19},{4,20},{5,21},{6,22},{7,23},{8,24},{9,... | collective-permute-start | bytes 663560 | tf_op jit(solution)/shard_map/ppermute | solution.py:55
  406.7 25.2 %collective-permute-start.70 = (bf16[48,2304]{1,0:T(8,128)(2,1)S(1)}, bf16[48,2304]{1,0:T(8,128)(2,1)S(1)}, u32[]{:S(2)}, u32[]{:S(2)}) collective-permute-start(bf16[48,2304]{1,0:T(8,128)(2,1)S(1)} %add_convert_fusion.19), channel_id=1, source_target_pairs={{0,1},{1,0},{2,3},{3,2},{4,5},{5,4},{6,7},{7,6},{8,9},{9,8},{10,11... | collective-permute-start | bytes 663560 | tf_op jit(solution)/shard_map/ppermute | solution.py:55
  408.2 31.2 %collective-permute-start.59 = (bf16[48,1920]{1,0:T(8,128)(2,1)S(1)}, bf16[48,1920]{1,0:T(8,128)(2,1)S(1)}, u32[]{:S(2)}, u32[]{:S(2)}) collective-permute-start(bf16[48,1920]{1,0:T(8,128)(2,1)S(1)} %pad_maximum_fusion.6), channel_id=1, source_target_pairs={{0,16},{1,17},{2,18},{3,19},{4,20},{5,21},{6,22},{7,23},{8,24},{9,... | collective-permute-start | bytes 552968 | tf_op jit(solution)/shard_map/ppermute | solution.py:55
  412.7 26.8 %collective-permute-start.60 = (bf16[48,1920]{1,0:T(8,128)(2,1)S(1)}, bf16[48,1920]{1,0:T(8,128)(2,1)S(1)}, u32[]{:S(2)}, u32[]{:S(2)}) collective-permute-start(bf16[48,1920]{1,0:T(8,128)(2,1)S(1)} %pad_maximum_fusion.7), channel_id=1, source_target_pairs={{0,24},{1,25},{2,26},{3,27},{4,28},{5,29},{6,30},{7,31},{8,0},{9,1... | collective-permute-start | bytes 552968 | tf_op jit(solution)/shard_map/ppermute | solution.py:55
  415.6 23.9 %collective-permute-start.58 = (bf16[48,1920]{1,0:T(8,128)(2,1)S(1)}, bf16[48,1920]{1,0:T(8,128)(2,1)S(1)}, u32[]{:S(2)}, u32[]{:S(2)}) collective-permute-start(bf16[48,1920]{1,0:T(8,128)(2,1)S(1)} %pad_maximum_fusion.5), channel_id=1, source_target_pairs={{0,8},{1,9},{2,10},{3,11},{4,12},{5,13},{6,14},{7,15},{8,16},{9,17... | collective-permute-start | bytes 552968 | tf_op jit(solution)/shard_map/ppermute | solution.py:55
  (72 other events, 1231.5 us)

commit v2 on v1

--- a/solution.py
+++ b/solution.py
@@ -19,7 +19,7 @@
 F32 = jnp.float32
 BF16 = jnp.bfloat16
 MIB = 1024 * 1024
-VMEM_LIMIT = {"ka": 13, "kb": 16, "kca": 20, "kcb": 22, "kd1": 12, "kd2": 18, "ke1": 12, "ke2": 16}
+VMEM_LIMIT = {"ka": 13, "kb": 16, "kca": 20, "kcb": 22, "kd1": 12, "kd2": 20, "ke1": 12, "ke2": 16}
 
 
 def nn(left, right):
@@ -119,25 +119,26 @@
     def specs(self):
         return [(a, True) for a in self.arrays]
 
-    def scratch(self, n):
+    def scratch(self, n, count=None):
+        lead = () if count is None else (count,)
         if self.packed:
-            return pltpu.VMEM((4 * self.n_z * self.rows, n), BF16)
-        return pltpu.VMEM((self.n_z, 2, 2, self.rows, n), BF16)
-
-    def sems(self):
-        return pltpu.SemaphoreType.DMA((len(self.arrays),))
-
-    def start(self, refs, dest, sems, src, n, at=0):
+            return pltpu.VMEM(lead + (4 * self.n_z * self.rows, n), BF16)
+        return pltpu.VMEM(lead + (self.n_z, 2, 2, self.rows, n), BF16)
+
+    def sems(self, count=1):
+        return pltpu.SemaphoreType.DMA((count * len(self.arrays),))
+
+    def start(self, refs, dest, sems, src, n, at=0, slot=0):
         _, y, c, _ = place()
         copies = []
         for i, ((m, b, e, j), ref) in enumerate(zip(self.metas, refs)):
             to = pl.ds(at + (0 if self.half is not None else m * n), n)
             if self.packed:
-                cp = pltpu.make_async_copy(ref.at[:, pl.ds(src, n)], dest.at[:, to], sems.at[i])
+                cp = pltpu.make_async_copy(ref.at[:, pl.ds(src, n)], dest.at[:, to], sems.at[slot * len(self.arrays) + i])
             else:
                 k = ref.shape[0]
                 cp = pltpu.make_async_copy(
-                    ref.at[:, :, pl.ds(src, n)], dest.at[pl.ds(j, k), y ^ b, c ^ e, :, to], sems.at[i]
+                    ref.at[:, :, pl.ds(src, n)], dest.at[pl.ds(j, k), y ^ b, c ^ e, :, to], sems.at[slot * len(self.arrays) + i]
                 )
             cp.start()
             copies.append(cp)
@@ -157,6 +158,14 @@
 def wait(copies):
     for cp in copies:
         cp.wait()
+
+
+def wait_for(turn, groups):
+    for i, copies in enumerate(groups):
+
+        @pl.when(turn == i)
+        def _(copies=copies):
+            wait(copies)
 
 
 def rms(values, gain):
@@ -402,13 +411,11 @@
     def body(*refs):
         x_ref, hot_ref = refs[:2]
         w_refs = refs[2 : 2 + k]
-        n1_ref, q_ref, k_ref, v_ref, o_ref, gain_ref, base_ref, lse_ref = refs[2 + k : 10 + k]
-        x_v, we, wq, wk, wv, sem_x, s_e, s_q, s_k, s_v = refs[10 + k :]
+        n1_ref, qkv_ref, o_ref, gain_ref, base_ref, lse_ref = refs[2 + k : 8 + k]
+        x_v, we, w, sem_x, s_e, s_w = refs[8 + k :]
         cx = sequence_copy(x_ref, x_v, sem_x)
         ce = ws.start(w_refs, we, s_e, 3 * hd, LANE)
-        cq = ws.start(w_refs, wq, s_q, 0, hd)
-        ck = ws.start(w_refs, wk, s_k, hd, hd)
-        cv = ws.start(w_refs, wv, s_v, 2 * hd, hd)
+        cw = [ws.start(w_refs, w.at[g], s_w, g * hd, hd, slot=g) for g in range(3)]
         cx.wait()
         x = x_v[...].astype(F32)
         scaled = x * lax.rsqrt(jnp.mean(x * x, axis=-1, keepdims=True) + EPS)
@@ -434,32 +441,28 @@
         base_ref[...] = jnp.zeros_like(base_ref)
         for a in range(2):
             base_ref[a * heads : (a + 1) * heads, :] = nn(extra[0:16, a * LANE : (a + 1) * LANE], hot_ref[...])[:heads]
-        n1 = (scaled * gains[0:1]).astype(BF16)
-        n1_ref[...] = n1
-        wait(cq)
-        q_ref[...] = nn(n1_ref[...], ws.value(wq, 0, w2)).astype(BF16)
-        wait(ck)
-        k_ref[...] = nn(n1_ref[...], ws.value(wk, 0, w2)).astype(BF16)
-        wait(cv)
-        v_ref[...] = nn(n1_ref[...], ws.value(wv, 0, w2)).astype(BF16)
-        attend_loop(q_ref, k_ref, v_ref, o_ref, lse_ref, base_ref)
+        n1_ref[...] = (scaled * gains[0:1]).astype(BF16)
+
+        def project(g, carry):
+            wait_for(g, cw)
+            qkv_ref[g] = nn(n1_ref[...], ws.value(w.at[g], 0, w2)).astype(BF16)
+            return carry
+
+        lax.fori_loop(0, 3, project, 0)
+        attend_loop(qkv_ref.at[0], qkv_ref.at[1], qkv_ref.at[2], o_ref, lse_ref, base_ref)
 
     row = ((L, w2), BF16)
     return call(
         body,
-        [((L, d), BF16), row, row, row, row, ((8, d), F32), ((16, L), F32), ((16, L), F32)],
+        [((L, d), BF16), ((3, L, w2), BF16), row, ((8, d), F32), ((16, L), F32), ((16, L), F32)],
         [(inputs, True), (base_hot, False)] + ws.specs(),
         [
             pltpu.VMEM((L, d), BF16),
             ws.scratch(2 * LANE),
-            ws.scratch(w2),
-            ws.scratch(w2),
-            ws.scratch(w2),
+            ws.scratch(w2, 3),
             DMA,
             ws.sems(),
-            ws.sems(),
-            ws.sems(),
-            ws.sems(),
+            ws.sems(3),
         ],
         "ka",
         3_000_000_000,
@@ -474,45 +477,61 @@
     def body(*refs):
         x_ref, enc_ref, a1_ref, gain_ref = refs[:4]
         w_refs = refs[4 : 4 + k]
-        r1_ref, r2_ref, n2_ref, q_ref, k_ref, v_ref, o_ref, n3_ref, lse_ref = refs[4 + k : 13 + k]
-        x_v, enc_v, w1, wq, wk, wv, w2v, sem_x, sem_e, s_1, s_q, s_k, s_v, s_2 = refs[13 + k :]
+        r1_ref, r2_ref, n2_ref, qkv_ref, o_ref, n3_ref, lse_ref = refs[4 + k : 11 + k]
+        x_v, enc_v, w, sem_x, sem_e, s_w = refs[11 + k :]
         ce = sequence_copy(enc_ref, enc_v, sem_e)
-        ck = ws.start(w_refs, wk, s_k, 2 * hd, hd)
-        cv = ws.start(w_refs, wv, s_v, 3 * hd, hd)
+        cw = {g: ws.start(w_refs, w.at[g], s_w, g * hd, hd, slot=g) for g in (2, 3)}
         cx = sequence_copy(x_ref, x_v, sem_x)
-        c1 = ws.start(w_refs, w1, s_1, 0, hd)
-        cq = ws.start(w_refs, wq, s_q, hd, hd)
-        c2 = ws.start(w_refs, w2v, s_2, 4 * hd, hd)
+        cw.update({g: ws.start(w_refs, w.at[g], s_w, g * hd, hd, slot=g) for g in (0, 1, 4)})
         ce.wait()
-        wait(ck)
-        k_ref[...] = nn(enc_v[...], ws.value(wk, 0, w2)).astype(BF16)
-        wait(cv)
-        v_ref[...] = nn(enc_v[...], ws.value(wv, 0, w2)).astype(BF16)
+
+        def project(g, carry):
+            wait_for(g, [cw[2], cw[3]])
+            qkv_ref[g + 1] = nn(enc_v[...], ws.value(w.at[g + 2], 0, w2)).astype(BF16)
+            return carry
+
+        lax.fori_loop(0, 2, project, 0)
         cx.wait()
-        wait(c1)
-        r1 = x_v[...].astype(F32) + nt(a1_ref[...], ws.value(w1, 0, w2))
-        r1_ref[...] = r1
-        n2 = rms(r1, gain_ref[1:2, :]).astype(BF16)
-        n2_ref[...] = n2
-        wait(cq)
-        q_ref[...] = nn(n2, ws.value(wq, 0, w2)).astype(BF16)
+        wait(cw[0])
+        wait(cw[1])
+
+        def resume(t, carry):
+            rows = pl.ds(pl.multiple_of(t * WIDE, WIDE), WIDE)
+            r1 = x_v[rows, :].astype(F32) + nt(a1_ref[rows, :], ws.value(w.at[0], 0, w2))
+            r1_ref[rows, :] = r1
+            n2 = rms(r1, gain_ref[1:2, :]).astype(BF16)
+            n2_ref[rows, :] = n2
+            qkv_ref[0, rows, :] = nn(n2, ws.value(w.at[1], 0, w2)).astype(BF16)
+            return carry
+
+        lax.fori_loop(0, L // WIDE, resume, 0)
         lse_ref[...] = jnp.zeros_like(lse_ref)
-        attend_loop(q_ref, k_ref, v_ref, o_ref, lse_ref, None)
-        wait(c2)
-        r2 = r1_ref[...] + nt(o_ref[...], ws.value(w2v, 0, w2))
-        r2_ref[...] = r2
-        n3_ref[...] = rms(r2, gain_ref[2:3, :]).astype(BF16)
+        attend_loop(qkv_ref.at[0], qkv_ref.at[1], qkv_ref.at[2], o_ref, lse_ref, None)
+        wait(cw[4])
+
+        def close(t, carry):
+            rows = pl.ds(pl.multiple_of(t * WIDE, WIDE), WIDE)
+            r2 = r1_ref[rows, :] + nt(o_ref[rows, :], ws.value(w.at[4], 0, w2))
+            r2_ref[rows, :] = r2
+            n3_ref[rows, :] = rms(r2, gain_ref[2:3, :]).astype(BF16)
+            return carry
+
+        lax.fori_loop(0, L // WIDE, close, 0)
 
     row = ((L, w2), BF16)
     wide = ((L, d), BF16)
     return call(
         body,
-        [((L, d), F32), ((L, d), F32), wide, row, row, row, row, wide, ((16, L), F32)],
+        [((L, d), F32), ((L, d), F32), wide, ((3, L, w2), BF16), row, wide, ((16, L), F32)],
         [(inputs, True), (encoded, True)] + near(attn_one, gains) + ws.specs(),
-        [pltpu.VMEM((L, d), BF16), pltpu.VMEM((L, d), BF16)]
-        + [ws.scratch(w2) for _ in range(5)]
-        + [DMA, DMA]
-        + [ws.sems() for _ in range(5)],
+        [
+            pltpu.VMEM((L, d), BF16),
+            pltpu.VMEM((L, d), BF16),
+            ws.scratch(w2, 5),
+            DMA,
+            DMA,
+            ws.sems(5),
+        ],
         "kb",
         5_000_000_000,
     )
@@ -537,7 +556,7 @@
         else:
             y_acc, b3_acc = rest[ng : ng + 2]
         g_refs, rest = rest[:ng], rest[ng + (5 if last else 2) :]
-        cot_v, wg, wu, wd, cot_t, n3_t, sem_c, s_g, s_u, s_d = rest
+        cot_v, wg, wu, wd, turned, lows, sem_c, s_g, s_u, s_d = rest
         cc = sequence_copy(cot_ref, cot_v, sem_c)
         cg = ws.start(w_refs, wg, s_g, 0, ff)
         cu = ws.start(w_refs, wu, s_u, ff, ff)
@@ -548,9 +567,9 @@
         else:
             y_acc[...] = jnp.zeros_like(y_acc)
             b3_acc[...] = jnp.zeros_like(b3_acc)
-        n3_t[...] = n3_ref[...].T
+        turned[0] = n3_ref[...].T
         cc.wait()
-        cot_t[...] = cot_v[...].T
+        turned[1] = cot_v[...].T
         wait(cg)
         wait(cu)
         wait(cd)
@@ -566,22 +585,32 @@
             both = 0.5 * (1.0 + th)
             gelu = u * both
             slope = both + 0.5 * u * (1.0 - th * th) * (GELU_C * (1.0 + (3.0 * GELU_A) * sq))
-            hidden = (gelu * up).astype(BF16)
-            gate_low = (bh * up * slope).astype(BF16)
-            up_low = (bh * gelu).astype(BF16)
-            y_acc[...] += nt(hidden, down)
-            b3_acc[...] += nt(gate_low, gate) + nt(up_low, upw)
-            parts.put(g_refs, None, at, nn(n3_t[...], gate_low))
-            parts.put(g_refs, None, pl.multiple_of(ff + at, LANE), nn(n3_t[...], up_low))
-            parts.put(g_refs, None, pl.multiple_of(2 * ff + at, LANE), nn(cot_t[...], hidden))
+            lows[2] = (gelu * up).astype(BF16)
+            lows[0] = (bh * up * slope).astype(BF16)
+            lows[1] = (bh * gelu).astype(BF16)
+            y_acc[...] += nt(lows[2], down)
+            b3_acc[...] += nt(lows[0], gate) + nt(lows[1], upw)
+
+            def weight(g, inner):
+                parts.put(g_refs, None, pl.multiple_of(g * ff + at, LANE), nn(turned[g // 2], lows[g]))
+                return inner
+
+            lax.fori_loop(0, 3, weight, 0)
             return carry
 
         lax.fori_loop(0, ff // tile, step, 0)
         if last:
-            y_ref[...] = y_acc[...].astype(BF16)
-            grad, dg = rms_back(r2_ref[...], gain_ref[2:3, :], b3_acc[...])
-            b2_ref[...] = cot_v[...].astype(F32) + grad
-            dg_ref[...] = dg
+            dg_ref[...] = jnp.zeros_like(dg_ref)
+
+            def finish(t, carry):
+                rows = pl.ds(pl.multiple_of(t * QB, QB), QB)
+                y_ref[rows, :] = y_acc[rows, :].astype(BF16)
+                grad, dg = rms_back(r2_ref[rows, :], gain_ref[2:3, :], b3_acc[rows, :])
+                b2_ref[rows, :] = cot_v[rows, :].astype(F32) + grad
+                dg_ref[...] += dg
+                return carry
+
+            lax.fori_loop(0, L // QB, finish, 0)
 
     full = ((L, d), F32)
     outs = parts.outs()
@@ -597,8 +626,8 @@
             ws.scratch(ff),
             ws.scratch(ff),
             ws.scratch(ff),
-            pltpu.VMEM((d, L), BF16),
-            pltpu.VMEM((d, L), BF16),
+            pltpu.VMEM((2, d, L), BF16),
+            pltpu.VMEM((3, L, tile), BF16),
             DMA,
             ws.sems(),
             ws.sems(),
@@ -610,21 +639,20 @@
     return parts.split(result[:ng]), result[ng:]
 
 
-def attention_backward(grid, back, q, k, v, attn, lse, base, pieces, first_col, hd, name):
+def attention_backward(grid, back, qkv, attn, lse, base, pieces, first_col, hd, name):
     ws = Weights(pieces, grid.n_z)
     n = len(ws.arrays)
     w2 = 2 * hd
     causal = base is not None
 
     def body(*refs):
-        b_ref, q_ref, k_ref, v_ref, o_ref, lse_ref = refs[:6]
-        base_ref = refs[6] if causal else None
-        refs = refs[7 if causal else 6 :]
+        b_ref, qkv_ref, o_ref, lse_ref = refs[:4]
+        base_ref = refs[4] if causal else None
+        refs = refs[5 if causal else 4 :]
         w_refs = refs[:n]
-        dq_ref, dk_ref, dv_ref = refs[n : n + 3]
-        off_ref = refs[n + 3] if causal else None
-        wo, do, p_ref, ds_ref = refs[n + (4 if causal else 3) : n + (8 if causal else 7)]
-        band_ref, s_o = refs[-2:]
+        out_ref = refs[n]
+        off_ref = refs[n + 1] if causal else None
+        wo, do, p_ref, ds_ref, band_ref, s_o = refs[-6:]
         co = ws.start(w_refs, wo, s_o, first_col, hd)
         if causal:
             off_ref[...] = jnp.zeros_like(off_ref)
@@ -632,14 +660,26 @@
         wait(co)
         do[...] = nn(low, ws.value(wo, 0, w2)).astype(BF16)
         attend_back_loop(
-            q_ref, k_ref, v_ref, o_ref, do, lse_ref, dq_ref, dk_ref, dv_ref, p_ref, ds_ref, base_ref, off_ref, band_ref
+            qkv_ref.at[0],
+            qkv_ref.at[1],
+            qkv_ref.at[2],
+            o_ref,
+            do,
+            lse_ref,
+            out_ref.at[0],
+            out_ref.at[1],
+            out_ref.at[2],
+            p_ref,
+            ds_ref,
+            base_ref,
+            off_ref,
+            band_ref,
         )
 
-    row = ((L, w2), BF16)
     return call(
         body,
-        [row, row, row] + ([((16, L), F32)] if causal else []),
-        near(back, q, k, v, attn, lse) + (near(base) if causal else []) + ws.specs(),
+        [((3, L, w2), BF16)] + ([((16, L), F32)] if causal else []),
+        near(back, qkv, attn, lse) + (near(base) if causal else []) + ws.specs(),
         [
             ws.scratch(w2),
             pltpu.VMEM((L, w2), BF16),
@@ -653,7 +693,7 @@
     )
 
 
-def cross_finish(grid, encoded, b2, r1, n2, dq, dk, dv, attn_one, attn_two, gains, pieces, d, hd):
+def cross_finish(grid, encoded, b2, r1, n2, grads, attn_one, attn_two, gains, pieces, d, hd):
     ws = Weights(pieces, grid.n_z)
     k = len(ws.arrays)
     w2 = 2 * hd
@@ -661,47 +701,73 @@
     ng = parts.count()
 
     def body(*refs):
-        enc_ref, b2_ref, r1_ref, n2_ref, dq_ref, dk_ref, dv_ref, a1_ref, a2_ref, gain_ref = refs[:10]
-        w_refs = refs[10 : 10 + k]
-        b1_ref, eg_ref, dg_ref = refs[10 + k : 13 + k]
-        g_refs = refs[13 + k : 13 + k + ng]
-        enc_v, wq, wk, wv, sem_e, s_q, s_k, s_v = refs[13 + k + ng :]
-        cq = ws.start(w_refs, wq, s_q, hd, hd)
+        enc_ref, b2_ref, r1_ref, n2_ref, dy_ref, a1_ref, a2_ref, gain_ref = refs[:8]
+        w_refs = refs[8 : 8 + k]
+        b1_ref, eg_ref, dg_ref = refs[8 + k : 11 + k]
+        g_refs = refs[11 + k : 11 + k + ng]
+        enc_v, w, turned, right, sem_e, s_w = refs[11 + k + ng :]
         ce = sequence_copy(enc_ref, enc_v, sem_e)
-        ck = ws.start(w_refs, wk, s_k, 2 * hd, hd)
-        cv = ws.start(w_refs, wv, s_v, 3 * hd, hd)
-        parts.put_halves(g_refs, hd, hd, nn(n2_ref[...].T, dq_ref[...]))
-        wait(cq)
-        grad, dg = rms_back(r1_ref[...], gain_ref[1:2, :], nt(dq_ref[...], ws.value(wq, 0, w2)))
-        dg_ref[...] = dg
-        b1 = b2_ref[...] + grad
-        b1_ref[...] = b1
-        parts.put_halves(g_refs, 0, hd, nn(b1.astype(BF16).T, a1_ref[...]))
+        cw = [ws.start(w_refs, w.at[g], s_w, (g + 1) * hd, hd, slot=g) for g in range(3)]
+        turned[3] = b2_ref[...].astype(BF16).T
+        right[1] = a2_ref[...]
+        right[0] = a1_ref[...]
+        turned[0] = n2_ref[...].T
+        wait(cw[0])
+        dg_ref[...] = jnp.zeros_like(dg_ref)
+
+        def resume(t, carry):
+            rows = pl.ds(pl.multiple_of(t * WIDE, WIDE), WIDE)
+            grad, dg = rms_back(r1_ref[rows, :], gain_ref[1:2, :], nt(dy_ref[0, rows, :], ws.value(w.at[0], 0, w2)))
+            dg_ref[...] += dg
+            b1_ref[rows, :] = b2_ref[rows, :] + grad
+            return carry
+
+        lax.fori_loop(0, L // WIDE, resume, 0)
+        turned[2] = b1_ref[...].astype(BF16).T
         ce.wait()
-        enc_t = enc_v[...].T
-        parts.put_halves(g_refs, 2 * hd, hd, nn(enc_t, dk_ref[...]))
-        parts.put_halves(g_refs, 3 * hd, hd, nn(enc_t, dv_ref[...]))
-        parts.put_halves(g_refs, 4 * hd, hd, nn(b2_ref[...].astype(BF16).T, a2_ref[...]))
-        wait(ck)
-        wait(cv)
-        eg = nt(dk_ref[...], ws.value(wk, 0, w2)) + nt(dv_ref[...], ws.value(wv, 0, w2))
-        eg_ref[...] = eg.astype(BF16)
+        turned[1] = enc_v[...].T
+
+        def inner(g, carry):
+            parts.put_halves(g_refs, pl.multiple_of((g + 1) * hd, LANE), hd, nn(turned[jnp.minimum(g, 1)], dy_ref[g]))
+            return carry
+
+        lax.fori_loop(0, 3, inner, 0)
+
+        def outer(g, carry):
+            parts.put_halves(g_refs, pl.multiple_of(g * 4 * hd, LANE), hd, nn(turned[2 + g], right[g]))
+            return carry
+
+        lax.fori_loop(0, 2, outer, 0)
+        wait(cw[1])
+        wait(cw[2])
+
+        def encoder(t, carry):
+            rows = pl.ds(pl.multiple_of(t * WIDE, WIDE), WIDE)
+            eg = nt(dy_ref[1, rows, :], ws.value(w.at[1], 0, w2)) + nt(dy_ref[2, rows, :], ws.value(w.at[2], 0, w2))
+            eg_ref[rows, :] = eg.astype(BF16)
+            return carry
+
+        lax.fori_loop(0, L // WIDE, encoder, 0)
 
     result = call(
         body,
         [((L, d), F32), ((L, d), BF16), ((1, d), F32)] + parts.outs(),
-        [(encoded, True)] + near(b2, r1, n2, dq, dk, dv, attn_one, attn_two, gains) + ws.specs(),
-        [pltpu.VMEM((L, d), BF16)]
-        + [ws.scratch(w2) for _ in range(3)]
-        + [DMA]
-        + [ws.sems() for _ in range(3)],
+        [(encoded, True)] + near(b2, r1, n2, grads, attn_one, attn_two, gains) + ws.specs(),
+        [
+            pltpu.VMEM((L, d), BF16),
+            ws.scratch(w2, 3),
+            pltpu.VMEM((4, d, L), BF16),
+            pltpu.VMEM((2, L, w2), BF16),
+            DMA,
+            ws.sems(3),
+        ],
         "kd2",
         5_000_000_000,
     )
     return result[:3], parts.split(result[3:])
 
 
-def self_finish(grid, inputs, b1, n1, dq, dk, dv, off, dg2, dg3, base_hot, gains, pieces, d, hd, heads):
+def self_finish(grid, inputs, b1, n1, grads, off, dg2, dg3, base_hot, gains, pieces, d, hd, heads):
     ws = Weights(pieces, grid.n_z)
     k = len(ws.arrays)
     w2 = 2 * hd
@@ -709,30 +775,28 @@
     ng = parts.count()
 
     def body(*refs):
-        x_ref, b1_ref, n1_ref, dq_ref, dk_ref, dv_ref, off_ref, dg2_ref, dg3_ref, hot_ref, gain_ref = refs[:11]
-        w_refs = refs[11 : 11 + k]
-        dx_ref = refs[11 + k]
-        g_refs = refs[12 + k : 12 + k + ng]
-        x_v, wq, wk, wv, sem_x, s_q, s_k, s_v = refs[12 + k + ng :]
-        cq = ws.start(w_refs, wq, s_q, 0, hd)
-        ck = ws.start(w_refs, wk, s_k, hd, hd)
-        cv = ws.start(w_refs, wv, s_v, 2 * hd, hd)
+        x_ref, b1_ref, n1_ref, dy_ref, off_ref, dg2_ref, dg3_ref, hot_ref, gain_ref = refs[:9]
+        w_refs = refs[9 : 9 + k]
+        dx_ref = refs[9 + k]
+        g_refs = refs[10 + k : 10 + k + ng]
+        x_v, w, turned, back, sem_x, s_w = refs[10 + k + ng :]
+        cw = [ws.start(w_refs, w.at[g], s_w, g * hd, hd, slot=g) for g in range(3)]
         cx = sequence_copy(x_ref, x_v, sem_x)
-        n1_t = n1_ref[...].T
-        parts.put_halves(g_refs, 0, hd, nn(n1_t, dq_ref[...]))
-        parts.put_halves(g_refs, hd, hd, nn(n1_t, dk_ref[...]))
-        parts.put_halves(g_refs, 2 * hd, hd, nn(n1_t, dv_ref[...]))
-        wait(cq)
-        back = nt(dq_ref[...], ws.value(wq, 0, w2))
-        wait(ck)
-        back = back + nt(dk_ref[...], ws.value(wk, 0, w2))
-        wait(cv)
-        back = back + nt(dv_ref[...], ws.value(wv, 0, w2))
+        turned[...] = n1_ref[...].T
+        back[...] = jnp.zeros_like(back)
+
+        def inner(g, carry):
+            parts.put_halves(g_refs, pl.multiple_of(g * hd, LANE), hd, nn(turned[...], dy_ref[g]))
+            wait_for(g, cw)
+            back[...] += nt(dy_ref[g], ws.value(w.at[g], 0, w2))
+            return carry
+
+        lax.fori_loop(0, 3, inner, 0)
         cx.wait()
-        grad, dg = rms_back(x_v[...].astype(F32), gain_ref[0:1, :], back)
+        grad, dg = rms_back(x_v[...].astype(F32), gain_ref[0:1, :], back[...])
         dx_ref[...] = (b1_ref[...] + grad).astype(BF16)
         dgs = jnp.concatenate([dg, dg2_ref[...], dg3_ref[...], jnp.zeros((5, d), F32)], axis=0)
-        turned = jnp.concatenate([jnp.zeros((NB, d), F32), dgs, jnp.zeros((LANE - NB - 8, d), F32)], axis=0).T
+        columns = jnp.concatenate([jnp.zeros((NB, d), F32), dgs, jnp.zeros((LANE - NB - 8, d), F32)], axis=0).T
         hot = hot_ref[...]
         sums = off_ref[...]
         table = jnp.zeros((16, LANE), F32)
@@ -745,16 +809,20 @@
         column = lax.broadcasted_iota(jnp.int32, (d, 16), 1)
         for a in range(2):
             spread = ((shard_row + a * heads == column) & (shard_row < heads)).astype(F32).astype(BF16)
-            parts.put(g_refs, a, 3 * hd, nn(spread, table) + turned)
+            parts.put(g_refs, a, 3 * hd, nn(spread, table) + columns)
 
     result = call(
         body,
         [((L, d), BF16)] + parts.outs(),
-        [(inputs, True)] + near(b1, n1, dq, dk, dv, off, dg2, dg3, base_hot, gains) + ws.specs(),
-        [pltpu.VMEM((L, d), BF16)]
-        + [ws.scratch(w2) for _ in range(3)]
-        + [DMA]
-        + [ws.sems() for _ in range(3)],
+        [(inputs, True)] + near(b1, n1, grads, off, dg2, dg3, base_hot, gains) + ws.specs(),
+        [
+            pltpu.VMEM((L, d), BF16),
+            ws.scratch(w2, 3),
+            pltpu.VMEM((d, L), BF16),
+            pltpu.VMEM((L, d), F32),
+            DMA,
+            ws.sems(3),
+        ],
         "ke2",
         4_000_000_000,
     )
@@ -877,8 +945,8 @@
 
         base_hot = (buckets[None, :] == lax.broadcasted_iota(jnp.int32, (LANE, L), 0)).astype(BF16)
 
-        n1, q1, k1, v1, at1, gains, base, lse1 = self_forward(grid, inputs, base_hot, pieces_one, d, hd, heads)
-        r1, r2, n2, q2, k2, v2, at2, n3, lse2 = cross_forward(grid, inputs, encoded, at1, gains, pieces_two, d, hd)
+        n1, qkv1, at1, gains, base, lse1 = self_forward(grid, inputs, base_hot, pieces_one, d, hd, heads)
+        r1, r2, n2, qkv2, at2, n3, lse2 = cross_forward(grid, inputs, encoded, at1, gains, pieces_two, d, hd)
         (own3, gone), (ya, ba) = feed_forward(grid, cotangent, n3, r2, gains, None, pieces_three, 0, d, ff)
         own3_got = grid.swap_c(gone)
         (other3, gone), (y, b2, dg3) = feed_forward(
@@ -886,17 +954,17 @@
         )
         other3_got = grid.swap_c(gone)
         y_far = grid.swap_m(y)
-        a3, bo3, bt3 = scatter_wide(grid, own3, own3_got, other3, other3_got, ff * 3 // 4 // LANE * LANE)
-        dq, dk, dv = attention_backward(grid, b2, q2, k2, v2, at2, lse2, None, pieces_two, 4 * hd, hd, "kd1")
+        a3, bo3, bt3 = scatter_wide(grid, own3, own3_got, other3, other3_got, ff * 5 // 4 // LANE * LANE)
+        (dy,) = attention_backward(grid, b2, qkv2, at2, lse2, None, pieces_two, 4 * hd, hd, "kd1")
         (b1, eg, dg2), (kept, gone) = cross_finish(
-            grid, encoded, b2, r1, n2, dq, dk, dv, at1, at2, gains, pieces_two, d, hd
+            grid, encoded, b2, r1, n2, dy, at1, at2, gains, pieces_two, d, hd
         )
         eg_far = grid.swap_m(eg)
         got = grid.swap_c(gone)
         kept2, far2, _ = scatter(grid, kept[0], got[0], kept[1], got[1], 7 * LANE)
-        dq, dk, dv, off = attention_backward(grid, b1, q1, k1, v1, at1, lse1, base, pieces_two, 0, hd, "ke1")
+        dy, off = attention_backward(grid, b1, qkv1, at1, lse1, base, pieces_two, 0, hd, "ke1")
         dx, (kept, gone) = self_finish(
-            grid, inputs, b1, n1, dq, dk, dv, off, dg2, dg3, base_hot, gains, pieces_one, d, hd, heads
+            grid, inputs, b1, n1, dy, off, dg2, dg3, base_hot, gains, pieces_one, d, hd, heads
         )
         got = grid.swap_c(gone)
         kept1, far1, (kept2, bt30, y, eg) = scatter(

time: 454 us -> 436 us (0.960); the launches traced: 448 us -> 436 us
  waiting for transfers between devices: 209 us -> 196 us
    ppermute x71, waiting for transfers between devices: 209 us -> 196 us  [send(): return lax.ppermute(v, AXES, self.perm(move))]
where the time goes in v2:
time: 436 us
  waiting for transfers between devices  196 us (45%)
  starting transfers between devices  98.1 us (22%)
  Pallas kernels  96.2 us (22%)
  local copies, waits for them, and re-layouts  30.9 us (7%)
  other arithmetic  12.9 us (3%)
    ppermute x71, waiting for transfers between devices, send(): return lax.ppermute(v, AXES, self.perm(move))  196 us
    ppermute x71, starting transfers between devices, send(): return lax.ppermute(v, AXES, self.perm(move))  98.1 us
    pallas_call x8, Pallas kernels, call(): pl.pallas_call(body, out_shape=tuple((jax.ShapeDtypeStruct(s, d) for s, d...  96.2 us
    unnamed x102, local copies, waits for them, and re-layouts  17.8 us
  transfers between devices with their start and end apart: 71, of which 29 were waited for; matrix products, arithmetic and copies ran while one was open for 5% of the time, Pallas kernels for 9%

profile of v2, /device:TPU:0, one launch (start us, length us, event | category | flops | bytes accessed | tf_op | source)
XLA Modules:
  0.0 435.7 jit_solution(6838611725081393404)
XLA Ops:
  7.7 5.1 %collective-permute-start.14 = (bf16[48,1920]{1,0:T(8,128)(2,1)}, bf16[48,1920]{1,0:T(8,128)(2,1)}, u32[]{:S(2)}, u32[]{:S(2)}) collective-permute-start(bf16[48,1920]{1,0:T(8,128)(2,1)} %bitcast_dynamic-update-slice_fusion.12), channel_id=1, source_target_pairs={{0,24},{1,25},{2,26},{3,27},{4,28},{5,29},{6,30},{7,31},{8,0},{9,1... | collective-permute-start | bytes 552968 | tf_op jit(solution)/shard_map/ppermute | solution.py:55
  15.4 2.0 collective-permute-start.1
  20.1 11.0 %collective-permute-done = bf16[48,1280]{1,0:T(8,128)(2,1)S(1)} collective-permute-done((bf16[48,1280]{1,0:T(8,128)(2,1)S(1)}, bf16[48,1280]{1,0:T(8,128)(2,1)S(1)}, u32[]{:S(2)}, u32[]{:S(2)}) %collective-permute-start) | collective-permute-done | bytes 122912 | tf_op jit(solution)/shard_map/ppermute | solution.py:55
  31.0 5.6 %collective-permute-done.1 = bf16[48,1280]{1,0:T(8,128)(2,1)} collective-permute-done((bf16[48,1280]{1,0:T(8,128)(2,1)S(1)}, bf16[48,1280]{1,0:T(8,128)(2,1)}, u32[]{:S(2)}, u32[]{:S(2)}) %collective-permute-start.1) | collective-permute-done | bytes 122912 | tf_op jit(solution)/shard_map/ppermute | solution.py:55
  36.6 5.5 %collective-permute-start.25 = (bf16[48,3072]{1,0:T(8,128)(2,1)S(1)}, bf16[48,3072]{1,0:T(8,128)(2,1)S(1)}, u32[]{:S(2)}, u32[]{:S(2)}) collective-permute-start(bf16[48,3072]{1,0:T(8,128)(2,1)S(1)} %pad_maximum_fusion.2), channel_id=1, source_target_pairs={{0,16},{1,17},{2,18},{3,19},{4,20},{5,21},{6,22},{7,23},{8,24},{9,... | collective-permute-start | bytes 884744 | tf_op jit(solution)/shard_map/ppermute | solution.py:55
  43.0 14.9 %collective-permute-start.24 = (bf16[48,3072]{1,0:T(8,128)(2,1)S(1)}, bf16[48,3072]{1,0:T(8,128)(2,1)S(1)}, u32[]{:S(2)}, u32[]{:S(2)}) collective-permute-start(bf16[48,3072]{1,0:T(8,128)(2,1)S(1)} %pad_maximum_fusion.2), channel_id=1, source_target_pairs={{0,8},{1,9},{2,10},{3,11},{4,12},{5,13},{6,14},{7,15},{8,16},{9,17... | collective-permute-start | bytes 884744 | tf_op jit(solution)/shard_map/ppermute | solution.py:55
  65.1 8.7 %collective-permute-done.4.refs_4_.refs_11_ = bf16[4,48,1280]{2,1,0:T(8,128)(2,1)S(1)} collective-permute-done((bf16[4,48,1280]{2,1,0:T(8,128)(2,1)S(1)}, bf16[4,48,1280]{2,1,0:T(8,128)(2,1)S(1)}, u32[]{:S(2)}, u32[]{:S(2)}) %collective-permute-start.4) | collective-permute-done | bytes 491552 | tf_op jit(solution)/shard_map/ppermute | solution.py:55
  78.7 20.3 %collective-permute-done.5.refs_5_.refs_12_ = bf16[2,48,1280]{2,1,0:T(8,128)(2,1)S(1)} collective-permute-done((bf16[2,48,1280]{2,1,0:T(8,128)(2,1)S(1)}, bf16[2,48,1280]{2,1,0:T(8,128)(2,1)S(1)}, u32[]{:S(2)}, u32[]{:S(2)}) %collective-permute-start.5) | collective-permute-done | bytes 245792 | tf_op jit(solution)/shard_map/ppermute | solution.py:55
  103.2 1.9 collective-permute-start.18
  106.8 26.6 %collective-permute-done.17.refs_7_.refs_11_.refs_8_ = bf16[2,48,1920]{2,1,0:T(8,128)(2,1)S(1)} collective-permute-done((bf16[2,48,1920]{2,1,0:T(8,128)(2,1)S(1)}, bf16[2,48,1920]{2,1,0:T(8,128)(2,1)S(1)}, u32[]{:S(2)}, u32[]{:S(2)}) %collective-permute-start.17) | collective-permute-done | bytes 368672 | tf_op jit(solution)/shard_map/ppermute | solution.py:55
  137.0 3.0 collective-permute-done.23.refs_13_.refs_17_.refs_14_
  140.0 1.7 collective-permute-start.32
  141.8 11.5 %shard_map.322 = (bf16[512,768]{1,0:T(8,128)(2,1)S(1)}, bf16[3,512,768]{2,1,0:T(8,128)(2,1)S(1)}, bf16[512,768]{1,0:T(8,128)(2,1)S(1)}, f32[8,768]{1,0:T(8,128)S...) custom-call(bf16[1024,768]{1,0:T(8,128)(2,1)} %refs_0_.11, bf16[128,512]{1,0:T(8,128)(2,1)S(1)} %fusion.15.refs_1_.refs_7_, ...), custom_call_target="tpu_custom_call" | custom-call | flops 3000000000 | bytes 10000000 | tf_op jit(solution)/shard_map/pallas_call | solution.py:326
  153.3 15.0 %shard_map.323 = (f32[512,768]{1,0:T(8,128)S(1)}, f32[512,768]{1,0:T(8,128)S(1)}, bf16[512,768]{1,0:T(8,128)(2,1)S(1)}, bf16[3,512,768]{2,1,0:T(8,128)(2,1)S(1)}...) custom-call(bf16[1024,768]{1,0:T(8,128)(2,1)} %refs_0_.11, ...), custom_call_target="tpu_custom_call" | custom-call | flops 5000000000 | bytes 10000000 | tf_op jit(solution)/shard_map/pallas_call | solution.py:326
  170.3 12.9 %shard_map.324 = (bf16[2,4,48,3072]{3,2,1,0:T(8,128)(2,1)S(1)}, bf16[2,4,48,3072]{3,2,1,0:T(8,128)(2,1)S(1)}, f32[512,768]{1,0:T(8,128)S(1)}, f32[512,768]{1,0:T(8,128)S(1)}) custom-call(bf16[1024,768]{1,0:T(8,128)(2,1)} %refs_0_.9, bf16[512,768]{1,0:T(8,128)(2,1)S(1)} %get-tuple-element.65.refs_1_, bf16[4,48,3072]{2,1,0:T(8,128)(2,1)} %copy-done.18, ...), custom_call_target="tpu_custom_call" | custom-call | flops 7500000256 | bytes 10000000 | tf_op jit(solution)/shard_map/pallas_call | solution.py:326
  187.5 14.1 %shard_map.325 = (bf16[2,4,48,3072]{3,2,1,0:T(8,128)(2,1)S(1)}, bf16[2,4,48,3072]{3,2,1,0:T(8,128)(2,1)S(1)}, bf16[512,768]{1,0:T(8,128)(2,1)S(1)}, f32[512,768]{1,0:T(8,128)S(1)}, f32[1,768]{1,0:T(1,128)S(1)}) custom-call(bf16[1024,768]{1,0:T(8,128)(2,1)} %refs_0_.9, bf16[512,768]{1,0:T(8,128)(2,1)S(1)} %get-tuple-element.65.refs_1_, ...), custom_call_target="tpu_custom_call" | custom-call | flops 7500000256 | bytes 10000000 | tf_op jit(solution)/shard_map/pallas_call | solution.py:326
  204.4 11.6 %shard_map.326.refs_4_ = bf16[3,512,768]{2,1,0:T(8,128)(2,1)S(1)} custom-call(f32[512,768]{1,0:T(8,128)S(1)} %get-tuple-element.69.refs_0_.refs_1_, bf16[3,512,768]{2,1,0:T(8,128)(2,1)S(1)} %get-tuple-element.72.refs_1_, bf16[512,768]{1,0:T(8,128)(2,1)S(1)} %get-tuple-element.73.refs_2_.refs_6_, f32[16,512]{1,0:T(8,128)S(1)} %get-tuple-element.74.refs_3_, ...), custom_call_target="tpu_custom_call" | custom-call | flops 3000000000 | bytes 10000000 | tf_op jit(solution)/shard_map/pallas_call | solution.py:326
  216.0 9.6 %shard_map.327 = (f32[512,768]{1,0:T(8,128)S(1)}, bf16[512,768]{1,0:T(8,128)(2,1)S(1)}, f32[1,768]{1,0:T(1,128)S(1)}, bf16[2,2,4,48,1920]{4,3,2,1,0:T(8,128)(2,1)S(1)}, bf16[2,2,4,48,1920]{4,3,2,1,0:T(8,128)(2,1)S(1)}) custom-call(bf16[1024,768]{1,0:T(8,128)(2,1)} %refs_0_.10, f32[512,768]{1,0:T(8,128)S(1)} %get-tuple-element.69.refs_0_.refs_1_, ...), custom_call_target="tpu_custom_call" | custom-call | flops 5000000000 | bytes 10000000 | tf_op jit(solution)/shard_map/pallas_call | solution.py:326
  225.6 12.1 %shard_map.328 = (bf16[3,512,768]{2,1,0:T(8,128)(2,1)S(1)}, f32[16,512]{1,0:T(8,128)S(1)}) custom-call(f32[512,768]{1,0:T(8,128)S(1)} %get-tuple-element.75.refs_0_.refs_1_, bf16[3,512,768]{2,1,0:T(8,128)(2,1)S(1)} %get-tuple-element.77.refs_1_, bf16[512,768]{1,0:T(8,128)(2,1)S(1)} %get-tuple-element.63.refs_2_.refs_5_, ...), custom_call_target="tpu_custom_call" | custom-call | flops 3000000000 | bytes 10000000 | tf_op jit(solution)/shard_map/pallas_call | solution.py:326
  237.8 9.5 %shard_map.329 = (bf16[512,768]{1,0:T(8,128)(2,1)S(1)}, bf16[2,2,4,48,1280]{4,3,2,1,0:T(8,128)(2,1)S(1)}, bf16[2,2,4,48,1280]{4,3,2,1,0:T(8,128)(2,1)}) custom-call(bf16[1024,768]{1,0:T(8,128)(2,1)} %refs_0_.11, f32[512,768]{1,0:T(8,128)S(1)} %get-tuple-element.75.refs_0_.refs_1_, bf16[512,768]{1,0:T(8,128)(2,1)S(1)} %get-tuple-element.76.refs_2_, ...), custom_call_target="tpu_custom_call" | custom-call | flops 4000000000 | bytes 10000000 | tf_op jit(solution)/shard_map/pallas_call | solution.py:326
  250.2 1.8 collective-permute-start.43
  253.9 32.9 %collective-permute-done.43 = bf16[512,768]{1,0:T(8,128)(2,1)S(1)} collective-permute-done((bf16[512,768]{1,0:T(8,128)(2,1)}, bf16[512,768]{1,0:T(8,128)(2,1)S(1)}, u32[]{:S(2)}, u32[]{:S(2)}) %collective-permute-start.43) | collective-permute-done | bytes 786464 | tf_op jit(solution)/shard_map/ppermute | solution.py:55
  286.9 1.9 maximum_convert_fusion.1
  294.7 1.8 collective-permute-start.52
  298.0 13.1 %collective-permute-done.41 = bf16[4,48,1792]{2,1,0:T(8,128)(2,1)S(1)} collective-permute-done((bf16[4,48,1792]{2,1,0:T(8,128)(2,1)S(1)}, bf16[4,48,1792]{2,1,0:T(8,128)(2,1)S(1)}, u32[]{:S(2)}, u32[]{:S(2)}) %collective-permute-start.41) | collective-permute-done | bytes 688160 | tf_op jit(solution)/shard_map/ppermute | solution.py:55
  311.1 1.7 collective-permute-start.38
  313.1 12.0 %collective-permute-done.54 = bf16[4,48,1792]{2,1,0:T(8,128)(2,1)S(1)} collective-permute-done((bf16[4,48,1792]{2,1,0:T(8,128)(2,1)S(1)}, bf16[4,48,1792]{2,1,0:T(8,128)(2,1)S(1)}, u32[]{:S(2)}, u32[]{:S(2)}) %collective-permute-start.54) | collective-permute-done | bytes 688160 | tf_op jit(solution)/shard_map/ppermute | solution.py:55
  326.9 3.4 collective-permute-done.52
  330.3 4.7 %collective-permute-start.67 = (bf16[48,1792]{1,0:T(8,128)(2,1)S(1)}, bf16[48,1792]{1,0:T(8,128)(2,1)S(1)}, u32[]{:S(2)}, u32[]{:S(2)}) collective-permute-start(bf16[48,1792]{1,0:T(8,128)(2,1)S(1)} %get-tuple-element.119), channel_id=1, source_target_pairs={{0,8},{1,9},{2,10},{3,11},{4,12},{5,13},{6,14},{7,15},{8,16},{9,17... | collective-permute-start | bytes 516104 | tf_op jit(solution)/shard_map/ppermute | solution.py:55
  335.4 9.1 %collective-permute-done.38 = bf16[2,4,48,896]{3,2,1,0:T(8,128)(2,1)S(1)} collective-permute-done((bf16[2,4,48,896]{3,2,1,0:T(8,128)(2,1)S(1)}, bf16[2,4,48,896]{3,2,1,0:T(8,128)(2,1)S(1)}, u32[]{:S(2)}, u32[]{:S(2)}) %collective-permute-start.38) | collective-permute-done | bytes 688160 | tf_op jit(solution)/shard_map/ppermute | solution.py:55
  344.8 6.8 %collective-permute-start.68 = (bf16[48,1792]{1,0:T(8,128)(2,1)S(1)}, bf16[48,1792]{1,0:T(8,128)(2,1)S(1)}, u32[]{:S(2)}, u32[]{:S(2)}) collective-permute-start(bf16[48,1792]{1,0:T(8,128)(2,1)S(1)} %get-tuple-element.121), channel_id=1, source_target_pairs={{0,16},{1,17},{2,18},{3,19},{4,20},{5,21},{6,22},{7,23},{8,24},{9,... | collective-permute-start | bytes 516104 | tf_op jit(solution)/shard_map/ppermute | solution.py:55
  352.0 1.9 collective-permute-start.64
  354.0 1.9 maximum_convert_fusion
  357.6 1.9 maximum_convert_fusion.2
  359.5 1.9 collective-permute-start.66
  361.9 5.6 %collective-permute-done.68 = bf16[48,1792]{1,0:T(8,128)(2,1)S(1)} collective-permute-done((bf16[48,1792]{1,0:T(8,128)(2,1)S(1)}, bf16[48,1792]{1,0:T(8,128)(2,1)S(1)}, u32[]{:S(2)}, u32[]{:S(2)}) %collective-permute-start.68) | collective-permute-done | bytes 172064 | tf_op jit(solution)/shard_map/ppermute | solution.py:55
  371.6 3.7 collective-permute-done.49
  376.9 2.7 collective-permute-done.50
  379.7 7.4 %collective-permute-done.45 = bf16[2,4,48,640]{3,2,1,0:T(8,128)(2,1)S(1)} collective-permute-done((bf16[2,4,48,640]{3,2,1,0:T(8,128)(2,1)S(1)}, bf16[2,4,48,640]{3,2,1,0:T(8,128)(2,1)S(1)}, u32[]{:S(2)}, u32[]{:S(2)}) %collective-permute-start.45) | collective-permute-done | bytes 491552 | tf_op jit(solution)/shard_map/ppermute | solution.py:55
  390.6 3.2 collective-permute-done.46
  395.5 3.0 collective-permute-start.65
  400.5 6.1 %collective-permute-done.62 = bf16[48,1280]{1,0:T(8,128)(2,1)S(1)} collective-permute-done((bf16[48,1280]{1,0:T(8,128)(2,1)S(1)}, bf16[48,1280]{1,0:T(8,128)(2,1)S(1)}, u32[]{:S(2)}, u32[]{:S(2)}) %collective-permute-start.62) | collective-permute-done | bytes 122912 | tf_op jit(solution)/shard_map/ppermute | solution.py:55
  406.7 3.1 collective-permute-start.60
  410.4 2.9 collective-permute-done.65
  413.3 2.8 collective-permute-start.55
  416.2 3.8 collective-permute-start.56
  420.9 5.6 %collective-permute-done.59 = bf16[48,1920]{1,0:T(8,128)(2,1)S(1)} collective-permute-done((bf16[48,1920]{1,0:T(8,128)(2,1)S(1)}, bf16[48,1920]{1,0:T(8,128)(2,1)S(1)}, u32[]{:S(2)}, u32[]{:S(2)}) %collective-permute-start.59) | collective-permute-done | bytes 184352 | tf_op jit(solution)/shard_map/ppermute | solution.py:55
  427.3 6.3 %collective-permute-done.56 = bf16[48,1280]{1,0:T(8,128)(2,1)S(1)} collective-permute-done((bf16[48,1280]{1,0:T(8,128)(2,1)S(1)}, bf16[48,1280]{1,0:T(8,128)(2,1)S(1)}, u32[]{:S(2)}, u32[]{:S(2)}) %collective-permute-start.56) | collective-permute-done | bytes 122912 | tf_op jit(solution)/shard_map/ppermute | solution.py:55
  (276 shorter events, 78.7 us)
Async XLA Ops:
  7.7 52.4 %collective-permute-start.14 = (bf16[48,1920]{1,0:T(8,128)(2,1)}, bf16[48,1920]{1,0:T(8,128)(2,1)}, u32[]{:S(2)}, u32[]{:S(2)}) collective-permute-start(bf16[48,1920]{1,0:T(8,128)(2,1)} %bitcast_dynamic-update-slice_fusion.12), channel_id=1, source_target_pairs={{0,24},{1,25},{2,26},{3,27},{4,28},{5,29},{6,30},{7,31},{8,0},{9,1... | collective-permute-start | bytes 552968 | tf_op jit(solution)/shard_map/ppermute | solution.py:55
  12.7 46.3 %collective-permute-start.13 = (bf16[48,1920]{1,0:T(8,128)(2,1)}, bf16[48,1920]{1,0:T(8,128)(2,1)}, u32[]{:S(2)}, u32[]{:S(2)}) collective-permute-start(bf16[48,1920]{1,0:T(8,128)(2,1)} %bitcast_dynamic-update-slice_fusion.12), channel_id=1, source_target_pairs={{0,16},{1,17},{2,18},{3,19},{4,20},{5,21},{6,22},{7,23},{8,24},{9,... | collective-permute-start | bytes 552968 | tf_op jit(solution)/shard_map/ppermute | solution.py:55
  12.7 45.2 %collective-permute-start.12 = (bf16[48,1920]{1,0:T(8,128)(2,1)}, bf16[48,1920]{1,0:T(8,128)(2,1)}, u32[]{:S(2)}, u32[]{:S(2)}) collective-permute-start(bf16[48,1920]{1,0:T(8,128)(2,1)} %bitcast_dynamic-update-slice_fusion.12), channel_id=1, source_target_pairs={{0,8},{1,9},{2,10},{3,11},{4,12},{5,13},{6,14},{7,15},{8,16},{9,17... | collective-permute-start | bytes 552968 | tf_op jit(solution)/shard_map/ppermute | solution.py:55
  15.4 21.2 %collective-permute-start.1 = (bf16[48,1280]{1,0:T(8,128)(2,1)S(1)}, bf16[48,1280]{1,0:T(8,128)(2,1)}, u32[]{:S(2)}, u32[]{:S(2)}) collective-permute-start(bf16[48,1280]{1,0:T(8,128)(2,1)S(1)} %get-tuple-element.112), channel_id=1, source_target_pairs={{0,16},{1,17},{2,18},{3,19},{4,20},{5,21},{6,22},{7,23},{8,24},{9,... | collective-permute-start | bytes 368648 | tf_op jit(solution)/shard_map/ppermute | solution.py:55
  36.6 28.5 %collective-permute-start.25 = (bf16[48,3072]{1,0:T(8,128)(2,1)S(1)}, bf16[48,3072]{1,0:T(8,128)(2,1)S(1)}, u32[]{:S(2)}, u32[]{:S(2)}) collective-permute-start(bf16[48,3072]{1,0:T(8,128)(2,1)S(1)} %pad_maximum_fusion.2), channel_id=1, source_target_pairs={{0,16},{1,17},{2,18},{3,19},{4,20},{5,21},{6,22},{7,23},{8,24},{9,... | collective-permute-start | bytes 884744 | tf_op jit(solution)/shard_map/ppermute | solution.py:55
  43.0 19.6 %collective-permute-start.24 = (bf16[48,3072]{1,0:T(8,128)(2,1)S(1)}, bf16[48,3072]{1,0:T(8,128)(2,1)S(1)}, u32[]{:S(2)}, u32[]{:S(2)}) collective-permute-start(bf16[48,3072]{1,0:T(8,128)(2,1)S(1)} %pad_maximum_fusion.2), channel_id=1, source_target_pairs={{0,8},{1,9},{2,10},{3,11},{4,12},{5,13},{6,14},{7,15},{8,16},{9,17... | collective-permute-start | bytes 884744 | tf_op jit(solution)/shard_map/ppermute | solution.py:55
  57.9 19.6 %collective-permute-start.26 = (bf16[48,3072]{1,0:T(8,128)(2,1)S(1)}, bf16[48,3072]{1,0:T(8,128)(2,1)S(1)}, u32[]{:S(2)}, u32[]{:S(2)}) collective-permute-start(bf16[48,3072]{1,0:T(8,128)(2,1)S(1)} %pad_maximum_fusion.2), channel_id=1, source_target_pairs={{0,24},{1,25},{2,26},{3,27},{4,28},{5,29},{6,30},{7,31},{8,0},{9,1... | collective-permute-start | bytes 884744 | tf_op jit(solution)/shard_map/ppermute | solution.py:55
  59.0 19.1 %collective-permute-start.7 = (bf16[4,48,1280]{2,1,0:T(8,128)(2,1)S(1)}, bf16[4,48,1280]{2,1,0:T(8,128)(2,1)S(1)}, u32[]{:S(2)}, u32[]{:S(2)}) collective-permute-start(bf16[4,48,1280]{2,1,0:T(8,128)(2,1)S(1)} %bitcast_dynamic-update-slice_fusion.8.refs_2_.refs_9_), channel_id=1, source_target_pairs={{0,2},{1,3},{2,0},{3,1},{4,6},{5,7},{6,4},{7,5},{8,10},{9,11},{10,... | collective-permute-start | bytes 1474568 | tf_op jit(solution)/shard_map/ppermute | solution.py:55
  65.1 35.6 %collective-permute-start.19 = (bf16[4,48,1920]{2,1,0:T(8,128)(2,1)S(1)}, bf16[4,48,1920]{2,1,0:T(8,128)(2,1)S(1)}, u32[]{:S(2)}, u32[]{:S(2)}) collective-permute-start(bf16[4,48,1920]{2,1,0:T(8,128)(2,1)S(1)} %bitcast_dynamic-update-slice_fusion.4.refs_4_.refs_8_.refs_5_), channel_id=1, source_target_pairs={{0,2},{1,3},{2,0},{3,1},{4,6},{5,7},{6,4},{7,5},{8,10},{9,11},{10,... | collective-permute-start | bytes 2211848 | tf_op jit(solution)/shard_map/ppermute | solution.py:55
  73.8 26.9 %collective-permute-start.16 = (bf16[4,48,1920]{2,1,0:T(8,128)(2,1)S(1)}, bf16[4,48,1920]{2,1,0:T(8,128)(2,1)S(1)}, u32[]{:S(2)}, u32[]{:S(2)}) collective-permute-start(bf16[4,48,1920]{2,1,0:T(8,128)(2,1)S(1)} %bitcast_dynamic-update-slice_fusion.4.refs_4_.refs_8_.refs_5_), channel_id=1, source_target_pairs={{0,1},{1,0},{2,3},{3,2},{4,5},{5,4},{6,7},{7,6},{8,9},{9,8},{10,11... | collective-permute-start | bytes 2211848 | tf_op jit(solution)/shard_map/ppermute | solution.py:55
  76.0 25.2 %collective-permute-start.15 = (bf16[4,48,1920]{2,1,0:T(8,128)(2,1)S(1)}, bf16[4,48,1920]{2,1,0:T(8,128)(2,1)S(1)}, u32[]{:S(2)}, u32[]{:S(2)}) collective-permute-start(bf16[4,48,1920]{2,1,0:T(8,128)(2,1)S(1)} %bitcast_dynamic-update-slice_fusion.4.refs_4_.refs_8_.refs_5_), channel_id=1, source_target_pairs={{0,4},{1,5},{2,6},{3,7},{4,0},{5,1},{6,2},{7,3},{8,12},{9,13},{10,... | collective-permute-start | bytes 2211848 | tf_op jit(solution)/shard_map/ppermute | solution.py:55
  77.6 21.5 %collective-permute-start.5 = (bf16[2,48,1280]{2,1,0:T(8,128)(2,1)S(1)}, bf16[2,48,1280]{2,1,0:T(8,128)(2,1)S(1)}, u32[]{:S(2)}, u32[]{:S(2)}) collective-permute-start(bf16[2,48,1280]{2,1,0:T(8,128)(2,1)S(1)} %slice.617), channel_id=1, source_target_pairs={{0,4},{1,5},{2,6},{3,7},{4,0},{5,1},{6,2},{7,3},{8,12},{9,13},{10,... | collective-permute-start | bytes 737288 | tf_op jit(solution)/shard_map/ppermute | solution.py:55
  78.1 21.0 %collective-permute-start.6 = (bf16[2,48,1280]{2,1,0:T(8,128)(2,1)S(1)}, bf16[2,48,1280]{2,1,0:T(8,128)(2,1)S(1)}, u32[]{:S(2)}, u32[]{:S(2)}) collective-permute-start(bf16[2,48,1280]{2,1,0:T(8,128)(2,1)S(1)} %slice.618), channel_id=1, source_target_pairs={{0,1},{1,0},{2,3},{3,2},{4,5},{5,4},{6,7},{7,6},{8,9},{9,8},{10,11... | collective-permute-start | bytes 737288 | tf_op jit(solution)/shard_map/ppermute | solution.py:55
  99.0 34.9 %collective-permute-start.30 = (bf16[4,48,3072]{2,1,0:T(8,128)(2,1)S(1)}, bf16[4,48,3072]{2,1,0:T(8,128)(2,1)S(1)}, u32[]{:S(2)}, u32[]{:S(2)}) collective-permute-start(bf16[4,48,3072]{2,1,0:T(8,128)(2,1)S(1)} %bitcast_dynamic-update-slice_fusion.refs_2_), channel_id=1, source_target_pairs={{0,1},{1,0},{2,3},{3,2},{4,5},{5,4},{6,7},{7,6},{8,9},{9,8},{10,11... | collective-permute-start | bytes 3538952 | tf_op jit(solution)/shard_map/ppermute | solution.py:55
  99.2 34.8 %collective-permute-start.27 = (bf16[4,48,3072]{2,1,0:T(8,128)(2,1)S(1)}, bf16[4,48,3072]{2,1,0:T(8,128)(2,1)S(1)}, u32[]{:S(2)}, u32[]{:S(2)}) collective-permute-start(bf16[4,48,3072]{2,1,0:T(8,128)(2,1)S(1)} %bitcast_dynamic-update-slice_fusion.refs_2_), channel_id=1, source_target_pairs={{0,4},{1,5},{2,6},{3,7},{4,0},{5,1},{6,2},{7,3},{8,12},{9,13},{10,... | collective-permute-start | bytes 3538952 | tf_op jit(solution)/shard_map/ppermute | solution.py:55
  102.5 30.8 %collective-permute-start.17 = (bf16[2,48,1920]{2,1,0:T(8,128)(2,1)S(1)}, bf16[2,48,1920]{2,1,0:T(8,128)(2,1)S(1)}, u32[]{:S(2)}, u32[]{:S(2)}) collective-permute-start(bf16[2,48,1920]{2,1,0:T(8,128)(2,1)S(1)} %slice.619), channel_id=1, source_target_pairs={{0,4},{1,5},{2,6},{3,7},{4,0},{5,1},{6,2},{7,3},{8,12},{9,13},{10,... | collective-permute-start | bytes 1105928 | tf_op jit(solution)/shard_map/ppermute | solution.py:55
  103.2 30.1 %collective-permute-start.18 = (bf16[2,48,1920]{2,1,0:T(8,128)(2,1)S(1)}, bf16[2,48,1920]{2,1,0:T(8,128)(2,1)S(1)}, u32[]{:S(2)}, u32[]{:S(2)}) collective-permute-start(bf16[2,48,1920]{2,1,0:T(8,128)(2,1)S(1)} %slice.620), channel_id=1, source_target_pairs={{0,1},{1,0},{2,3},{3,2},{4,5},{5,4},{6,7},{7,6},{8,9},{9,8},{10,11... | collective-permute-start | bytes 1105928 | tf_op jit(solution)/shard_map/ppermute | solution.py:55
  106.7 28.7 %collective-permute-start.21 = (bf16[4,48,1920]{2,1,0:T(8,128)(2,1)S(1)}, bf16[4,48,1920]{2,1,0:T(8,128)(2,1)S(1)}, u32[]{:S(2)}, u32[]{:S(2)}) collective-permute-start(bf16[4,48,1920]{2,1,0:T(8,128)(2,1)S(1)} %collective-permute-done.16.refs_6_.refs_10_.refs_7_), channel_id=1, source_target_pairs={{0,2},{1,3},{2,0},{3,1},{4,6},{5,7},{6,4},{7,5},{8,10},{9,11},{10,... | collective-permute-start | bytes 2211848 | tf_op jit(solution)/shard_map/ppermute | solution.py:55
  133.9 35.0 %collective-permute-start.28 = (bf16[4,48,3072]{2,1,0:T(8,128)(2,1)S(1)}, bf16[4,48,3072]{2,1,0:T(8,128)(2,1)S(1)}, u32[]{:S(2)}, u32[]{:S(2)}) collective-permute-start(bf16[4,48,3072]{2,1,0:T(8,128)(2,1)S(1)} %bitcast_dynamic-update-slice_fusion.refs_2_), channel_id=1, source_target_pairs={{0,2},{1,3},{2,0},{3,1},{4,6},{5,7},{6,4},{7,5},{8,10},{9,11},{10,... | collective-permute-start | bytes 3538952 | tf_op jit(solution)/shard_map/ppermute | solution.py:55
  134.0 34.9 %collective-permute-start.29 = (bf16[4,48,3072]{2,1,0:T(8,128)(2,1)S(1)}, bf16[4,48,3072]{2,1,0:T(8,128)(2,1)S(1)}, u32[]{:S(2)}, u32[]{:S(2)}) collective-permute-start(bf16[4,48,3072]{2,1,0:T(8,128)(2,1)S(1)} %collective-permute-done.27.refs_3_), channel_id=1, source_target_pairs={{0,2},{1,3},{2,0},{3,1},{4,6},{5,7},{6,4},{7,5},{8,10},{9,11},{10,... | collective-permute-start | bytes 3538952 | tf_op jit(solution)/shard_map/ppermute | solution.py:55
  135.4 32.9 %collective-permute-start.31 = (bf16[2,48,3072]{2,1,0:T(8,128)(2,1)S(1)}, bf16[2,48,3072]{2,1,0:T(8,128)(2,1)S(1)}, u32[]{:S(2)}, u32[]{:S(2)}) collective-permute-start(bf16[2,48,3072]{2,1,0:T(8,128)(2,1)S(1)} %slice.621), channel_id=1, source_target_pairs={{0,4},{1,5},{2,6},{3,7},{4,0},{5,1},{6,2},{7,3},{8,12},{9,13},{10,... | collective-permute-start | bytes 1769480 | tf_op jit(solution)/shard_map/ppermute | solution.py:55
  140.0 28.6 %collective-permute-start.32 = (bf16[2,48,3072]{2,1,0:T(8,128)(2,1)S(1)}, bf16[2,48,3072]{2,1,0:T(8,128)(2,1)S(1)}, u32[]{:S(2)}, u32[]{:S(2)}) collective-permute-start(bf16[2,48,3072]{2,1,0:T(8,128)(2,1)S(1)} %slice.622), channel_id=1, source_target_pairs={{0,1},{1,0},{2,3},{3,2},{4,5},{5,4},{6,7},{7,6},{8,9},{9,8},{10,11... | collective-permute-start | bytes 1769480 | tf_op jit(solution)/shard_map/ppermute | solution.py:55
  141.7 44.4 %collective-permute-start.33 = (bf16[4,48,3072]{2,1,0:T(8,128)(2,1)S(1)}, bf16[4,48,3072]{2,1,0:T(8,128)(2,1)S(1)}, u32[]{:S(2)}, u32[]{:S(2)}) collective-permute-start(bf16[4,48,3072]{2,1,0:T(8,128)(2,1)S(1)} %collective-permute-done.30.refs_6_), channel_id=1, source_target_pairs={{0,2},{1,3},{2,0},{3,1},{4,6},{5,7},{6,4},{7,5},{8,10},{9,11},{10,... | collective-permute-start | bytes 3538952 | tf_op jit(solution)/shard_map/ppermute | solution.py:55
  168.3 17.8 %collective-permute-start.34 = (bf16[2,48,3072]{2,1,0:T(8,128)(2,1)S(1)}, bf16[2,48,3072]{2,1,0:T(8,128)(2,1)S(1)}, u32[]{:S(2)}, u32[]{:S(2)}) collective-permute-start(bf16[2,48,3072]{2,1,0:T(8,128)(2,1)S(1)} %collective-permute-done.31.refs_7_), channel_id=1, source_target_pairs={{0,2},{1,3},{2,0},{3,1},{4,6},{5,7},{6,4},{7,5},{8,10},{9,11},{10,... | collective-permute-start | bytes 1769480 | tf_op jit(solution)/shard_map/ppermute | solution.py:55
  168.7 17.5 %collective-permute-start.35 = (bf16[2,48,3072]{2,1,0:T(8,128)(2,1)S(1)}, bf16[2,48,3072]{2,1,0:T(8,128)(2,1)S(1)}, u32[]{:S(2)}, u32[]{:S(2)}) collective-permute-start(bf16[2,48,3072]{2,1,0:T(8,128)(2,1)S(1)} %collective-permute-done.32.refs_8_), channel_id=1, source_target_pairs={{0,2},{1,3},{2,0},{3,1},{4,6},{5,7},{6,4},{7,5},{8,10},{9,11},{10,... | collective-permute-start | bytes 1769480 | tf_op jit(solution)/shard_map/ppermute | solution.py:55
  249.5 39.3 %collective-permute-start.36 = (bf16[2,2,4,48,1280]{4,3,2,1,0:T(8,128)(2,1)}, bf16[2,2,4,48,1280]{4,3,2,1,0:T(8,128)(2,1)}, u32[]{:S(2)}, u32[]{:S(2)}) collective-permute-start(bf16[2,2,4,48,1280]{4,3,2,1,0:T(8,128)(2,1)} %get-tuple-element.85), channel_id=1, source_target_pairs={{0,2},{1,3},{2,0},{3,1},{4,6},{5,7},{6,4},{7,5},{8,10},{9,11},{10,... | collective-permute-start | bytes 5898248 | tf_op jit(solution)/shard_map/ppermute | solution.py:55
  249.7 45.0 %collective-permute-start.51 = (bf16[2,4,48,3072]{3,2,1,0:T(8,128)(2,1)}, bf16[2,4,48,3072]{3,2,1,0:T(8,128)(2,1)S(1)}, u32[]{:S(2)}, u32[]{:S(2)}) collective-permute-start(bf16[2,4,48,3072]{3,2,1,0:T(8,128)(2,1)} %copy-done.13), channel_id=1, source_target_pairs={{0,2},{1,3},{2,0},{3,1},{4,6},{5,7},{6,4},{7,5},{8,10},{9,11},{10,... | collective-permute-start | bytes 7077896 | tf_op jit(solution)/shard_map/ppermute | solution.py:55
  250.0 102.0 %collective-permute-start.42 = (bf16[512,768]{1,0:T(8,128)(2,1)}, bf16[512,768]{1,0:T(8,128)(2,1)S(1)}, u32[]{:S(2)}, u32[]{:S(2)}) collective-permute-start(bf16[512,768]{1,0:T(8,128)(2,1)} %copy-done.5), channel_id=1, source_target_pairs={{0,1},{1,0},{2,3},{3,2},{4,5},{5,4},{6,7},{7,6},{8,9},{9,8},{10,11... | collective-permute-start | bytes 2359304 | tf_op jit(solution)/shard_map/ppermute | solution.py:55
  250.2 40.8 %collective-permute-start.40 = (bf16[2,4,48,3072]{3,2,1,0:T(8,128)(2,1)}, bf16[2,4,48,3072]{3,2,1,0:T(8,128)(2,1)S(1)}, u32[]{:S(2)}, u32[]{:S(2)}) collective-permute-start(bf16[2,4,48,3072]{3,2,1,0:T(8,128)(2,1)} %copy-done.14), channel_id=1, source_target_pairs={{0,2},{1,3},{2,0},{3,1},{4,6},{5,7},{6,4},{7,5},{8,10},{9,11},{10,... | collective-permute-start | bytes 7077896 | tf_op jit(solution)/shard_map/ppermute | solution.py:55
  250.2 36.5 %collective-permute-start.43 = (bf16[512,768]{1,0:T(8,128)(2,1)}, bf16[512,768]{1,0:T(8,128)(2,1)S(1)}, u32[]{:S(2)}, u32[]{:S(2)}) collective-permute-start(bf16[512,768]{1,0:T(8,128)(2,1)} %copy-done.9), channel_id=1, source_target_pairs={{0,1},{1,0},{2,3},{3,2},{4,5},{5,4},{6,7},{7,6},{8,9},{9,8},{10,11... | collective-permute-start | bytes 2359304 | tf_op jit(solution)/shard_map/ppermute | solution.py:55
  288.8 67.1 %collective-permute-start.44 = (bf16[512,768]{1,0:T(8,128)(2,1)S(1)}, bf16[512,768]{1,0:T(8,128)(2,1)S(1)}, u32[]{:S(2)}, u32[]{:S(2)}) collective-permute-start(bf16[512,768]{1,0:T(8,128)(2,1)S(1)} %copy-done.8), channel_id=1, source_target_pairs={{0,1},{1,0},{2,3},{3,2},{4,5},{5,4},{6,7},{7,6},{8,9},{9,8},{10,11... | collective-permute-start | bytes 2359304 | tf_op jit(solution)/shard_map/ppermute | solution.py:55
  292.7 18.4 %collective-permute-start.41 = (bf16[4,48,1792]{2,1,0:T(8,128)(2,1)S(1)}, bf16[4,48,1792]{2,1,0:T(8,128)(2,1)S(1)}, u32[]{:S(2)}, u32[]{:S(2)}) collective-permute-start(bf16[4,48,1792]{2,1,0:T(8,128)(2,1)S(1)} %fusion), channel_id=1, source_target_pairs={{0,4},{1,5},{2,6},{3,7},{4,0},{5,1},{6,2},{7,3},{8,12},{9,13},{10,... | collective-permute-start | bytes 2064392 | tf_op jit(solution)/shard_map/ppermute | solution.py:55
  294.7 35.6 %collective-permute-start.52 = (bf16[2,4,48,1280]{3,2,1,0:T(8,128)(2,1)S(1)}, bf16[2,4,48,1280]{3,2,1,0:T(8,128)(2,1)S(1)}, u32[]{:S(2)}, u32[]{:S(2)}) collective-permute-start(bf16[2,4,48,1280]{3,2,1,0:T(8,128)(2,1)S(1)} %add_convert_fusion), channel_id=1, source_target_pairs={{0,1},{1,0},{2,3},{3,2},{4,5},{5,4},{6,7},{7,6},{8,9},{9,8},{10,11... | collective-permute-start | bytes 2949128 | tf_op jit(solution)/shard_map/ppermute | solution.py:55
  296.7 28.4 %collective-permute-start.54 = (bf16[4,48,1792]{2,1,0:T(8,128)(2,1)S(1)}, bf16[4,48,1792]{2,1,0:T(8,128)(2,1)S(1)}, u32[]{:S(2)}, u32[]{:S(2)}) collective-permute-start(bf16[4,48,1792]{2,1,0:T(8,128)(2,1)S(1)} %fusion.1), channel_id=1, source_target_pairs={{0,4},{1,5},{2,6},{3,7},{4,0},{5,1},{6,2},{7,3},{8,12},{9,13},{10,... | collective-permute-start | bytes 2064392 | tf_op jit(solution)/shard_map/ppermute | solution.py:55
  311.1 33.4 %collective-permute-start.38 = (bf16[2,4,48,896]{3,2,1,0:T(8,128)(2,1)S(1)}, bf16[2,4,48,896]{3,2,1,0:T(8,128)(2,1)S(1)}, u32[]{:S(2)}, u32[]{:S(2)}) collective-permute-start(bf16[2,4,48,896]{3,2,1,0:T(8,128)(2,1)S(1)} %add_convert_fusion.3), channel_id=1, source_target_pairs={{0,1},{1,0},{2,3},{3,2},{4,5},{5,4},{6,7},{7,6},{8,9},{9,8},{10,11... | collective-permute-start | bytes 2064392 | tf_op jit(solution)/shard_map/ppermute | solution.py:55
  325.1 19.7 %collective-permute-start.39 = (bf16[2,4,48,1024]{3,2,1,0:T(8,128)(2,1)S(1)}, bf16[2,4,48,1024]{3,2,1,0:T(8,128)(2,1)S(1)}, u32[]{:S(2)}, u32[]{:S(2)}) collective-permute-start(bf16[2,4,48,1024]{3,2,1,0:T(8,128)(2,1)S(1)} %pad_maximum_fusion), channel_id=1, source_target_pairs={{0,4},{1,5},{2,6},{3,7},{4,0},{5,1},{6,2},{7,3},{8,12},{9,13},{10,... | collective-permute-start | bytes 2359304 | tf_op jit(solution)/shard_map/ppermute | solution.py:55
  330.3 29.2 %collective-permute-start.67 = (bf16[48,1792]{1,0:T(8,128)(2,1)S(1)}, bf16[48,1792]{1,0:T(8,128)(2,1)S(1)}, u32[]{:S(2)}, u32[]{:S(2)}) collective-permute-start(bf16[48,1792]{1,0:T(8,128)(2,1)S(1)} %get-tuple-element.119), channel_id=1, source_target_pairs={{0,8},{1,9},{2,10},{3,11},{4,12},{5,13},{6,14},{7,15},{8,16},{9,17... | collective-permute-start | bytes 516104 | tf_op jit(solution)/shard_map/ppermute | solution.py:55
  344.6 16.8 %collective-permute-start.69 = (bf16[48,1792]{1,0:T(8,128)(2,1)S(1)}, bf16[48,1792]{1,0:T(8,128)(2,1)S(1)}, u32[]{:S(2)}, u32[]{:S(2)}) collective-permute-start(bf16[48,1792]{1,0:T(8,128)(2,1)S(1)} %get-tuple-element.120), channel_id=1, source_target_pairs={{0,24},{1,25},{2,26},{3,27},{4,28},{5,29},{6,30},{7,31},{8,0},{9,1... | collective-permute-start | bytes 516104 | tf_op jit(solution)/shard_map/ppermute | solution.py:55
  344.8 22.7 %collective-permute-start.68 = (bf16[48,1792]{1,0:T(8,128)(2,1)S(1)}, bf16[48,1792]{1,0:T(8,128)(2,1)S(1)}, u32[]{:S(2)}, u32[]{:S(2)}) collective-permute-start(bf16[48,1792]{1,0:T(8,128)(2,1)S(1)} %get-tuple-element.121), channel_id=1, source_target_pairs={{0,16},{1,17},{2,18},{3,19},{4,20},{5,21},{6,22},{7,23},{8,24},{9,... | collective-permute-start | bytes 516104 | tf_op jit(solution)/shard_map/ppermute | solution.py:55
  352.0 54.7 %collective-permute-start.64 = (bf16[48,1792]{1,0:T(8,128)(2,1)S(1)}, bf16[48,1792]{1,0:T(8,128)(2,1)S(1)}, u32[]{:S(2)}, u32[]{:S(2)}) collective-permute-start(bf16[48,1792]{1,0:T(8,128)(2,1)S(1)} %get-tuple-element.115), channel_id=1, source_target_pairs={{0,8},{1,9},{2,10},{3,11},{4,12},{5,13},{6,14},{7,15},{8,16},{9,17... | collective-permute-start | bytes 516104 | tf_op jit(solution)/shard_map/ppermute | solution.py:55
  359.5 50.3 %collective-permute-start.66 = (bf16[48,1792]{1,0:T(8,128)(2,1)S(1)}, bf16[48,1792]{1,0:T(8,128)(2,1)S(1)}, u32[]{:S(2)}, u32[]{:S(2)}) collective-permute-start(bf16[48,1792]{1,0:T(8,128)(2,1)S(1)} %get-tuple-element.116), channel_id=1, source_target_pairs={{0,24},{1,25},{2,26},{3,27},{4,28},{5,29},{6,30},{7,31},{8,0},{9,1... | collective-permute-start | bytes 516104 | tf_op jit(solution)/shard_map/ppermute | solution.py:55
  370.0 17.1 %collective-permute-start.45 = (bf16[2,4,48,640]{3,2,1,0:T(8,128)(2,1)S(1)}, bf16[2,4,48,640]{3,2,1,0:T(8,128)(2,1)S(1)}, u32[]{:S(2)}, u32[]{:S(2)}) collective-permute-start(bf16[2,4,48,640]{3,2,1,0:T(8,128)(2,1)S(1)} %add_convert_fusion.6), channel_id=1, source_target_pairs={{0,1},{1,0},{2,3},{3,2},{4,5},{5,4},{6,7},{7,6},{8,9},{9,8},{10,11... | collective-permute-start | bytes 1474568 | tf_op jit(solution)/shard_map/ppermute | solution.py:55
  395.5 17.8 %collective-permute-start.65 = (bf16[48,1792]{1,0:T(8,128)(2,1)S(1)}, bf16[48,1792]{1,0:T(8,128)(2,1)S(1)}, u32[]{:S(2)}, u32[]{:S(2)}) collective-permute-start(bf16[48,1792]{1,0:T(8,128)(2,1)S(1)} %get-tuple-element.117), channel_id=1, source_target_pairs={{0,16},{1,17},{2,18},{3,19},{4,20},{5,21},{6,22},{7,23},{8,24},{9,... | collective-permute-start | bytes 516104 | tf_op jit(solution)/shard_map/ppermute | solution.py:55
  399.1 17.1 %collective-permute-start.70 = (bf16[48,1792]{1,0:T(8,128)(2,1)S(1)}, bf16[48,1792]{1,0:T(8,128)(2,1)S(1)}, u32[]{:S(2)}, u32[]{:S(2)}) collective-permute-start(bf16[48,1792]{1,0:T(8,128)(2,1)S(1)} %add_convert_fusion.19), channel_id=1, source_target_pairs={{0,1},{1,0},{2,3},{3,2},{4,5},{5,4},{6,7},{7,6},{8,9},{9,8},{10,11... | collective-permute-start | bytes 516104 | tf_op jit(solution)/shard_map/ppermute | solution.py:55
  406.6 19.9 %collective-permute-start.59 = (bf16[48,1920]{1,0:T(8,128)(2,1)S(1)}, bf16[48,1920]{1,0:T(8,128)(2,1)S(1)}, u32[]{:S(2)}, u32[]{:S(2)}) collective-permute-start(bf16[48,1920]{1,0:T(8,128)(2,1)S(1)} %pad_maximum_fusion.6), channel_id=1, source_target_pairs={{0,16},{1,17},{2,18},{3,19},{4,20},{5,21},{6,22},{7,23},{8,24},{9,... | collective-permute-start | bytes 552968 | tf_op jit(solution)/shard_map/ppermute | solution.py:55
  406.7 19.8 %collective-permute-start.60 = (bf16[48,1920]{1,0:T(8,128)(2,1)S(1)}, bf16[48,1920]{1,0:T(8,128)(2,1)S(1)}, u32[]{:S(2)}, u32[]{:S(2)}) collective-permute-start(bf16[48,1920]{1,0:T(8,128)(2,1)S(1)} %pad_maximum_fusion.7), channel_id=1, source_target_pairs={{0,24},{1,25},{2,26},{3,27},{4,28},{5,29},{6,30},{7,31},{8,0},{9,1... | collective-permute-start | bytes 552968 | tf_op jit(solution)/shard_map/ppermute | solution.py:55
  409.8 16.7 %collective-permute-start.58 = (bf16[48,1920]{1,0:T(8,128)(2,1)S(1)}, bf16[48,1920]{1,0:T(8,128)(2,1)S(1)}, u32[]{:S(2)}, u32[]{:S(2)}) collective-permute-start(bf16[48,1920]{1,0:T(8,128)(2,1)S(1)} %pad_maximum_fusion.5), channel_id=1, source_target_pairs={{0,8},{1,9},{2,10},{3,11},{4,12},{5,13},{6,14},{7,15},{8,16},{9,17... | collective-permute-start | bytes 552968 | tf_op jit(solution)/shard_map/ppermute | solution.py:55
  416.2 17.4 %collective-permute-start.56 = (bf16[48,1280]{1,0:T(8,128)(2,1)S(1)}, bf16[48,1280]{1,0:T(8,128)(2,1)S(1)}, u32[]{:S(2)}, u32[]{:S(2)}) collective-permute-start(bf16[48,1280]{1,0:T(8,128)(2,1)S(1)} %pad_maximum_fusion.9), channel_id=1, source_target_pairs={{0,16},{1,17},{2,18},{3,19},{4,20},{5,21},{6,22},{7,23},{8,24},{9,... | collective-permute-start | bytes 368648 | tf_op jit(solution)/shard_map/ppermute | solution.py:55
  (72 other events, 1216.8 us)

commit v3 on v2

--- a/solution.py
+++ b/solution.py
@@ -19,7 +19,7 @@
 F32 = jnp.float32
 BF16 = jnp.bfloat16
 MIB = 1024 * 1024
-VMEM_LIMIT = {"ka": 13, "kb": 16, "kca": 20, "kcb": 22, "kd1": 12, "kd2": 20, "ke1": 12, "ke2": 16}
+VMEM_LIMIT = {"ka": 13, "kb": 16, "kca": 23, "kcb": 25, "kd1": 12, "kd2": 22, "ke1": 12, "ke2": 16}
 
 
 def nn(left, right):
@@ -106,15 +106,37 @@
     return [(whole[m], m, None, None, 0) for m in range(2)]
 
 
+def gather_late(grid, block):
+    rows, cols = block.shape
+    n = grid.n_z
+    z, y, c, _ = place()
+    by_m = grid.swap_m(block)
+    by_y = grid.swap_y(block)
+    diag = grid.send(block, lambda z, y, c, m: (z, 1 - y, c, 1 - m))
+    own = jnp.stack([block, by_y, by_m, diag]).reshape(2, 2, rows, cols)
+    mine = jnp.stack([own] + [grid.shift_z(own, d) for d in range(1, n)])
+    other = grid.swap_c(mine)
+    if rows % 16 == 0:
+        return [(mine, "late", 0), (other, "late", 1)]
+    whole = jnp.stack([mine, other])
+    whole = jnp.take(whole, (z - jnp.arange(n)) % n, axis=1)
+    whole = jnp.take(whole, jnp.arange(2) ^ y, axis=3)
+    whole = jnp.take(whole, jnp.arange(2) ^ c, axis=0)
+    whole = whole.transpose(2, 1, 3, 0, 4, 5).reshape(2, n * 4 * rows, cols)
+    return [(whole[m], m, None, None, 0) for m in range(2)]
+
+
 class Weights:
     def __init__(self, pieces, n_z, half=None):
-        chosen = [p for p in pieces if half is None or p[1] == half]
+        chosen = [p for p in pieces if half is None or p[1] in (half, "late")]
         self.arrays = [p[0] for p in chosen]
         self.metas = [p[1:] for p in chosen]
-        self.packed = self.metas[0][1] is None
+        self.late = self.metas[0][0] == "late"
+        self.packed = not self.late and self.metas[0][1] is None
         self.n_z = n_z
-        self.rows = pieces[0][0].shape[1] if not self.packed else pieces[0][0].shape[0] // (4 * n_z)
+        self.rows = pieces[0][0].shape[-2] if not self.packed else pieces[0][0].shape[0] // (4 * n_z)
         self.half = half
+        self.each = len(self.arrays) * (2 * n_z if self.late else 1)
 
     def specs(self):
         return [(a, True) for a in self.arrays]
@@ -126,19 +148,31 @@
         return pltpu.VMEM(lead + (self.n_z, 2, 2, self.rows, n), BF16)
 
     def sems(self, count=1):
-        return pltpu.SemaphoreType.DMA((count * len(self.arrays),))
+        return pltpu.SemaphoreType.DMA((count * self.each,))
 
     def start(self, refs, dest, sems, src, n, at=0, slot=0):
-        _, y, c, _ = place()
+        z, y, c, _ = place()
         copies = []
-        for i, ((m, b, e, j), ref) in enumerate(zip(self.metas, refs)):
+        if self.late:
+            for (_, e), ref in zip(self.metas, refs):
+                for d in range(self.n_z):
+                    for b in range(2):
+                        cp = pltpu.make_async_copy(
+                            ref.at[d, self.half, b, :, pl.ds(src, n)],
+                            dest.at[lax.rem(z - d + self.n_z, self.n_z), y ^ b, c ^ e, :, pl.ds(at, n)],
+                            sems.at[slot * self.each + len(copies)],
+                        )
+                        cp.start()
+                        copies.append(cp)
+            return copies
+        for (m, b, e, j), ref in zip(self.metas, refs):
             to = pl.ds(at + (0 if self.half is not None else m * n), n)
             if self.packed:
-                cp = pltpu.make_async_copy(ref.at[:, pl.ds(src, n)], dest.at[:, to], sems.at[slot * len(self.arrays) + i])
+                cp = pltpu.make_async_copy(ref.at[:, pl.ds(src, n)], dest.at[:, to], sems.at[slot * self.each + len(copies)])
             else:
                 k = ref.shape[0]
                 cp = pltpu.make_async_copy(
-                    ref.at[:, :, pl.ds(src, n)], dest.at[pl.ds(j, k), y ^ b, c ^ e, :, to], sems.at[slot * len(self.arrays) + i]
+                    ref.at[:, :, pl.ds(src, n)], dest.at[pl.ds(j, k), y ^ b, c ^ e, :, to], sems.at[slot * self.each + len(copies)]
                 )
             cp.start()
             copies.append(cp)
@@ -417,8 +451,6 @@
         ce = ws.start(w_refs, we, s_e, 3 * hd, LANE)
         cw = [ws.start(w_refs, w.at[g], s_w, g * hd, hd, slot=g) for g in range(3)]
         cx.wait()
-        x = x_v[...].astype(F32)
-        scaled = x * lax.rsqrt(jnp.mean(x * x, axis=-1, keepdims=True) + EPS)
         wait(ce)
         extra = ws.value(we, 0, 2 * LANE)
         rows = ws.rows
@@ -441,7 +473,13 @@
         base_ref[...] = jnp.zeros_like(base_ref)
         for a in range(2):
             base_ref[a * heads : (a + 1) * heads, :] = nn(extra[0:16, a * LANE : (a + 1) * LANE], hot_ref[...])[:heads]
-        n1_ref[...] = (scaled * gains[0:1]).astype(BF16)
+
+        def normalize(t, carry):
+            rows = pl.ds(pl.multiple_of(t * QB, QB), QB)
+            n1_ref[rows, :] = rms(x_v[rows, :].astype(F32), gain_ref[0:1, :]).astype(BF16)
+            return carry
+
+        lax.fori_loop(0, L // QB, normalize, 0)
 
         def project(g, carry):
             wait_for(g, cw)
@@ -537,12 +575,20 @@
     )
 
 
-def feed_forward(grid, cotangent, n3, r2, gains, carried, pieces, half, d, ff):
+def late_columns(ff):
+    return ff // 2 // LANE * LANE
+
+
+def feed_forward(grid, cotangent, n3, r2, gains, carried, pieces, late, half, d, ff, others=()):
     ws = Weights(pieces, grid.n_z, half)
-    k = len(ws.arrays)
+    wl = Weights(late, grid.n_z, half)
+    ks = len(ws.arrays)
+    k = ks + len(wl.arrays)
     tile = min(256, ff)
+    wide = min(512, ff)
+    late_cols = late_columns(ff)
     last = carried is not None
-    extra_in = 4 if last else 0
+    extra_in = 5 if last else len(others)
     parts = Parts(grid, d, 3 * ff, False)
     ng = parts.count()
 
@@ -551,32 +597,46 @@
         w_refs = refs[2 + extra_in : 2 + extra_in + k]
         rest = refs[2 + extra_in + k :]
         if last:
-            r2_ref, gain_ref, yin_ref, bin_ref = refs[2:6]
+            r2_ref, gain_ref, yin_ref, bin_ref, turned = refs[2:7]
             y_ref, b2_ref, dg_ref, y_acc, b3_acc = rest[ng : ng + 5]
         else:
-            y_acc, b3_acc = rest[ng : ng + 2]
-        g_refs, rest = rest[:ng], rest[ng + (5 if last else 2) :]
-        cot_v, wg, wu, wd, turned, lows, sem_c, s_g, s_u, s_d = rest
+            enc_ref, *other_refs = refs[2 : 2 + extra_in]
+            y_acc, b3_acc, turned, turned_others = rest[ng : ng + 4]
+        g_refs, rest = rest[:ng], rest[ng + (5 if last else 4) :]
+        cot_v, enc_v, wg, wu, wd, lows, pending, sem_c, sem_e, s_g, s_u, s_d, s_l = rest
         cc = sequence_copy(cot_ref, cot_v, sem_c)
-        cg = ws.start(w_refs, wg, s_g, 0, ff)
-        cu = ws.start(w_refs, wu, s_u, ff, ff)
-        cd = ws.start(w_refs, wd, s_d, 2 * ff, ff)
+        cg = ws.start(w_refs[:ks], wg, s_g, 0, ff)
+        cu = ws.start(w_refs[:ks], wu, s_u, ff, ff)
+        cd = ws.start(w_refs[:ks], wd, s_d, 2 * ff, ff - late_cols)
+        cd += wl.start(w_refs[ks:], wd, s_l, 0, late_cols, at=ff - late_cols)
         if last:
             y_acc[...] = r2_ref[...] + yin_ref[...]
             b3_acc[...] = bin_ref[...]
         else:
+            ce = sequence_copy(enc_ref, enc_v, sem_e)
             y_acc[...] = jnp.zeros_like(y_acc)
             b3_acc[...] = jnp.zeros_like(b3_acc)
-        turned[0] = n3_ref[...].T
+            ce.wait()
         cc.wait()
-        turned[1] = cot_v[...].T
+        if not last:
+
+            def turn(t, carry):
+                rows = pl.ds(pl.multiple_of(t * QB, QB), QB)
+                turned[0, :, rows] = n3_ref[rows, :].T
+                turned[1, :, rows] = cot_v[rows, :].T
+                for i, ref in enumerate(other_refs):
+                    turned_others[i, :, rows] = ref[rows, :].T
+                turned_others[len(others) - 1, :, rows] = enc_v[rows, :].T
+                return carry
+
+            lax.fori_loop(0, L // QB, turn, 0)
         wait(cg)
         wait(cu)
         wait(cd)
 
         def step(t, carry):
             at = pl.multiple_of(t * tile, LANE)
-            gate, upw, down = ws.columns(wg, at, tile), ws.columns(wu, at, tile), ws.columns(wd, at, tile)
+            gate, upw, down = ws.columns(wg, at, tile), ws.columns(wu, at, tile), wl.columns(wd, at, tile)
             u = nn(n3_ref[...], gate)
             up = nn(n3_ref[...], upw)
             bh = nn(cot_v[...], down)
@@ -585,20 +645,27 @@
             both = 0.5 * (1.0 + th)
             gelu = u * both
             slope = both + 0.5 * u * (1.0 - th * th) * (GELU_C * (1.0 + (3.0 * GELU_A) * sq))
-            lows[2] = (gelu * up).astype(BF16)
-            lows[0] = (bh * up * slope).astype(BF16)
-            lows[1] = (bh * gelu).astype(BF16)
-            y_acc[...] += nt(lows[2], down)
-            b3_acc[...] += nt(lows[0], gate) + nt(lows[1], upw)
-
-            def weight(g, inner):
-                parts.put(g_refs, None, pl.multiple_of(g * ff + at, LANE), nn(turned[g // 2], lows[g]))
-                return inner
-
-            lax.fori_loop(0, 3, weight, 0)
+            hidden = (gelu * up).astype(BF16)
+            gate_low = (bh * up * slope).astype(BF16)
+            up_low = (bh * gelu).astype(BF16)
+            y_acc[...] += nt(hidden, down)
+            b3_acc[...] += nt(gate_low, gate) + nt(up_low, upw)
+            for g, low in enumerate((gate_low, up_low, hidden)):
+                lows[g, :, pl.ds(at, tile)] = low
             return carry
 
         lax.fori_loop(0, ff // tile, step, 0)
+        pending[...] = jnp.zeros_like(pending)
+
+        def weight(t, before):
+            parts.put(g_refs, None, pl.multiple_of(before, LANE), pending[...])
+            g = t // (ff // wide)
+            at = pl.multiple_of(lax.rem(t, ff // wide) * wide, LANE)
+            pending[...] = nn(turned[g // 2], lows[g, :, pl.ds(at, wide)]).astype(BF16)
+            return g * ff + at
+
+        at_last = lax.fori_loop(0, 3 * ff // wide, weight, jnp.int32(0))
+        parts.put(g_refs, None, pl.multiple_of(at_last, LANE), pending[...])
         if last:
             dg_ref[...] = jnp.zeros_like(dg_ref)
 
@@ -614,24 +681,34 @@
 
     full = ((L, d), F32)
     outs = parts.outs()
-    outs += [((L, d), BF16), full, ((1, d), F32)] if last else [full, full]
+    if last:
+        outs += [((L, d), BF16), full, ((1, d), F32)]
+    else:
+        outs += [full, full, ((2, d, L), BF16), ((len(others), d, L), BF16)]
     scratch = [pltpu.VMEM((L, d), F32), pltpu.VMEM((L, d), F32)] if last else []
     result = call(
         body,
         outs,
-        [(cotangent, True)] + near(n3) + (near(r2, gains, *carried) if last else []) + ws.specs(),
+        [(cotangent, True)]
+        + near(n3)
+        + (near(r2, gains, *carried) if last else [(others[0], True)] + near(*others[1:]))
+        + ws.specs()
+        + wl.specs(),
         scratch
         + [
             pltpu.VMEM((L, d), BF16),
+            pltpu.VMEM((8, LANE) if last else (L, d), BF16),
             ws.scratch(ff),
             ws.scratch(ff),
             ws.scratch(ff),
-            pltpu.VMEM((2, d, L), BF16),
-            pltpu.VMEM((3, L, tile), BF16),
+            pltpu.VMEM((3, L, ff), BF16),
+            pltpu.VMEM((d, wide), BF16),
+            DMA,
             DMA,
             ws.sems(),
             ws.sems(),
             ws.sems(),
+            wl.sems(),
         ],
         "kcb" if last else "kca",
         7_500_000_000,
@@ -693,7 +770,7 @@
     )
 
 
-def cross_finish(grid, encoded, b2, r1, n2, grads, attn_one, attn_two, gains, pieces, d, hd):
+def cross_finish(grid, b2, r1, ready, grads, attn_one, attn_two, gains, pieces, d, hd):
     ws = Weights(pieces, grid.n_z)
     k = len(ws.arrays)
     w2 = 2 * hd
@@ -701,17 +778,17 @@
     ng = parts.count()
 
     def body(*refs):
-        enc_ref, b2_ref, r1_ref, n2_ref, dy_ref, a1_ref, a2_ref, gain_ref = refs[:8]
-        w_refs = refs[8 : 8 + k]
-        b1_ref, eg_ref, dg_ref = refs[8 + k : 11 + k]
-        g_refs = refs[11 + k : 11 + k + ng]
-        enc_v, w, turned, right, sem_e, s_w = refs[11 + k + ng :]
-        ce = sequence_copy(enc_ref, enc_v, sem_e)
+        b2_ref, r1_ref, ready_ref, dy_ref, a1_ref, a2_ref, gain_ref = refs[:7]
+        w_refs = refs[7 : 7 + k]
+        b1_ref, eg_ref, dg_ref = refs[7 + k : 10 + k]
+        g_refs = refs[10 + k : 10 + k + ng]
+        w, turned, right, s_w = refs[10 + k + ng :]
         cw = [ws.start(w_refs, w.at[g], s_w, (g + 1) * hd, hd, slot=g) for g in range(3)]
-        turned[3] = b2_ref[...].astype(BF16).T
-        right[1] = a2_ref[...]
+        turned[1] = b2_ref[...].astype(BF16).T
         right[0] = a1_ref[...]
-        turned[0] = n2_ref[...].T
+        for g in range(3):
+            right[g + 1] = dy_ref[g]
+        right[4] = a2_ref[...]
         wait(cw[0])
         dg_ref[...] = jnp.zeros_like(dg_ref)
 
@@ -723,21 +800,17 @@
             return carry
 
         lax.fori_loop(0, L // WIDE, resume, 0)
-        turned[2] = b1_ref[...].astype(BF16).T
-        ce.wait()
-        turned[1] = enc_v[...].T
-
-        def inner(g, carry):
-            parts.put_halves(g_refs, pl.multiple_of((g + 1) * hd, LANE), hd, nn(turned[jnp.minimum(g, 1)], dy_ref[g]))
+        turned[0] = b1_ref[...].astype(BF16).T
+        turned[2] = ready_ref[1]
+        turned[3] = ready_ref[2]
+
+        def weight(t, carry):
+            parts.put_halves(g_refs, pl.multiple_of(2 * t * hd, LANE), hd, nn(turned[3 * t], right[2 * t]))
+            parts.put_halves(g_refs, pl.multiple_of((2 * t + 1) * hd, LANE), hd, nn(turned[2 + t], right[2 * t + 1]))
             return carry
 
-        lax.fori_loop(0, 3, inner, 0)
-
-        def outer(g, carry):
-            parts.put_halves(g_refs, pl.multiple_of(g * 4 * hd, LANE), hd, nn(turned[2 + g], right[g]))
-            return carry
-
-        lax.fori_loop(0, 2, outer, 0)
+        lax.fori_loop(0, 2, weight, 0)
+        parts.put_halves(g_refs, 4 * hd, hd, nn(turned[1], right[4]))
         wait(cw[1])
         wait(cw[2])
 
@@ -752,13 +825,11 @@
     result = call(
         body,
         [((L, d), F32), ((L, d), BF16), ((1, d), F32)] + parts.outs(),
-        [(encoded, True)] + near(b2, r1, n2, grads, attn_one, attn_two, gains) + ws.specs(),
+        near(b2, r1, ready, grads, attn_one, attn_two, gains) + ws.specs(),
         [
-            pltpu.VMEM((L, d), BF16),
             ws.scratch(w2, 3),
             pltpu.VMEM((4, d, L), BF16),
-            pltpu.VMEM((2, L, w2), BF16),
-            DMA,
+            pltpu.VMEM((5, L, w2), BF16),
             ws.sems(3),
         ],
         "kd2",
@@ -767,7 +838,7 @@
     return result[:3], parts.split(result[3:])
 
 
-def self_finish(grid, inputs, b1, n1, grads, off, dg2, dg3, base_hot, gains, pieces, d, hd, heads):
+def self_finish(grid, inputs, b1, ready, grads, off, dg2, dg3, base_hot, gains, pieces, d, hd, heads):
     ws = Weights(pieces, grid.n_z)
     k = len(ws.arrays)
     w2 = 2 * hd
@@ -775,26 +846,34 @@
     ng = parts.count()
 
     def body(*refs):
-        x_ref, b1_ref, n1_ref, dy_ref, off_ref, dg2_ref, dg3_ref, hot_ref, gain_ref = refs[:9]
+        x_ref, b1_ref, ready_ref, dy_ref, off_ref, dg2_ref, dg3_ref, hot_ref, gain_ref = refs[:9]
         w_refs = refs[9 : 9 + k]
         dx_ref = refs[9 + k]
         g_refs = refs[10 + k : 10 + k + ng]
-        x_v, w, turned, back, sem_x, s_w = refs[10 + k + ng :]
+        x_v, w, back, pending, sem_x, s_w = refs[10 + k + ng :]
         cw = [ws.start(w_refs, w.at[g], s_w, g * hd, hd, slot=g) for g in range(3)]
         cx = sequence_copy(x_ref, x_v, sem_x)
-        turned[...] = n1_ref[...].T
         back[...] = jnp.zeros_like(back)
 
         def inner(g, carry):
-            parts.put_halves(g_refs, pl.multiple_of(g * hd, LANE), hd, nn(turned[...], dy_ref[g]))
             wait_for(g, cw)
+            parts.put_halves(g_refs, pl.multiple_of(jnp.maximum(g - 1, 0) * hd, LANE), hd, pending[...])
+            pending[...] = nn(ready_ref[0], dy_ref[g]).astype(BF16)
             back[...] += nt(dy_ref[g], ws.value(w.at[g], 0, w2))
             return carry
 
+        pending[...] = jnp.zeros_like(pending)
         lax.fori_loop(0, 3, inner, 0)
+        parts.put_halves(g_refs, 2 * hd, hd, pending[...])
         cx.wait()
-        grad, dg = rms_back(x_v[...].astype(F32), gain_ref[0:1, :], back[...])
-        dx_ref[...] = (b1_ref[...] + grad).astype(BF16)
+
+        def finish(t, dg):
+            rows = pl.ds(pl.multiple_of(t * QB, QB), QB)
+            grad, own = rms_back(x_v[rows, :].astype(F32), gain_ref[0:1, :], back[rows, :])
+            dx_ref[rows, :] = (b1_ref[rows, :] + grad).astype(BF16)
+            return dg + own
+
+        dg = lax.fori_loop(0, L // QB, finish, jnp.zeros((1, d), F32))
         dgs = jnp.concatenate([dg, dg2_ref[...], dg3_ref[...], jnp.zeros((5, d), F32)], axis=0)
         columns = jnp.concatenate([jnp.zeros((NB, d), F32), dgs, jnp.zeros((LANE - NB - 8, d), F32)], axis=0).T
         hot = hot_ref[...]
@@ -814,12 +893,12 @@
     result = call(
         body,
         [((L, d), BF16)] + parts.outs(),
-        [(inputs, True)] + near(b1, n1, grads, off, dg2, dg3, base_hot, gains) + ws.specs(),
+        [(inputs, True)] + near(b1, ready, grads, off, dg2, dg3, base_hot, gains) + ws.specs(),
         [
             pltpu.VMEM((L, d), BF16),
             ws.scratch(w2, 3),
-            pltpu.VMEM((d, L), BF16),
             pltpu.VMEM((L, d), F32),
+            pltpu.VMEM((d, w2), BF16),
             DMA,
             ws.sems(3),
         ],
@@ -938,33 +1017,38 @@
         )
         group_one = jnp.concatenate([query_self, keys_self, values_self, extra], axis=1)
         group_two = jnp.concatenate([output_self.T, query_cross, keys_cross, values_cross, output_cross.T], axis=1)
-        group_three = jnp.concatenate([gate_weight, up_weight, down_weight.T], axis=1)
+        turned = down_weight.T
+        early = ff - late_columns(ff)
+        group_three = jnp.concatenate([gate_weight, up_weight, turned[:, :early]], axis=1)
         pieces_one = gather(grid, group_one)
         pieces_two = gather(grid, group_two)
         pieces_three = gather(grid, group_three)
+        pieces_four = gather_late(grid, turned[:, early:])
 
         base_hot = (buckets[None, :] == lax.broadcasted_iota(jnp.int32, (LANE, L), 0)).astype(BF16)
 
         n1, qkv1, at1, gains, base, lse1 = self_forward(grid, inputs, base_hot, pieces_one, d, hd, heads)
         r1, r2, n2, qkv2, at2, n3, lse2 = cross_forward(grid, inputs, encoded, at1, gains, pieces_two, d, hd)
-        (own3, gone), (ya, ba) = feed_forward(grid, cotangent, n3, r2, gains, None, pieces_three, 0, d, ff)
+        (own3, gone), (ya, ba, turned, turned_others) = feed_forward(
+            grid, cotangent, n3, r2, gains, None, pieces_three, pieces_four, 0, d, ff, (encoded, n1, n2)
+        )
         own3_got = grid.swap_c(gone)
         (other3, gone), (y, b2, dg3) = feed_forward(
-            grid, cotangent, n3, r2, gains, (ya, ba), pieces_three, 1, d, ff
+            grid, cotangent, n3, r2, gains, (ya, ba, turned), pieces_three, pieces_four, 1, d, ff
         )
         other3_got = grid.swap_c(gone)
         y_far = grid.swap_m(y)
-        a3, bo3, bt3 = scatter_wide(grid, own3, own3_got, other3, other3_got, ff * 5 // 4 // LANE * LANE)
+        a3, bo3, bt3 = scatter_wide(grid, own3, own3_got, other3, other3_got, 6 * LANE)
         (dy,) = attention_backward(grid, b2, qkv2, at2, lse2, None, pieces_two, 4 * hd, hd, "kd1")
         (b1, eg, dg2), (kept, gone) = cross_finish(
-            grid, encoded, b2, r1, n2, dy, at1, at2, gains, pieces_two, d, hd
+            grid, b2, r1, turned_others, dy, at1, at2, gains, pieces_two, d, hd
         )
         eg_far = grid.swap_m(eg)
         got = grid.swap_c(gone)
         kept2, far2, _ = scatter(grid, kept[0], got[0], kept[1], got[1], 7 * LANE)
         dy, off = attention_backward(grid, b1, qkv1, at1, lse1, base, pieces_two, 0, hd, "ke1")
         dx, (kept, gone) = self_finish(
-            grid, inputs, b1, n1, dy, off, dg2, dg3, base_hot, gains, pieces_one, d, hd, heads
+            grid, inputs, b1, turned_others, dy, off, dg2, dg3, base_hot, gains, pieces_one, d, hd, heads
         )
         got = grid.swap_c(gone)
         kept1, far1, (kept2, bt30, y, eg) = scatter(
@@ -974,9 +1058,9 @@
         z2, _ = settle(grid, joined(kept2, far2))
         w1 = joined(kept1, far1)
         dx_far = grid.swap_m(dx)
-        z1, (z20, a30, b30) = settle(grid, w1, (z2[0], a3[0], b3[0]))
         layer_output = both_sequences(y, y_far)
         encoded_gradient = both_sequences(eg, eg_far)
+        z1, (z20, a30, b30) = settle(grid, w1, (z2[0], a3[0], b3[0]))
         input_gradient = both_sequences(dx, dx_far)
         s3 = jnp.concatenate([summed([a30] + a3[1:]), summed([b30] + b3[1:])], axis=-1)
         s2 = summed([z20] + z2[1:])

time: 436 us -> 453 us (1.039)
  starting transfers between devices: 98.1 us -> 116 us
  local copies, waits for them, and re-layouts: 30.9 us -> 24.6 us
    ppermute x71 -> x78, starting transfers between devices: 98.1 us -> 116 us  [send(): return lax.ppermute(v, AXES, self.perm(move))]
    dynamic_update_slice x10, local copies, waits for them, and re-layouts: 4.9 us -> 0.19 us  [gather(): lax.dynamic_update_slice(own, got[d][None], (lax.rem(z - d + n, n), 0, 0))]
    ppermute x71 -> x78, waiting for transfers between devices: 196 us -> 200 us  [send(): return lax.ppermute(v, AXES, self.perm(move))]
    unnamed x102 -> x104, local copies, waits for them, and re-layouts: 17.8 us -> 15.4 us
  transfers between devices with their start and end apart: 71 -> 78, of which waited for: 29 -> 23; matrix products, arithmetic and copies ran while one was open for 5% -> 5% of each run, Pallas kernels for 9% -> 9%
where the time goes in v3:
time: 453 us; the launch traced here: 452 us
  waiting for transfers between devices  200 us (44%)
  starting transfers between devices  116 us (26%)
  Pallas kernels  96.2 us (21%)
  local copies, waits for them, and re-layouts  24.6 us (5%)
  other arithmetic  13 us (3%)
    ppermute x78, waiting for transfers between devices, send(): return lax.ppermute(v, AXES, self.perm(move))  200 us
    ppermute x78, starting transfers between devices, send(): return lax.ppermute(v, AXES, self.perm(move))  116 us
    pallas_call x8, Pallas kernels, call(): pl.pallas_call(body, out_shape=tuple((jax.ShapeDtypeStruct(s, d) for s, d...  96.2 us
    unnamed x104, local copies, waits for them, and re-layouts  15.4 us
  transfers between devices with their start and end apart: 78, of which 23 were waited for; matrix products, arithmetic and copies ran while one was open for 5% of the time, Pallas kernels for 9%

profile of v3, /device:TPU:0, one launch (start us, length us, event | category | flops | bytes accessed | tf_op | source)
XLA Modules:
  0.0 452.3 jit_solution(16265807612277231580)
XLA Ops:
  2.2 3.0 collective-permute-start.31
  10.5 4.1 collective-permute-start.14
  17.6 3.4 collective-permute-start.12
  21.1 3.3 collective-permute-done
  24.8 14.4 %collective-permute-done.1 = bf16[48,1280]{1,0:T(8,128)(2,1)S(1)} collective-permute-done((bf16[48,1280]{1,0:T(8,128)(2,1)S(1)}, bf16[48,1280]{1,0:T(8,128)(2,1)S(1)}, u32[]{:S(2)}, u32[]{:S(2)}) %collective-permute-start.1) | collective-permute-done | bytes 122912 | tf_op jit(solution)/shard_map/ppermute | solution.py:55
  39.2 10.9 %collective-permute-start.24 = (bf16[48,2560]{1,0:T(8,128)(2,1)S(1)}, bf16[48,2560]{1,0:T(8,128)(2,1)S(1)}, u32[]{:S(2)}, u32[]{:S(2)}) collective-permute-start(bf16[48,2560]{1,0:T(8,128)(2,1)S(1)} %pad_maximum_fusion.3), channel_id=1, source_target_pairs={{0,8},{1,9},{2,10},{3,11},{4,12},{5,13},{6,14},{7,15},{8,16},{9,17... | collective-permute-start | bytes 737288 | tf_op jit(solution)/shard_map/ppermute | solution.py:55
  53.4 8.2 %collective-permute-done.24 = bf16[48,2560]{1,0:T(8,128)(2,1)S(1)} collective-permute-done((bf16[48,2560]{1,0:T(8,128)(2,1)S(1)}, bf16[48,2560]{1,0:T(8,128)(2,1)S(1)}, u32[]{:S(2)}, u32[]{:S(2)}) %collective-permute-start.24) | collective-permute-done | bytes 245792 | tf_op jit(solution)/shard_map/ppermute | solution.py:55
  61.7 8.4 %collective-permute-start.33 = (bf16[2,2,48,512]{3,2,1,0:T(8,128)(2,1)S(1)}, bf16[2,2,48,512]{3,2,1,0:T(8,128)(2,1)S(1)}, u32[]{:S(2)}, u32[]{:S(2)}) collective-permute-start(bf16[2,2,48,512]{3,2,1,0:T(8,128)(2,1)S(1)} %bitcast.240), channel_id=1, source_target_pairs={{0,8},{1,9},{2,10},{3,11},{4,12},{5,13},{6,14},{7,15},{8,16},{9,17... | collective-permute-start | bytes 589832 | tf_op jit(solution)/shard_map/ppermute | solution.py:55
  71.7 9.3 %collective-permute-done.3.refs_3_.refs_10_ = bf16[4,48,1280]{2,1,0:T(8,128)(2,1)S(1)} collective-permute-done((bf16[4,48,1280]{2,1,0:T(8,128)(2,1)S(1)}, bf16[4,48,1280]{2,1,0:T(8,128)(2,1)S(1)}, u32[]{:S(2)}, u32[]{:S(2)}) %collective-permute-start.3) | collective-permute-done | bytes 491552 | tf_op jit(solution)/shard_map/ppermute | solution.py:55
  84.6 3.0 collective-permute-done.26
  92.5 14.1 %collective-permute-done.16.refs_6_.refs_9_.refs_7_ = bf16[4,48,1920]{2,1,0:T(8,128)(2,1)S(1)} collective-permute-done((bf16[4,48,1920]{2,1,0:T(8,128)(2,1)S(1)}, bf16[4,48,1920]{2,1,0:T(8,128)(2,1)S(1)}, u32[]{:S(2)}, u32[]{:S(2)}) %collective-permute-start.16) | collective-permute-done | bytes 737312 | tf_op jit(solution)/shard_map/ppermute | solution.py:55
  111.5 26.8 %collective-permute-done.17.refs_7_.refs_10_.refs_8_ = bf16[2,48,1920]{2,1,0:T(8,128)(2,1)S(1)} collective-permute-done((bf16[2,48,1920]{2,1,0:T(8,128)(2,1)S(1)}, bf16[2,48,1920]{2,1,0:T(8,128)(2,1)S(1)}, u32[]{:S(2)}, u32[]{:S(2)}) %collective-permute-start.17) | collective-permute-done | bytes 368672 | tf_op jit(solution)/shard_map/ppermute | solution.py:55
  142.2 11.5 %shard_map.322 = (bf16[512,768]{1,0:T(8,128)(2,1)S(1)}, bf16[3,512,768]{2,1,0:T(8,128)(2,1)S(1)}, bf16[512,768]{1,0:T(8,128)(2,1)S(1)}, f32[8,768]{1,0:T(8,128)S...) custom-call(bf16[1024,768]{1,0:T(8,128)(2,1)} %refs_0_.9, bf16[128,512]{1,0:T(8,128)(2,1)S(1)} %fusion.15.refs_1_.refs_7_, ...), custom_call_target="tpu_custom_call" | custom-call | flops 3000000000 | bytes 10000000 | tf_op jit(solution)/shard_map/pallas_call | solution.py:360
  154.6 14.9 %shard_map.323 = (f32[512,768]{1,0:T(8,128)S(1)}, f32[512,768]{1,0:T(8,128)S(1)}, bf16[512,768]{1,0:T(8,128)(2,1)S(1)}, bf16[3,512,768]{2,1,0:T(8,128)(2,1)S(1)}...) custom-call(bf16[1024,768]{1,0:T(8,128)(2,1)} %refs_0_.9, ...), custom_call_target="tpu_custom_call" | custom-call | flops 5000000000 | bytes 10000000 | tf_op jit(solution)/shard_map/pallas_call | solution.py:360
  171.4 13.7 %shard_map.324 = (bf16[2,4,48,3072]{3,2,1,0:T(8,128)(2,1)S(1)}, bf16[2,4,48,3072]{3,2,1,0:T(8,128)(2,1)S(1)}, f32[512,768]{1,0:T(8,128)S(1)}, f32[512,768]{1,0:T...) custom-call(bf16[1024,768]{1,0:T(8,128)(2,1)} %refs_0_.8, ...), custom_call_target="tpu_custom_call" | custom-call | flops 7500000256 | bytes 10000000 | tf_op jit(solution)/shard_map/pallas_call | solution.py:360
  189.4 13.5 %shard_map.325 = (bf16[2,4,48,3072]{3,2,1,0:T(8,128)(2,1)S(1)}, bf16[2,4,48,3072]{3,2,1,0:T(8,128)(2,1)S(1)}, bf16[512,768]{1,0:T(8,128)(2,1)S(1)}, f32[512,768]{1,0:T(8,128)S(1)}, f32[1,768]{1,0:T(1,128)S(1)}) custom-call(bf16[1024,768]{1,0:T(8,128)(2,1)} %refs_0_.8, bf16[512,768]{1,0:T(8,128)(2,1)S(1)} %get-tuple-element.67.refs_1_, ...), custom_call_target="tpu_custom_call" | custom-call | flops 7500000256 | bytes 10000000 | tf_op jit(solution)/shard_map/pallas_call | solution.py:360
  204.3 12.5 %shard_map.326.refs_3_ = bf16[3,512,768]{2,1,0:T(8,128)(2,1)S(1)} custom-call(f32[512,768]{1,0:T(8,128)S(1)} %get-tuple-element.74.refs_0_, bf16[3,512,768]{2,1,0:T(8,128)(2,1)S(1)} %get-tuple-element.77.refs_1_, bf16[512,768]{1,0:T(8,128)(2,1)S(1)} %get-tuple-element.78.refs_2_.refs_5_, f32[16,512]{1,0:T(8,128)S(1)} %get-tuple-element.79.refs_3_, ...), custom_call_target="tpu_custom_call" | custom-call | flops 3000000000 | bytes 10000000 | tf_op jit(solution)/shard_map/pallas_call | solution.py:360
  216.8 8.8 %shard_map.327 = (f32[512,768]{1,0:T(8,128)S(1)}, bf16[512,768]{1,0:T(8,128)(2,1)S(1)}, f32[1,768]{1,0:T(1,128)S(1)}, bf16[2,2,4,48,1920]{4,3,2,1,0:T(8,128)(2,1)S(1)}, bf16[2,2,4,48,1920]{4,3,2,1,0:T(8,128)(2,1)S(1)}) custom-call(f32[512,768]{1,0:T(8,128)S(1)} %get-tuple-element.74.refs_0_, f32[512,768]{1,0:T(8,128)S(1)} %get-tuple-element.75.refs_1_, ...), custom_call_target="tpu_custom_call" | custom-call | flops 5000000000 | bytes 10000000 | tf_op jit(solution)/shard_map/pallas_call | solution.py:360
  225.6 12.1 %shard_map.328 = (bf16[3,512,768]{2,1,0:T(8,128)(2,1)S(1)}, f32[16,512]{1,0:T(8,128)S(1)}) custom-call(f32[512,768]{1,0:T(8,128)S(1)} %get-tuple-element.80.refs_0_.refs_1_, bf16[3,512,768]{2,1,0:T(8,128)(2,1)S(1)} %get-tuple-element.81.refs_1_, bf16[512,768]{1,0:T(8,128)(2,1)S(1)} %get-tuple-element.65.refs_2_.refs_4_, ...), custom_call_target="tpu_custom_call" | custom-call | flops 3000000000 | bytes 10000000 | tf_op jit(solution)/shard_map/pallas_call | solution.py:360
  237.8 9.2 %shard_map.329 = (bf16[512,768]{1,0:T(8,128)(2,1)S(1)}, bf16[2,2,4,48,1280]{4,3,2,1,0:T(8,128)(2,1)S(1)}, bf16[2,2,4,48,1280]{4,3,2,1,0:T(8,128)(2,1)}) custom-call(bf16[1024,768]{1,0:T(8,128)(2,1)} %refs_0_.9, f32[512,768]{1,0:T(8,128)S(1)} %get-tuple-element.80.refs_0_.refs_1_, bf16[3,768,512]{2,1,0:T(8,128)(2,1)S(1)} %get-tuple-element.76.refs_2_, ...), custom_call_target="tpu_custom_call" | custom-call | flops 4000000000 | bytes 10000000 | tf_op jit(solution)/shard_map/pallas_call | solution.py:360
  253.6 32.8 %collective-permute-done.50 = bf16[512,768]{1,0:T(8,128)(2,1)S(1)} collective-permute-done((bf16[512,768]{1,0:T(8,128)(2,1)}, bf16[512,768]{1,0:T(8,128)(2,1)S(1)}, u32[]{:S(2)}, u32[]{:S(2)}) %collective-permute-start.50) | collective-permute-done | bytes 786464 | tf_op jit(solution)/shard_map/ppermute | solution.py:55
  287.9 1.9 maximum_convert_fusion.1
  290.9 1.6 slice_bitcast_fusion.4
  296.5 21.2 %collective-permute-done.59 = bf16[2,4,48,768]{3,2,1,0:T(8,128)(2,1)S(1)} collective-permute-done((bf16[2,4,48,768]{3,2,1,0:T(8,128)(2,1)S(1)}, bf16[2,4,48,768]{3,2,1,0:T(8,128)(2,1)S(1)}, u32[]{:S(2)}, u32[]{:S(2)}) %collective-permute-start.59) | collective-permute-done | bytes 589856 | tf_op jit(solution)/shard_map/ppermute | solution.py:55
  322.7 17.6 %collective-permute-done.48 = bf16[4,48,2304]{2,1,0:T(8,128)(2,1)S(1)} collective-permute-done((bf16[4,48,2304]{2,1,0:T(8,128)(2,1)S(1)}, bf16[4,48,2304]{2,1,0:T(8,128)(2,1)S(1)}, u32[]{:S(2)}, u32[]{:S(2)}) %collective-permute-start.48) | collective-permute-done | bytes 884768 | tf_op jit(solution)/shard_map/ppermute | solution.py:55
  341.4 5.1 %collective-permute-done.60 = bf16[4,48,768]{2,1,0:T(8,128)(2,1)S(1)} collective-permute-done((bf16[4,48,768]{2,1,0:T(8,128)(2,1)S(1)}, bf16[4,48,768]{2,1,0:T(8,128)(2,1)S(1)}, u32[]{:S(2)}, u32[]{:S(2)}) %collective-permute-start.60) | collective-permute-done | bytes 294944 | tf_op jit(solution)/shard_map/ppermute | solution.py:55
  346.6 2.5 collective-permute-start.71
  350.8 10.1 %collective-permute-done.46 = bf16[2,4,48,1024]{3,2,1,0:T(8,128)(2,1)S(1)} collective-permute-done((bf16[2,4,48,1024]{3,2,1,0:T(8,128)(2,1)S(1)}, bf16[2,4,48,1024]{3,2,1,0:T(8,128)(2,1)S(1)}, u32[]{:S(2)}, u32[]{:S(2)}) %collective-permute-start.46) | collective-permute-done | bytes 786464 | tf_op jit(solution)/shard_map/ppermute | solution.py:55
  360.9 2.5 collective-permute-start.74
  365.2 2.2 collective-permute-start.75
  367.5 3.6 collective-permute-done.74
  371.1 8.4 %collective-permute-start.68 = (bf16[48,768]{1,0:T(8,128)(2,1)S(1)}, bf16[48,768]{1,0:T(8,128)(2,1)S(1)}, u32[]{:S(2)}, u32[]{:S(2)}) collective-permute-start(bf16[48,768]{1,0:T(8,128)(2,1)S(1)} %get-tuple-element.156), channel_id=1, source_target_pairs={{0,8},{1,9},{2,10},{3,11},{4,12},{5,13},{6,14},{7,15},{8,16},{9,17... | collective-permute-start | bytes 221192 | tf_op jit(solution)/shard_map/ppermute | solution.py:55
  380.3 3.3 collective-permute-done.75
  385.2 1.9 maximum_convert_fusion
  387.1 1.9 maximum_convert_fusion.2
  389.6 5.9 %collective-permute-done.57 = bf16[4,48,1024]{2,1,0:T(8,128)(2,1)S(1)} collective-permute-done((bf16[4,48,1024]{2,1,0:T(8,128)(2,1)S(1)}, bf16[4,48,1024]{2,1,0:T(8,128)(2,1)S(1)}, u32[]{:S(2)}, u32[]{:S(2)}) %collective-permute-start.57) | collective-permute-done | bytes 393248 | tf_op jit(solution)/shard_map/ppermute | solution.py:55
  396.6 6.6 %collective-permute-done.52 = bf16[2,4,48,640]{3,2,1,0:T(8,128)(2,1)S(1)} collective-permute-done((bf16[2,4,48,640]{3,2,1,0:T(8,128)(2,1)S(1)}, bf16[2,4,48,640]{3,2,1,0:T(8,128)(2,1)S(1)}, u32[]{:S(2)}, u32[]{:S(2)}) %collective-permute-start.52) | collective-permute-done | bytes 491552 | tf_op jit(solution)/shard_map/ppermute | solution.py:55
  403.2 2.2 collective-permute-done.54
  408.2 3.8 collective-permute-done.53
  412.1 2.5 collective-permute-start.70
  414.9 3.0 collective-permute-start.72
  417.9 2.7 collective-permute-start.77
  420.6 1.6 collective-permute-done.69
  422.3 8.9 %collective-permute-start.67 = (bf16[48,1920]{1,0:T(8,128)(2,1)S(1)}, bf16[48,1920]{1,0:T(8,128)(2,1)S(1)}, u32[]{:S(2)}, u32[]{:S(2)}) collective-permute-start(bf16[48,1920]{1,0:T(8,128)(2,1)S(1)} %pad_maximum_fusion.9), channel_id=1, source_target_pairs={{0,24},{1,25},{2,26},{3,27},{4,28},{5,29},{6,30},{7,31},{8,0},{9,1... | collective-permute-start | bytes 552968 | tf_op jit(solution)/shard_map/ppermute | solution.py:55
  431.8 6.2 %collective-permute-start.62 = (bf16[48,1280]{1,0:T(8,128)(2,1)S(1)}, bf16[48,1280]{1,0:T(8,128)(2,1)S(1)}, u32[]{:S(2)}, u32[]{:S(2)}) collective-permute-start(bf16[48,1280]{1,0:T(8,128)(2,1)S(1)} %pad_maximum_fusion.10), channel_id=1, source_target_pairs={{0,8},{1,9},{2,10},{3,11},{4,12},{5,13},{6,14},{7,15},{8,16},{9,17... | collective-permute-start | bytes 368648 | tf_op jit(solution)/shard_map/ppermute | solution.py:55
  438.0 3.4 collective-permute-start.63
  442.4 2.4 collective-permute-start.64
  445.6 4.6 %collective-permute-done.63 = bf16[48,1280]{1,0:T(8,128)(2,1)S(1)} collective-permute-done((bf16[48,1280]{1,0:T(8,128)(2,1)S(1)}, bf16[48,1280]{1,0:T(8,128)(2,1)S(1)}, u32[]{:S(2)}, u32[]{:S(2)}) %collective-permute-start.63) | collective-permute-done | bytes 122912 | tf_op jit(solution)/shard_map/ppermute | solution.py:55
  (295 shorter events, 74.9 us)
Async XLA Ops:
  10.5 41.3 %collective-permute-start.14 = (bf16[48,1920]{1,0:T(8,128)(2,1)S(1)}, bf16[48,1920]{1,0:T(8,128)(2,1)S(1)}, u32[]{:S(2)}, u32[]{:S(2)}) collective-permute-start(bf16[48,1920]{1,0:T(8,128)(2,1)S(1)} %bitcast_dynamic-update-slice_fusion.12), channel_id=1, source_target_pairs={{0,24},{1,25},{2,26},{3,27},{4,28},{5,29},{6,30},{7,31},{8,0},{9,1... | collective-permute-start | bytes 552968 | tf_op jit(solution)/shard_map/ppermute | solution.py:55
  16.6 33.7 %collective-permute-start.13 = (bf16[48,1920]{1,0:T(8,128)(2,1)S(1)}, bf16[48,1920]{1,0:T(8,128)(2,1)S(1)}, u32[]{:S(2)}, u32[]{:S(2)}) collective-permute-start(bf16[48,1920]{1,0:T(8,128)(2,1)S(1)} %bitcast_dynamic-update-slice_fusion.12), channel_id=1, source_target_pairs={{0,16},{1,17},{2,18},{3,19},{4,20},{5,21},{6,22},{7,23},{8,24},{9,... | collective-permute-start | bytes 552968 | tf_op jit(solution)/shard_map/ppermute | solution.py:55
  17.6 32.5 %collective-permute-start.12 = (bf16[48,1920]{1,0:T(8,128)(2,1)S(1)}, bf16[48,1920]{1,0:T(8,128)(2,1)S(1)}, u32[]{:S(2)}, u32[]{:S(2)}) collective-permute-start(bf16[48,1920]{1,0:T(8,128)(2,1)S(1)} %bitcast_dynamic-update-slice_fusion.12), channel_id=1, source_target_pairs={{0,8},{1,9},{2,10},{3,11},{4,12},{5,13},{6,14},{7,15},{8,16},{9,17... | collective-permute-start | bytes 552968 | tf_op jit(solution)/shard_map/ppermute | solution.py:55
  21.0 18.2 %collective-permute-start.1 = (bf16[48,1280]{1,0:T(8,128)(2,1)S(1)}, bf16[48,1280]{1,0:T(8,128)(2,1)S(1)}, u32[]{:S(2)}, u32[]{:S(2)}) collective-permute-start(bf16[48,1280]{1,0:T(8,128)(2,1)S(1)} %get-tuple-element.116), channel_id=1, source_target_pairs={{0,16},{1,17},{2,18},{3,19},{4,20},{5,21},{6,22},{7,23},{8,24},{9,... | collective-permute-start | bytes 368648 | tf_op jit(solution)/shard_map/ppermute | solution.py:55
  39.2 43.9 %collective-permute-start.25 = (bf16[48,2560]{1,0:T(8,128)(2,1)S(1)}, bf16[48,2560]{1,0:T(8,128)(2,1)S(1)}, u32[]{:S(2)}, u32[]{:S(2)}) collective-permute-start(bf16[48,2560]{1,0:T(8,128)(2,1)S(1)} %pad_maximum_fusion.3), channel_id=1, source_target_pairs={{0,16},{1,17},{2,18},{3,19},{4,20},{5,21},{6,22},{7,23},{8,24},{9,... | collective-permute-start | bytes 737288 | tf_op jit(solution)/shard_map/ppermute | solution.py:55
  39.2 22.4 %collective-permute-start.24 = (bf16[48,2560]{1,0:T(8,128)(2,1)S(1)}, bf16[48,2560]{1,0:T(8,128)(2,1)S(1)}, u32[]{:S(2)}, u32[]{:S(2)}) collective-permute-start(bf16[48,2560]{1,0:T(8,128)(2,1)S(1)} %pad_maximum_fusion.3), channel_id=1, source_target_pairs={{0,8},{1,9},{2,10},{3,11},{4,12},{5,13},{6,14},{7,15},{8,16},{9,17... | collective-permute-start | bytes 737288 | tf_op jit(solution)/shard_map/ppermute | solution.py:55
  50.2 30.8 %collective-permute-start.35 = (bf16[2,2,48,512]{3,2,1,0:T(8,128)(2,1)S(1)}, bf16[2,2,48,512]{3,2,1,0:T(8,128)(2,1)S(1)}, u32[]{:S(2)}, u32[]{:S(2)}) collective-permute-start(bf16[2,2,48,512]{3,2,1,0:T(8,128)(2,1)S(1)} %bitcast.238), channel_id=1, source_target_pairs={{0,24},{1,25},{2,26},{3,27},{4,28},{5,29},{6,30},{7,31},{8,0},{9,1... | collective-permute-start | bytes 589832 | tf_op jit(solution)/shard_map/ppermute | solution.py:55
  50.3 19.8 %collective-permute-start.4 = (bf16[4,48,1280]{2,1,0:T(8,128)(2,1)S(1)}, bf16[4,48,1280]{2,1,0:T(8,128)(2,1)S(1)}, u32[]{:S(2)}, u32[]{:S(2)}) collective-permute-start(bf16[4,48,1280]{2,1,0:T(8,128)(2,1)S(1)} %bitcast_dynamic-update-slice_fusion.8.refs_2_.refs_9_), channel_id=1, source_target_pairs={{0,1},{1,0},{2,3},{3,2},{4,5},{5,4},{6,7},{7,6},{8,9},{9,8},{10,11... | collective-permute-start | bytes 1474568 | tf_op jit(solution)/shard_map/ppermute | solution.py:55
  51.9 29.2 %collective-permute-start.34 = (bf16[2,2,48,512]{3,2,1,0:T(8,128)(2,1)S(1)}, bf16[2,2,48,512]{3,2,1,0:T(8,128)(2,1)S(1)}, u32[]{:S(2)}, u32[]{:S(2)}) collective-permute-start(bf16[2,2,48,512]{3,2,1,0:T(8,128)(2,1)S(1)} %bitcast.239), channel_id=1, source_target_pairs={{0,16},{1,17},{2,18},{3,19},{4,20},{5,21},{6,22},{7,23},{8,24},{9,... | collective-permute-start | bytes 589832 | tf_op jit(solution)/shard_map/ppermute | solution.py:55
  61.7 19.9 %collective-permute-start.33 = (bf16[2,2,48,512]{3,2,1,0:T(8,128)(2,1)S(1)}, bf16[2,2,48,512]{3,2,1,0:T(8,128)(2,1)S(1)}, u32[]{:S(2)}, u32[]{:S(2)}) collective-permute-start(bf16[2,2,48,512]{3,2,1,0:T(8,128)(2,1)S(1)} %bitcast.240), channel_id=1, source_target_pairs={{0,8},{1,9},{2,10},{3,11},{4,12},{5,13},{6,14},{7,15},{8,16},{9,17... | collective-permute-start | bytes 589832 | tf_op jit(solution)/shard_map/ppermute | solution.py:55
  87.6 19.0 %collective-permute-start.16 = (bf16[4,48,1920]{2,1,0:T(8,128)(2,1)S(1)}, bf16[4,48,1920]{2,1,0:T(8,128)(2,1)S(1)}, u32[]{:S(2)}, u32[]{:S(2)}) collective-permute-start(bf16[4,48,1920]{2,1,0:T(8,128)(2,1)S(1)} %bitcast_dynamic-update-slice_fusion.4.refs_4_.refs_7_.refs_5_), channel_id=1, source_target_pairs={{0,1},{1,0},{2,3},{3,2},{4,5},{5,4},{6,7},{7,6},{8,9},{9,8},{10,11... | collective-permute-start | bytes 2211848 | tf_op jit(solution)/shard_map/ppermute | solution.py:55
  89.3 18.8 %collective-permute-start.15 = (bf16[4,48,1920]{2,1,0:T(8,128)(2,1)S(1)}, bf16[4,48,1920]{2,1,0:T(8,128)(2,1)S(1)}, u32[]{:S(2)}, u32[]{:S(2)}) collective-permute-start(bf16[4,48,1920]{2,1,0:T(8,128)(2,1)S(1)} %bitcast_dynamic-update-slice_fusion.4.refs_4_.refs_7_.refs_5_), channel_id=1, source_target_pairs={{0,4},{1,5},{2,6},{3,7},{4,0},{5,1},{6,2},{7,3},{8,12},{9,13},{10,... | collective-permute-start | bytes 2211848 | tf_op jit(solution)/shard_map/ppermute | solution.py:55
  90.9 17.7 %collective-permute-start.36 = (bf16[4,2,2,48,512]{4,3,2,1,0:T(8,128)(2,1)S(1)}, bf16[4,2,2,48,512]{4,3,2,1,0:T(8,128)(2,1)S(1)}, u32[]{:S(2)}, u32[]{:S(2)}) collective-permute-start(bf16[4,2,2,48,512]{4,3,2,1,0:T(8,128)(2,1)S(1)} %pad_maximum_fusion.refs_9_.refs_13_), channel_id=1, source_target_pairs={{0,2},{1,3},{2,0},{3,1},{4,6},{5,7},{6,4},{7,5},{8,10},{9,11},{10,... | collective-permute-start | bytes 2359304 | tf_op jit(solution)/shard_map/ppermute | solution.py:55
  92.0 16.7 %collective-permute-start.9 = (bf16[4,48,1280]{2,1,0:T(8,128)(2,1)S(1)}, bf16[4,48,1280]{2,1,0:T(8,128)(2,1)S(1)}, u32[]{:S(2)}, u32[]{:S(2)}) collective-permute-start(bf16[4,48,1280]{2,1,0:T(8,128)(2,1)S(1)} %collective-permute-done.4.refs_4_.refs_11_), channel_id=1, source_target_pairs={{0,2},{1,3},{2,0},{3,1},{4,6},{5,7},{6,4},{7,5},{8,10},{9,11},{10,... | collective-permute-start | bytes 1474568 | tf_op jit(solution)/shard_map/ppermute | solution.py:55
  92.0 17.2 %collective-permute-start.8 = (bf16[4,48,1280]{2,1,0:T(8,128)(2,1)S(1)}, bf16[4,48,1280]{2,1,0:T(8,128)(2,1)S(1)}, u32[]{:S(2)}, u32[]{:S(2)}) collective-permute-start(bf16[4,48,1280]{2,1,0:T(8,128)(2,1)S(1)} %collective-permute-done.3.refs_3_.refs_10_), channel_id=1, source_target_pairs={{0,2},{1,3},{2,0},{3,1},{4,6},{5,7},{6,4},{7,5},{8,10},{9,11},{10,... | collective-permute-start | bytes 1474568 | tf_op jit(solution)/shard_map/ppermute | solution.py:55
  106.6 31.7 %collective-permute-start.37 = (bf16[4,48,2560]{2,1,0:T(8,128)(2,1)S(1)}, bf16[4,48,2560]{2,1,0:T(8,128)(2,1)S(1)}, u32[]{:S(2)}, u32[]{:S(2)}) collective-permute-start(bf16[4,48,2560]{2,1,0:T(8,128)(2,1)S(1)} %bitcast_dynamic-update-slice_fusion.refs_5_), channel_id=1, source_target_pairs={{0,1},{1,0},{2,3},{3,2},{4,5},{5,4},{6,7},{7,6},{8,9},{9,8},{10,11... | collective-permute-start | bytes 2949128 | tf_op jit(solution)/shard_map/ppermute | solution.py:55
  108.1 30.8 %collective-permute-start.27 = (bf16[4,48,2560]{2,1,0:T(8,128)(2,1)S(1)}, bf16[4,48,2560]{2,1,0:T(8,128)(2,1)S(1)}, u32[]{:S(2)}, u32[]{:S(2)}) collective-permute-start(bf16[4,48,2560]{2,1,0:T(8,128)(2,1)S(1)} %bitcast_dynamic-update-slice_fusion.refs_5_), channel_id=1, source_target_pairs={{0,4},{1,5},{2,6},{3,7},{4,0},{5,1},{6,2},{7,3},{8,12},{9,13},{10,... | collective-permute-start | bytes 2949128 | tf_op jit(solution)/shard_map/ppermute | solution.py:55
  109.2 29.1 %collective-permute-start.17 = (bf16[2,48,1920]{2,1,0:T(8,128)(2,1)S(1)}, bf16[2,48,1920]{2,1,0:T(8,128)(2,1)S(1)}, u32[]{:S(2)}, u32[]{:S(2)}) collective-permute-start(bf16[2,48,1920]{2,1,0:T(8,128)(2,1)S(1)} %slice.627), channel_id=1, source_target_pairs={{0,4},{1,5},{2,6},{3,7},{4,0},{5,1},{6,2},{7,3},{8,12},{9,13},{10,... | collective-permute-start | bytes 1105928 | tf_op jit(solution)/shard_map/ppermute | solution.py:55
  110.8 29.5 %collective-permute-start.21 = (bf16[4,48,1920]{2,1,0:T(8,128)(2,1)S(1)}, bf16[4,48,1920]{2,1,0:T(8,128)(2,1)S(1)}, u32[]{:S(2)}, u32[]{:S(2)}) collective-permute-start(bf16[4,48,1920]{2,1,0:T(8,128)(2,1)S(1)} %collective-permute-done.16.refs_6_.refs_9_.refs_7_), channel_id=1, source_target_pairs={{0,2},{1,3},{2,0},{3,1},{4,6},{5,7},{6,4},{7,5},{8,10},{9,11},{10,... | collective-permute-start | bytes 2211848 | tf_op jit(solution)/shard_map/ppermute | solution.py:55
  110.9 27.9 %collective-permute-start.18 = (bf16[2,48,1920]{2,1,0:T(8,128)(2,1)S(1)}, bf16[2,48,1920]{2,1,0:T(8,128)(2,1)S(1)}, u32[]{:S(2)}, u32[]{:S(2)}) collective-permute-start(bf16[2,48,1920]{2,1,0:T(8,128)(2,1)S(1)} %slice.628), channel_id=1, source_target_pairs={{0,1},{1,0},{2,3},{3,2},{4,5},{5,4},{6,7},{7,6},{8,9},{9,8},{10,11... | collective-permute-start | bytes 1105928 | tf_op jit(solution)/shard_map/ppermute | solution.py:55
  138.9 31.2 %collective-permute-start.28 = (bf16[4,48,2560]{2,1,0:T(8,128)(2,1)S(1)}, bf16[4,48,2560]{2,1,0:T(8,128)(2,1)S(1)}, u32[]{:S(2)}, u32[]{:S(2)}) collective-permute-start(bf16[4,48,2560]{2,1,0:T(8,128)(2,1)S(1)} %bitcast_dynamic-update-slice_fusion.refs_5_), channel_id=1, source_target_pairs={{0,2},{1,3},{2,0},{3,1},{4,6},{5,7},{6,4},{7,5},{8,10},{9,11},{10,... | collective-permute-start | bytes 2949128 | tf_op jit(solution)/shard_map/ppermute | solution.py:55
  140.0 30.1 %collective-permute-start.29 = (bf16[4,48,2560]{2,1,0:T(8,128)(2,1)S(1)}, bf16[4,48,2560]{2,1,0:T(8,128)(2,1)S(1)}, u32[]{:S(2)}, u32[]{:S(2)}) collective-permute-start(bf16[4,48,2560]{2,1,0:T(8,128)(2,1)S(1)} %collective-permute-done.27.refs_6_), channel_id=1, source_target_pairs={{0,2},{1,3},{2,0},{3,1},{4,6},{5,7},{6,4},{7,5},{8,10},{9,11},{10,... | collective-permute-start | bytes 2949128 | tf_op jit(solution)/shard_map/ppermute | solution.py:55
  140.3 29.2 %collective-permute-start.38 = (bf16[2,48,2560]{2,1,0:T(8,128)(2,1)S(1)}, bf16[2,48,2560]{2,1,0:T(8,128)(2,1)S(1)}, u32[]{:S(2)}, u32[]{:S(2)}) collective-permute-start(bf16[2,48,2560]{2,1,0:T(8,128)(2,1)S(1)} %slice.631), channel_id=1, source_target_pairs={{0,4},{1,5},{2,6},{3,7},{4,0},{5,1},{6,2},{7,3},{8,12},{9,13},{10,... | collective-permute-start | bytes 1474568 | tf_op jit(solution)/shard_map/ppermute | solution.py:55
  141.6 28.0 %collective-permute-start.39 = (bf16[2,48,2560]{2,1,0:T(8,128)(2,1)S(1)}, bf16[2,48,2560]{2,1,0:T(8,128)(2,1)S(1)}, u32[]{:S(2)}, u32[]{:S(2)}) collective-permute-start(bf16[2,48,2560]{2,1,0:T(8,128)(2,1)S(1)} %slice.632), channel_id=1, source_target_pairs={{0,1},{1,0},{2,3},{3,2},{4,5},{5,4},{6,7},{7,6},{8,9},{9,8},{10,11... | collective-permute-start | bytes 1474568 | tf_op jit(solution)/shard_map/ppermute | solution.py:55
  153.8 34.4 %collective-permute-start.40 = (bf16[4,48,2560]{2,1,0:T(8,128)(2,1)S(1)}, bf16[4,48,2560]{2,1,0:T(8,128)(2,1)S(1)}, u32[]{:S(2)}, u32[]{:S(2)}) collective-permute-start(bf16[4,48,2560]{2,1,0:T(8,128)(2,1)S(1)} %collective-permute-done.37.refs_7_), channel_id=1, source_target_pairs={{0,2},{1,3},{2,0},{3,1},{4,6},{5,7},{6,4},{7,5},{8,10},{9,11},{10,... | collective-permute-start | bytes 2949128 | tf_op jit(solution)/shard_map/ppermute | solution.py:55
  169.6 18.6 %collective-permute-start.41 = (bf16[2,48,2560]{2,1,0:T(8,128)(2,1)S(1)}, bf16[2,48,2560]{2,1,0:T(8,128)(2,1)S(1)}, u32[]{:S(2)}, u32[]{:S(2)}) collective-permute-start(bf16[2,48,2560]{2,1,0:T(8,128)(2,1)S(1)} %collective-permute-done.38.refs_8_), channel_id=1, source_target_pairs={{0,2},{1,3},{2,0},{3,1},{4,6},{5,7},{6,4},{7,5},{8,10},{9,11},{10,... | collective-permute-start | bytes 1474568 | tf_op jit(solution)/shard_map/ppermute | solution.py:55
  169.7 18.5 %collective-permute-start.42 = (bf16[2,48,2560]{2,1,0:T(8,128)(2,1)S(1)}, bf16[2,48,2560]{2,1,0:T(8,128)(2,1)S(1)}, u32[]{:S(2)}, u32[]{:S(2)}) collective-permute-start(bf16[2,48,2560]{2,1,0:T(8,128)(2,1)S(1)} %collective-permute-done.39.refs_9_), channel_id=1, source_target_pairs={{0,2},{1,3},{2,0},{3,1},{4,6},{5,7},{6,4},{7,5},{8,10},{9,11},{10,... | collective-permute-start | bytes 1474568 | tf_op jit(solution)/shard_map/ppermute | solution.py:55
  249.2 40.6 %collective-permute-start.43 = (bf16[2,2,4,48,1280]{4,3,2,1,0:T(8,128)(2,1)}, bf16[2,2,4,48,1280]{4,3,2,1,0:T(8,128)(2,1)}, u32[]{:S(2)}, u32[]{:S(2)}) collective-permute-start(bf16[2,2,4,48,1280]{4,3,2,1,0:T(8,128)(2,1)} %get-tuple-element.89), channel_id=1, source_target_pairs={{0,2},{1,3},{2,0},{3,1},{4,6},{5,7},{6,4},{7,5},{8,10},{9,11},{10,... | collective-permute-start | bytes 5898248 | tf_op jit(solution)/shard_map/ppermute | solution.py:55
  249.3 43.5 %collective-permute-start.58 = (bf16[2,4,48,3072]{3,2,1,0:T(8,128)(2,1)}, bf16[2,4,48,3072]{3,2,1,0:T(8,128)(2,1)S(1)}, u32[]{:S(2)}, u32[]{:S(2)}) collective-permute-start(bf16[2,4,48,3072]{3,2,1,0:T(8,128)(2,1)} %copy-done.13), channel_id=1, source_target_pairs={{0,2},{1,3},{2,0},{3,1},{4,6},{5,7},{6,4},{7,5},{8,10},{9,11},{10,... | collective-permute-start | bytes 7077896 | tf_op jit(solution)/shard_map/ppermute | solution.py:55
  249.7 114.0 %collective-permute-start.49 = (bf16[512,768]{1,0:T(8,128)(2,1)}, bf16[512,768]{1,0:T(8,128)(2,1)S(1)}, u32[]{:S(2)}, u32[]{:S(2)}) collective-permute-start(bf16[512,768]{1,0:T(8,128)(2,1)} %copy-done.5), channel_id=1, source_target_pairs={{0,1},{1,0},{2,3},{3,2},{4,5},{5,4},{6,7},{7,6},{8,9},{9,8},{10,11... | collective-permute-start | bytes 2359304 | tf_op jit(solution)/shard_map/ppermute | solution.py:55
  251.1 44.2 %collective-permute-start.47 = (bf16[2,4,48,3072]{3,2,1,0:T(8,128)(2,1)}, bf16[2,4,48,3072]{3,2,1,0:T(8,128)(2,1)S(1)}, u32[]{:S(2)}, u32[]{:S(2)}) collective-permute-start(bf16[2,4,48,3072]{3,2,1,0:T(8,128)(2,1)} %copy-done.14), channel_id=1, source_target_pairs={{0,2},{1,3},{2,0},{3,1},{4,6},{5,7},{6,4},{7,5},{8,10},{9,11},{10,... | collective-permute-start | bytes 7077896 | tf_op jit(solution)/shard_map/ppermute | solution.py:55
  251.1 35.2 %collective-permute-start.50 = (bf16[512,768]{1,0:T(8,128)(2,1)}, bf16[512,768]{1,0:T(8,128)(2,1)S(1)}, u32[]{:S(2)}, u32[]{:S(2)}) collective-permute-start(bf16[512,768]{1,0:T(8,128)(2,1)} %copy-done.9), channel_id=1, source_target_pairs={{0,1},{1,0},{2,3},{3,2},{4,5},{5,4},{6,7},{7,6},{8,9},{9,8},{10,11... | collective-permute-start | bytes 2359304 | tf_op jit(solution)/shard_map/ppermute | solution.py:55
  286.3 78.9 %collective-permute-start.51 = (bf16[512,768]{1,0:T(8,128)(2,1)S(1)}, bf16[512,768]{1,0:T(8,128)(2,1)S(1)}, u32[]{:S(2)}, u32[]{:S(2)}) collective-permute-start(bf16[512,768]{1,0:T(8,128)(2,1)S(1)} %copy-done.8), channel_id=1, source_target_pairs={{0,1},{1,0},{2,3},{3,2},{4,5},{5,4},{6,7},{7,6},{8,9},{9,8},{10,11... | collective-permute-start | bytes 2359304 | tf_op jit(solution)/shard_map/ppermute | solution.py:55
  290.9 28.0 %collective-permute-start.44 = (bf16[2,2,4,48,1920]{4,3,2,1,0:T(8,128)(2,1)S(1)}, bf16[2,2,4,48,1920]{4,3,2,1,0:T(8,128)(2,1)S(1)}, u32[]{:S(2)}, u32[]{:S(2)}) collective-permute-start(bf16[2,2,4,48,1920]{4,3,2,1,0:T(8,128)(2,1)S(1)} %copy-done.12), channel_id=1, source_target_pairs={{0,2},{1,3},{2,0},{3,1},{4,6},{5,7},{6,4},{7,5},{8,10},{9,11},{10,... | collective-permute-start | bytes 8847368 | tf_op jit(solution)/shard_map/ppermute | solution.py:55
  294.4 26.4 %collective-permute-start.61 = (bf16[4,48,2304]{2,1,0:T(8,128)(2,1)S(1)}, bf16[4,48,2304]{2,1,0:T(8,128)(2,1)S(1)}, u32[]{:S(2)}, u32[]{:S(2)}) collective-permute-start(bf16[4,48,2304]{2,1,0:T(8,128)(2,1)S(1)} %fusion.1), channel_id=1, source_target_pairs={{0,4},{1,5},{2,6},{3,7},{4,0},{5,1},{6,2},{7,3},{8,12},{9,13},{10,... | collective-permute-start | bytes 2654216 | tf_op jit(solution)/shard_map/ppermute | solution.py:55
  295.6 22.2 %collective-permute-start.59 = (bf16[2,4,48,768]{3,2,1,0:T(8,128)(2,1)S(1)}, bf16[2,4,48,768]{3,2,1,0:T(8,128)(2,1)S(1)}, u32[]{:S(2)}, u32[]{:S(2)}) collective-permute-start(bf16[2,4,48,768]{3,2,1,0:T(8,128)(2,1)S(1)} %add_convert_fusion.3), channel_id=1, source_target_pairs={{0,1},{1,0},{2,3},{3,2},{4,5},{5,4},{6,7},{7,6},{8,9},{9,8},{10,11... | collective-permute-start | bytes 1769480 | tf_op jit(solution)/shard_map/ppermute | solution.py:55
  317.7 22.5 %collective-permute-start.48 = (bf16[4,48,2304]{2,1,0:T(8,128)(2,1)S(1)}, bf16[4,48,2304]{2,1,0:T(8,128)(2,1)S(1)}, u32[]{:S(2)}, u32[]{:S(2)}) collective-permute-start(bf16[4,48,2304]{2,1,0:T(8,128)(2,1)S(1)} %fusion), channel_id=1, source_target_pairs={{0,4},{1,5},{2,6},{3,7},{4,0},{5,1},{6,2},{7,3},{8,12},{9,13},{10,... | collective-permute-start | bytes 2654216 | tf_op jit(solution)/shard_map/ppermute | solution.py:55
  318.8 27.7 %collective-permute-start.60 = (bf16[4,48,768]{2,1,0:T(8,128)(2,1)S(1)}, bf16[4,48,768]{2,1,0:T(8,128)(2,1)S(1)}, u32[]{:S(2)}, u32[]{:S(2)}) collective-permute-start(bf16[4,48,768]{2,1,0:T(8,128)(2,1)S(1)} %get-tuple-element.126), channel_id=1, source_target_pairs={{0,4},{1,5},{2,6},{3,7},{4,0},{5,1},{6,2},{7,3},{8,12},{9,13},{10,... | collective-permute-start | bytes 884744 | tf_op jit(solution)/shard_map/ppermute | solution.py:55
  320.8 28.3 %collective-permute-start.45 = (bf16[2,4,48,896]{3,2,1,0:T(8,128)(2,1)S(1)}, bf16[2,4,48,896]{3,2,1,0:T(8,128)(2,1)S(1)}, u32[]{:S(2)}, u32[]{:S(2)}) collective-permute-start(bf16[2,4,48,896]{3,2,1,0:T(8,128)(2,1)S(1)} %add_convert_fusion.2), channel_id=1, source_target_pairs={{0,1},{1,0},{2,3},{3,2},{4,5},{5,4},{6,7},{7,6},{8,9},{9,8},{10,11... | collective-permute-start | bytes 2064392 | tf_op jit(solution)/shard_map/ppermute | solution.py:55
  340.2 20.6 %collective-permute-start.46 = (bf16[2,4,48,1024]{3,2,1,0:T(8,128)(2,1)S(1)}, bf16[2,4,48,1024]{3,2,1,0:T(8,128)(2,1)S(1)}, u32[]{:S(2)}, u32[]{:S(2)}) collective-permute-start(bf16[2,4,48,1024]{3,2,1,0:T(8,128)(2,1)S(1)} %pad_maximum_fusion.1), channel_id=1, source_target_pairs={{0,4},{1,5},{2,6},{3,7},{4,0},{5,1},{6,2},{7,3},{8,12},{9,13},{10,... | collective-permute-start | bytes 2359304 | tf_op jit(solution)/shard_map/ppermute | solution.py:55
  346.6 75.7 %collective-permute-start.71 = (bf16[48,2304]{1,0:T(8,128)(2,1)S(1)}, bf16[48,2304]{1,0:T(8,128)(2,1)S(1)}, u32[]{:S(2)}, u32[]{:S(2)}) collective-permute-start(bf16[48,2304]{1,0:T(8,128)(2,1)S(1)} %get-tuple-element.117), channel_id=1, source_target_pairs={{0,8},{1,9},{2,10},{3,11},{4,12},{5,13},{6,14},{7,15},{8,16},{9,17... | collective-permute-start | bytes 663560 | tf_op jit(solution)/shard_map/ppermute | solution.py:55
  349.1 82.0 %collective-permute-start.73 = (bf16[48,2304]{1,0:T(8,128)(2,1)S(1)}, bf16[48,2304]{1,0:T(8,128)(2,1)S(1)}, u32[]{:S(2)}, u32[]{:S(2)}) collective-permute-start(bf16[48,2304]{1,0:T(8,128)(2,1)S(1)} %get-tuple-element.118), channel_id=1, source_target_pairs={{0,24},{1,25},{2,26},{3,27},{4,28},{5,29},{6,30},{7,31},{8,0},{9,1... | collective-permute-start | bytes 663560 | tf_op jit(solution)/shard_map/ppermute | solution.py:55
  365.2 18.4 %collective-permute-start.75 = (bf16[48,2304]{1,0:T(8,128)(2,1)S(1)}, bf16[48,2304]{1,0:T(8,128)(2,1)S(1)}, u32[]{:S(2)}, u32[]{:S(2)}) collective-permute-start(bf16[48,2304]{1,0:T(8,128)(2,1)S(1)} %get-tuple-element.123), channel_id=1, source_target_pairs={{0,16},{1,17},{2,18},{3,19},{4,20},{5,21},{6,22},{7,23},{8,24},{9,... | collective-permute-start | bytes 663560 | tf_op jit(solution)/shard_map/ppermute | solution.py:55
  371.1 43.8 %collective-permute-start.68 = (bf16[48,768]{1,0:T(8,128)(2,1)S(1)}, bf16[48,768]{1,0:T(8,128)(2,1)S(1)}, u32[]{:S(2)}, u32[]{:S(2)}) collective-permute-start(bf16[48,768]{1,0:T(8,128)(2,1)S(1)} %get-tuple-element.156), channel_id=1, source_target_pairs={{0,8},{1,9},{2,10},{3,11},{4,12},{5,13},{6,14},{7,15},{8,16},{9,17... | collective-permute-start | bytes 221192 | tf_op jit(solution)/shard_map/ppermute | solution.py:55
  414.9 16.9 %collective-permute-start.72 = (bf16[48,2304]{1,0:T(8,128)(2,1)S(1)}, bf16[48,2304]{1,0:T(8,128)(2,1)S(1)}, u32[]{:S(2)}, u32[]{:S(2)}) collective-permute-start(bf16[48,2304]{1,0:T(8,128)(2,1)S(1)} %get-tuple-element.119), channel_id=1, source_target_pairs={{0,16},{1,17},{2,18},{3,19},{4,20},{5,21},{6,22},{7,23},{8,24},{9,... | collective-permute-start | bytes 663560 | tf_op jit(solution)/shard_map/ppermute | solution.py:55
  417.9 20.2 %collective-permute-start.77 = (bf16[48,2304]{1,0:T(8,128)(2,1)S(1)}, bf16[48,2304]{1,0:T(8,128)(2,1)S(1)}, u32[]{:S(2)}, u32[]{:S(2)}) collective-permute-start(bf16[48,2304]{1,0:T(8,128)(2,1)S(1)} %add_convert_fusion.19), channel_id=1, source_target_pairs={{0,1},{1,0},{2,3},{3,2},{4,5},{5,4},{6,7},{7,6},{8,9},{9,8},{10,11... | collective-permute-start | bytes 663560 | tf_op jit(solution)/shard_map/ppermute | solution.py:55
  422.2 20.2 %collective-permute-start.66 = (bf16[48,1920]{1,0:T(8,128)(2,1)S(1)}, bf16[48,1920]{1,0:T(8,128)(2,1)S(1)}, u32[]{:S(2)}, u32[]{:S(2)}) collective-permute-start(bf16[48,1920]{1,0:T(8,128)(2,1)S(1)} %pad_maximum_fusion.8), channel_id=1, source_target_pairs={{0,16},{1,17},{2,18},{3,19},{4,20},{5,21},{6,22},{7,23},{8,24},{9,... | collective-permute-start | bytes 552968 | tf_op jit(solution)/shard_map/ppermute | solution.py:55
  422.3 22.5 %collective-permute-start.67 = (bf16[48,1920]{1,0:T(8,128)(2,1)S(1)}, bf16[48,1920]{1,0:T(8,128)(2,1)S(1)}, u32[]{:S(2)}, u32[]{:S(2)}) collective-permute-start(bf16[48,1920]{1,0:T(8,128)(2,1)S(1)} %pad_maximum_fusion.9), channel_id=1, source_target_pairs={{0,24},{1,25},{2,26},{3,27},{4,28},{5,29},{6,30},{7,31},{8,0},{9,1... | collective-permute-start | bytes 552968 | tf_op jit(solution)/shard_map/ppermute | solution.py:55
  (80 other events, 1372.3 us)

commit v4 on v3

--- a/solution.py
+++ b/solution.py
@@ -19,7 +19,7 @@
 F32 = jnp.float32
 BF16 = jnp.bfloat16
 MIB = 1024 * 1024
-VMEM_LIMIT = {"ka": 13, "kb": 16, "kca": 23, "kcb": 25, "kd1": 12, "kd2": 22, "ke1": 12, "ke2": 16}
+VMEM_LIMIT = {"ka": 11, "kb": 14, "kca": 20, "kcb": 20, "kd1": 10, "kd2": 20, "ke1": 10, "ke2": 13}
 
 
 def nn(left, right):
@@ -912,7 +912,7 @@
     return (left.astype(F32) + right.astype(F32)).astype(BF16)
 
 
-def scatter(grid, own, own_got, other, other_got, first, held=None):
+def scatter(grid, own, own_got, other, other_got, first, held=None, later=None):
     sent_a = added(other[..., :first], other_got[..., :first])
     sent_b = jnp.stack([added(v[1, ..., first:], g[1, ..., first:]) for v, g in ((own, own_got), (other, other_got))])
     if held is not None:
@@ -923,10 +923,13 @@
     def a_sum(i):
         return added3(own[i, ..., :first], own_got[i, ..., :first], got[i])
 
-    far_a = grid.swap_y(a_sum(1))
-    far_b = grid.swap_m(added3(other[0, ..., first:], other_got[0, ..., first:], got_b[1]))
+    sent_a, sent_b = a_sum(1), added3(other[0, ..., first:], other_got[0, ..., first:], got_b[1])
+    if later is not None:
+        sent_a, sent_b, later = lax.optimization_barrier((sent_a, sent_b, later))
+    far_a = grid.swap_y(sent_a)
+    far_b = grid.swap_m(sent_b)
     wa, wb = a_sum(0), added3(own[0, ..., first:], own_got[0, ..., first:], got_b[0])
-    return (wa, wb), (far_a, far_b), held
+    return (wa, wb), (far_a, far_b), held, later
 
 
 def joined(kept, far):
@@ -1045,14 +1048,14 @@
         )
         eg_far = grid.swap_m(eg)
         got = grid.swap_c(gone)
-        kept2, far2, _ = scatter(grid, kept[0], got[0], kept[1], got[1], 7 * LANE)
+        kept2, far2, _, _ = scatter(grid, kept[0], got[0], kept[1], got[1], 7 * LANE)
         dy, off = attention_backward(grid, b1, qkv1, at1, lse1, base, pieces_two, 0, hd, "ke1")
         dx, (kept, gone) = self_finish(
             grid, inputs, b1, turned_others, dy, off, dg2, dg3, base_hot, gains, pieces_one, d, hd, heads
         )
         got = grid.swap_c(gone)
-        kept1, far1, (kept2, bt30, y, eg) = scatter(
-            grid, kept[0], got[0], kept[1], got[1], 5 * LANE, (kept2, bt3[0], y, eg)
+        kept1, far1, (kept2, bt30), (y, eg) = scatter(
+            grid, kept[0], got[0], kept[1], got[1], 5 * LANE, (kept2, bt3[0]), (y, eg)
         )
         b3 = bo3 + [grid.swap_m(summed([bt30] + bt3[1:]).astype(BF16))]
         z2, _ = settle(grid, joined(kept2, far2))

time: 453 us -> 451 us (level)
  starting transfers between devices: 116 us -> 93.9 us
  waiting for transfers between devices: 200 us -> 220 us
    ppermute x78, starting transfers between devices: 116 us -> 93.9 us  [send(): return lax.ppermute(v, AXES, self.perm(move))]
    ppermute x78, waiting for transfers between devices: 200 us -> 220 us  [send(): return lax.ppermute(v, AXES, self.perm(move))]
  transfers between devices with their start and end apart: 78 -> 78, of which waited for: 23 -> 24; matrix products, arithmetic and copies ran while one was open for 5% -> 5% of each run, Pallas kernels for 9% -> 9%
where the time goes in v4:
time: 451 us; the launch traced here: 450 us
  waiting for transfers between devices  220 us (49%)
  Pallas kernels  95.1 us (21%)
  starting transfers between devices  93.9 us (21%)
  local copies, waits for them, and re-layouts  26.1 us (6%)
  other arithmetic  13 us (3%)
    ppermute x78, waiting for transfers between devices, send(): return lax.ppermute(v, AXES, self.perm(move))  220 us
    pallas_call x8, Pallas kernels, call(): pl.pallas_call(body, out_shape=tuple((jax.ShapeDtypeStruct(s, d) for s, d...  95.1 us
    ppermute x78, starting transfers between devices, send(): return lax.ppermute(v, AXES, self.perm(move))  93.9 us
    unnamed x104, local copies, waits for them, and re-layouts  16.9 us
  transfers between devices with their start and end apart: 78, of which 24 were waited for; matrix products, arithmetic and copies ran while one was open for 5% of the time, Pallas kernels for 9%

profile of v4, /device:TPU:0, one launch (start us, length us, event | category | flops | bytes accessed | tf_op | source)
XLA Modules:
  0.0 450.2 jit_solution(6143914372049306241)
XLA Ops:
  2.2 3.0 collective-permute-start.31
  10.5 4.1 collective-permute-start.14
  17.6 3.4 collective-permute-start.12
  21.1 3.3 collective-permute-done
  24.8 14.4 %collective-permute-done.1 = bf16[48,1280]{1,0:T(8,128)(2,1)S(1)} collective-permute-done((bf16[48,1280]{1,0:T(8,128)(2,1)S(1)}, bf16[48,1280]{1,0:T(8,128)(2,1)S(1)}, u32[]{:S(2)}, u32[]{:S(2)}) %collective-permute-start.1) | collective-permute-done | bytes 122912 | tf_op jit(solution)/shard_map/ppermute | solution.py:55
  39.2 10.9 %collective-permute-start.24 = (bf16[48,2560]{1,0:T(8,128)(2,1)S(1)}, bf16[48,2560]{1,0:T(8,128)(2,1)S(1)}, u32[]{:S(2)}, u32[]{:S(2)}) collective-permute-start(bf16[48,2560]{1,0:T(8,128)(2,1)S(1)} %pad_maximum_fusion.3), channel_id=1, source_target_pairs={{0,8},{1,9},{2,10},{3,11},{4,12},{5,13},{6,14},{7,15},{8,16},{9,17... | collective-permute-start | bytes 737288 | tf_op jit(solution)/shard_map/ppermute | solution.py:55
  50.3 1.6 collective-permute-start.4
  51.9 1.5 collective-permute-start.34
  53.4 8.2 %collective-permute-done.24 = bf16[48,2560]{1,0:T(8,128)(2,1)S(1)} collective-permute-done((bf16[48,2560]{1,0:T(8,128)(2,1)S(1)}, bf16[48,2560]{1,0:T(8,128)(2,1)S(1)}, u32[]{:S(2)}, u32[]{:S(2)}) %collective-permute-start.24) | collective-permute-done | bytes 245792 | tf_op jit(solution)/shard_map/ppermute | solution.py:55
  61.7 8.4 %collective-permute-start.33 = (bf16[2,2,48,512]{3,2,1,0:T(8,128)(2,1)S(1)}, bf16[2,2,48,512]{3,2,1,0:T(8,128)(2,1)S(1)}, u32[]{:S(2)}, u32[]{:S(2)}) collective-permute-start(bf16[2,2,48,512]{3,2,1,0:T(8,128)(2,1)S(1)} %bitcast.240), channel_id=1, source_target_pairs={{0,8},{1,9},{2,10},{3,11},{4,12},{5,13},{6,14},{7,15},{8,16},{9,17... | collective-permute-start | bytes 589832 | tf_op jit(solution)/shard_map/ppermute | solution.py:55
  70.1 1.5 collective-permute-start.3
  71.7 9.3 %collective-permute-done.3.refs_3_.refs_10_ = bf16[4,48,1280]{2,1,0:T(8,128)(2,1)S(1)} collective-permute-done((bf16[4,48,1280]{2,1,0:T(8,128)(2,1)S(1)}, bf16[4,48,1280]{2,1,0:T(8,128)(2,1)S(1)}, u32[]{:S(2)}, u32[]{:S(2)}) %collective-permute-start.3) | collective-permute-done | bytes 491552 | tf_op jit(solution)/shard_map/ppermute | solution.py:55
  84.6 3.0 collective-permute-done.26
  89.3 1.6 collective-permute-start.15
  92.5 14.1 %collective-permute-done.16.refs_6_.refs_9_.refs_7_ = bf16[4,48,1920]{2,1,0:T(8,128)(2,1)S(1)} collective-permute-done((bf16[4,48,1920]{2,1,0:T(8,128)(2,1)S(1)}, bf16[4,48,1920]{2,1,0:T(8,128)(2,1)S(1)}, u32[]{:S(2)}, u32[]{:S(2)}) %collective-permute-start.16) | collective-permute-done | bytes 737312 | tf_op jit(solution)/shard_map/ppermute | solution.py:55
  109.2 1.6 collective-permute-start.17
  111.5 26.8 %collective-permute-done.17.refs_7_.refs_10_.refs_8_ = bf16[2,48,1920]{2,1,0:T(8,128)(2,1)S(1)} collective-permute-done((bf16[2,48,1920]{2,1,0:T(8,128)(2,1)S(1)}, bf16[2,48,1920]{2,1,0:T(8,128)(2,1)S(1)}, u32[]{:S(2)}, u32[]{:S(2)}) %collective-permute-start.17) | collective-permute-done | bytes 368672 | tf_op jit(solution)/shard_map/ppermute | solution.py:55
  142.2 11.5 %shard_map.322 = (bf16[512,768]{1,0:T(8,128)(2,1)S(1)}, bf16[3,512,768]{2,1,0:T(8,128)(2,1)S(1)}, bf16[512,768]{1,0:T(8,128)(2,1)S(1)}, f32[8,768]{1,0:T(8,128)S...) custom-call(bf16[1024,768]{1,0:T(8,128)(2,1)} %refs_0_.9, bf16[128,512]{1,0:T(8,128)(2,1)S(1)} %fusion.15.refs_1_.refs_7_, ...), custom_call_target="tpu_custom_call" | custom-call | flops 3000000000 | bytes 10000000 | tf_op jit(solution)/shard_map/pallas_call | solution.py:360
  154.6 14.9 %shard_map.323 = (f32[512,768]{1,0:T(8,128)S(1)}, f32[512,768]{1,0:T(8,128)S(1)}, bf16[512,768]{1,0:T(8,128)(2,1)S(1)}, bf16[3,512,768]{2,1,0:T(8,128)(2,1)S(1)}...) custom-call(bf16[1024,768]{1,0:T(8,128)(2,1)} %refs_0_.9, ...), custom_call_target="tpu_custom_call" | custom-call | flops 5000000000 | bytes 10000000 | tf_op jit(solution)/shard_map/pallas_call | solution.py:360
  171.4 13.5 %shard_map.324 = (bf16[2,4,48,3072]{3,2,1,0:T(8,128)(2,1)S(1)}, bf16[2,4,48,3072]{3,2,1,0:T(8,128)(2,1)S(1)}, f32[512,768]{1,0:T(8,128)S(1)}, f32[512,768]{1,0:T...) custom-call(bf16[1024,768]{1,0:T(8,128)(2,1)} %refs_0_.8, ...), custom_call_target="tpu_custom_call" | custom-call | flops 7500000256 | bytes 10000000 | tf_op jit(solution)/shard_map/pallas_call | solution.py:360
  189.1 13.5 %shard_map.325 = (bf16[2,4,48,3072]{3,2,1,0:T(8,128)(2,1)S(1)}, bf16[2,4,48,3072]{3,2,1,0:T(8,128)(2,1)S(1)}, bf16[512,768]{1,0:T(8,128)(2,1)S(1)}, f32[512,768]{1,0:T(8,128)S(1)}, f32[1,768]{1,0:T(1,128)S(1)}) custom-call(bf16[1024,768]{1,0:T(8,128)(2,1)} %refs_0_.8, bf16[512,768]{1,0:T(8,128)(2,1)S(1)} %get-tuple-element.69.refs_1_, ...), custom_call_target="tpu_custom_call" | custom-call | flops 7500000256 | bytes 10000000 | tf_op jit(solution)/shard_map/pallas_call | solution.py:360
  205.5 11.6 %shard_map.326.refs_3_ = bf16[3,512,768]{2,1,0:T(8,128)(2,1)S(1)} custom-call(f32[512,768]{1,0:T(8,128)S(1)} %get-tuple-element.76.refs_0_, bf16[3,512,768]{2,1,0:T(8,128)(2,1)S(1)} %get-tuple-element.79.refs_1_, bf16[512,768]{1,0:T(8,128)(2,1)S(1)} %get-tuple-element.80.refs_2_.refs_5_, f32[16,512]{1,0:T(8,128)S(1)} %get-tuple-element.81.refs_3_, ...), custom_call_target="tpu_custom_call" | custom-call | flops 3000000000 | bytes 10000000 | tf_op jit(solution)/shard_map/pallas_call | solution.py:360
  217.2 8.8 %shard_map.327 = (f32[512,768]{1,0:T(8,128)S(1)}, bf16[512,768]{1,0:T(8,128)(2,1)S(1)}, f32[1,768]{1,0:T(1,128)S(1)}, bf16[2,2,4,48,1920]{4,3,2,1,0:T(8,128)(2,1)S(1)}, bf16[2,2,4,48,1920]{4,3,2,1,0:T(8,128)(2,1)S(1)}) custom-call(f32[512,768]{1,0:T(8,128)S(1)} %get-tuple-element.76.refs_0_, f32[512,768]{1,0:T(8,128)S(1)} %get-tuple-element.77.refs_1_, ...), custom_call_target="tpu_custom_call" | custom-call | flops 5000000000 | bytes 10000000 | tf_op jit(solution)/shard_map/pallas_call | solution.py:360
  226.0 12.1 %shard_map.328 = (bf16[3,512,768]{2,1,0:T(8,128)(2,1)S(1)}, f32[16,512]{1,0:T(8,128)S(1)}) custom-call(f32[512,768]{1,0:T(8,128)S(1)} %get-tuple-element.82.refs_0_.refs_1_, bf16[3,512,768]{2,1,0:T(8,128)(2,1)S(1)} %get-tuple-element.83.refs_1_, bf16[512,768]{1,0:T(8,128)(2,1)S(1)} %get-tuple-element.67.refs_2_.refs_4_, ...), custom_call_target="tpu_custom_call" | custom-call | flops 3000000000 | bytes 10000000 | tf_op jit(solution)/shard_map/pallas_call | solution.py:360
  238.2 9.2 %shard_map.329 = (bf16[512,768]{1,0:T(8,128)(2,1)S(1)}, bf16[2,2,4,48,1280]{4,3,2,1,0:T(8,128)(2,1)S(1)}, bf16[2,2,4,48,1280]{4,3,2,1,0:T(8,128)(2,1)}) custom-call(bf16[1024,768]{1,0:T(8,128)(2,1)} %refs_0_.9, f32[512,768]{1,0:T(8,128)S(1)} %get-tuple-element.82.refs_0_.refs_1_, bf16[3,768,512]{2,1,0:T(8,128)(2,1)S(1)} %get-tuple-element.78.refs_2_, ...), custom_call_target="tpu_custom_call" | custom-call | flops 4000000000 | bytes 10000000 | tf_op jit(solution)/shard_map/pallas_call | solution.py:360
  252.1 1.6 slice_bitcast_fusion.7
  254.0 32.8 %collective-permute-done.52 = bf16[512,768]{1,0:T(8,128)(2,1)S(1)} collective-permute-done((bf16[512,768]{1,0:T(8,128)(2,1)}, bf16[512,768]{1,0:T(8,128)(2,1)S(1)}, u32[]{:S(2)}, u32[]{:S(2)}) %collective-permute-start.52) | collective-permute-done | bytes 786464 | tf_op jit(solution)/shard_map/ppermute | solution.py:55
  288.3 1.9 maximum_convert_fusion.1
  291.2 1.6 slice_bitcast_fusion.5
  296.9 21.2 %collective-permute-done.59 = bf16[2,4,48,768]{3,2,1,0:T(8,128)(2,1)S(1)} collective-permute-done((bf16[2,4,48,768]{3,2,1,0:T(8,128)(2,1)S(1)}, bf16[2,4,48,768]{3,2,1,0:T(8,128)(2,1)S(1)}, u32[]{:S(2)}, u32[]{:S(2)}) %collective-permute-start.59) | collective-permute-done | bytes 589856 | tf_op jit(solution)/shard_map/ppermute | solution.py:55
  323.0 17.6 %collective-permute-done.48 = bf16[4,48,2304]{2,1,0:T(8,128)(2,1)S(1)} collective-permute-done((bf16[4,48,2304]{2,1,0:T(8,128)(2,1)S(1)}, bf16[4,48,2304]{2,1,0:T(8,128)(2,1)S(1)}, u32[]{:S(2)}, u32[]{:S(2)}) %collective-permute-start.48) | collective-permute-done | bytes 884768 | tf_op jit(solution)/shard_map/ppermute | solution.py:55
  341.8 5.1 %collective-permute-done.60 = bf16[4,48,768]{2,1,0:T(8,128)(2,1)S(1)} collective-permute-done((bf16[4,48,768]{2,1,0:T(8,128)(2,1)S(1)}, bf16[4,48,768]{2,1,0:T(8,128)(2,1)S(1)}, u32[]{:S(2)}, u32[]{:S(2)}) %collective-permute-start.60) | collective-permute-done | bytes 294944 | tf_op jit(solution)/shard_map/ppermute | solution.py:55
  347.0 2.5 collective-permute-start.74
  351.2 10.1 %collective-permute-done.46 = bf16[2,4,48,1024]{3,2,1,0:T(8,128)(2,1)S(1)} collective-permute-done((bf16[2,4,48,1024]{3,2,1,0:T(8,128)(2,1)S(1)}, bf16[2,4,48,1024]{3,2,1,0:T(8,128)(2,1)S(1)}, u32[]{:S(2)}, u32[]{:S(2)}) %collective-permute-start.46) | collective-permute-done | bytes 786464 | tf_op jit(solution)/shard_map/ppermute | solution.py:55
  361.3 3.9 collective-permute-start.75
  366.8 11.1 %collective-permute-done.75 = bf16[48,2304]{1,0:T(8,128)(2,1)S(1)} collective-permute-done((bf16[48,2304]{1,0:T(8,128)(2,1)S(1)}, bf16[48,2304]{1,0:T(8,128)(2,1)S(1)}, u32[]{:S(2)}, u32[]{:S(2)}) %collective-permute-start.75) | collective-permute-done | bytes 221216 | tf_op jit(solution)/shard_map/ppermute | solution.py:55
  380.2 9.7 %collective-permute-done.57 = bf16[4,48,1024]{2,1,0:T(8,128)(2,1)S(1)} collective-permute-done((bf16[4,48,1024]{2,1,0:T(8,128)(2,1)S(1)}, bf16[4,48,1024]{2,1,0:T(8,128)(2,1)S(1)}, u32[]{:S(2)}, u32[]{:S(2)}) %collective-permute-start.57) | collective-permute-done | bytes 393248 | tf_op jit(solution)/shard_map/ppermute | solution.py:55
  390.9 7.9 %collective-permute-done.49 = bf16[2,4,48,640]{3,2,1,0:T(8,128)(2,1)S(1)} collective-permute-done((bf16[2,4,48,640]{3,2,1,0:T(8,128)(2,1)S(1)}, bf16[2,4,48,640]{3,2,1,0:T(8,128)(2,1)S(1)}, u32[]{:S(2)}, u32[]{:S(2)}) %collective-permute-start.49) | collective-permute-done | bytes 491552 | tf_op jit(solution)/shard_map/ppermute | solution.py:55
  403.8 1.9 maximum_convert_fusion
  405.7 1.9 maximum_convert_fusion.2
  407.6 2.9 collective-permute-start.70
  410.9 3.0 collective-permute-start.72
  415.1 6.2 %collective-permute-done.69 = bf16[48,768]{1,0:T(8,128)(2,1)S(1)} collective-permute-done((bf16[48,768]{1,0:T(8,128)(2,1)S(1)}, bf16[48,768]{1,0:T(8,128)(2,1)S(1)}, u32[]{:S(2)}, u32[]{:S(2)}) %collective-permute-start.69) | collective-permute-done | bytes 73760 | tf_op jit(solution)/shard_map/ppermute | solution.py:55
  423.5 4.6 %collective-permute-done.72 = bf16[48,2304]{1,0:T(8,128)(2,1)S(1)} collective-permute-done((bf16[48,2304]{1,0:T(8,128)(2,1)S(1)}, bf16[48,2304]{1,0:T(8,128)(2,1)S(1)}, u32[]{:S(2)}, u32[]{:S(2)}) %collective-permute-start.72) | collective-permute-done | bytes 221216 | tf_op jit(solution)/shard_map/ppermute | solution.py:55
  428.1 3.9 collective-permute-start.62
  432.0 3.5 collective-permute-start.63
  436.5 4.8 %collective-permute-done.66 = bf16[48,1920]{1,0:T(8,128)(2,1)S(1)} collective-permute-done((bf16[48,1920]{1,0:T(8,128)(2,1)S(1)}, bf16[48,1920]{1,0:T(8,128)(2,1)S(1)}, u32[]{:S(2)}, u32[]{:S(2)}) %collective-permute-start.66) | collective-permute-done | bytes 184352 | tf_op jit(solution)/shard_map/ppermute | solution.py:55
  442.1 5.8 %collective-permute-done.63 = bf16[48,1280]{1,0:T(8,128)(2,1)S(1)} collective-permute-done((bf16[48,1280]{1,0:T(8,128)(2,1)S(1)}, bf16[48,1280]{1,0:T(8,128)(2,1)S(1)}, u32[]{:S(2)}, u32[]{:S(2)}) %collective-permute-start.63) | collective-permute-done | bytes 122912 | tf_op jit(solution)/shard_map/ppermute | solution.py:55
  (295 shorter events, 71.1 us)
Async XLA Ops:
  10.5 41.3 %collective-permute-start.14 = (bf16[48,1920]{1,0:T(8,128)(2,1)S(1)}, bf16[48,1920]{1,0:T(8,128)(2,1)S(1)}, u32[]{:S(2)}, u32[]{:S(2)}) collective-permute-start(bf16[48,1920]{1,0:T(8,128)(2,1)S(1)} %bitcast_dynamic-update-slice_fusion.12), channel_id=1, source_target_pairs={{0,24},{1,25},{2,26},{3,27},{4,28},{5,29},{6,30},{7,31},{8,0},{9,1... | collective-permute-start | bytes 552968 | tf_op jit(solution)/shard_map/ppermute | solution.py:55
  16.6 33.7 %collective-permute-start.13 = (bf16[48,1920]{1,0:T(8,128)(2,1)S(1)}, bf16[48,1920]{1,0:T(8,128)(2,1)S(1)}, u32[]{:S(2)}, u32[]{:S(2)}) collective-permute-start(bf16[48,1920]{1,0:T(8,128)(2,1)S(1)} %bitcast_dynamic-update-slice_fusion.12), channel_id=1, source_target_pairs={{0,16},{1,17},{2,18},{3,19},{4,20},{5,21},{6,22},{7,23},{8,24},{9,... | collective-permute-start | bytes 552968 | tf_op jit(solution)/shard_map/ppermute | solution.py:55
  17.6 32.5 %collective-permute-start.12 = (bf16[48,1920]{1,0:T(8,128)(2,1)S(1)}, bf16[48,1920]{1,0:T(8,128)(2,1)S(1)}, u32[]{:S(2)}, u32[]{:S(2)}) collective-permute-start(bf16[48,1920]{1,0:T(8,128)(2,1)S(1)} %bitcast_dynamic-update-slice_fusion.12), channel_id=1, source_target_pairs={{0,8},{1,9},{2,10},{3,11},{4,12},{5,13},{6,14},{7,15},{8,16},{9,17... | collective-permute-start | bytes 552968 | tf_op jit(solution)/shard_map/ppermute | solution.py:55
  21.0 18.2 %collective-permute-start.1 = (bf16[48,1280]{1,0:T(8,128)(2,1)S(1)}, bf16[48,1280]{1,0:T(8,128)(2,1)S(1)}, u32[]{:S(2)}, u32[]{:S(2)}) collective-permute-start(bf16[48,1280]{1,0:T(8,128)(2,1)S(1)} %get-tuple-element.120), channel_id=1, source_target_pairs={{0,16},{1,17},{2,18},{3,19},{4,20},{5,21},{6,22},{7,23},{8,24},{9,... | collective-permute-start | bytes 368648 | tf_op jit(solution)/shard_map/ppermute | solution.py:55
  39.2 43.9 %collective-permute-start.25 = (bf16[48,2560]{1,0:T(8,128)(2,1)S(1)}, bf16[48,2560]{1,0:T(8,128)(2,1)S(1)}, u32[]{:S(2)}, u32[]{:S(2)}) collective-permute-start(bf16[48,2560]{1,0:T(8,128)(2,1)S(1)} %pad_maximum_fusion.3), channel_id=1, source_target_pairs={{0,16},{1,17},{2,18},{3,19},{4,20},{5,21},{6,22},{7,23},{8,24},{9,... | collective-permute-start | bytes 737288 | tf_op jit(solution)/shard_map/ppermute | solution.py:55
  39.2 22.4 %collective-permute-start.24 = (bf16[48,2560]{1,0:T(8,128)(2,1)S(1)}, bf16[48,2560]{1,0:T(8,128)(2,1)S(1)}, u32[]{:S(2)}, u32[]{:S(2)}) collective-permute-start(bf16[48,2560]{1,0:T(8,128)(2,1)S(1)} %pad_maximum_fusion.3), channel_id=1, source_target_pairs={{0,8},{1,9},{2,10},{3,11},{4,12},{5,13},{6,14},{7,15},{8,16},{9,17... | collective-permute-start | bytes 737288 | tf_op jit(solution)/shard_map/ppermute | solution.py:55
  50.2 30.8 %collective-permute-start.35 = (bf16[2,2,48,512]{3,2,1,0:T(8,128)(2,1)S(1)}, bf16[2,2,48,512]{3,2,1,0:T(8,128)(2,1)S(1)}, u32[]{:S(2)}, u32[]{:S(2)}) collective-permute-start(bf16[2,2,48,512]{3,2,1,0:T(8,128)(2,1)S(1)} %bitcast.238), channel_id=1, source_target_pairs={{0,24},{1,25},{2,26},{3,27},{4,28},{5,29},{6,30},{7,31},{8,0},{9,1... | collective-permute-start | bytes 589832 | tf_op jit(solution)/shard_map/ppermute | solution.py:55
  50.3 19.8 %collective-permute-start.4 = (bf16[4,48,1280]{2,1,0:T(8,128)(2,1)S(1)}, bf16[4,48,1280]{2,1,0:T(8,128)(2,1)S(1)}, u32[]{:S(2)}, u32[]{:S(2)}) collective-permute-start(bf16[4,48,1280]{2,1,0:T(8,128)(2,1)S(1)} %bitcast_dynamic-update-slice_fusion.8.refs_2_.refs_9_), channel_id=1, source_target_pairs={{0,1},{1,0},{2,3},{3,2},{4,5},{5,4},{6,7},{7,6},{8,9},{9,8},{10,11... | collective-permute-start | bytes 1474568 | tf_op jit(solution)/shard_map/ppermute | solution.py:55
  51.9 29.2 %collective-permute-start.34 = (bf16[2,2,48,512]{3,2,1,0:T(8,128)(2,1)S(1)}, bf16[2,2,48,512]{3,2,1,0:T(8,128)(2,1)S(1)}, u32[]{:S(2)}, u32[]{:S(2)}) collective-permute-start(bf16[2,2,48,512]{3,2,1,0:T(8,128)(2,1)S(1)} %bitcast.239), channel_id=1, source_target_pairs={{0,16},{1,17},{2,18},{3,19},{4,20},{5,21},{6,22},{7,23},{8,24},{9,... | collective-permute-start | bytes 589832 | tf_op jit(solution)/shard_map/ppermute | solution.py:55
  61.7 19.9 %collective-permute-start.33 = (bf16[2,2,48,512]{3,2,1,0:T(8,128)(2,1)S(1)}, bf16[2,2,48,512]{3,2,1,0:T(8,128)(2,1)S(1)}, u32[]{:S(2)}, u32[]{:S(2)}) collective-permute-start(bf16[2,2,48,512]{3,2,1,0:T(8,128)(2,1)S(1)} %bitcast.240), channel_id=1, source_target_pairs={{0,8},{1,9},{2,10},{3,11},{4,12},{5,13},{6,14},{7,15},{8,16},{9,17... | collective-permute-start | bytes 589832 | tf_op jit(solution)/shard_map/ppermute | solution.py:55
  87.6 19.0 %collective-permute-start.16 = (bf16[4,48,1920]{2,1,0:T(8,128)(2,1)S(1)}, bf16[4,48,1920]{2,1,0:T(8,128)(2,1)S(1)}, u32[]{:S(2)}, u32[]{:S(2)}) collective-permute-start(bf16[4,48,1920]{2,1,0:T(8,128)(2,1)S(1)} %bitcast_dynamic-update-slice_fusion.4.refs_4_.refs_7_.refs_5_), channel_id=1, source_target_pairs={{0,1},{1,0},{2,3},{3,2},{4,5},{5,4},{6,7},{7,6},{8,9},{9,8},{10,11... | collective-permute-start | bytes 2211848 | tf_op jit(solution)/shard_map/ppermute | solution.py:55
  89.3 18.8 %collective-permute-start.15 = (bf16[4,48,1920]{2,1,0:T(8,128)(2,1)S(1)}, bf16[4,48,1920]{2,1,0:T(8,128)(2,1)S(1)}, u32[]{:S(2)}, u32[]{:S(2)}) collective-permute-start(bf16[4,48,1920]{2,1,0:T(8,128)(2,1)S(1)} %bitcast_dynamic-update-slice_fusion.4.refs_4_.refs_7_.refs_5_), channel_id=1, source_target_pairs={{0,4},{1,5},{2,6},{3,7},{4,0},{5,1},{6,2},{7,3},{8,12},{9,13},{10,... | collective-permute-start | bytes 2211848 | tf_op jit(solution)/shard_map/ppermute | solution.py:55
  90.9 17.7 %collective-permute-start.36 = (bf16[4,2,2,48,512]{4,3,2,1,0:T(8,128)(2,1)S(1)}, bf16[4,2,2,48,512]{4,3,2,1,0:T(8,128)(2,1)S(1)}, u32[]{:S(2)}, u32[]{:S(2)}) collective-permute-start(bf16[4,2,2,48,512]{4,3,2,1,0:T(8,128)(2,1)S(1)} %pad_maximum_fusion.refs_9_.refs_13_), channel_id=1, source_target_pairs={{0,2},{1,3},{2,0},{3,1},{4,6},{5,7},{6,4},{7,5},{8,10},{9,11},{10,... | collective-permute-start | bytes 2359304 | tf_op jit(solution)/shard_map/ppermute | solution.py:55
  92.0 17.2 %collective-permute-start.8 = (bf16[4,48,1280]{2,1,0:T(8,128)(2,1)S(1)}, bf16[4,48,1280]{2,1,0:T(8,128)(2,1)S(1)}, u32[]{:S(2)}, u32[]{:S(2)}) collective-permute-start(bf16[4,48,1280]{2,1,0:T(8,128)(2,1)S(1)} %collective-permute-done.3.refs_3_.refs_10_), channel_id=1, source_target_pairs={{0,2},{1,3},{2,0},{3,1},{4,6},{5,7},{6,4},{7,5},{8,10},{9,11},{10,... | collective-permute-start | bytes 1474568 | tf_op jit(solution)/shard_map/ppermute | solution.py:55
  106.6 31.7 %collective-permute-start.37 = (bf16[4,48,2560]{2,1,0:T(8,128)(2,1)S(1)}, bf16[4,48,2560]{2,1,0:T(8,128)(2,1)S(1)}, u32[]{:S(2)}, u32[]{:S(2)}) collective-permute-start(bf16[4,48,2560]{2,1,0:T(8,128)(2,1)S(1)} %bitcast_dynamic-update-slice_fusion.refs_5_), channel_id=1, source_target_pairs={{0,1},{1,0},{2,3},{3,2},{4,5},{5,4},{6,7},{7,6},{8,9},{9,8},{10,11... | collective-permute-start | bytes 2949128 | tf_op jit(solution)/shard_map/ppermute | solution.py:55
  108.1 30.8 %collective-permute-start.27 = (bf16[4,48,2560]{2,1,0:T(8,128)(2,1)S(1)}, bf16[4,48,2560]{2,1,0:T(8,128)(2,1)S(1)}, u32[]{:S(2)}, u32[]{:S(2)}) collective-permute-start(bf16[4,48,2560]{2,1,0:T(8,128)(2,1)S(1)} %bitcast_dynamic-update-slice_fusion.refs_5_), channel_id=1, source_target_pairs={{0,4},{1,5},{2,6},{3,7},{4,0},{5,1},{6,2},{7,3},{8,12},{9,13},{10,... | collective-permute-start | bytes 2949128 | tf_op jit(solution)/shard_map/ppermute | solution.py:55
  109.2 29.1 %collective-permute-start.17 = (bf16[2,48,1920]{2,1,0:T(8,128)(2,1)S(1)}, bf16[2,48,1920]{2,1,0:T(8,128)(2,1)S(1)}, u32[]{:S(2)}, u32[]{:S(2)}) collective-permute-start(bf16[2,48,1920]{2,1,0:T(8,128)(2,1)S(1)} %slice.627), channel_id=1, source_target_pairs={{0,4},{1,5},{2,6},{3,7},{4,0},{5,1},{6,2},{7,3},{8,12},{9,13},{10,... | collective-permute-start | bytes 1105928 | tf_op jit(solution)/shard_map/ppermute | solution.py:55
  110.8 29.5 %collective-permute-start.21 = (bf16[4,48,1920]{2,1,0:T(8,128)(2,1)S(1)}, bf16[4,48,1920]{2,1,0:T(8,128)(2,1)S(1)}, u32[]{:S(2)}, u32[]{:S(2)}) collective-permute-start(bf16[4,48,1920]{2,1,0:T(8,128)(2,1)S(1)} %collective-permute-done.16.refs_6_.refs_9_.refs_7_), channel_id=1, source_target_pairs={{0,2},{1,3},{2,0},{3,1},{4,6},{5,7},{6,4},{7,5},{8,10},{9,11},{10,... | collective-permute-start | bytes 2211848 | tf_op jit(solution)/shard_map/ppermute | solution.py:55
  110.9 27.9 %collective-permute-start.18 = (bf16[2,48,1920]{2,1,0:T(8,128)(2,1)S(1)}, bf16[2,48,1920]{2,1,0:T(8,128)(2,1)S(1)}, u32[]{:S(2)}, u32[]{:S(2)}) collective-permute-start(bf16[2,48,1920]{2,1,0:T(8,128)(2,1)S(1)} %slice.628), channel_id=1, source_target_pairs={{0,1},{1,0},{2,3},{3,2},{4,5},{5,4},{6,7},{7,6},{8,9},{9,8},{10,11... | collective-permute-start | bytes 1105928 | tf_op jit(solution)/shard_map/ppermute | solution.py:55
  138.9 31.2 %collective-permute-start.28 = (bf16[4,48,2560]{2,1,0:T(8,128)(2,1)S(1)}, bf16[4,48,2560]{2,1,0:T(8,128)(2,1)S(1)}, u32[]{:S(2)}, u32[]{:S(2)}) collective-permute-start(bf16[4,48,2560]{2,1,0:T(8,128)(2,1)S(1)} %bitcast_dynamic-update-slice_fusion.refs_5_), channel_id=1, source_target_pairs={{0,2},{1,3},{2,0},{3,1},{4,6},{5,7},{6,4},{7,5},{8,10},{9,11},{10,... | collective-permute-start | bytes 2949128 | tf_op jit(solution)/shard_map/ppermute | solution.py:55
  140.0 30.1 %collective-permute-start.29 = (bf16[4,48,2560]{2,1,0:T(8,128)(2,1)S(1)}, bf16[4,48,2560]{2,1,0:T(8,128)(2,1)S(1)}, u32[]{:S(2)}, u32[]{:S(2)}) collective-permute-start(bf16[4,48,2560]{2,1,0:T(8,128)(2,1)S(1)} %collective-permute-done.27.refs_6_), channel_id=1, source_target_pairs={{0,2},{1,3},{2,0},{3,1},{4,6},{5,7},{6,4},{7,5},{8,10},{9,11},{10,... | collective-permute-start | bytes 2949128 | tf_op jit(solution)/shard_map/ppermute | solution.py:55
  140.3 29.2 %collective-permute-start.38 = (bf16[2,48,2560]{2,1,0:T(8,128)(2,1)S(1)}, bf16[2,48,2560]{2,1,0:T(8,128)(2,1)S(1)}, u32[]{:S(2)}, u32[]{:S(2)}) collective-permute-start(bf16[2,48,2560]{2,1,0:T(8,128)(2,1)S(1)} %slice.631), channel_id=1, source_target_pairs={{0,4},{1,5},{2,6},{3,7},{4,0},{5,1},{6,2},{7,3},{8,12},{9,13},{10,... | collective-permute-start | bytes 1474568 | tf_op jit(solution)/shard_map/ppermute | solution.py:55
  141.6 28.0 %collective-permute-start.39 = (bf16[2,48,2560]{2,1,0:T(8,128)(2,1)S(1)}, bf16[2,48,2560]{2,1,0:T(8,128)(2,1)S(1)}, u32[]{:S(2)}, u32[]{:S(2)}) collective-permute-start(bf16[2,48,2560]{2,1,0:T(8,128)(2,1)S(1)} %slice.632), channel_id=1, source_target_pairs={{0,1},{1,0},{2,3},{3,2},{4,5},{5,4},{6,7},{7,6},{8,9},{9,8},{10,11... | collective-permute-start | bytes 1474568 | tf_op jit(solution)/shard_map/ppermute | solution.py:55
  153.8 34.1 %collective-permute-start.40 = (bf16[4,48,2560]{2,1,0:T(8,128)(2,1)S(1)}, bf16[4,48,2560]{2,1,0:T(8,128)(2,1)S(1)}, u32[]{:S(2)}, u32[]{:S(2)}) collective-permute-start(bf16[4,48,2560]{2,1,0:T(8,128)(2,1)S(1)} %collective-permute-done.37.refs_7_), channel_id=1, source_target_pairs={{0,2},{1,3},{2,0},{3,1},{4,6},{5,7},{6,4},{7,5},{8,10},{9,11},{10,... | collective-permute-start | bytes 2949128 | tf_op jit(solution)/shard_map/ppermute | solution.py:55
  169.6 18.3 %collective-permute-start.41 = (bf16[2,48,2560]{2,1,0:T(8,128)(2,1)S(1)}, bf16[2,48,2560]{2,1,0:T(8,128)(2,1)S(1)}, u32[]{:S(2)}, u32[]{:S(2)}) collective-permute-start(bf16[2,48,2560]{2,1,0:T(8,128)(2,1)S(1)} %collective-permute-done.38.refs_8_), channel_id=1, source_target_pairs={{0,2},{1,3},{2,0},{3,1},{4,6},{5,7},{6,4},{7,5},{8,10},{9,11},{10,... | collective-permute-start | bytes 1474568 | tf_op jit(solution)/shard_map/ppermute | solution.py:55
  169.7 18.3 %collective-permute-start.42 = (bf16[2,48,2560]{2,1,0:T(8,128)(2,1)S(1)}, bf16[2,48,2560]{2,1,0:T(8,128)(2,1)S(1)}, u32[]{:S(2)}, u32[]{:S(2)}) collective-permute-start(bf16[2,48,2560]{2,1,0:T(8,128)(2,1)S(1)} %collective-permute-done.39.refs_9_), channel_id=1, source_target_pairs={{0,2},{1,3},{2,0},{3,1},{4,6},{5,7},{6,4},{7,5},{8,10},{9,11},{10,... | collective-permute-start | bytes 1474568 | tf_op jit(solution)/shard_map/ppermute | solution.py:55
  249.6 40.6 %collective-permute-start.43 = (bf16[2,2,4,48,1280]{4,3,2,1,0:T(8,128)(2,1)}, bf16[2,2,4,48,1280]{4,3,2,1,0:T(8,128)(2,1)}, u32[]{:S(2)}, u32[]{:S(2)}) collective-permute-start(bf16[2,2,4,48,1280]{4,3,2,1,0:T(8,128)(2,1)} %get-tuple-element.91), channel_id=1, source_target_pairs={{0,2},{1,3},{2,0},{3,1},{4,6},{5,7},{6,4},{7,5},{8,10},{9,11},{10,... | collective-permute-start | bytes 5898248 | tf_op jit(solution)/shard_map/ppermute | solution.py:55
  249.7 43.5 %collective-permute-start.58 = (bf16[2,4,48,3072]{3,2,1,0:T(8,128)(2,1)}, bf16[2,4,48,3072]{3,2,1,0:T(8,128)(2,1)S(1)}, u32[]{:S(2)}, u32[]{:S(2)}) collective-permute-start(bf16[2,4,48,3072]{3,2,1,0:T(8,128)(2,1)} %copy-done.13), channel_id=1, source_target_pairs={{0,2},{1,3},{2,0},{3,1},{4,6},{5,7},{6,4},{7,5},{8,10},{9,11},{10,... | collective-permute-start | bytes 7077896 | tf_op jit(solution)/shard_map/ppermute | solution.py:55
  250.1 151.2 %collective-permute-start.51 = (bf16[512,768]{1,0:T(8,128)(2,1)}, bf16[512,768]{1,0:T(8,128)(2,1)S(1)}, u32[]{:S(2)}, u32[]{:S(2)}) collective-permute-start(bf16[512,768]{1,0:T(8,128)(2,1)} %copy-done.5), channel_id=1, source_target_pairs={{0,1},{1,0},{2,3},{3,2},{4,5},{5,4},{6,7},{7,6},{8,9},{9,8},{10,11... | collective-permute-start | bytes 2359304 | tf_op jit(solution)/shard_map/ppermute | solution.py:55
  251.5 44.2 %collective-permute-start.47 = (bf16[2,4,48,3072]{3,2,1,0:T(8,128)(2,1)}, bf16[2,4,48,3072]{3,2,1,0:T(8,128)(2,1)S(1)}, u32[]{:S(2)}, u32[]{:S(2)}) collective-permute-start(bf16[2,4,48,3072]{3,2,1,0:T(8,128)(2,1)} %copy-done.14), channel_id=1, source_target_pairs={{0,2},{1,3},{2,0},{3,1},{4,6},{5,7},{6,4},{7,5},{8,10},{9,11},{10,... | collective-permute-start | bytes 7077896 | tf_op jit(solution)/shard_map/ppermute | solution.py:55
  251.5 35.2 %collective-permute-start.52 = (bf16[512,768]{1,0:T(8,128)(2,1)}, bf16[512,768]{1,0:T(8,128)(2,1)S(1)}, u32[]{:S(2)}, u32[]{:S(2)}) collective-permute-start(bf16[512,768]{1,0:T(8,128)(2,1)} %copy-done.9), channel_id=1, source_target_pairs={{0,1},{1,0},{2,3},{3,2},{4,5},{5,4},{6,7},{7,6},{8,9},{9,8},{10,11... | collective-permute-start | bytes 2359304 | tf_op jit(solution)/shard_map/ppermute | solution.py:55
  286.7 115.5 %collective-permute-start.53 = (bf16[512,768]{1,0:T(8,128)(2,1)S(1)}, bf16[512,768]{1,0:T(8,128)(2,1)S(1)}, u32[]{:S(2)}, u32[]{:S(2)}) collective-permute-start(bf16[512,768]{1,0:T(8,128)(2,1)S(1)} %copy-done.8), channel_id=1, source_target_pairs={{0,1},{1,0},{2,3},{3,2},{4,5},{5,4},{6,7},{7,6},{8,9},{9,8},{10,11... | collective-permute-start | bytes 2359304 | tf_op jit(solution)/shard_map/ppermute | solution.py:55
  291.2 28.0 %collective-permute-start.44 = (bf16[2,2,4,48,1920]{4,3,2,1,0:T(8,128)(2,1)S(1)}, bf16[2,2,4,48,1920]{4,3,2,1,0:T(8,128)(2,1)S(1)}, u32[]{:S(2)}, u32[]{:S(2)}) collective-permute-start(bf16[2,2,4,48,1920]{4,3,2,1,0:T(8,128)(2,1)S(1)} %copy-done.12), channel_id=1, source_target_pairs={{0,2},{1,3},{2,0},{3,1},{4,6},{5,7},{6,4},{7,5},{8,10},{9,11},{10,... | collective-permute-start | bytes 8847368 | tf_op jit(solution)/shard_map/ppermute | solution.py:55
  294.8 26.4 %collective-permute-start.61 = (bf16[4,48,2304]{2,1,0:T(8,128)(2,1)S(1)}, bf16[4,48,2304]{2,1,0:T(8,128)(2,1)S(1)}, u32[]{:S(2)}, u32[]{:S(2)}) collective-permute-start(bf16[4,48,2304]{2,1,0:T(8,128)(2,1)S(1)} %fusion.1), channel_id=1, source_target_pairs={{0,4},{1,5},{2,6},{3,7},{4,0},{5,1},{6,2},{7,3},{8,12},{9,13},{10,... | collective-permute-start | bytes 2654216 | tf_op jit(solution)/shard_map/ppermute | solution.py:55
  295.9 22.2 %collective-permute-start.59 = (bf16[2,4,48,768]{3,2,1,0:T(8,128)(2,1)S(1)}, bf16[2,4,48,768]{3,2,1,0:T(8,128)(2,1)S(1)}, u32[]{:S(2)}, u32[]{:S(2)}) collective-permute-start(bf16[2,4,48,768]{3,2,1,0:T(8,128)(2,1)S(1)} %add_convert_fusion.3), channel_id=1, source_target_pairs={{0,1},{1,0},{2,3},{3,2},{4,5},{5,4},{6,7},{7,6},{8,9},{9,8},{10,11... | collective-permute-start | bytes 1769480 | tf_op jit(solution)/shard_map/ppermute | solution.py:55
  318.1 22.5 %collective-permute-start.48 = (bf16[4,48,2304]{2,1,0:T(8,128)(2,1)S(1)}, bf16[4,48,2304]{2,1,0:T(8,128)(2,1)S(1)}, u32[]{:S(2)}, u32[]{:S(2)}) collective-permute-start(bf16[4,48,2304]{2,1,0:T(8,128)(2,1)S(1)} %fusion), channel_id=1, source_target_pairs={{0,4},{1,5},{2,6},{3,7},{4,0},{5,1},{6,2},{7,3},{8,12},{9,13},{10,... | collective-permute-start | bytes 2654216 | tf_op jit(solution)/shard_map/ppermute | solution.py:55
  319.2 27.7 %collective-permute-start.60 = (bf16[4,48,768]{2,1,0:T(8,128)(2,1)S(1)}, bf16[4,48,768]{2,1,0:T(8,128)(2,1)S(1)}, u32[]{:S(2)}, u32[]{:S(2)}) collective-permute-start(bf16[4,48,768]{2,1,0:T(8,128)(2,1)S(1)} %get-tuple-element.130), channel_id=1, source_target_pairs={{0,4},{1,5},{2,6},{3,7},{4,0},{5,1},{6,2},{7,3},{8,12},{9,13},{10,... | collective-permute-start | bytes 884744 | tf_op jit(solution)/shard_map/ppermute | solution.py:55
  321.2 28.3 %collective-permute-start.45 = (bf16[2,4,48,896]{3,2,1,0:T(8,128)(2,1)S(1)}, bf16[2,4,48,896]{3,2,1,0:T(8,128)(2,1)S(1)}, u32[]{:S(2)}, u32[]{:S(2)}) collective-permute-start(bf16[2,4,48,896]{3,2,1,0:T(8,128)(2,1)S(1)} %add_convert_fusion.2), channel_id=1, source_target_pairs={{0,1},{1,0},{2,3},{3,2},{4,5},{5,4},{6,7},{7,6},{8,9},{9,8},{10,11... | collective-permute-start | bytes 2064392 | tf_op jit(solution)/shard_map/ppermute | solution.py:55
  340.6 20.6 %collective-permute-start.46 = (bf16[2,4,48,1024]{3,2,1,0:T(8,128)(2,1)S(1)}, bf16[2,4,48,1024]{3,2,1,0:T(8,128)(2,1)S(1)}, u32[]{:S(2)}, u32[]{:S(2)}) collective-permute-start(bf16[2,4,48,1024]{3,2,1,0:T(8,128)(2,1)S(1)} %pad_maximum_fusion.1), channel_id=1, source_target_pairs={{0,4},{1,5},{2,6},{3,7},{4,0},{5,1},{6,2},{7,3},{8,12},{9,13},{10,... | collective-permute-start | bytes 2359304 | tf_op jit(solution)/shard_map/ppermute | solution.py:55
  347.0 18.6 %collective-permute-start.74 = (bf16[48,2304]{1,0:T(8,128)(2,1)S(1)}, bf16[48,2304]{1,0:T(8,128)(2,1)S(1)}, u32[]{:S(2)}, u32[]{:S(2)}) collective-permute-start(bf16[48,2304]{1,0:T(8,128)(2,1)S(1)} %get-tuple-element.125), channel_id=1, source_target_pairs={{0,8},{1,9},{2,10},{3,11},{4,12},{5,13},{6,14},{7,15},{8,16},{9,17... | collective-permute-start | bytes 663560 | tf_op jit(solution)/shard_map/ppermute | solution.py:55
  365.5 55.8 %collective-permute-start.71 = (bf16[48,2304]{1,0:T(8,128)(2,1)S(1)}, bf16[48,2304]{1,0:T(8,128)(2,1)S(1)}, u32[]{:S(2)}, u32[]{:S(2)}) collective-permute-start(bf16[48,2304]{1,0:T(8,128)(2,1)S(1)} %get-tuple-element.121), channel_id=1, source_target_pairs={{0,8},{1,9},{2,10},{3,11},{4,12},{5,13},{6,14},{7,15},{8,16},{9,17... | collective-permute-start | bytes 663560 | tf_op jit(solution)/shard_map/ppermute | solution.py:55
  379.4 19.4 %collective-permute-start.49 = (bf16[2,4,48,640]{3,2,1,0:T(8,128)(2,1)S(1)}, bf16[2,4,48,640]{3,2,1,0:T(8,128)(2,1)S(1)}, u32[]{:S(2)}, u32[]{:S(2)}) collective-permute-start(bf16[2,4,48,640]{3,2,1,0:T(8,128)(2,1)S(1)} %add_convert_fusion.4), channel_id=1, source_target_pairs={{0,1},{1,0},{2,3},{3,2},{4,5},{5,4},{6,7},{7,6},{8,9},{9,8},{10,11... | collective-permute-start | bytes 1474568 | tf_op jit(solution)/shard_map/ppermute | solution.py:55
  398.8 24.0 %collective-permute-start.73 = (bf16[48,2304]{1,0:T(8,128)(2,1)S(1)}, bf16[48,2304]{1,0:T(8,128)(2,1)S(1)}, u32[]{:S(2)}, u32[]{:S(2)}) collective-permute-start(bf16[48,2304]{1,0:T(8,128)(2,1)S(1)} %get-tuple-element.122), channel_id=1, source_target_pairs={{0,24},{1,25},{2,26},{3,27},{4,28},{5,29},{6,30},{7,31},{8,0},{9,1... | collective-permute-start | bytes 663560 | tf_op jit(solution)/shard_map/ppermute | solution.py:55
  410.9 17.2 %collective-permute-start.72 = (bf16[48,2304]{1,0:T(8,128)(2,1)S(1)}, bf16[48,2304]{1,0:T(8,128)(2,1)S(1)}, u32[]{:S(2)}, u32[]{:S(2)}) collective-permute-start(bf16[48,2304]{1,0:T(8,128)(2,1)S(1)} %get-tuple-element.123), channel_id=1, source_target_pairs={{0,16},{1,17},{2,18},{3,19},{4,20},{5,21},{6,22},{7,23},{8,24},{9,... | collective-permute-start | bytes 663560 | tf_op jit(solution)/shard_map/ppermute | solution.py:55
  413.8 18.1 %collective-permute-start.77 = (bf16[48,2304]{1,0:T(8,128)(2,1)S(1)}, bf16[48,2304]{1,0:T(8,128)(2,1)S(1)}, u32[]{:S(2)}, u32[]{:S(2)}) collective-permute-start(bf16[48,2304]{1,0:T(8,128)(2,1)S(1)} %add_convert_fusion.19), channel_id=1, source_target_pairs={{0,1},{1,0},{2,3},{3,2},{4,5},{5,4},{6,7},{7,6},{8,9},{9,8},{10,11... | collective-permute-start | bytes 663560 | tf_op jit(solution)/shard_map/ppermute | solution.py:55
  421.3 19.9 %collective-permute-start.66 = (bf16[48,1920]{1,0:T(8,128)(2,1)S(1)}, bf16[48,1920]{1,0:T(8,128)(2,1)S(1)}, u32[]{:S(2)}, u32[]{:S(2)}) collective-permute-start(bf16[48,1920]{1,0:T(8,128)(2,1)S(1)} %pad_maximum_fusion.8), channel_id=1, source_target_pairs={{0,16},{1,17},{2,18},{3,19},{4,20},{5,21},{6,22},{7,23},{8,24},{9,... | collective-permute-start | bytes 552968 | tf_op jit(solution)/shard_map/ppermute | solution.py:55
  421.4 19.9 %collective-permute-start.67 = (bf16[48,1920]{1,0:T(8,128)(2,1)S(1)}, bf16[48,1920]{1,0:T(8,128)(2,1)S(1)}, u32[]{:S(2)}, u32[]{:S(2)}) collective-permute-start(bf16[48,1920]{1,0:T(8,128)(2,1)S(1)} %pad_maximum_fusion.9), channel_id=1, source_target_pairs={{0,24},{1,25},{2,26},{3,27},{4,28},{5,29},{6,30},{7,31},{8,0},{9,1... | collective-permute-start | bytes 552968 | tf_op jit(solution)/shard_map/ppermute | solution.py:55
  422.8 18.5 %collective-permute-start.65 = (bf16[48,1920]{1,0:T(8,128)(2,1)S(1)}, bf16[48,1920]{1,0:T(8,128)(2,1)S(1)}, u32[]{:S(2)}, u32[]{:S(2)}) collective-permute-start(bf16[48,1920]{1,0:T(8,128)(2,1)S(1)} %pad_maximum_fusion.7), channel_id=1, source_target_pairs={{0,8},{1,9},{2,10},{3,11},{4,12},{5,13},{6,14},{7,15},{8,16},{9,17... | collective-permute-start | bytes 552968 | tf_op jit(solution)/shard_map/ppermute | solution.py:55
  (80 other events, 1366.0 us)

commit v5 on v3

--- a/solution.py
+++ b/solution.py
@@ -437,7 +437,11 @@
 DMA = pltpu.SemaphoreType.DMA
 
 
-def self_forward(grid, inputs, base_hot, pieces, d, hd, heads):
+def one_hot(bucket_row):
+    return (lax.broadcasted_iota(jnp.int32, (LANE, L), 0) == bucket_row).astype(F32).astype(BF16)
+
+
+def self_forward(grid, inputs, bucket_row, pieces, d, hd, heads):
     ws = Weights(pieces, grid.n_z)
     k = len(ws.arrays)
     w2 = 2 * hd
@@ -471,8 +475,9 @@
         gain_ref[...] = gains
         lse_ref[...] = jnp.zeros_like(lse_ref)
         base_ref[...] = jnp.zeros_like(base_ref)
+        hot = one_hot(hot_ref[...])
         for a in range(2):
-            base_ref[a * heads : (a + 1) * heads, :] = nn(extra[0:16, a * LANE : (a + 1) * LANE], hot_ref[...])[:heads]
+            base_ref[a * heads : (a + 1) * heads, :] = nn(extra[0:16, a * LANE : (a + 1) * LANE], hot)[:heads]
 
         def normalize(t, carry):
             rows = pl.ds(pl.multiple_of(t * QB, QB), QB)
@@ -493,7 +498,7 @@
     return call(
         body,
         [((L, d), BF16), ((3, L, w2), BF16), row, ((8, d), F32), ((16, L), F32), ((16, L), F32)],
-        [(inputs, True), (base_hot, False)] + ws.specs(),
+        [(inputs, True), (bucket_row, False)] + ws.specs(),
         [
             pltpu.VMEM((L, d), BF16),
             ws.scratch(2 * LANE),
@@ -838,7 +843,7 @@
     return result[:3], parts.split(result[3:])
 
 
-def self_finish(grid, inputs, b1, ready, grads, off, dg2, dg3, base_hot, gains, pieces, d, hd, heads):
+def self_finish(grid, inputs, b1, ready, grads, off, dg2, dg3, bucket_row, gains, pieces, d, hd, heads):
     ws = Weights(pieces, grid.n_z)
     k = len(ws.arrays)
     w2 = 2 * hd
@@ -876,7 +881,7 @@
         dg = lax.fori_loop(0, L // QB, finish, jnp.zeros((1, d), F32))
         dgs = jnp.concatenate([dg, dg2_ref[...], dg3_ref[...], jnp.zeros((5, d), F32)], axis=0)
         columns = jnp.concatenate([jnp.zeros((NB, d), F32), dgs, jnp.zeros((LANE - NB - 8, d), F32)], axis=0).T
-        hot = hot_ref[...]
+        hot = one_hot(hot_ref[...])
         sums = off_ref[...]
         table = jnp.zeros((16, LANE), F32)
         for _ in range(3):
@@ -893,7 +898,7 @@
     result = call(
         body,
         [((L, d), BF16)] + parts.outs(),
-        [(inputs, True)] + near(b1, ready, grads, off, dg2, dg3, base_hot, gains) + ws.specs(),
+        [(inputs, True)] + near(b1, ready, grads, off, dg2, dg3, bucket_row, gains) + ws.specs(),
         [
             pltpu.VMEM((L, d), BF16),
             ws.scratch(w2, 3),
@@ -1025,9 +1030,9 @@
         pieces_three = gather(grid, group_three)
         pieces_four = gather_late(grid, turned[:, early:])
 
-        base_hot = (buckets[None, :] == lax.broadcasted_iota(jnp.int32, (LANE, L), 0)).astype(BF16)
-
-        n1, qkv1, at1, gains, base, lse1 = self_forward(grid, inputs, base_hot, pieces_one, d, hd, heads)
+        bucket_row = buckets[None, :]
+
+        n1, qkv1, at1, gains, base, lse1 = self_forward(grid, inputs, bucket_row, pieces_one, d, hd, heads)
         r1, r2, n2, qkv2, at2, n3, lse2 = cross_forward(grid, inputs, encoded, at1, gains, pieces_two, d, hd)
         (own3, gone), (ya, ba, turned, turned_others) = feed_forward(
             grid, cotangent, n3, r2, gains, None, pieces_three, pieces_four, 0, d, ff, (encoded, n1, n2)
@@ -1048,7 +1053,7 @@
         kept2, far2, _ = scatter(grid, kept[0], got[0], kept[1], got[1], 7 * LANE)
         dy, off = attention_backward(grid, b1, qkv1, at1, lse1, base, pieces_two, 0, hd, "ke1")
         dx, (kept, gone) = self_finish(
-            grid, inputs, b1, turned_others, dy, off, dg2, dg3, base_hot, gains, pieces_one, d, hd, heads
+            grid, inputs, b1, turned_others, dy, off, dg2, dg3, bucket_row, gains, pieces_one, d, hd, heads
         )
         got = grid.swap_c(gone)
         kept1, far1, (kept2, bt30, y, eg) = scatter(

time: 453 us -> 452 us (level)
  no operation moved by 1% of the time
where the time goes in v5:
time: 452 us
  waiting for transfers between devices  201 us (44%)
  starting transfers between devices  116 us (26%)
  Pallas kernels  95.6 us (21%)
  local copies, waits for them, and re-layouts  24.6 us (5%)
  other arithmetic  13 us (3%)
    ppermute x78, waiting for transfers between devices, send(): return lax.ppermute(v, AXES, self.perm(move))  201 us
    ppermute x78, starting transfers between devices, send(): return lax.ppermute(v, AXES, self.perm(move))  116 us
    pallas_call x8, Pallas kernels, call(): pl.pallas_call(body, out_shape=tuple((jax.ShapeDtypeStruct(s, d) for s, d...  95.6 us
    unnamed x104, local copies, waits for them, and re-layouts  15.4 us
  transfers between devices with their start and end apart: 78, of which 23 were waited for; matrix products, arithmetic and copies ran while one was open for 5% of the time, Pallas kernels for 9%

profile of v5, /device:TPU:0, one launch (start us, length us, event | category | flops | bytes accessed | tf_op | source)
XLA Modules:
  0.0 451.7 jit_solution(11244260060576429388)
XLA Ops:
  2.2 3.0 collective-permute-start.31
  10.5 4.1 collective-permute-start.14
  17.6 3.4 collective-permute-start.12
  21.1 3.3 collective-permute-done
  24.8 14.4 %collective-permute-done.1 = bf16[48,1280]{1,0:T(8,128)(2,1)S(1)} collective-permute-done((bf16[48,1280]{1,0:T(8,128)(2,1)S(1)}, bf16[48,1280]{1,0:T(8,128)(2,1)S(1)}, u32[]{:S(2)}, u32[]{:S(2)}) %collective-permute-start.1) | collective-permute-done | bytes 122912 | tf_op jit(solution)/shard_map/ppermute | solution.py:55
  39.2 10.9 %collective-permute-start.24 = (bf16[48,2560]{1,0:T(8,128)(2,1)S(1)}, bf16[48,2560]{1,0:T(8,128)(2,1)S(1)}, u32[]{:S(2)}, u32[]{:S(2)}) collective-permute-start(bf16[48,2560]{1,0:T(8,128)(2,1)S(1)} %pad_maximum_fusion.3), channel_id=1, source_target_pairs={{0,8},{1,9},{2,10},{3,11},{4,12},{5,13},{6,14},{7,15},{8,16},{9,17... | collective-permute-start | bytes 737288 | tf_op jit(solution)/shard_map/ppermute | solution.py:55
  53.4 8.2 %collective-permute-done.24 = bf16[48,2560]{1,0:T(8,128)(2,1)S(1)} collective-permute-done((bf16[48,2560]{1,0:T(8,128)(2,1)S(1)}, bf16[48,2560]{1,0:T(8,128)(2,1)S(1)}, u32[]{:S(2)}, u32[]{:S(2)}) %collective-permute-start.24) | collective-permute-done | bytes 245792 | tf_op jit(solution)/shard_map/ppermute | solution.py:55
  61.7 8.4 %collective-permute-start.33 = (bf16[2,2,48,512]{3,2,1,0:T(8,128)(2,1)S(1)}, bf16[2,2,48,512]{3,2,1,0:T(8,128)(2,1)S(1)}, u32[]{:S(2)}, u32[]{:S(2)}) collective-permute-start(bf16[2,2,48,512]{3,2,1,0:T(8,128)(2,1)S(1)} %bitcast.243), channel_id=1, source_target_pairs={{0,8},{1,9},{2,10},{3,11},{4,12},{5,13},{6,14},{7,15},{8,16},{9,17... | collective-permute-start | bytes 589832 | tf_op jit(solution)/shard_map/ppermute | solution.py:55
  71.7 9.3 %collective-permute-done.3.refs_3_.refs_10_ = bf16[4,48,1280]{2,1,0:T(8,128)(2,1)S(1)} collective-permute-done((bf16[4,48,1280]{2,1,0:T(8,128)(2,1)S(1)}, bf16[4,48,1280]{2,1,0:T(8,128)(2,1)S(1)}, u32[]{:S(2)}, u32[]{:S(2)}) %collective-permute-start.3) | collective-permute-done | bytes 491552 | tf_op jit(solution)/shard_map/ppermute | solution.py:55
  84.6 3.0 collective-permute-done.26
  92.5 14.1 %collective-permute-done.16.refs_6_.refs_9_.refs_7_ = bf16[4,48,1920]{2,1,0:T(8,128)(2,1)S(1)} collective-permute-done((bf16[4,48,1920]{2,1,0:T(8,128)(2,1)S(1)}, bf16[4,48,1920]{2,1,0:T(8,128)(2,1)S(1)}, u32[]{:S(2)}, u32[]{:S(2)}) %collective-permute-start.16) | collective-permute-done | bytes 737312 | tf_op jit(solution)/shard_map/ppermute | solution.py:55
  111.5 26.8 %collective-permute-done.17.refs_7_.refs_10_.refs_8_ = bf16[2,48,1920]{2,1,0:T(8,128)(2,1)S(1)} collective-permute-done((bf16[2,48,1920]{2,1,0:T(8,128)(2,1)S(1)}, bf16[2,48,1920]{2,1,0:T(8,128)(2,1)S(1)}, u32[]{:S(2)}, u32[]{:S(2)}) %collective-permute-start.17) | collective-permute-done | bytes 368672 | tf_op jit(solution)/shard_map/ppermute | solution.py:55
  142.2 11.5 %shard_map.322 = (bf16[512,768]{1,0:T(8,128)(2,1)S(1)}, bf16[3,512,768]{2,1,0:T(8,128)(2,1)S(1)}, bf16[512,768]{1,0:T(8,128)(2,1)S(1)}, f32[8,768]{1,0:T(8,128)S...) custom-call(bf16[1024,768]{1,0:T(8,128)(2,1)} %refs_0_.9, s32[1,512]{1,0:T(1,128)S(1)} %bitcast.239, ...), custom_call_target="tpu_custom_call" | custom-call | flops 3000000000 | bytes 10000000 | tf_op jit(solution)/shard_map/pallas_call | solution.py:360
  154.6 14.8 %shard_map.323 = (f32[512,768]{1,0:T(8,128)S(1)}, f32[512,768]{1,0:T(8,128)S(1)}, bf16[512,768]{1,0:T(8,128)(2,1)S(1)}, bf16[3,512,768]{2,1,0:T(8,128)(2,1)S(1)}...) custom-call(bf16[1024,768]{1,0:T(8,128)(2,1)} %refs_0_.9, ...), custom_call_target="tpu_custom_call" | custom-call | flops 5000000000 | bytes 10000000 | tf_op jit(solution)/shard_map/pallas_call | solution.py:360
  171.4 13.5 %shard_map.324 = (bf16[2,4,48,3072]{3,2,1,0:T(8,128)(2,1)S(1)}, bf16[2,4,48,3072]{3,2,1,0:T(8,128)(2,1)S(1)}, f32[512,768]{1,0:T(8,128)S(1)}, f32[512,768]{1,0:T...) custom-call(bf16[1024,768]{1,0:T(8,128)(2,1)} %refs_0_.8, ...), custom_call_target="tpu_custom_call" | custom-call | flops 7500000256 | bytes 10000000 | tf_op jit(solution)/shard_map/pallas_call | solution.py:360
  189.1 13.4 %shard_map.325 = (bf16[2,4,48,3072]{3,2,1,0:T(8,128)(2,1)S(1)}, bf16[2,4,48,3072]{3,2,1,0:T(8,128)(2,1)S(1)}, bf16[512,768]{1,0:T(8,128)(2,1)S(1)}, f32[512,768]{1,0:T(8,128)S(1)}, f32[1,768]{1,0:T(1,128)S(1)}) custom-call(bf16[1024,768]{1,0:T(8,128)(2,1)} %refs_0_.8, bf16[512,768]{1,0:T(8,128)(2,1)S(1)} %get-tuple-element.67.refs_1_, ...), custom_call_target="tpu_custom_call" | custom-call | flops 7500000256 | bytes 10000000 | tf_op jit(solution)/shard_map/pallas_call | solution.py:360
  203.9 12.5 %shard_map.326.refs_3_ = bf16[3,512,768]{2,1,0:T(8,128)(2,1)S(1)} custom-call(f32[512,768]{1,0:T(8,128)S(1)} %get-tuple-element.74.refs_0_, bf16[3,512,768]{2,1,0:T(8,128)(2,1)S(1)} %get-tuple-element.77.refs_1_, bf16[512,768]{1,0:T(8,128)(2,1)S(1)} %get-tuple-element.78.refs_2_.refs_5_, f32[16,512]{1,0:T(8,128)S(1)} %get-tuple-element.79.refs_3_, ...), custom_call_target="tpu_custom_call" | custom-call | flops 3000000000 | bytes 10000000 | tf_op jit(solution)/shard_map/pallas_call | solution.py:360
  216.4 8.8 %shard_map.327 = (f32[512,768]{1,0:T(8,128)S(1)}, bf16[512,768]{1,0:T(8,128)(2,1)S(1)}, f32[1,768]{1,0:T(1,128)S(1)}, bf16[2,2,4,48,1920]{4,3,2,1,0:T(8,128)(2,1)S(1)}, bf16[2,2,4,48,1920]{4,3,2,1,0:T(8,128)(2,1)S(1)}) custom-call(f32[512,768]{1,0:T(8,128)S(1)} %get-tuple-element.74.refs_0_, f32[512,768]{1,0:T(8,128)S(1)} %get-tuple-element.75.refs_1_, ...), custom_call_target="tpu_custom_call" | custom-call | flops 5000000000 | bytes 10000000 | tf_op jit(solution)/shard_map/pallas_call | solution.py:360
  225.2 12.1 %shard_map.328 = (bf16[3,512,768]{2,1,0:T(8,128)(2,1)S(1)}, f32[16,512]{1,0:T(8,128)S(1)}) custom-call(f32[512,768]{1,0:T(8,128)S(1)} %get-tuple-element.80.refs_0_.refs_1_, bf16[3,512,768]{2,1,0:T(8,128)(2,1)S(1)} %get-tuple-element.81.refs_1_, bf16[512,768]{1,0:T(8,128)(2,1)S(1)} %get-tuple-element.65.refs_2_.refs_4_, ...), custom_call_target="tpu_custom_call" | custom-call | flops 3000000000 | bytes 10000000 | tf_op jit(solution)/shard_map/pallas_call | solution.py:360
  237.3 9.2 %shard_map.329 = (bf16[512,768]{1,0:T(8,128)(2,1)S(1)}, bf16[2,2,4,48,1280]{4,3,2,1,0:T(8,128)(2,1)S(1)}, bf16[2,2,4,48,1280]{4,3,2,1,0:T(8,128)(2,1)}) custom-call(bf16[1024,768]{1,0:T(8,128)(2,1)} %refs_0_.9, f32[512,768]{1,0:T(8,128)S(1)} %get-tuple-element.80.refs_0_.refs_1_, bf16[3,768,512]{2,1,0:T(8,128)(2,1)S(1)} %get-tuple-element.76.refs_2_, ...), custom_call_target="tpu_custom_call" | custom-call | flops 4000000000 | bytes 10000000 | tf_op jit(solution)/shard_map/pallas_call | solution.py:360
  253.0 32.8 %collective-permute-done.50 = bf16[512,768]{1,0:T(8,128)(2,1)S(1)} collective-permute-done((bf16[512,768]{1,0:T(8,128)(2,1)}, bf16[512,768]{1,0:T(8,128)(2,1)S(1)}, u32[]{:S(2)}, u32[]{:S(2)}) %collective-permute-start.50) | collective-permute-done | bytes 786464 | tf_op jit(solution)/shard_map/ppermute | solution.py:55
  287.3 1.9 maximum_convert_fusion.1
  290.3 1.6 slice_bitcast_fusion.4
  295.9 21.3 %collective-permute-done.59 = bf16[2,4,48,768]{3,2,1,0:T(8,128)(2,1)S(1)} collective-permute-done((bf16[2,4,48,768]{3,2,1,0:T(8,128)(2,1)S(1)}, bf16[2,4,48,768]{3,2,1,0:T(8,128)(2,1)S(1)}, u32[]{:S(2)}, u32[]{:S(2)}) %collective-permute-start.59) | collective-permute-done | bytes 589856 | tf_op jit(solution)/shard_map/ppermute | solution.py:55
  322.1 17.6 %collective-permute-done.48 = bf16[4,48,2304]{2,1,0:T(8,128)(2,1)S(1)} collective-permute-done((bf16[4,48,2304]{2,1,0:T(8,128)(2,1)S(1)}, bf16[4,48,2304]{2,1,0:T(8,128)(2,1)S(1)}, u32[]{:S(2)}, u32[]{:S(2)}) %collective-permute-start.48) | collective-permute-done | bytes 884768 | tf_op jit(solution)/shard_map/ppermute | solution.py:55
  340.8 5.2 %collective-permute-done.60 = bf16[4,48,768]{2,1,0:T(8,128)(2,1)S(1)} collective-permute-done((bf16[4,48,768]{2,1,0:T(8,128)(2,1)S(1)}, bf16[4,48,768]{2,1,0:T(8,128)(2,1)S(1)}, u32[]{:S(2)}, u32[]{:S(2)}) %collective-permute-start.60) | collective-permute-done | bytes 294944 | tf_op jit(solution)/shard_map/ppermute | solution.py:55
  346.0 2.5 collective-permute-start.71
  350.2 10.1 %collective-permute-done.46 = bf16[2,4,48,1024]{3,2,1,0:T(8,128)(2,1)S(1)} collective-permute-done((bf16[2,4,48,1024]{3,2,1,0:T(8,128)(2,1)S(1)}, bf16[2,4,48,1024]{3,2,1,0:T(8,128)(2,1)S(1)}, u32[]{:S(2)}, u32[]{:S(2)}) %collective-permute-start.46) | collective-permute-done | bytes 786464 | tf_op jit(solution)/shard_map/ppermute | solution.py:55
  360.3 2.5 collective-permute-start.74
  364.6 2.2 collective-permute-start.75
  366.9 3.6 collective-permute-done.74
  370.5 8.3 %collective-permute-start.68 = (bf16[48,768]{1,0:T(8,128)(2,1)S(1)}, bf16[48,768]{1,0:T(8,128)(2,1)S(1)}, u32[]{:S(2)}, u32[]{:S(2)}) collective-permute-start(bf16[48,768]{1,0:T(8,128)(2,1)S(1)} %get-tuple-element.156), channel_id=1, source_target_pairs={{0,8},{1,9},{2,10},{3,11},{4,12},{5,13},{6,14},{7,15},{8,16},{9,17... | collective-permute-start | bytes 221192 | tf_op jit(solution)/shard_map/ppermute | solution.py:55
  379.6 3.4 collective-permute-done.75
  384.5 1.9 maximum_convert_fusion
  386.4 1.9 maximum_convert_fusion.2
  389.0 5.9 %collective-permute-done.57 = bf16[4,48,1024]{2,1,0:T(8,128)(2,1)S(1)} collective-permute-done((bf16[4,48,1024]{2,1,0:T(8,128)(2,1)S(1)}, bf16[4,48,1024]{2,1,0:T(8,128)(2,1)S(1)}, u32[]{:S(2)}, u32[]{:S(2)}) %collective-permute-start.57) | collective-permute-done | bytes 393248 | tf_op jit(solution)/shard_map/ppermute | solution.py:55
  396.0 6.6 %collective-permute-done.52 = bf16[2,4,48,640]{3,2,1,0:T(8,128)(2,1)S(1)} collective-permute-done((bf16[2,4,48,640]{3,2,1,0:T(8,128)(2,1)S(1)}, bf16[2,4,48,640]{3,2,1,0:T(8,128)(2,1)S(1)}, u32[]{:S(2)}, u32[]{:S(2)}) %collective-permute-start.52) | collective-permute-done | bytes 491552 | tf_op jit(solution)/shard_map/ppermute | solution.py:55
  402.6 2.3 collective-permute-done.54
  407.6 3.9 collective-permute-done.53
  411.5 2.5 collective-permute-start.70
  414.3 3.0 collective-permute-start.72
  417.3 2.7 collective-permute-start.77
  420.0 1.8 collective-permute-done.69
  421.8 8.8 %collective-permute-start.67 = (bf16[48,1920]{1,0:T(8,128)(2,1)S(1)}, bf16[48,1920]{1,0:T(8,128)(2,1)S(1)}, u32[]{:S(2)}, u32[]{:S(2)}) collective-permute-start(bf16[48,1920]{1,0:T(8,128)(2,1)S(1)} %pad_maximum_fusion.9), channel_id=1, source_target_pairs={{0,24},{1,25},{2,26},{3,27},{4,28},{5,29},{6,30},{7,31},{8,0},{9,1... | collective-permute-start | bytes 552968 | tf_op jit(solution)/shard_map/ppermute | solution.py:55
  431.2 6.2 %collective-permute-start.62 = (bf16[48,1280]{1,0:T(8,128)(2,1)S(1)}, bf16[48,1280]{1,0:T(8,128)(2,1)S(1)}, u32[]{:S(2)}, u32[]{:S(2)}) collective-permute-start(bf16[48,1280]{1,0:T(8,128)(2,1)S(1)} %pad_maximum_fusion.10), channel_id=1, source_target_pairs={{0,8},{1,9},{2,10},{3,11},{4,12},{5,13},{6,14},{7,15},{8,16},{9,17... | collective-permute-start | bytes 368648 | tf_op jit(solution)/shard_map/ppermute | solution.py:55
  437.4 3.4 collective-permute-start.63
  441.8 2.4 collective-permute-start.64
  445.0 4.6 %collective-permute-done.63 = bf16[48,1280]{1,0:T(8,128)(2,1)S(1)} collective-permute-done((bf16[48,1280]{1,0:T(8,128)(2,1)S(1)}, bf16[48,1280]{1,0:T(8,128)(2,1)S(1)}, u32[]{:S(2)}, u32[]{:S(2)}) %collective-permute-start.63) | collective-permute-done | bytes 122912 | tf_op jit(solution)/shard_map/ppermute | solution.py:55
  (294 shorter events, 74.7 us)
Async XLA Ops:
  10.5 41.3 %collective-permute-start.14 = (bf16[48,1920]{1,0:T(8,128)(2,1)S(1)}, bf16[48,1920]{1,0:T(8,128)(2,1)S(1)}, u32[]{:S(2)}, u32[]{:S(2)}) collective-permute-start(bf16[48,1920]{1,0:T(8,128)(2,1)S(1)} %bitcast_dynamic-update-slice_fusion.12), channel_id=1, source_target_pairs={{0,24},{1,25},{2,26},{3,27},{4,28},{5,29},{6,30},{7,31},{8,0},{9,1... | collective-permute-start | bytes 552968 | tf_op jit(solution)/shard_map/ppermute | solution.py:55
  16.6 33.7 %collective-permute-start.13 = (bf16[48,1920]{1,0:T(8,128)(2,1)S(1)}, bf16[48,1920]{1,0:T(8,128)(2,1)S(1)}, u32[]{:S(2)}, u32[]{:S(2)}) collective-permute-start(bf16[48,1920]{1,0:T(8,128)(2,1)S(1)} %bitcast_dynamic-update-slice_fusion.12), channel_id=1, source_target_pairs={{0,16},{1,17},{2,18},{3,19},{4,20},{5,21},{6,22},{7,23},{8,24},{9,... | collective-permute-start | bytes 552968 | tf_op jit(solution)/shard_map/ppermute | solution.py:55
  17.6 32.5 %collective-permute-start.12 = (bf16[48,1920]{1,0:T(8,128)(2,1)S(1)}, bf16[48,1920]{1,0:T(8,128)(2,1)S(1)}, u32[]{:S(2)}, u32[]{:S(2)}) collective-permute-start(bf16[48,1920]{1,0:T(8,128)(2,1)S(1)} %bitcast_dynamic-update-slice_fusion.12), channel_id=1, source_target_pairs={{0,8},{1,9},{2,10},{3,11},{4,12},{5,13},{6,14},{7,15},{8,16},{9,17... | collective-permute-start | bytes 552968 | tf_op jit(solution)/shard_map/ppermute | solution.py:55
  21.0 18.2 %collective-permute-start.1 = (bf16[48,1280]{1,0:T(8,128)(2,1)S(1)}, bf16[48,1280]{1,0:T(8,128)(2,1)S(1)}, u32[]{:S(2)}, u32[]{:S(2)}) collective-permute-start(bf16[48,1280]{1,0:T(8,128)(2,1)S(1)} %get-tuple-element.116), channel_id=1, source_target_pairs={{0,16},{1,17},{2,18},{3,19},{4,20},{5,21},{6,22},{7,23},{8,24},{9,... | collective-permute-start | bytes 368648 | tf_op jit(solution)/shard_map/ppermute | solution.py:55
  39.2 43.9 %collective-permute-start.25 = (bf16[48,2560]{1,0:T(8,128)(2,1)S(1)}, bf16[48,2560]{1,0:T(8,128)(2,1)S(1)}, u32[]{:S(2)}, u32[]{:S(2)}) collective-permute-start(bf16[48,2560]{1,0:T(8,128)(2,1)S(1)} %pad_maximum_fusion.3), channel_id=1, source_target_pairs={{0,16},{1,17},{2,18},{3,19},{4,20},{5,21},{6,22},{7,23},{8,24},{9,... | collective-permute-start | bytes 737288 | tf_op jit(solution)/shard_map/ppermute | solution.py:55
  39.2 22.4 %collective-permute-start.24 = (bf16[48,2560]{1,0:T(8,128)(2,1)S(1)}, bf16[48,2560]{1,0:T(8,128)(2,1)S(1)}, u32[]{:S(2)}, u32[]{:S(2)}) collective-permute-start(bf16[48,2560]{1,0:T(8,128)(2,1)S(1)} %pad_maximum_fusion.3), channel_id=1, source_target_pairs={{0,8},{1,9},{2,10},{3,11},{4,12},{5,13},{6,14},{7,15},{8,16},{9,17... | collective-permute-start | bytes 737288 | tf_op jit(solution)/shard_map/ppermute | solution.py:55
  50.2 30.8 %collective-permute-start.35 = (bf16[2,2,48,512]{3,2,1,0:T(8,128)(2,1)S(1)}, bf16[2,2,48,512]{3,2,1,0:T(8,128)(2,1)S(1)}, u32[]{:S(2)}, u32[]{:S(2)}) collective-permute-start(bf16[2,2,48,512]{3,2,1,0:T(8,128)(2,1)S(1)} %bitcast.241), channel_id=1, source_target_pairs={{0,24},{1,25},{2,26},{3,27},{4,28},{5,29},{6,30},{7,31},{8,0},{9,1... | collective-permute-start | bytes 589832 | tf_op jit(solution)/shard_map/ppermute | solution.py:55
  50.3 19.8 %collective-permute-start.4 = (bf16[4,48,1280]{2,1,0:T(8,128)(2,1)S(1)}, bf16[4,48,1280]{2,1,0:T(8,128)(2,1)S(1)}, u32[]{:S(2)}, u32[]{:S(2)}) collective-permute-start(bf16[4,48,1280]{2,1,0:T(8,128)(2,1)S(1)} %bitcast_dynamic-update-slice_fusion.8.refs_2_.refs_9_), channel_id=1, source_target_pairs={{0,1},{1,0},{2,3},{3,2},{4,5},{5,4},{6,7},{7,6},{8,9},{9,8},{10,11... | collective-permute-start | bytes 1474568 | tf_op jit(solution)/shard_map/ppermute | solution.py:55
  51.9 29.2 %collective-permute-start.34 = (bf16[2,2,48,512]{3,2,1,0:T(8,128)(2,1)S(1)}, bf16[2,2,48,512]{3,2,1,0:T(8,128)(2,1)S(1)}, u32[]{:S(2)}, u32[]{:S(2)}) collective-permute-start(bf16[2,2,48,512]{3,2,1,0:T(8,128)(2,1)S(1)} %bitcast.242), channel_id=1, source_target_pairs={{0,16},{1,17},{2,18},{3,19},{4,20},{5,21},{6,22},{7,23},{8,24},{9,... | collective-permute-start | bytes 589832 | tf_op jit(solution)/shard_map/ppermute | solution.py:55
  61.7 19.9 %collective-permute-start.33 = (bf16[2,2,48,512]{3,2,1,0:T(8,128)(2,1)S(1)}, bf16[2,2,48,512]{3,2,1,0:T(8,128)(2,1)S(1)}, u32[]{:S(2)}, u32[]{:S(2)}) collective-permute-start(bf16[2,2,48,512]{3,2,1,0:T(8,128)(2,1)S(1)} %bitcast.243), channel_id=1, source_target_pairs={{0,8},{1,9},{2,10},{3,11},{4,12},{5,13},{6,14},{7,15},{8,16},{9,17... | collective-permute-start | bytes 589832 | tf_op jit(solution)/shard_map/ppermute | solution.py:55
  87.6 19.0 %collective-permute-start.16 = (bf16[4,48,1920]{2,1,0:T(8,128)(2,1)S(1)}, bf16[4,48,1920]{2,1,0:T(8,128)(2,1)S(1)}, u32[]{:S(2)}, u32[]{:S(2)}) collective-permute-start(bf16[4,48,1920]{2,1,0:T(8,128)(2,1)S(1)} %bitcast_dynamic-update-slice_fusion.4.refs_4_.refs_7_.refs_5_), channel_id=1, source_target_pairs={{0,1},{1,0},{2,3},{3,2},{4,5},{5,4},{6,7},{7,6},{8,9},{9,8},{10,11... | collective-permute-start | bytes 2211848 | tf_op jit(solution)/shard_map/ppermute | solution.py:55
  89.3 18.8 %collective-permute-start.15 = (bf16[4,48,1920]{2,1,0:T(8,128)(2,1)S(1)}, bf16[4,48,1920]{2,1,0:T(8,128)(2,1)S(1)}, u32[]{:S(2)}, u32[]{:S(2)}) collective-permute-start(bf16[4,48,1920]{2,1,0:T(8,128)(2,1)S(1)} %bitcast_dynamic-update-slice_fusion.4.refs_4_.refs_7_.refs_5_), channel_id=1, source_target_pairs={{0,4},{1,5},{2,6},{3,7},{4,0},{5,1},{6,2},{7,3},{8,12},{9,13},{10,... | collective-permute-start | bytes 2211848 | tf_op jit(solution)/shard_map/ppermute | solution.py:55
  90.9 17.7 %collective-permute-start.36 = (bf16[4,2,2,48,512]{4,3,2,1,0:T(8,128)(2,1)S(1)}, bf16[4,2,2,48,512]{4,3,2,1,0:T(8,128)(2,1)S(1)}, u32[]{:S(2)}, u32[]{:S(2)}) collective-permute-start(bf16[4,2,2,48,512]{4,3,2,1,0:T(8,128)(2,1)S(1)} %pad_maximum_fusion.refs_9_.refs_13_), channel_id=1, source_target_pairs={{0,2},{1,3},{2,0},{3,1},{4,6},{5,7},{6,4},{7,5},{8,10},{9,11},{10,... | collective-permute-start | bytes 2359304 | tf_op jit(solution)/shard_map/ppermute | solution.py:55
  91.9 16.7 %collective-permute-start.9 = (bf16[4,48,1280]{2,1,0:T(8,128)(2,1)S(1)}, bf16[4,48,1280]{2,1,0:T(8,128)(2,1)S(1)}, u32[]{:S(2)}, u32[]{:S(2)}) collective-permute-start(bf16[4,48,1280]{2,1,0:T(8,128)(2,1)S(1)} %collective-permute-done.4.refs_4_.refs_11_), channel_id=1, source_target_pairs={{0,2},{1,3},{2,0},{3,1},{4,6},{5,7},{6,4},{7,5},{8,10},{9,11},{10,... | collective-permute-start | bytes 1474568 | tf_op jit(solution)/shard_map/ppermute | solution.py:55
  92.0 17.2 %collective-permute-start.8 = (bf16[4,48,1280]{2,1,0:T(8,128)(2,1)S(1)}, bf16[4,48,1280]{2,1,0:T(8,128)(2,1)S(1)}, u32[]{:S(2)}, u32[]{:S(2)}) collective-permute-start(bf16[4,48,1280]{2,1,0:T(8,128)(2,1)S(1)} %collective-permute-done.3.refs_3_.refs_10_), channel_id=1, source_target_pairs={{0,2},{1,3},{2,0},{3,1},{4,6},{5,7},{6,4},{7,5},{8,10},{9,11},{10,... | collective-permute-start | bytes 1474568 | tf_op jit(solution)/shard_map/ppermute | solution.py:55
  106.6 31.7 %collective-permute-start.37 = (bf16[4,48,2560]{2,1,0:T(8,128)(2,1)S(1)}, bf16[4,48,2560]{2,1,0:T(8,128)(2,1)S(1)}, u32[]{:S(2)}, u32[]{:S(2)}) collective-permute-start(bf16[4,48,2560]{2,1,0:T(8,128)(2,1)S(1)} %bitcast_dynamic-update-slice_fusion.refs_5_), channel_id=1, source_target_pairs={{0,1},{1,0},{2,3},{3,2},{4,5},{5,4},{6,7},{7,6},{8,9},{9,8},{10,11... | collective-permute-start | bytes 2949128 | tf_op jit(solution)/shard_map/ppermute | solution.py:55
  108.1 30.8 %collective-permute-start.27 = (bf16[4,48,2560]{2,1,0:T(8,128)(2,1)S(1)}, bf16[4,48,2560]{2,1,0:T(8,128)(2,1)S(1)}, u32[]{:S(2)}, u32[]{:S(2)}) collective-permute-start(bf16[4,48,2560]{2,1,0:T(8,128)(2,1)S(1)} %bitcast_dynamic-update-slice_fusion.refs_5_), channel_id=1, source_target_pairs={{0,4},{1,5},{2,6},{3,7},{4,0},{5,1},{6,2},{7,3},{8,12},{9,13},{10,... | collective-permute-start | bytes 2949128 | tf_op jit(solution)/shard_map/ppermute | solution.py:55
  109.2 29.1 %collective-permute-start.17 = (bf16[2,48,1920]{2,1,0:T(8,128)(2,1)S(1)}, bf16[2,48,1920]{2,1,0:T(8,128)(2,1)S(1)}, u32[]{:S(2)}, u32[]{:S(2)}) collective-permute-start(bf16[2,48,1920]{2,1,0:T(8,128)(2,1)S(1)} %slice.627), channel_id=1, source_target_pairs={{0,4},{1,5},{2,6},{3,7},{4,0},{5,1},{6,2},{7,3},{8,12},{9,13},{10,... | collective-permute-start | bytes 1105928 | tf_op jit(solution)/shard_map/ppermute | solution.py:55
  110.8 29.4 %collective-permute-start.21 = (bf16[4,48,1920]{2,1,0:T(8,128)(2,1)S(1)}, bf16[4,48,1920]{2,1,0:T(8,128)(2,1)S(1)}, u32[]{:S(2)}, u32[]{:S(2)}) collective-permute-start(bf16[4,48,1920]{2,1,0:T(8,128)(2,1)S(1)} %collective-permute-done.16.refs_6_.refs_9_.refs_7_), channel_id=1, source_target_pairs={{0,2},{1,3},{2,0},{3,1},{4,6},{5,7},{6,4},{7,5},{8,10},{9,11},{10,... | collective-permute-start | bytes 2211848 | tf_op jit(solution)/shard_map/ppermute | solution.py:55
  110.9 27.9 %collective-permute-start.18 = (bf16[2,48,1920]{2,1,0:T(8,128)(2,1)S(1)}, bf16[2,48,1920]{2,1,0:T(8,128)(2,1)S(1)}, u32[]{:S(2)}, u32[]{:S(2)}) collective-permute-start(bf16[2,48,1920]{2,1,0:T(8,128)(2,1)S(1)} %slice.628), channel_id=1, source_target_pairs={{0,1},{1,0},{2,3},{3,2},{4,5},{5,4},{6,7},{7,6},{8,9},{9,8},{10,11... | collective-permute-start | bytes 1105928 | tf_op jit(solution)/shard_map/ppermute | solution.py:55
  138.9 31.1 %collective-permute-start.28 = (bf16[4,48,2560]{2,1,0:T(8,128)(2,1)S(1)}, bf16[4,48,2560]{2,1,0:T(8,128)(2,1)S(1)}, u32[]{:S(2)}, u32[]{:S(2)}) collective-permute-start(bf16[4,48,2560]{2,1,0:T(8,128)(2,1)S(1)} %bitcast_dynamic-update-slice_fusion.refs_5_), channel_id=1, source_target_pairs={{0,2},{1,3},{2,0},{3,1},{4,6},{5,7},{6,4},{7,5},{8,10},{9,11},{10,... | collective-permute-start | bytes 2949128 | tf_op jit(solution)/shard_map/ppermute | solution.py:55
  140.0 30.1 %collective-permute-start.29 = (bf16[4,48,2560]{2,1,0:T(8,128)(2,1)S(1)}, bf16[4,48,2560]{2,1,0:T(8,128)(2,1)S(1)}, u32[]{:S(2)}, u32[]{:S(2)}) collective-permute-start(bf16[4,48,2560]{2,1,0:T(8,128)(2,1)S(1)} %collective-permute-done.27.refs_6_), channel_id=1, source_target_pairs={{0,2},{1,3},{2,0},{3,1},{4,6},{5,7},{6,4},{7,5},{8,10},{9,11},{10,... | collective-permute-start | bytes 2949128 | tf_op jit(solution)/shard_map/ppermute | solution.py:55
  140.3 29.2 %collective-permute-start.38 = (bf16[2,48,2560]{2,1,0:T(8,128)(2,1)S(1)}, bf16[2,48,2560]{2,1,0:T(8,128)(2,1)S(1)}, u32[]{:S(2)}, u32[]{:S(2)}) collective-permute-start(bf16[2,48,2560]{2,1,0:T(8,128)(2,1)S(1)} %slice.631), channel_id=1, source_target_pairs={{0,4},{1,5},{2,6},{3,7},{4,0},{5,1},{6,2},{7,3},{8,12},{9,13},{10,... | collective-permute-start | bytes 1474568 | tf_op jit(solution)/shard_map/ppermute | solution.py:55
  141.6 28.0 %collective-permute-start.39 = (bf16[2,48,2560]{2,1,0:T(8,128)(2,1)S(1)}, bf16[2,48,2560]{2,1,0:T(8,128)(2,1)S(1)}, u32[]{:S(2)}, u32[]{:S(2)}) collective-permute-start(bf16[2,48,2560]{2,1,0:T(8,128)(2,1)S(1)} %slice.632), channel_id=1, source_target_pairs={{0,1},{1,0},{2,3},{3,2},{4,5},{5,4},{6,7},{7,6},{8,9},{9,8},{10,11... | collective-permute-start | bytes 1474568 | tf_op jit(solution)/shard_map/ppermute | solution.py:55
  153.8 34.0 %collective-permute-start.40 = (bf16[4,48,2560]{2,1,0:T(8,128)(2,1)S(1)}, bf16[4,48,2560]{2,1,0:T(8,128)(2,1)S(1)}, u32[]{:S(2)}, u32[]{:S(2)}) collective-permute-start(bf16[4,48,2560]{2,1,0:T(8,128)(2,1)S(1)} %collective-permute-done.37.refs_7_), channel_id=1, source_target_pairs={{0,2},{1,3},{2,0},{3,1},{4,6},{5,7},{6,4},{7,5},{8,10},{9,11},{10,... | collective-permute-start | bytes 2949128 | tf_op jit(solution)/shard_map/ppermute | solution.py:55
  169.5 18.3 %collective-permute-start.41 = (bf16[2,48,2560]{2,1,0:T(8,128)(2,1)S(1)}, bf16[2,48,2560]{2,1,0:T(8,128)(2,1)S(1)}, u32[]{:S(2)}, u32[]{:S(2)}) collective-permute-start(bf16[2,48,2560]{2,1,0:T(8,128)(2,1)S(1)} %collective-permute-done.38.refs_8_), channel_id=1, source_target_pairs={{0,2},{1,3},{2,0},{3,1},{4,6},{5,7},{6,4},{7,5},{8,10},{9,11},{10,... | collective-permute-start | bytes 1474568 | tf_op jit(solution)/shard_map/ppermute | solution.py:55
  169.6 18.2 %collective-permute-start.42 = (bf16[2,48,2560]{2,1,0:T(8,128)(2,1)S(1)}, bf16[2,48,2560]{2,1,0:T(8,128)(2,1)S(1)}, u32[]{:S(2)}, u32[]{:S(2)}) collective-permute-start(bf16[2,48,2560]{2,1,0:T(8,128)(2,1)S(1)} %collective-permute-done.39.refs_9_), channel_id=1, source_target_pairs={{0,2},{1,3},{2,0},{3,1},{4,6},{5,7},{6,4},{7,5},{8,10},{9,11},{10,... | collective-permute-start | bytes 1474568 | tf_op jit(solution)/shard_map/ppermute | solution.py:55
  248.6 40.6 %collective-permute-start.43 = (bf16[2,2,4,48,1280]{4,3,2,1,0:T(8,128)(2,1)}, bf16[2,2,4,48,1280]{4,3,2,1,0:T(8,128)(2,1)}, u32[]{:S(2)}, u32[]{:S(2)}) collective-permute-start(bf16[2,2,4,48,1280]{4,3,2,1,0:T(8,128)(2,1)} %get-tuple-element.89), channel_id=1, source_target_pairs={{0,2},{1,3},{2,0},{3,1},{4,6},{5,7},{6,4},{7,5},{8,10},{9,11},{10,... | collective-permute-start | bytes 5898248 | tf_op jit(solution)/shard_map/ppermute | solution.py:55
  248.8 43.5 %collective-permute-start.58 = (bf16[2,4,48,3072]{3,2,1,0:T(8,128)(2,1)}, bf16[2,4,48,3072]{3,2,1,0:T(8,128)(2,1)S(1)}, u32[]{:S(2)}, u32[]{:S(2)}) collective-permute-start(bf16[2,4,48,3072]{3,2,1,0:T(8,128)(2,1)} %copy-done.13), channel_id=1, source_target_pairs={{0,2},{1,3},{2,0},{3,1},{4,6},{5,7},{6,4},{7,5},{8,10},{9,11},{10,... | collective-permute-start | bytes 7077896 | tf_op jit(solution)/shard_map/ppermute | solution.py:55
  249.1 114.0 %collective-permute-start.49 = (bf16[512,768]{1,0:T(8,128)(2,1)}, bf16[512,768]{1,0:T(8,128)(2,1)S(1)}, u32[]{:S(2)}, u32[]{:S(2)}) collective-permute-start(bf16[512,768]{1,0:T(8,128)(2,1)} %copy-done.5), channel_id=1, source_target_pairs={{0,1},{1,0},{2,3},{3,2},{4,5},{5,4},{6,7},{7,6},{8,9},{9,8},{10,11... | collective-permute-start | bytes 2359304 | tf_op jit(solution)/shard_map/ppermute | solution.py:55
  250.6 44.2 %collective-permute-start.47 = (bf16[2,4,48,3072]{3,2,1,0:T(8,128)(2,1)}, bf16[2,4,48,3072]{3,2,1,0:T(8,128)(2,1)S(1)}, u32[]{:S(2)}, u32[]{:S(2)}) collective-permute-start(bf16[2,4,48,3072]{3,2,1,0:T(8,128)(2,1)} %copy-done.14), channel_id=1, source_target_pairs={{0,2},{1,3},{2,0},{3,1},{4,6},{5,7},{6,4},{7,5},{8,10},{9,11},{10,... | collective-permute-start | bytes 7077896 | tf_op jit(solution)/shard_map/ppermute | solution.py:55
  250.6 35.2 %collective-permute-start.50 = (bf16[512,768]{1,0:T(8,128)(2,1)}, bf16[512,768]{1,0:T(8,128)(2,1)S(1)}, u32[]{:S(2)}, u32[]{:S(2)}) collective-permute-start(bf16[512,768]{1,0:T(8,128)(2,1)} %copy-done.9), channel_id=1, source_target_pairs={{0,1},{1,0},{2,3},{3,2},{4,5},{5,4},{6,7},{7,6},{8,9},{9,8},{10,11... | collective-permute-start | bytes 2359304 | tf_op jit(solution)/shard_map/ppermute | solution.py:55
  285.8 78.8 %collective-permute-start.51 = (bf16[512,768]{1,0:T(8,128)(2,1)S(1)}, bf16[512,768]{1,0:T(8,128)(2,1)S(1)}, u32[]{:S(2)}, u32[]{:S(2)}) collective-permute-start(bf16[512,768]{1,0:T(8,128)(2,1)S(1)} %copy-done.8), channel_id=1, source_target_pairs={{0,1},{1,0},{2,3},{3,2},{4,5},{5,4},{6,7},{7,6},{8,9},{9,8},{10,11... | collective-permute-start | bytes 2359304 | tf_op jit(solution)/shard_map/ppermute | solution.py:55
  290.3 27.9 %collective-permute-start.44 = (bf16[2,2,4,48,1920]{4,3,2,1,0:T(8,128)(2,1)S(1)}, bf16[2,2,4,48,1920]{4,3,2,1,0:T(8,128)(2,1)S(1)}, u32[]{:S(2)}, u32[]{:S(2)}) collective-permute-start(bf16[2,2,4,48,1920]{4,3,2,1,0:T(8,128)(2,1)S(1)} %copy-done.12), channel_id=1, source_target_pairs={{0,2},{1,3},{2,0},{3,1},{4,6},{5,7},{6,4},{7,5},{8,10},{9,11},{10,... | collective-permute-start | bytes 8847368 | tf_op jit(solution)/shard_map/ppermute | solution.py:55
  293.9 26.4 %collective-permute-start.61 = (bf16[4,48,2304]{2,1,0:T(8,128)(2,1)S(1)}, bf16[4,48,2304]{2,1,0:T(8,128)(2,1)S(1)}, u32[]{:S(2)}, u32[]{:S(2)}) collective-permute-start(bf16[4,48,2304]{2,1,0:T(8,128)(2,1)S(1)} %fusion.1), channel_id=1, source_target_pairs={{0,4},{1,5},{2,6},{3,7},{4,0},{5,1},{6,2},{7,3},{8,12},{9,13},{10,... | collective-permute-start | bytes 2654216 | tf_op jit(solution)/shard_map/ppermute | solution.py:55
  294.9 22.2 %collective-permute-start.59 = (bf16[2,4,48,768]{3,2,1,0:T(8,128)(2,1)S(1)}, bf16[2,4,48,768]{3,2,1,0:T(8,128)(2,1)S(1)}, u32[]{:S(2)}, u32[]{:S(2)}) collective-permute-start(bf16[2,4,48,768]{3,2,1,0:T(8,128)(2,1)S(1)} %add_convert_fusion.3), channel_id=1, source_target_pairs={{0,1},{1,0},{2,3},{3,2},{4,5},{5,4},{6,7},{7,6},{8,9},{9,8},{10,11... | collective-permute-start | bytes 1769480 | tf_op jit(solution)/shard_map/ppermute | solution.py:55
  317.2 22.5 %collective-permute-start.48 = (bf16[4,48,2304]{2,1,0:T(8,128)(2,1)S(1)}, bf16[4,48,2304]{2,1,0:T(8,128)(2,1)S(1)}, u32[]{:S(2)}, u32[]{:S(2)}) collective-permute-start(bf16[4,48,2304]{2,1,0:T(8,128)(2,1)S(1)} %fusion), channel_id=1, source_target_pairs={{0,4},{1,5},{2,6},{3,7},{4,0},{5,1},{6,2},{7,3},{8,12},{9,13},{10,... | collective-permute-start | bytes 2654216 | tf_op jit(solution)/shard_map/ppermute | solution.py:55
  318.3 27.8 %collective-permute-start.60 = (bf16[4,48,768]{2,1,0:T(8,128)(2,1)S(1)}, bf16[4,48,768]{2,1,0:T(8,128)(2,1)S(1)}, u32[]{:S(2)}, u32[]{:S(2)}) collective-permute-start(bf16[4,48,768]{2,1,0:T(8,128)(2,1)S(1)} %get-tuple-element.126), channel_id=1, source_target_pairs={{0,4},{1,5},{2,6},{3,7},{4,0},{5,1},{6,2},{7,3},{8,12},{9,13},{10,... | collective-permute-start | bytes 884744 | tf_op jit(solution)/shard_map/ppermute | solution.py:55
  320.3 28.3 %collective-permute-start.45 = (bf16[2,4,48,896]{3,2,1,0:T(8,128)(2,1)S(1)}, bf16[2,4,48,896]{3,2,1,0:T(8,128)(2,1)S(1)}, u32[]{:S(2)}, u32[]{:S(2)}) collective-permute-start(bf16[2,4,48,896]{3,2,1,0:T(8,128)(2,1)S(1)} %add_convert_fusion.2), channel_id=1, source_target_pairs={{0,1},{1,0},{2,3},{3,2},{4,5},{5,4},{6,7},{7,6},{8,9},{9,8},{10,11... | collective-permute-start | bytes 2064392 | tf_op jit(solution)/shard_map/ppermute | solution.py:55
  339.7 20.6 %collective-permute-start.46 = (bf16[2,4,48,1024]{3,2,1,0:T(8,128)(2,1)S(1)}, bf16[2,4,48,1024]{3,2,1,0:T(8,128)(2,1)S(1)}, u32[]{:S(2)}, u32[]{:S(2)}) collective-permute-start(bf16[2,4,48,1024]{3,2,1,0:T(8,128)(2,1)S(1)} %pad_maximum_fusion.1), channel_id=1, source_target_pairs={{0,4},{1,5},{2,6},{3,7},{4,0},{5,1},{6,2},{7,3},{8,12},{9,13},{10,... | collective-permute-start | bytes 2359304 | tf_op jit(solution)/shard_map/ppermute | solution.py:55
  346.0 75.8 %collective-permute-start.71 = (bf16[48,2304]{1,0:T(8,128)(2,1)S(1)}, bf16[48,2304]{1,0:T(8,128)(2,1)S(1)}, u32[]{:S(2)}, u32[]{:S(2)}) collective-permute-start(bf16[48,2304]{1,0:T(8,128)(2,1)S(1)} %get-tuple-element.117), channel_id=1, source_target_pairs={{0,8},{1,9},{2,10},{3,11},{4,12},{5,13},{6,14},{7,15},{8,16},{9,17... | collective-permute-start | bytes 663560 | tf_op jit(solution)/shard_map/ppermute | solution.py:55
  348.6 82.0 %collective-permute-start.73 = (bf16[48,2304]{1,0:T(8,128)(2,1)S(1)}, bf16[48,2304]{1,0:T(8,128)(2,1)S(1)}, u32[]{:S(2)}, u32[]{:S(2)}) collective-permute-start(bf16[48,2304]{1,0:T(8,128)(2,1)S(1)} %get-tuple-element.118), channel_id=1, source_target_pairs={{0,24},{1,25},{2,26},{3,27},{4,28},{5,29},{6,30},{7,31},{8,0},{9,1... | collective-permute-start | bytes 663560 | tf_op jit(solution)/shard_map/ppermute | solution.py:55
  364.6 18.4 %collective-permute-start.75 = (bf16[48,2304]{1,0:T(8,128)(2,1)S(1)}, bf16[48,2304]{1,0:T(8,128)(2,1)S(1)}, u32[]{:S(2)}, u32[]{:S(2)}) collective-permute-start(bf16[48,2304]{1,0:T(8,128)(2,1)S(1)} %get-tuple-element.123), channel_id=1, source_target_pairs={{0,16},{1,17},{2,18},{3,19},{4,20},{5,21},{6,22},{7,23},{8,24},{9,... | collective-permute-start | bytes 663560 | tf_op jit(solution)/shard_map/ppermute | solution.py:55
  370.5 43.8 %collective-permute-start.68 = (bf16[48,768]{1,0:T(8,128)(2,1)S(1)}, bf16[48,768]{1,0:T(8,128)(2,1)S(1)}, u32[]{:S(2)}, u32[]{:S(2)}) collective-permute-start(bf16[48,768]{1,0:T(8,128)(2,1)S(1)} %get-tuple-element.156), channel_id=1, source_target_pairs={{0,8},{1,9},{2,10},{3,11},{4,12},{5,13},{6,14},{7,15},{8,16},{9,17... | collective-permute-start | bytes 221192 | tf_op jit(solution)/shard_map/ppermute | solution.py:55
  414.3 16.9 %collective-permute-start.72 = (bf16[48,2304]{1,0:T(8,128)(2,1)S(1)}, bf16[48,2304]{1,0:T(8,128)(2,1)S(1)}, u32[]{:S(2)}, u32[]{:S(2)}) collective-permute-start(bf16[48,2304]{1,0:T(8,128)(2,1)S(1)} %get-tuple-element.119), channel_id=1, source_target_pairs={{0,16},{1,17},{2,18},{3,19},{4,20},{5,21},{6,22},{7,23},{8,24},{9,... | collective-permute-start | bytes 663560 | tf_op jit(solution)/shard_map/ppermute | solution.py:55
  417.3 20.2 %collective-permute-start.77 = (bf16[48,2304]{1,0:T(8,128)(2,1)S(1)}, bf16[48,2304]{1,0:T(8,128)(2,1)S(1)}, u32[]{:S(2)}, u32[]{:S(2)}) collective-permute-start(bf16[48,2304]{1,0:T(8,128)(2,1)S(1)} %add_convert_fusion.19), channel_id=1, source_target_pairs={{0,1},{1,0},{2,3},{3,2},{4,5},{5,4},{6,7},{7,6},{8,9},{9,8},{10,11... | collective-permute-start | bytes 663560 | tf_op jit(solution)/shard_map/ppermute | solution.py:55
  421.7 20.0 %collective-permute-start.66 = (bf16[48,1920]{1,0:T(8,128)(2,1)S(1)}, bf16[48,1920]{1,0:T(8,128)(2,1)S(1)}, u32[]{:S(2)}, u32[]{:S(2)}) collective-permute-start(bf16[48,1920]{1,0:T(8,128)(2,1)S(1)} %pad_maximum_fusion.8), channel_id=1, source_target_pairs={{0,16},{1,17},{2,18},{3,19},{4,20},{5,21},{6,22},{7,23},{8,24},{9,... | collective-permute-start | bytes 552968 | tf_op jit(solution)/shard_map/ppermute | solution.py:55
  421.8 22.4 %collective-permute-start.67 = (bf16[48,1920]{1,0:T(8,128)(2,1)S(1)}, bf16[48,1920]{1,0:T(8,128)(2,1)S(1)}, u32[]{:S(2)}, u32[]{:S(2)}) collective-permute-start(bf16[48,1920]{1,0:T(8,128)(2,1)S(1)} %pad_maximum_fusion.9), channel_id=1, source_target_pairs={{0,24},{1,25},{2,26},{3,27},{4,28},{5,29},{6,30},{7,31},{8,0},{9,1... | collective-permute-start | bytes 552968 | tf_op jit(solution)/shard_map/ppermute | solution.py:55
  (80 other events, 1365.4 us)
